TPU v7x, 32 devices: a whole 2x2x4 slice. The times are simulated.
32 devices in a mesh: seq: 8 (over z, y), ctx: 4 (over x, core).
Axes of the slice: x: 2, y: 2, z: 4, core: 2. Of those that a mesh axis runs over, the one named last changes fastest.
Arguments:
- inputs: bfloat16 [8, 1024, 1536], P('seq', 'ctx'), may hold values from -6 to 6
- cotangent: bfloat16 [8, 1024, 1536], P('seq', 'ctx'), may hold values from -6 to 6
- segment_ids: int32 [8, 1024], P('seq'), may hold values from 0 to 2, never falling along the last dimension, each value on 1 to 512 neighbouring positions
- expert_ids: int32 [8, 1024, 8], P('seq', 'ctx'), may hold values from 0 to 15, all different within a row; in each aligned block of 256 rows (0 to 255, 256 to 511, ..., all dimensions but the last counted through in order) at most 128 rows name the same one
- adapter_ids: int32 [8], replicated, may hold values from 0 to 7
- gain_one: float32 [1536], replicated, may hold values from 0.25 to 1.75
- w_qkv: bfloat16 [1536, 2560], P('seq'), may hold values from -0.21875 to 0.21875
- w_out: bfloat16 [1536, 1536], P('seq'), may hold values from -0.625 to 0.625
- gain_two: float32 [1536], replicated, may hold values from 0.25 to 1.75
- router: bfloat16 [1536, 16], replicated, may hold values from -0.078125 to 0.078125
- w_gate_up: bfloat16 [16, 1536, 1024], P('seq'), may hold values from -0.15625 to 0.15625
- w_down: bfloat16 [16, 512, 1536], P('seq'), may hold values from -1 to 1
- qkv_down: bfloat16 [8, 1536, 48], replicated, may hold values from -0.15625 to 0.15625
- qkv_up: bfloat16 [8, 16, 2560], replicated, may hold values from -0.75 to 0.75
- out_down: bfloat16 [8, 1536, 16], replicated, may hold values from -0.15625 to 0.15625
- out_up: bfloat16 [8, 16, 1536], replicated, may hold values from -1.5 to 1.5
- gu_down: bfloat16 [8, 1536, 32], replicated, may hold values from -0.15625 to 0.15625
- gu_up: bfloat16 [8, 2, 16, 512], replicated, may hold values from -0.75 to 0.75
- down_a: bfloat16 [8, 512, 16], replicated, may hold values from -0.25 to 0.25
- down_b: bfloat16 [8, 16, 1536], replicated, may hold values from -1.5 to 1.5
Outputs:
- layer_output: bfloat16 [8, 1024, 1536], P('seq', 'ctx')
- input_grad: float32 [8, 1024, 1536], P('seq', 'ctx')
- grad_qkv_down: float32 [8, 1536, 48], replicated
- grad_qkv_up: float32 [8, 16, 2560], replicated
- grad_out_down: float32 [8, 1536, 16], replicated
- grad_out_up: float32 [8, 16, 1536], replicated
- grad_gu_down: float32 [8, 1536, 32], replicated
- grad_gu_up: float32 [8, 2, 16, 512], replicated
- grad_down_a: float32 [8, 512, 16], replicated
- grad_down_b: float32 [8, 16, 1536], replicated
Inputs may be any that keep to these rules, and one draw needn't show every extreme that they name: `expert_ids`: each token names 8 different experts; in the rows of one device no expert is named more than 128 times, a bound that some block reaches. `segment_ids`: along each sequence the ids never fall; a document has at most min(2000, 512) positions, and one has exactly that many.
All inputs are finite; a program needn't handle non-finite values.
Results may differ from a plain program's by a relative error of at most 0.02.
Values may be sent and summed in bfloat16 or wider, within the bound.
No kernel may reach another device: no remote copies, remote signals or barrier semaphores. Data moves between devices by JAX's collectives and lax.ppermute only.
A program may use at most 256 MiB of HBM per device.

v0:
```python
import jax
import jax.numpy as jnp
from jax import lax
from jax.sharding import PartitionSpec as P

D = 1536
HEADS = 24
KV_HEADS = 8
HEAD_DIM = 64
FF = 512
TOPK = 8
RANK = 16
ADAPT = 8
E_DEV = 2
CAP = 128
QW = 1536
KVW = 512


NORM_EPS = 1e-05


def rotary(values, offsets, direction):
    half_dim = values.shape[-1] // 2
    frequency = 10000.0 ** (-2.0 * jnp.arange(half_dim).astype(jnp.float32) / values.shape[-1])
    angles = offsets.astype(jnp.float32)[:, None] * frequency[None, :]
    cosine = jnp.cos(angles)[:, None, :]
    sine_part = direction * jnp.sin(angles)[:, None, :]
    first_half = values[..., :half_dim]
    second_half = values[..., half_dim:]
    return jnp.concatenate(
        [
            first_half * cosine - second_half * sine_part,
            second_half * cosine + first_half * sine_part,
        ],
        axis=-1,
    )


def storage_positions(ctx_count, tok_count):
    half_len = tok_count // 2
    row_index = jnp.arange(tok_count * ctx_count)
    device_of = row_index // tok_count
    within = row_index % tok_count
    which_block = jnp.where(within < half_len, device_of, 2 * ctx_count - 1 - device_of)
    return which_block * half_len + within % half_len


def document_offsets(seg_row):
    row_index = jnp.arange(seg_row.shape[0])
    change = jnp.concatenate([jnp.ones((1,), jnp.bool_), seg_row[1:] != seg_row[:-1]])
    starts = lax.cummax(jnp.where(change, row_index, 0), axis=0)
    return row_index - starts


def norm_backward(values, inverse, gain_vec, upstream):
    scaled = gain_vec * upstream
    return inverse * scaled - values * inverse**3 * jnp.mean(
        values * scaled, axis=-1, keepdims=True
    )


def lowp_dot(left_arr, right_arr):
    return jnp.dot(left_arr, right_arr, preferred_element_type=jnp.float32)


def on_device(
    inputs,
    cotangent,
    segment_ids,
    expert_ids,
    adapter_ids,
    gain_one,
    w_qkv,
    w_out,
    gain_two,
    router,
    w_gate_up,
    w_down,
    qkv_down,
    qkv_up,
    out_down,
    out_up,
    gu_down,
    gu_up,
    down_a,
    down_b,
):
    ctx_count = lax.axis_size("ctx")
    seq_count = lax.axis_size("seq")
    ctx_index = lax.axis_index("ctx")
    seq_index = lax.axis_index("seq")
    tok_count = inputs.shape[1]
    length = tok_count * ctx_count
    group_size = HEADS // KV_HEADS
    expert_total = router.shape[1]
    slot_total = expert_total * CAP
    bf_type = jnp.bfloat16
    fl_type = jnp.float32
    position = storage_positions(ctx_count, tok_count)
    seg_row = segment_ids[0]
    key_offset = document_offsets(seg_row)[position]
    key_segment = seg_row[position]
    own_start = ctx_index * tok_count
    query_pos = lax.dynamic_slice_in_dim(position, own_start, tok_count, 0)
    query_offset = lax.dynamic_slice_in_dim(key_offset, own_start, tok_count, 0)
    query_segment = lax.dynamic_slice_in_dim(key_segment, own_start, tok_count, 0)
    adapter = adapter_ids[seq_index]

    def pick_table(table_arg):
        return lax.dynamic_index_in_dim(table_arg, adapter, 0, keepdims=False)

    qkv_sel = pick_table(qkv_down)
    up_sel = pick_table(qkv_up)
    out_down_sel = pick_table(out_down)
    out_up_sel = pick_table(out_up)
    gu_down_sel = pick_table(gu_down)
    own_onehot = (jnp.arange(ADAPT) == adapter).astype(fl_type)
    source_hot = adapter_ids[:, None] == jnp.arange(ADAPT)[None, :]
    source_float = source_hot.astype(fl_type)
    source_half = source_hot.astype(bf_type)
    src_gate_up = jnp.einsum(
        "sa,aqrf->sqrf", source_half, gu_up, preferred_element_type=fl_type
    ).astype(bf_type)
    src_down_a = jnp.einsum(
        "sa,afr->sfr", source_half, down_a, preferred_element_type=fl_type
    ).astype(bf_type)
    src_down_b = jnp.einsum(
        "sa,ard->srd", source_half, down_b, preferred_element_type=fl_type
    ).astype(bf_type)
    qkv_full, out_full = (
        lax.all_gather(w_qkv, "seq", axis=0, tiled=True),
        lax.all_gather(w_out, "seq", axis=0, tiled=True),
    )
    features = inputs[0].astype(fl_type)
    inv_one = lax.rsqrt(jnp.mean(features * features, axis=-1, keepdims=True) + NORM_EPS)
    h_one = (features * inv_one * gain_one).astype(bf_type)
    rank_qkv = lowp_dot(h_one, qkv_sel).astype(bf_type)
    main_proj = lowp_dot(h_one, qkv_full)
    q_pre = main_proj[:, :QW] + lowp_dot(rank_qkv[:, :RANK], up_sel[:, :QW])
    k_pre = main_proj[:, QW : QW + KVW] + lowp_dot(
        rank_qkv[:, RANK : 2 * RANK], up_sel[:, QW : QW + KVW]
    )
    v_pre = main_proj[:, QW + KVW :] + lowp_dot(rank_qkv[:, 2 * RANK :], up_sel[:, QW + KVW :])
    queries = (
        rotary(q_pre.reshape(tok_count, HEADS, HEAD_DIM), query_offset, 1.0)
        .astype(bf_type)
        .reshape(tok_count, KV_HEADS, group_size, HEAD_DIM)
    )
    keys_own = (
        rotary(k_pre.reshape(tok_count, KV_HEADS, HEAD_DIM), query_offset, 1.0)
        .astype(bf_type)
        .reshape(tok_count, KVW)
    )
    values_own = v_pre.astype(bf_type)
    keys_all, values_all = (
        lax.all_gather(keys_own, "ctx", axis=0, tiled=True),
        lax.all_gather(values_own, "ctx", axis=0, tiled=True),
    )
    block_len = min(512, length)
    starts = jnp.arange(length // block_len) * block_len
    stat_shape = (KV_HEADS, group_size, tok_count)

    def block_scores(start_row):
        key_block = lax.dynamic_slice_in_dim(keys_all, start_row, block_len, 0).reshape(
            block_len, KV_HEADS, HEAD_DIM
        )
        value_block = lax.dynamic_slice_in_dim(values_all, start_row, block_len, 0).reshape(
            block_len, KV_HEADS, HEAD_DIM
        )
        scores = (
            jnp.einsum("tgrd,kgd->grtk", queries, key_block, preferred_element_type=fl_type) * 0.125
        )
        key_pos = lax.dynamic_slice_in_dim(position, start_row, block_len, 0)
        key_seg = lax.dynamic_slice_in_dim(key_segment, start_row, block_len, 0)
        allowed = (query_segment[:, None] == key_seg[None, :]) & (
            key_pos[None, :] <= query_pos[:, None]
        )
        return (scores, allowed, key_block, value_block)

    def first_pass(carried, start_row):
        peak_val, total_val = carried
        scores, allowed, unused_keys, unused_values = block_scores(start_row)
        scores = jnp.where(allowed, scores, -1e30)
        new_peak = jnp.maximum(peak_val, jnp.max(scores, axis=-1))
        total_val = total_val * jnp.exp(peak_val - new_peak) + jnp.sum(
            jnp.where(allowed, jnp.exp(scores - new_peak[..., None]), 0.0), axis=-1
        )
        return ((new_peak, total_val), None)

    (peak_val, total_val), unused_stats = lax.scan(
        first_pass, (jnp.full(stat_shape, -1e30, fl_type), jnp.zeros(stat_shape, fl_type)), starts
    )
    log_total = peak_val + jnp.log(total_val)

    def second_pass(summed, start_row):
        scores, allowed, unused_keys, value_block = block_scores(start_row)
        prob_vals = jnp.where(allowed, jnp.exp(scores - log_total[..., None]), 0.0)
        summed = summed + jnp.einsum(
            "grtk,kgd->tgrd", prob_vals.astype(bf_type), value_block, preferred_element_type=fl_type
        )
        return (summed, None)

    head_shape = (tok_count, KV_HEADS, group_size, HEAD_DIM)
    summed, unused_out = lax.scan(second_pass, jnp.zeros(head_shape, fl_type), starts)
    attended = summed.reshape(tok_count, QW).astype(bf_type)
    rank_out = lowp_dot(attended, out_down_sel).astype(bf_type)
    y_one = features + lowp_dot(attended, out_full) + lowp_dot(rank_out, out_up_sel)
    inv_two = lax.rsqrt(jnp.mean(y_one * y_one, axis=-1, keepdims=True) + NORM_EPS)
    h_two = (y_one * inv_two * gain_two).astype(bf_type)
    logits = lowp_dot(h_two, router)
    chosen = expert_ids[0]
    chosen_hot = chosen[:, :, None] == jnp.arange(expert_total)[None, None, :]
    picked = jnp.sum(jnp.where(chosen_hot, logits[:, None, :], 0.0), axis=-1)
    top_val = jnp.max(picked, axis=-1, keepdims=True)
    weights = jnp.exp(picked - top_val)
    gate_vals = weights / jnp.sum(weights, axis=-1, keepdims=True)
    rank_gu = lowp_dot(h_two, gu_down_sel).astype(bf_type)
    flat_expert = chosen.reshape(-1)
    expert_hot = (flat_expert[:, None] == jnp.arange(expert_total)[None, :]).astype(jnp.int32)
    rank_of = jnp.sum(jnp.cumsum(expert_hot, axis=0) * expert_hot, axis=1) - 1
    slot_of = flat_expert * CAP + rank_of
    pair_index = (
        jnp.zeros((slot_total,), jnp.int32)
        .at[slot_of]
        .set(jnp.arange(tok_count * TOPK, dtype=jnp.int32))
    )
    slot_live = jnp.zeros((slot_total,), bf_type).at[slot_of].set(1.0)
    slot_token = pair_index // TOPK
    send_rows = (h_two[slot_token] * slot_live[:, None]).reshape(seq_count, E_DEV, CAP, D)
    send_rank = (rank_gu[slot_token] * slot_live[:, None]).reshape(seq_count, E_DEV, CAP, 2 * RANK)
    rows_in = lax.all_to_all(send_rows, "seq", split_axis=0, concat_axis=0, tiled=True)
    rank_in = lax.all_to_all(send_rank, "seq", split_axis=0, concat_axis=0, tiled=True)
    both_pre = jnp.einsum("secd,edf->secf", rows_in, w_gate_up, preferred_element_type=fl_type)
    gate_pre = both_pre[..., :FF] + jnp.einsum(
        "secr,srf->secf", rank_in[..., :RANK], src_gate_up[:, 0], preferred_element_type=fl_type
    )
    up_pre = both_pre[..., FF:] + jnp.einsum(
        "secr,srf->secf", rank_in[..., RANK:], src_gate_up[:, 1], preferred_element_type=fl_type
    )
    activated = (jax.nn.silu(gate_pre) * up_pre).astype(bf_type)
    rank_down = jnp.einsum(
        "secf,sfr->secr", activated, src_down_a, preferred_element_type=fl_type
    ).astype(bf_type)
    result = (
        jnp.einsum("secf,efd->secd", activated, w_down, preferred_element_type=fl_type)
        + jnp.einsum("secr,srd->secd", rank_down, src_down_b, preferred_element_type=fl_type)
    ).astype(bf_type)
    returned = lax.all_to_all(result, "seq", split_axis=0, concat_axis=0, tiled=True)
    expert_tok = (
        returned.reshape(slot_total, D)[slot_of].reshape(tok_count, TOPK, D).astype(fl_type)
    )
    y_two = y_one + jnp.einsum("tk,tkd->td", gate_vals, expert_tok)
    layer_output = y_two.astype(bf_type)[None]
    grad_two = cotangent[0].astype(fl_type)
    d_gates = jnp.einsum("td,tkd->tk", grad_two, expert_tok)
    d_picked = gate_vals * (d_gates - jnp.sum(gate_vals * d_gates, axis=-1, keepdims=True))
    d_logits = jnp.sum(jnp.where(chosen_hot, d_picked[..., None], 0.0), axis=1).astype(bf_type)
    d_copies = (
        (gate_vals[..., None] * grad_two[:, None, :]).astype(bf_type).reshape(tok_count * TOPK, D)
    )
    send_grads = (d_copies[pair_index] * slot_live[:, None]).reshape(seq_count, E_DEV, CAP, D)
    grads_in = lax.all_to_all(send_grads, "seq", split_axis=0, concat_axis=0, tiled=True)
    sigmoid_val = jax.nn.sigmoid(gate_pre)
    silu_val = gate_pre * sigmoid_val
    activated = (silu_val * up_pre).astype(bf_type)
    rank_down = jnp.einsum(
        "secf,sfr->secr", activated, src_down_a, preferred_element_type=fl_type
    ).astype(bf_type)
    grad_down_b_src = jnp.einsum(
        "secr,secd->srd", rank_down, grads_in, preferred_element_type=fl_type
    )
    d_rank_down = jnp.einsum(
        "secd,srd->secr", grads_in, src_down_b, preferred_element_type=fl_type
    ).astype(bf_type)
    grad_down_a_src = jnp.einsum(
        "secf,secr->sfr", activated, d_rank_down, preferred_element_type=fl_type
    )
    d_activated = jnp.einsum(
        "secd,efd->secf", grads_in, w_down, preferred_element_type=fl_type
    ) + jnp.einsum("secr,sfr->secf", d_rank_down, src_down_a, preferred_element_type=fl_type)
    d_gate = (d_activated * up_pre * sigmoid_val * (1.0 + gate_pre * (1.0 - sigmoid_val))).astype(
        bf_type
    )
    d_up = (d_activated * silu_val).astype(bf_type)
    grad_gate_up_src = jnp.stack(
        [
            jnp.einsum(
                "secr,secf->srf", rank_in[..., :RANK], d_gate, preferred_element_type=fl_type
            ),
            jnp.einsum("secr,secf->srf", rank_in[..., RANK:], d_up, preferred_element_type=fl_type),
        ],
        axis=1,
    )
    d_rank = jnp.concatenate(
        [
            jnp.einsum("secf,srf->secr", d_gate, src_gate_up[:, 0], preferred_element_type=fl_type),
            jnp.einsum("secf,srf->secr", d_up, src_gate_up[:, 1], preferred_element_type=fl_type),
        ],
        axis=-1,
    ).astype(bf_type)
    d_rows = jnp.einsum(
        "secf,edf->secd",
        jnp.concatenate([d_gate, d_up], axis=-1),
        w_gate_up,
        preferred_element_type=fl_type,
    ).astype(bf_type)
    backward_out = (d_rows, d_rank, grad_gate_up_src, grad_down_a_src, grad_down_b_src)
    d_rows, d_rank, grad_gate_up_src, grad_down_a_src, grad_down_b_src = backward_out
    rows_back, rank_back = (
        lax.all_to_all(d_rows, "seq", split_axis=0, concat_axis=0, tiled=True),
        lax.all_to_all(d_rank, "seq", split_axis=0, concat_axis=0, tiled=True),
    )
    d_rows_tok = jnp.sum(
        rows_back.reshape(slot_total, D)[slot_of].reshape(tok_count, TOPK, D).astype(fl_type),
        axis=1,
    )
    d_rank_gu = jnp.sum(
        rank_back.reshape(slot_total, 2 * RANK)[slot_of]
        .reshape(tok_count, TOPK, 2 * RANK)
        .astype(fl_type),
        axis=1,
    ).astype(bf_type)
    d_h_two = d_rows_tok + lowp_dot(d_logits, router.T) + lowp_dot(d_rank_gu, gu_down_sel.T)
    d_y_one = grad_two + norm_backward(y_one, inv_two, gain_two, d_h_two)
    d_attn = d_y_one.astype(bf_type)
    grad_out_up_own = lowp_dot(rank_out.T, d_attn)
    d_rank_out = lowp_dot(d_attn, out_up_sel.T).astype(bf_type)
    grad_out_down_own = lowp_dot(attended.T, d_rank_out)
    d_attended = (lowp_dot(d_attn, out_full.T) + lowp_dot(d_rank_out, out_down_sel.T)).astype(
        bf_type
    )
    d_heads = d_attended.reshape(head_shape)
    row_delta = jnp.transpose(jnp.sum(d_heads.astype(fl_type) * summed, axis=-1), (1, 2, 0))

    def back_pass(d_query, start_row):
        scores, allowed, key_block, value_block = block_scores(start_row)
        prob_vals = jnp.where(allowed, jnp.exp(scores - log_total[..., None]), 0.0)
        d_value = jnp.einsum(
            "grtk,tgrd->kgd", prob_vals.astype(bf_type), d_heads, preferred_element_type=fl_type
        )
        d_prob = jnp.einsum("tgrd,kgd->grtk", d_heads, value_block, preferred_element_type=fl_type)
        d_score = (prob_vals * (d_prob - row_delta[..., None])).astype(bf_type)
        d_query = (
            d_query
            + jnp.einsum("grtk,kgd->tgrd", d_score, key_block, preferred_element_type=fl_type)
            * 0.125
        )
        d_key = (
            jnp.einsum("grtk,tgrd->kgd", d_score, queries, preferred_element_type=fl_type) * 0.125
        )
        return (d_query, (d_key.reshape(block_len, KVW), d_value.reshape(block_len, KVW)))

    d_query, (key_terms, value_terms) = lax.scan(back_pass, jnp.zeros(head_shape, fl_type), starts)
    d_keys, d_values = (
        lax.psum_scatter(
            key_terms.reshape(length, KVW).astype(jnp.bfloat16),
            "ctx",
            scatter_dimension=0,
            tiled=True,
        ).astype(jnp.float32),
        lax.psum_scatter(
            value_terms.reshape(length, KVW).astype(jnp.bfloat16),
            "ctx",
            scatter_dimension=0,
            tiled=True,
        ).astype(jnp.float32),
    )
    q_grad = (
        rotary(d_query.reshape(tok_count, HEADS, HEAD_DIM), query_offset, -1.0)
        .reshape(tok_count, QW)
        .astype(bf_type)
    )
    k_grad = (
        rotary(d_keys.reshape(tok_count, KV_HEADS, HEAD_DIM), query_offset, -1.0)
        .reshape(tok_count, KVW)
        .astype(bf_type)
    )
    v_grad = d_values.astype(bf_type)
    d_qkv = jnp.concatenate([q_grad, k_grad, v_grad], axis=1)
    grad_qkv_up_own = jnp.concatenate(
        [
            lowp_dot(rank_qkv[:, :RANK].T, q_grad),
            lowp_dot(rank_qkv[:, RANK : 2 * RANK].T, k_grad),
            lowp_dot(rank_qkv[:, 2 * RANK :].T, v_grad),
        ],
        axis=1,
    )
    d_rank_qkv = jnp.concatenate(
        [
            lowp_dot(q_grad, up_sel[:, :QW].T),
            lowp_dot(k_grad, up_sel[:, QW : QW + KVW].T),
            lowp_dot(v_grad, up_sel[:, QW + KVW :].T),
        ],
        axis=1,
    ).astype(bf_type)
    grad_qkv_down_own = lowp_dot(h_one.T, d_rank_qkv)
    d_h_one = lowp_dot(d_qkv, qkv_full.T) + lowp_dot(d_rank_qkv, qkv_sel.T)
    input_grad = (d_y_one + norm_backward(features, inv_one, gain_one, d_h_one))[None]
    grad_gu_down_own = lowp_dot(h_two.T, d_rank_gu)

    def place_slot(grad_term):
        return own_onehot.reshape((ADAPT,) + (1,) * grad_term.ndim) * grad_term[None]

    term_gu_up = jnp.einsum("sa,sqrf->aqrf", source_float, grad_gate_up_src)
    term_down_a = jnp.einsum("sa,sfr->afr", source_float, grad_down_a_src)
    term_down_b = jnp.einsum("sa,srd->ard", source_float, grad_down_b_src)
    term_qkv_down = place_slot(grad_qkv_down_own)
    term_qkv_up = place_slot(grad_qkv_up_own)
    term_out_down = place_slot(grad_out_down_own)
    term_out_up = place_slot(grad_out_up_own)
    term_gu_down = place_slot(grad_gu_down_own)
    summed_grads = lax.psum(
        (
            term_qkv_down,
            term_qkv_up,
            term_out_down,
            term_out_up,
            term_gu_down,
            term_gu_up,
            term_down_a,
            term_down_b,
        ),
        ("seq", "ctx"),
    )
    (
        grad_qkv_down,
        grad_qkv_up,
        grad_out_down,
        grad_out_up,
        grad_gu_down,
        grad_gu_up,
        grad_down_a,
        grad_down_b,
    ) = summed_grads
    return (
        layer_output,
        input_grad,
        grad_qkv_down,
        grad_qkv_up,
        grad_out_down,
        grad_out_up,
        grad_gu_down,
        grad_gu_up,
        grad_down_a,
        grad_down_b,
    )


def solution(mesh):
    placed = (
        P("seq", "ctx", None),
        P("seq", "ctx", None),
        P("seq", None),
        P("seq", "ctx", None),
        P(),
        P(),
        P("seq", None),
        P("seq", None),
        P(),
        P(),
        P("seq", None, None),
        P("seq", None, None),
        P(),
        P(),
        P(),
        P(),
        P(),
        P(),
        P(),
        P(),
    )
    return jax.shard_map(
        on_device,
        mesh=mesh,
        in_specs=placed,
        out_specs=(
            P("seq", "ctx", None),
            P("seq", "ctx", None),
            P(),
            P(),
            P(),
            P(),
            P(),
            P(),
            P(),
            P(),
        ),
        check_vma=False,
    )
```

profile of v0, /device:TPU:0, one launch (start us, length us, event | category | flops | bytes accessed | tf_op | source)
XLA Modules:
  0.0 1365.0 jit_solution(7928695785129502328)
XLA Ops:
  17.4 114.0 %all-gather.5.cloned.1.call-done = bf16[1536,2560]{1,0:T(8,128)(2,1)} async-done(((bf16[192,2560]{1,0:T(8,128)(2,1)}), bf16[1536,2560]{1,0:T(8,128)(2,1)}) %all-gather.5.cloned.1.call-update) | async-done | bytes 7864336 | tf_op jit(solution)/shard_map/all_gather | solution.py:132
  152.8 8.1 reduce-window.19
  162.0 8.0 scatter_custom_fusion
  175.4 14.8 %scatter_custom_fusion.1 = bf16[2048]{0:T(1024)(128)(2,1)S(1)} fusion(s32[2048]{0:T(1024)S(1)} %bitcast.469, bf16[2048]{0:T(1024)(128)(2,1)S(1)} %broadcast.479, bf16[]{:T(256)} %constant.193.clone.1), kind=kCustom, calls=%fused_computation.334 | custom fusion | bytes 4098 | tf_op jit(solution)/shard_map/scatter | solution.py:228
  201.0 37.1 %while.39 = (s32[]{:T(128)}, f32[8,3,256]{2,1,0:T(4,128)S(1)}, f32[8,3,256]{2,1,0:T(4,128)S(1)}, s32[256]{0:T(256)S(1)}, s32[2]{0:T(128)S(1)}, /*index=5*/s32[10...) while((s32[]{:T(128)}, f32[8,3,256]{2,1,0:T(4,128)S(1)}, ...), condition=%wide.region_6.7_spmd.clone, body=%wide.region_3.6_spmd.clone.sunk | while | flops 428242944 | bytes 28252352 | solution.py:191
  205.3 7.8 fusion.307
  238.1 23.8 %while.40 = (s32[]{:T(128)}, f32[256,8,3,64]{0,3,2,1:T(8,128)}, s32[2]{0:T(128)S(1)}, bf16[1024,512]{0,1:T(8,128)(2,1)}, s32[256]{0:T(256)S(1)}, /*index=5*/s32[...) while((s32[]{:T(128)}, f32[256,8,3,64]{0,3,2,1:T(8,128)}, ...), condition=%wide.region_8.9_spmd.clone, body=%wide.region_7.8_spmd.clone.sunk | while | flops 819068928 | bytes 7379145 | solution.py:205
  273.2 14.5 %gather_fusion.2 = bf16[2048,1536]{1,0:T(8,128)(2,1)} fusion(bf16[256,1536]{1,0:T(8,128)(2,1)} %multiply_convert_fusion.3, s32[2048]{0:T(1024)S(1)} %get-tuple-element.573), kind=kCustom, calls=%fused_computation.2 | custom fusion | bytes 12591104 | tf_op jit(solution)/shard_map/gather | solution.py:230
  289.3 8.1 gather_fusion.3
  321.6 131.9 %all-to-all-done = bf16[8,2,128,1536]{3,2,1,0:T(8,128)(2,1)} async-done(((bf16[8,2,128,1536]{3,2,1,0:T(8,128)(2,1)}), bf16[8,2,128,1536]{3,2,1,0:T(8,128)(2,1)}, u32[]{:S(2)}, u32[]{:S(2)}) %all-to-all-start) | async-done | bytes 6291488 | tf_op jit(solution)/shard_map/all_to_all | solution.py:232
  453.5 9.7 fusion.44
  496.3 131.0 %all-to-all-done.2 = bf16[8,2,128,1536]{3,2,1,0:T(8,128)(2,1)} async-done(((bf16[8,2,128,1536]{3,2,1,0:T(8,128)(2,1)}), bf16[8,2,128,1536]{3,2,1,0:T(8,128)(2,1)}, u32[]{:S(2)}, u32[]{:S(2)}) %all-to-all-start.2) | async-done | bytes 6291488 | tf_op jit(solution)/shard_map/all_to_all | solution.py:249
  627.3 17.0 %gather_fusion.4 = bf16[2048,1536]{1,0:T(8,128)(2,1)} fusion(bf16[2048,1536]{1,0:T(8,128)(2,1)} %bitcast.41, s32[2048]{0:T(1024)} %broadcast_clamp_fusion), kind=kCustom, calls=%fused_computation.4 | custom fusion | bytes 12591104 | tf_op jit(solution)/shard_map/gather | solution.py:251
  661.4 17.0 %gather_fusion.5 = bf16[2048,1536]{1,0:T(8,128)(2,1)} fusion(bf16[2048,1536]{1,0:T(8,128)(2,1)} %fusion.25, s32[2048]{0:T(1024)} %get-tuple-element.572), kind=kCustom, calls=%fused_computation.5 | custom fusion | bytes 12591104 | tf_op jit(solution)/shard_map/gather | solution.py:262
  681.7 141.7 %all_to_all.30 = bf16[8,2,128,1536]{3,2,1,0:T(8,128)(2,1)S(1)} all-to-all(bf16[8,2,128,1536]{3,2,1,0:T(8,128)(2,1)S(1)} %broadcast_multiply_fusion), channel_id=1, replica_groups=mesh['seq'=8,'ctx'=4] {'seq'}, dimensions={0} | all-to-all | bytes 12582912 | tf_op jit(solution)/shard_map/all_to_all | solution.py:263
  838.3 9.5 convert_bitcast_fusion
  878.0 116.2 %all-to-all-done.4 = bf16[8,2,128,1536]{3,2,1,0:T(8,128)(2,1)} async-done(((bf16[8,2,128,1536]{3,2,1,0:T(8,128)(2,1)}), bf16[8,2,128,1536]{3,2,1,0:T(8,128)(2,1)}, u32[]{:S(2)}, u32[]{:S(2)}) %all-to-all-start.4) | async-done | bytes 6291488 | tf_op jit(solution)/shard_map/all_to_all | solution.py:311
  994.3 16.8 %gather_fusion.6 = bf16[2048,1536]{1,0:T(8,128)(2,1)} fusion(bf16[2048,1536]{1,0:T(8,128)(2,1)} %bitcast.54, s32[2048]{0:T(1024)S(1)} %copy-done.63), kind=kCustom, calls=%fused_computation.6 | custom fusion | bytes 12591104 | tf_op jit(solution)/shard_map/gather | solution.py:315
  1031.8 73.4 %while.41 = (s32[]{:T(128)}, f32[256,8,3,64]{0,3,2,1:T(8,128)S(1)}, bf16[2,512,512]{2,1,0:T(8,128)(2,1)}, bf16[2,512,512]{2,1,0:T(8,128)(2,1)}, s32[2]{0:T(128)S...) while((s32[]{:T(128)}, f32[256,8,3,64]{0,3,2,1:T(8,128)S(1)}, ...), condition=%wide.region_25.26_spmd.clone, body=%wide.region_24.25_spmd.clone.sunk | while | flops 2046820352 | bytes 130079584 | solution.py:354
  1052.2 8.0 fusion.325
  1088.9 8.0 fusion.325
  1118.1 11.3 reduce-scatter.3.cloned.1.call-done
  1133.3 24.1 %reduce-scatter.5.cloned.1.call-done = bf16[256,512]{0,1:T(8,128)(2,1)} async-done(((bf16[1024,512]{0,1:T(8,128)(2,1)}), bf16[256,512]{0,1:T(8,128)(2,1)}) %reduce-scatter.5.cloned.1.call-update) | async-done | bytes 262160 | tf_op jit(solution)/shard_map/reduce_scatter | solution.py:362
  1174.1 172.9 %all-reduce.3.cloned.1.call-done = (f32[8,1536,48]{1,2,0:T(8,128)}, f32[8,16,2560]{2,1,0:T(8,128)}, f32[8,1536,16]{1,2,0:T(8,128)}, f32[8,16,1536]{2,1,0:T(8,128...) async-done(((f32[8,1536,48]{1,2,0:T(8,128)}, f32[8,16,2560]{2,1,0:T(8,128)}, f32[8,1536,16]{1,2,0:T(8,128)}, ...) | async-done | bytes 8388624 | tf_op jit(solution)/shard_map/psum | solution.py:413
  (450 shorter events, 344.7 us)
Async XLA Ops:
  7.2 460.4 %copy-start = (bf16[2,512,1536]{2,1,0:T(8,128)(2,1)S(1)}, bf16[2,512,1536]{2,1,0:T(8,128)(2,1)}, u32[]{:S(2)}) copy-start(bf16[2,512,1536]{2,1,0:T(8,128)(2,1)} %param.37) | copy-start | bytes 9437188
  7.2 124.2 %copy-start.86 = (f32[1536]{0:T(1024)S(1)}, f32[1536]{0:T(1024)}, u32[]{:S(2)}) copy-start(f32[1536]{0:T(1024)} %param.31) | copy-start | bytes 18436
  7.2 124.2 %all-gather.5.cloned.1.call-start = ((), (), s32[]{:S(2)}) async-start(), calls=%async_computation.8 | async-start | bytes 8847360 | tf_op jit(solution)/shard_map/all_gather | solution.py:132
  7.9 190.8 %all-gather.7.cloned.1.call-start = ((), (), s32[]{:S(2)}) async-start(), calls=%async_computation.9 | async-start | bytes 1310720 | tf_op jit(solution)/shard_map/all_gather | solution.py:158
  14.9 122.3 %copy-start.91 = (f32[256]{0:T(256)}, f32[256]{0:T(256)S(1)}, u32[]{:S(2)}) copy-start(f32[256]{0:T(256)S(1)} %get-tuple-element.578) | copy-start | bytes 3076
  16.5 173.7 %copy-start.64 = (bf16[256,48]{0,1:T(8,128)(2,1)}, bf16[256,48]{0,1:T(8,128)(2,1)S(1)}, u32[]{:S(2)}) copy-start(bf16[256,48]{0,1:T(8,128)(2,1)S(1)} %convolution_convert_fusion.4) | copy-start | bytes 73732
  17.4 172.8 %copy-start.35 = (bf16[16,2560]{1,0:T(8,128)(2,1)}, bf16[16,2560]{1,0:T(8,128)(2,1)S(1)}, u32[]{:S(2)}) copy-start(bf16[16,2560]{1,0:T(8,128)(2,1)S(1)} %dynamic-slice_bitcast_fusion) | copy-start | bytes 245764
  139.6 61.4 %all-gather.9.cloned.1.call-start = ((), (), s32[]{:S(2)}) async-start(), calls=%async_computation.10 | async-start | bytes 1310720 | tf_op jit(solution)/shard_map/all_gather | solution.py:157
  145.2 51.0 %copy-start.31 = (f32[256,32]{0,1:T(8,128)}, f32[256,32]{0,1:T(8,128)S(1)}, u32[]{:S(2)}) copy-start(f32[256,32]{0,1:T(8,128)S(1)} %get-tuple-element.576) | copy-start | bytes 98308
  151.2 114.2 %all-gather.11.cloned.1.call-start = ((), (), s32[]{:S(2)}) async-start(), calls=%async_computation.11 | async-start | bytes 5308416 | tf_op jit(solution)/shard_map/all_gather | solution.py:133
  162.0 31.2 %copy-start.76 = (s32[2048,1]{0,1:T(1,128)}, s32[2048,1]{0,1:T(1,128)S(1)}, u32[]{:S(2)}) copy-start(s32[2048,1]{0,1:T(1,128)S(1)} %compare_select_fusion) | copy-start | bytes 24580
  190.2 112.9 %copy-start.69 = (bf16[2048]{0:T(1024)(128)(2,1)}, bf16[2048]{0:T(1024)(128)(2,1)S(1)}, u32[]{:S(2)}) copy-start(bf16[2048]{0:T(1024)(128)(2,1)S(1)} %scatter_custom_fusion.1) | copy-start | bytes 12292
  299.3 11.1 all-to-all-start.1
  311.0 142.5 %all-to-all-start = ((bf16[8,2,128,1536]{3,2,1,0:T(8,128)(2,1)}), bf16[8,2,128,1536]{3,2,1,0:T(8,128)(2,1)}, u32[]{:S(2)}, u32[]{:S(2)}) async-start(bf16[8,2,128,1536]{3,2,1,0:T(8,128)(2,1)} %broadcast_multiply_fusion.1), calls=%async_computation | async-start | bytes 12582912 | tf_op jit(solution)/shard_map/all_to_all | solution.py:232
  484.9 142.3 %all-to-all-start.2 = ((bf16[8,2,128,1536]{3,2,1,0:T(8,128)(2,1)}), bf16[8,2,128,1536]{3,2,1,0:T(8,128)(2,1)}, u32[]{:S(2)}, u32[]{:S(2)}) async-start(bf16[8,2,128,1536]{3,2,1,0:T(8,128)(2,1)} %copy.217), calls=%async_computation.2 | async-start | bytes 12582912 | tf_op jit(solution)/shard_map/all_to_all | solution.py:249
  494.6 149.7 %copy-start.59 = (f32[256,8]{0,1:T(8,128)}, f32[256,8]{0,1:T(8,128)S(1)}, u32[]{:S(2)}) copy-start(f32[256,8]{0,1:T(8,128)S(1)} %select_reduce_fusion.2) | copy-start | bytes 24580
  834.4 16.4 %all-to-all-start.5 = ((bf16[8,2,128,32]{2,3,1,0:T(8,128)(2,1)}), bf16[8,2,128,32]{2,3,1,0:T(8,128)(2,1)S(1)}, u32[]{:S(2)}, u32[]{:S(2)}) async-start(bf16[8,2,128,32]{2,3,1,0:T(8,128)(2,1)} %pad_maximum_fusion.6), calls=%async_computation.5 | async-start | bytes 262144 | tf_op jit(solution)/shard_map/all_to_all | solution.py:312
  850.8 143.4 %all-to-all-start.4 = ((bf16[8,2,128,1536]{3,2,1,0:T(8,128)(2,1)}), bf16[8,2,128,1536]{3,2,1,0:T(8,128)(2,1)}, u32[]{:S(2)}, u32[]{:S(2)}) async-start(bf16[8,2,128,1536]{3,2,1,0:T(8,128)(2,1)} %copy.223), calls=%async_computation.4 | async-start | bytes 12582912 | tf_op jit(solution)/shard_map/all_to_all | solution.py:311
  857.0 272.4 %reduce-scatter.3.cloned.1.call-start = ((), (), s32[]{:S(2)}) async-start(), calls=%async_computation.12 | async-start | bytes 1310720 | tf_op jit(solution)/shard_map/reduce_scatter | solution.py:356
  1031.8 73.5 %copy-start.80 = (s32[8]{0:T(128)S(1)}, s32[8]{0:T(128)}, u32[]{:S(2)}) copy-start(s32[8]{0:T(128)} %param.30) | copy-start | bytes 100
  1031.8 75.4 %copy-start.27 = (bf16[8,16,1536]{2,1,0:T(8,128)(2,1)S(1)}, bf16[8,16,1536]{2,1,0:T(8,128)(2,1)}, u32[]{:S(2)}) copy-start(bf16[8,16,1536]{2,1,0:T(8,128)(2,1)} %convolution_bitcast_fusion.1) | copy-start | bytes 1179652
  1105.3 52.1 %reduce-scatter.5.cloned.1.call-start = ((), (), s32[]{:S(2)}) async-start(), calls=%async_computation.13 | async-start | bytes 1310720 | tf_op jit(solution)/shard_map/reduce_scatter | solution.py:362
  1115.3 231.6 %all-reduce.3.cloned.1.call-start = ((), (), s32[]{:S(2)}) async-start(), calls=%async_computation.14 | async-start | bytes 16777216 | tf_op jit(solution)/shard_map/psum | solution.py:413
  1118.1 44.3 %copy-start.13 = (bf16[1,256,1536]{2,1,0:T(8,128)(2,1)S(1)}, bf16[1,256,1536]{2,1,0:T(8,128)(2,1)}, u32[]{:S(2)}) copy-start(bf16[1,256,1536]{2,1,0:T(8,128)(2,1)} %param.26) | copy-start | bytes 2359300
  (92 other events, 421.4 us)
Sparse Core Ops, SparseCore 0:
  10.2 121.0 all-gather.4
  139.7 14.9 all-gather.6
  156.8 16.8 all-gather.8
  175.7 79.8 all-gather.10
  1105.4 23.9 reduce-scatter.2
  1132.4 24.8 reduce-scatter.4
  1165.4 181.4 all-reduce.2
where the time goes:
time: 1380 us; the launch traced here: 1370 us
  waiting for transfers between devices  704 us (51%)
  matrix products  195 us (14%)
  local copies, waits for them, and re-layouts  190 us (14%)
  blocking collectives  142 us (10%)
  other arithmetic  80.3 us (6%)
  starting transfers between devices  24.1 us (2%)
  between operations  17.7 us (1%)
    psum x1, waiting for transfers between devices, on_device(): lax.psum((term_qkv_down, term_qkv_up, term_out_down, term_out_up, term_gu...  173 us
    all_to_all x1, blocking collectives, on_device(): lax.all_to_all(send_grads, 'seq', split_axis=0, concat_axis=0, tiled=True)  142 us
    all_to_all x1, waiting for transfers between devices, on_device(): lax.all_to_all(send_rows, 'seq', split_axis=0, concat_axis=0, tiled=True)  132 us
    all_to_all x1, waiting for transfers between devices, on_device(): lax.all_to_all(result, 'seq', split_axis=0, concat_axis=0, tiled=True)  131 us
    all_to_all x1, waiting for transfers between devices, on_device(): lax.all_to_all(d_rows, 'seq', split_axis=0, concat_axis=0, tiled=True)  116 us
    all_gather x1, waiting for transfers between devices, on_device(): lax.all_gather(w_qkv, 'seq', axis=0, tiled=True)  114 us
    dot_general x27, matrix products, lowp_dot(): return jnp.dot(left_arr, right_arr, preferred_element_type=jnp.float32)  44 us
  transfers between devices with their start and end apart: 12, of which 8 were waited for; matrix products, arithmetic and copies ran while one was open for 15% of the time, Pallas kernels for 0%

commit v1 on v0

v1 whole, which is shorter than its diff:
```python
import functools

import jax
import jax.numpy as jnp
from jax import lax
from jax.experimental import pallas as pl
from jax.experimental.pallas import tpu as pltpu
from jax.sharding import PartitionSpec as P

D = 1536
HEADS = 24
KV_HEADS = 8
HEAD_DIM = 64
FF = 512
RANK = 16
ADAPT = 8
E_DEV = 2
CAP = 128
QW = 1536
KVW = 512
NORM_EPS = 1e-05

GROUPS = KV_HEADS // 2
PAIRS = HEADS // KV_HEADS
QG = QW // GROUPS
KG = KVW // GROUPS
LOCAL = QG + 2 * KG
PAIR_ORDER = (0, 3, 1, 4, 2, 5)
BLK = 256
LANES = 128
EXP_AT = 2 * RANK
GATE_AT = 96
EXT = D + LANES
NEG = -1e30

BF = jnp.bfloat16
F32 = jnp.float32
NT = (((1,), (1,)), ((), ()))
TN = (((0,), (0,)), ((), ()))


def dot(left_arr, right_arr):
    return jnp.dot(left_arr, right_arr, preferred_element_type=F32)


def dot_nt(left_arr, right_arr):
    return lax.dot_general(left_arr, right_arr, NT, preferred_element_type=F32)


def dot_tn(left_arr, right_arr):
    return lax.dot_general(left_arr, right_arr, TN, preferred_element_type=F32)


def swap(block, axis, mask):
    count = lax.axis_size(axis)
    return lax.ppermute(block, axis, [(i, i ^ mask) for i in range(count)])


def gather_slots(block, axis, masks):
    slots = {0: block}
    for mask in masks:
        for have in list(slots):
            slots[have ^ mask] = swap(slots[have], axis, mask)
    return [slots[m] for m in range(len(slots))]


def gather_seq(block):
    count = lax.axis_size("seq")
    if count != 8:
        return gather_slots(block, "seq", doublings(count))
    even = [block] + [swap(block, "seq", m) for m in (2, 4, 6)]
    odd = [swap(item, "seq", 1) for item in even]
    return [item for both in zip(even, odd) for item in both]


def doublings(count):
    return [1 << bit for bit in range(count.bit_length() - 1)]


def add_low(left_arr, right_arr):
    return (left_arr.astype(F32) + right_arr.astype(F32)).astype(BF)


def reduce_slots(parts, axis, masks):
    parts = dict(enumerate(parts))
    for step, mask in enumerate(masks):
        last = step == len(masks) - 1
        for m in [m for m in parts if m & mask]:
            arrived = swap(parts.pop(m), axis, mask)
            mine = parts[m ^ mask]
            parts[m ^ mask] = (
                mine.astype(F32) + arrived.astype(F32) if last else add_low(mine, arrived)
            )
    return parts[0]


def reduce_seq(parts):
    count = lax.axis_size("seq")
    if count != 8:
        return reduce_slots(parts, "seq", doublings(count))
    total = None
    for m in (6, 4, 2, 0):
        arrived = swap(parts[m + 1], "seq", 1)
        if m:
            arrived = swap(add_low(parts[m], arrived), "seq", m)
        else:
            arrived = arrived.astype(F32) + parts[0].astype(F32)
        arrived = arrived.astype(F32)
        total = arrived if total is None else total + arrived
    return total


def rotate(values, cosine, sine, sign):
    lane = lax.broadcasted_iota(jnp.int32, values.shape, 1)
    ahead = pltpu.roll(values, LANES - HEAD_DIM // 2, 1)
    behind = pltpu.roll(values, HEAD_DIM // 2, 1)
    other = jnp.where(lane % HEAD_DIM < HEAD_DIM // 2, ahead, behind)
    return values * cosine + (sign * other) * sine


def project_kernel(order_ref, h_ref, t_ref, up_ref, cos_ref, sin_ref, *rest):
    shards = rest[:-3]
    qkv_ref, full_ref, w_ref = rest[-3:]
    rows = shards[0].shape[0]

    @pl.when(pl.program_id(0) == 0)
    def _():
        for m, shard in enumerate(shards):
            start = pl.multiple_of(order_ref[m] * rows, rows)
            w_ref[pl.ds(start, rows), :] = shard[...]
        full_ref[...] = w_ref[...]

    pre = dot(h_ref[...], w_ref[...]) + dot(t_ref[...], up_ref[...])
    cosine, sine = cos_ref[...], sin_ref[...]
    for j in range(LOCAL // LANES):
        part = pre[:, j * LANES : (j + 1) * LANES]
        if j <= PAIRS:
            part = rotate(part, cosine, sine, 1.0)
        if j < PAIRS:
            part = part * 0.125
        qkv_ref[:, j * LANES : (j + 1) * LANES] = part.astype(BF)


def project(order, h_one, rank_qkv, up_diag, cosine, sine, shards):
    length = h_one.shape[0]
    rows = shards[0].shape[0]
    per_block = lambda width: pl.BlockSpec((BLK, width), lambda i, order: (i, 0))
    whole = lambda shape: pl.BlockSpec(shape, lambda i, order: (0, 0))
    return pl.pallas_call(
        project_kernel,
        grid_spec=pltpu.PrefetchScalarGridSpec(
            num_scalar_prefetch=1,
            grid=(length // BLK,),
            in_specs=[
                per_block(D),
                per_block(3 * RANK),
                whole((3 * RANK, LOCAL)),
                per_block(LANES),
                per_block(LANES),
            ]
            + [whole((rows, LOCAL))] * len(shards),
            out_specs=[per_block(LOCAL), whole((D, LOCAL))],
            scratch_shapes=[pltpu.VMEM((D, LOCAL), BF)],
        ),
        out_shape=[
            jax.ShapeDtypeStruct((length, LOCAL), BF),
            jax.ShapeDtypeStruct((D, LOCAL), BF),
        ],
        cost_estimate=pl.CostEstimate(
            flops=2 * length * D * LOCAL, bytes_accessed=2 * length * (D + LOCAL), transcendentals=0
        ),
        name="project",
    )(order, h_one, rank_qkv, up_diag, cosine, sine, *shards)


def half_mask(shape, half):
    lane = lax.broadcasted_iota(jnp.int32, shape, 1)
    return (lane < HEAD_DIM) if half == 0 else (lane >= HEAD_DIM)


def stack_rows(place_ref, source_ref, target_ref, first_lane):
    half = BLK // 2
    for b in range(source_ref.shape[0] // half):
        rows = pl.ds(pl.multiple_of(place_ref[b] * half, half), half)
        for pair in range(PAIRS):
            at = (b // 2) * PAIRS * BLK + pair * BLK + (b % 2) * half
            lanes = slice(first_lane + pair * LANES, first_lane + (pair + 1) * LANES)
            target_ref[at : at + half, :] = source_ref[rows, lanes]


def split_keys(place_ref, qkv_ref, first_lane, target_ref, ones):
    half = BLK // 2
    for b in range(qkv_ref.shape[0] // half):
        rows = pl.ds(pl.multiple_of(place_ref[b] * half, half), half)
        both = qkv_ref[rows, first_lane : first_lane + LANES]
        for side in range(2):
            other = jnp.zeros_like(both)
            if ones:
                lane = lax.broadcasted_iota(jnp.int32, both.shape, 1)
                spare = HEAD_DIM if side == 0 else 0
                other = jnp.where(lane == spare, 1.0, 0.0).astype(BF)
            target_ref[side, b * half : (b + 1) * half, :] = jnp.where(
                half_mask(both.shape, side), both, other
            )


def tile_bias(start_col, q_first, k_first):
    shape = (BLK, BLK)
    key = k_first + lax.broadcasted_iota(jnp.int32, shape, 1)
    query = q_first + lax.broadcasted_iota(jnp.int32, shape, 0)
    bias = jnp.where((key >= start_col) & (key <= query), 0.0, NEG)
    return jnp.concatenate([bias] * PAIRS, axis=0)


def attend_kernel(place_ref, first_ref, qkv_ref, start_ref, o_ref, lse_ref, q_s, k_s, v_s, m_s, acc_s):
    stack_rows(place_ref, qkv_ref, q_s, 0)
    split_keys(place_ref, qkv_ref, QG, k_s, False)
    split_keys(place_ref, qkv_ref, QG + KG, v_s, True)
    half = BLK // 2
    tall = PAIRS * BLK

    def query_block(qb, unused):
        q_first = pl.multiple_of(qb * BLK, BLK)
        q_rows = pl.ds(pl.multiple_of(qb * tall, tall), tall)
        start_col = start_ref[pl.ds(q_first, BLK), :]
        m_s[...] = jnp.full(m_s.shape, NEG, F32)
        acc_s[...] = jnp.zeros(acc_s.shape, F32)

        def key_block(kb, unused):
            k_first = pl.multiple_of(kb * BLK, BLK)
            bias = tile_bias(start_col, q_first, k_first)
            queries = q_s[q_rows, :]
            for side in range(2):
                scores = dot_nt(queries, k_s[side, pl.ds(k_first, BLK), :]) + bias
                old = m_s[side]
                new = jnp.maximum(old, jnp.max(scores, axis=1, keepdims=True))
                prob = jnp.exp(scores - new)
                m_s[side] = new
                acc_s[side] = acc_s[side] * jnp.exp(old - new) + dot(
                    prob.astype(BF), v_s[side, pl.ds(k_first, BLK), :]
                )
            return unused

        lax.fori_loop(first_ref[qb], qb + 1, key_block, 0)
        low, high = acc_s[0], acc_s[1]
        low_sum = low[:, HEAD_DIM : HEAD_DIM + 1]
        high_sum = high[:, 0:1]
        is_low = half_mask(low.shape, 0)
        out = jnp.where(is_low, low / low_sum, high / high_sum).astype(BF)
        lse_ref[q_rows, :] = jnp.where(
            is_low, m_s[0] + jnp.log(low_sum), m_s[1] + jnp.log(high_sum)
        )
        for i in range(2):
            rows = pl.ds(pl.multiple_of(place_ref[2 * qb + i] * half, half), half)
            for pair in range(PAIRS):
                at = pair * BLK + i * half
                o_ref[rows, pair * LANES : (pair + 1) * LANES] = out[at : at + half, :]
        return unused

    lax.fori_loop(0, qkv_ref.shape[0] // BLK, query_block, 0)


SMEM_SPEC = pl.BlockSpec(memory_space=pltpu.SMEM)
VMEM_SPEC = pl.BlockSpec(memory_space=pltpu.VMEM)


def attend(place, first, qkv, start_col):
    length = qkv.shape[0]
    tall = PAIRS * BLK
    return pl.pallas_call(
        attend_kernel,
        in_specs=[SMEM_SPEC, SMEM_SPEC, VMEM_SPEC, VMEM_SPEC],
        out_specs=[VMEM_SPEC, VMEM_SPEC],
        out_shape=[
            jax.ShapeDtypeStruct((length, QG), BF),
            jax.ShapeDtypeStruct((PAIRS * length, LANES), F32),
        ],
        scratch_shapes=[
            pltpu.VMEM((PAIRS * length, LANES), BF),
            pltpu.VMEM((2, length, LANES), BF),
            pltpu.VMEM((2, length, LANES), BF),
            pltpu.VMEM((2, tall, 1), F32),
            pltpu.VMEM((2, tall, LANES), F32),
        ],
        cost_estimate=pl.CostEstimate(
            flops=4 * length * length * QG, bytes_accessed=8 * length * QG, transcendentals=0
        ),
        name="attend",
    )(place, first, qkv, start_col)


def attend_back_kernel(
    place_ref,
    first_ref,
    qkv_ref,
    start_ref,
    o_ref,
    lse_ref,
    do_ref,
    cos_ref,
    sin_ref,
    dqkv_ref,
    q_s,
    o_s,
    do_s,
    k_s,
    v_s,
    dk_s,
    dv_s,
    dq_s,
):
    stack_rows(place_ref, qkv_ref, q_s, 0)
    stack_rows(place_ref, o_ref, o_s, 0)
    stack_rows(place_ref, do_ref, do_s, 0)
    split_keys(place_ref, qkv_ref, QG, k_s, False)
    split_keys(place_ref, qkv_ref, QG + KG, v_s, False)
    dk_s[...] = jnp.zeros(dk_s.shape, F32)
    dv_s[...] = jnp.zeros(dv_s.shape, F32)
    half = BLK // 2
    tall = PAIRS * BLK

    def query_block(qb, unused):
        q_first = pl.multiple_of(qb * BLK, BLK)
        q_rows = pl.ds(pl.multiple_of(qb * tall, tall), tall)
        start_col = start_ref[pl.ds(q_first, BLK), :]
        dq_s[...] = jnp.zeros(dq_s.shape, F32)
        product = do_s[q_rows, :].astype(F32) * o_s[q_rows, :].astype(F32)
        lse = lse_ref[q_rows, :]
        lse_of = (lse[:, 0:1], lse[:, HEAD_DIM : HEAD_DIM + 1])
        delta_of = [
            jnp.sum(jnp.where(half_mask(product.shape, side), product, 0.0), axis=1, keepdims=True)
            for side in range(2)
        ]

        def key_block(kb, unused):
            k_first = pl.multiple_of(kb * BLK, BLK)
            k_rows = pl.ds(k_first, BLK)
            bias = tile_bias(start_col, q_first, k_first)
            queries = q_s[q_rows, :]
            d_out = do_s[q_rows, :]
            for side in range(2):
                keys = k_s[side, k_rows, :]
                scores = dot_nt(queries, keys) + bias
                prob = jnp.exp(scores - lse_of[side])
                d_prob = dot_nt(d_out, v_s[side, k_rows, :])
                d_score = (prob * (d_prob - delta_of[side])).astype(BF)
                dv_s[side, k_rows, :] += dot_tn(prob.astype(BF), d_out)
                dk_s[side, k_rows, :] += dot_tn(d_score, queries)
                dq_s[...] += dot(d_score, keys)
            return unused

        lax.fori_loop(first_ref[qb], qb + 1, key_block, 0)
        for i in range(2):
            rows = pl.ds(pl.multiple_of(place_ref[2 * qb + i] * half, half), half)
            cosine, sine = cos_ref[rows, :], sin_ref[rows, :]
            for pair in range(PAIRS):
                at = pair * BLK + i * half
                back = rotate(dq_s[at : at + half, :] * 0.125, cosine, sine, -1.0)
                dqkv_ref[rows, pair * LANES : (pair + 1) * LANES] = back.astype(BF)
        return unused

    lax.fori_loop(0, qkv_ref.shape[0] // BLK, query_block, 0)
    for b in range(qkv_ref.shape[0] // half):
        rows = pl.ds(pl.multiple_of(place_ref[b] * half, half), half)
        at = slice(b * half, (b + 1) * half)
        is_low = half_mask((half, LANES), 0)
        back = jnp.where(is_low, dk_s[0, at, :], dk_s[1, at, :])
        back = rotate(back, cos_ref[rows, :], sin_ref[rows, :], -1.0)
        dqkv_ref[rows, QG : QG + KG] = back.astype(BF)
        dqkv_ref[rows, QG + KG : LOCAL] = jnp.where(is_low, dv_s[0, at, :], dv_s[1, at, :]).astype(BF)


def attend_back(place, first, qkv, start_col, out, lse, d_out, cosine, sine):
    length = qkv.shape[0]
    tall = PAIRS * BLK
    stacked = pltpu.VMEM((PAIRS * length, LANES), BF)
    return pl.pallas_call(
        attend_back_kernel,
        in_specs=[SMEM_SPEC, SMEM_SPEC] + [VMEM_SPEC] * 7,
        out_specs=VMEM_SPEC,
        out_shape=jax.ShapeDtypeStruct((length, LOCAL), BF),
        scratch_shapes=[
            stacked,
            stacked,
            stacked,
            pltpu.VMEM((2, length, LANES), BF),
            pltpu.VMEM((2, length, LANES), BF),
            pltpu.VMEM((2, length, LANES), F32),
            pltpu.VMEM((2, length, LANES), F32),
            pltpu.VMEM((tall, LANES), F32),
        ],
        cost_estimate=pl.CostEstimate(
            flops=10 * length * length * QG, bytes_accessed=16 * length * QG, transcendentals=0
        ),
        name="attend_back",
    )(place, first, qkv, start_col, out, lse, d_out, cosine, sine)


def expert_kernel(ids_ref, h_refs, p_refs, wgu_ref, wd_ref, tables, y_refs, d_refs, scratch):
    aux_w, gu_refs, da_refs, db_refs = tables
    aux_s, gu_s, sel_s, yrow_s, drow_s, grad_s = scratch
    step = pl.program_id(0)
    wide = lax.broadcasted_iota(jnp.int32, (h_refs[0].shape[0], LANES), 1)
    count = len(h_refs)
    lane = EXP_AT + ids_ref[count] + step

    @pl.when(step == 0)
    def _():
        grad_s[...] = jnp.zeros(grad_s.shape, F32)
        gu_s[...] = jnp.zeros(gu_s.shape, BF)
        for j in range(count):
            gu_s[j, 0, 0:RANK, :] = gu_refs[j][0, 0]
            gu_s[j, 1, RANK : 2 * RANK, :] = gu_refs[j][0, 1]
            both = dot_nt(h_refs[j][...], aux_w[j][0])
            chosen = p_refs[j][:, D:EXT].astype(F32) > 0.0
            picked = jnp.where(chosen, both, NEG)
            weights = jnp.exp(picked - jnp.max(picked, axis=1, keepdims=True))
            gates = weights / jnp.sum(weights, axis=1, keepdims=True)
            aux_s[j] = jnp.where(wide < EXP_AT, both, gates)

    rows, extra, upstream = [], [], []
    for j in range(count):
        ranks = p_refs[j][:, D:EXT].astype(F32)
        column = jnp.sum(jnp.where(wide == lane, ranks, 0.0), axis=1, keepdims=True)
        tall = ranks.T
        which = lax.broadcasted_iota(jnp.int32, tall.shape, 0)
        row = jnp.sum(jnp.where(which == lane, tall, 0.0), axis=0, keepdims=True)
        slot = lax.broadcasted_iota(jnp.int32, (CAP, tall.shape[1]), 0).astype(F32) + 1.0
        take = jnp.where(slot == row, 1.0, 0.0).astype(BF)
        sel_s[j, step] = jnp.where(wide.astype(F32) + 1.0 == column, 1.0, 0.0).astype(BF)
        aux = aux_s[j]
        gate = jnp.sum(jnp.where(wide == lane, aux, 0.0), axis=1, keepdims=True)
        gate_one = gate.astype(BF).astype(F32)
        gate_two = (gate - gate_one).astype(BF).astype(F32)
        gate_three = gate - gate_one - gate_two
        aux = jnp.where(wide < EXP_AT, aux, 0.0)
        aux = jnp.where(wide == GATE_AT, gate_one, aux)
        aux = jnp.where(wide == GATE_AT + 1, gate_two, aux)
        aux = jnp.where(wide == GATE_AT + 2, gate_three, aux)
        rows.append(dot(take, h_refs[j][...]).astype(BF))
        extra.append(dot(take, aux.astype(BF)))
        upstream.append(dot(take, p_refs[j][:, :D]))

    def each(make):
        return jnp.concatenate([make(j) for j in range(count)], axis=0)

    part = lambda arr, j: arr[j * CAP : (j + 1) * CAP]
    low_extra = [item.astype(BF) for item in extra]
    narrow = lax.broadcasted_iota(jnp.int32, (CAP, LANES), 1)
    gate = each(
        lambda j: jnp.sum(
            jnp.where((narrow >= GATE_AT) & (narrow < GATE_AT + 3), extra[j], 0.0),
            axis=1,
            keepdims=True,
        )
    )
    both = dot(jnp.concatenate(rows, axis=0), wgu_ref[0])
    gate_pre = both[:, :FF] + each(lambda j: dot(low_extra[j], gu_s[j, 0]))
    up_pre = both[:, FF:] + each(lambda j: dot(low_extra[j], gu_s[j, 1]))
    sigmoid = jax.nn.sigmoid(gate_pre)
    silu = gate_pre * sigmoid
    active = (silu * up_pre).astype(BF)
    down = [dot_nt(part(active, j), da_refs[j][0]).astype(BF) for j in range(count)]
    result = dot(active, wd_ref[0]) + each(lambda j: dot(down[j], db_refs[j][0]))
    result = result.astype(BF).astype(F32)
    grad_in = jnp.concatenate(upstream, axis=0)
    d_gate_val = jnp.sum(grad_in * result, axis=1, keepdims=True)
    weighted = (gate * result).astype(BF)
    d_result = (gate * grad_in).astype(BF)
    d_down = [dot_nt(part(d_result, j), db_refs[j][0]).astype(BF) for j in range(count)]
    d_active = dot_nt(d_result, wd_ref[0]) + each(lambda j: dot(d_down[j], da_refs[j][0]))
    d_gate = (d_active * up_pre * sigmoid * (1.0 + gate_pre * (1.0 - sigmoid))).astype(BF)
    d_up = (d_active * silu).astype(BF)
    d_rows = dot_nt(jnp.concatenate([d_gate, d_up], axis=1), wgu_ref[0]).astype(BF)
    for j in range(count):
        at = pl.ds(pl.multiple_of(step * CAP, CAP), CAP)
        yrow_s[j, at, :] = part(weighted, j)
        drow_s[j, at, :D] = part(d_rows, j)
        d_extra = dot_nt(part(d_gate, j), gu_s[j, 0]) + dot_nt(part(d_up, j), gu_s[j, 1])
        d_extra = d_extra + jnp.where(narrow == lane, part(d_gate_val, j), 0.0)
        drow_s[j, at, D:] = d_extra.astype(BF)
        grad_s[j, 0:RANK, 0:FF] += dot_tn(low_extra[j], part(d_gate, j))[0:RANK]
        grad_s[j, 0:RANK, FF : 2 * FF] += dot_tn(low_extra[j], part(d_up, j))[RANK : 2 * RANK]
        grad_s[j, 0:RANK, 2 * FF :] += dot_tn(d_down[j], part(active, j))
        grad_s[j, RANK:, :] += dot_tn(down[j], part(d_result, j))

    @pl.when(step == E_DEV - 1)
    def _():
        for j in range(count):
            tokens = h_refs[j].shape[0]
            put = jnp.concatenate([sel_s[j, e] for e in range(E_DEV)], axis=1)
            y_refs[j][:tokens, :] = dot(put, yrow_s[j]).astype(BF)
            y_refs[j][tokens:, :] = grad_s[j].astype(BF)
            d_refs[j][...] = dot(put, drow_s[j]).astype(BF)


def experts(adapters, base, rows, packs, w_gate_up, w_down, aux_w, gu_up, down_a, down_b):
    count = len(rows)
    tokens = rows[0].shape[0]
    whole = lambda width: pl.BlockSpec((tokens, width), lambda e, ids: (0, 0))

    def table(shape, j):
        return pl.BlockSpec((1,) + shape, lambda e, ids: (ids[j],) + (0,) * len(shape))

    def body(ids_ref, *refs):
        refs = list(refs)
        take = lambda n: [refs.pop(0) for _ in range(n)]
        h_refs, p_refs = take(count), take(count)
        wgu_ref, wd_ref = take(2)
        tables = [take(count) for _ in range(4)]
        y_refs, d_refs = take(count), take(count)
        expert_kernel(ids_ref, h_refs, p_refs, wgu_ref, wd_ref, tables, y_refs, d_refs, refs)

    picked = [(LANES, D), (2, RANK, FF), (RANK, FF), (RANK, D)]
    shapes = [(tokens + 2 * RANK, D)] * count + [(tokens, EXT)] * count
    outs = pl.pallas_call(
        body,
        grid_spec=pltpu.PrefetchScalarGridSpec(
            num_scalar_prefetch=1,
            grid=(E_DEV,),
            in_specs=[whole(D)] * count
            + [whole(EXT)] * count
            + [
                pl.BlockSpec((1, D, 2 * FF), lambda e, ids: (e, 0, 0)),
                pl.BlockSpec((1, FF, D), lambda e, ids: (e, 0, 0)),
            ]
            + [table(shape, j) for shape in picked for j in range(count)],
            out_specs=[pl.BlockSpec(shape, lambda e, ids: (0, 0)) for shape in shapes],
            scratch_shapes=[
                pltpu.VMEM((count, tokens, LANES), F32),
                pltpu.VMEM((count, 2, LANES, FF), BF),
                pltpu.VMEM((count, E_DEV, tokens, CAP), BF),
                pltpu.VMEM((count, E_DEV * CAP, D), BF),
                pltpu.VMEM((count, E_DEV * CAP, EXT), BF),
                pltpu.VMEM((count, 2 * RANK, D), F32),
            ],
        ),
        out_shape=[jax.ShapeDtypeStruct(shape, BF) for shape in shapes],
        cost_estimate=pl.CostEstimate(
            flops=16 * count * E_DEV * CAP * D * FF,
            bytes_accessed=2 * E_DEV * 3 * D * FF + 8 * count * tokens * D,
            transcendentals=0,
        ),
        name="experts",
    )(
        jnp.concatenate([adapters, base[None]]).astype(jnp.int32),
        *rows,
        *packs,
        w_gate_up,
        w_down,
        *([aux_w] * count),
        *([gu_up] * count),
        *([down_a] * count),
        *([down_b] * count),
    )
    return outs[:count], outs[count:]


def norm_backward(values, inverse, gain_vec, upstream):
    scaled = gain_vec * upstream
    return inverse * scaled - values * inverse**3 * jnp.mean(
        values * scaled, axis=-1, keepdims=True
    )


def pair_columns(columns):
    lead = columns.shape[:-1]
    heads = columns.reshape(lead + (2 * PAIRS, HEAD_DIM))
    return heads[..., jnp.array(PAIR_ORDER), :].reshape(lead + (QG,))


def local_columns(table, group):
    lead = table.shape[:-1]
    cut = lambda first, width: lax.dynamic_slice_in_dim(
        table, first + group * width, width, table.ndim - 1
    )
    return cut(0, QG), cut(QW, KG), cut(QW + KVW, KG)


def on_device(
    inputs,
    cotangent,
    segment_ids,
    expert_ids,
    adapter_ids,
    gain_one,
    w_qkv,
    w_out,
    gain_two,
    router,
    w_gate_up,
    w_down,
    qkv_down,
    qkv_up,
    out_down,
    out_up,
    gu_down,
    gu_up,
    down_a,
    down_b,
):
    ctx_count = lax.axis_size("ctx")
    seq_count = lax.axis_size("seq")
    ctx_index = lax.axis_index("ctx")
    seq_index = lax.axis_index("seq")
    tokens = inputs.shape[1]
    length = tokens * ctx_count
    experts_all = router.shape[1]
    copies = ctx_count // GROUPS
    group = ctx_index // copies
    half = tokens // 2
    ctx_masks = doublings(ctx_count)[::-1]
    seq_slots = seq_index ^ jnp.arange(seq_count)
    ctx_slots = ctx_index ^ jnp.arange(ctx_count)
    group_slots = group ^ jnp.arange(GROUPS)
    own_rows = inputs[0]

    row_slots = gather_slots(own_rows, "ctx", ctx_masks)
    own_q, own_k, own_v = local_columns(w_qkv, group)
    own_cols = jnp.concatenate([pair_columns(own_q), own_k, own_v], axis=1)
    col_slots = gather_seq(own_cols)
    chosen = expert_ids[0]
    hot = jnp.any(chosen[:, :, None] == jnp.arange(experts_all)[None, None, :], axis=1)
    hot_low = hot.astype(BF)
    before = (jnp.arange(tokens)[:, None] >= jnp.arange(tokens)[None, :]).astype(BF)
    ranks = dot(before, hot_low).astype(BF) * hot_low
    ranks = jnp.pad(ranks, ((0, 0), (EXP_AT, LANES - EXP_AT - experts_all)))
    pack_slots = gather_seq(jnp.concatenate([cotangent[0], ranks], axis=1))
    out_part = D // ctx_count
    own_out = lax.dynamic_slice_in_dim(w_out, ctx_index * out_part, out_part, 1)
    out_slots = jnp.stack(gather_seq(own_out))[seq_slots].reshape(QW, out_part)
    out_all = jnp.stack(gather_slots(out_slots, "ctx", ctx_masks))[ctx_slots]
    out_all = jnp.transpose(out_all, (1, 0, 2)).reshape(GROUPS, 2, PAIRS, HEAD_DIM, D)
    out_all = jnp.transpose(out_all, (0, 2, 1, 3, 4)).reshape(GROUPS, QG, D)[group_slots]
    out_all = out_all.reshape(QW, D)

    seg_row = segment_ids[0]
    position = jnp.arange(length)
    start = jnp.sum((seg_row[None, :] < seg_row[:, None]).astype(jnp.int32), axis=1)
    block_id = jnp.stack([ctx_slots, 2 * ctx_count - 1 - ctx_slots], axis=1).reshape(-1)
    block_of = jnp.arange(2 * ctx_count)
    owner = jnp.minimum(block_of, 2 * ctx_count - 1 - block_of)
    place = (2 * (owner ^ ctx_index) + (block_of >= ctx_count)).astype(jnp.int32)
    first = (start[::BLK] // BLK).astype(jnp.int32)
    offset = (position - start).reshape(2 * ctx_count, half)[block_id].reshape(-1)
    frequency = 10000.0 ** (
        -2.0 * jnp.arange(HEAD_DIM // 2).astype(F32) / HEAD_DIM
    )
    angles = offset.astype(F32)[:, None] * frequency[None, :]
    cosine, sine = jnp.cos(angles), jnp.sin(angles)
    cosine = jnp.concatenate([cosine] * 4, axis=1)
    sine = jnp.concatenate([-sine, sine, -sine, sine], axis=1)
    start_col = start[:, None]
    adapter = adapter_ids[seq_index]
    slot_adapters = adapter_ids[seq_slots]

    def pick(table):
        return lax.dynamic_index_in_dim(table, adapter, 0, keepdims=False)

    qkv_down_sel = pick(qkv_down)
    up_q, up_k, up_v = local_columns(pick(qkv_up), group)
    up_q = pair_columns(up_q)
    up_diag = jnp.concatenate(
        [
            jnp.pad(up_q, ((0, 0), (0, 2 * KG))),
            jnp.pad(up_k, ((0, 0), (QG, KG))),
            jnp.pad(up_v, ((0, 0), (QG + KG, 0))),
        ],
        axis=0,
    )
    out_down_sel = pick(out_down).reshape(GROUPS, 2, PAIRS, HEAD_DIM, RANK)
    out_down_sel = jnp.transpose(out_down_sel, (0, 2, 1, 3, 4)).reshape(GROUPS, QG, RANK)
    out_down_sel = out_down_sel[group_slots].reshape(QW, RANK)
    out_up_sel = pick(out_up)
    gu_down_sel = pick(gu_down)
    aux_w = jnp.concatenate(
        [
            jnp.swapaxes(gu_down, 1, 2),
            jnp.broadcast_to(router.T[None], (ADAPT, experts_all, D)),
            jnp.zeros((ADAPT, LANES - 2 * RANK - experts_all, D), BF),
        ],
        axis=1,
    )
    down_a_t = jnp.swapaxes(down_a, 1, 2)

    features = own_rows.astype(F32)
    inv_one = lax.rsqrt(jnp.mean(features * features, axis=-1, keepdims=True) + NORM_EPS)
    all_rows = jnp.concatenate(row_slots, axis=0).astype(F32)
    inv_all = lax.rsqrt(jnp.mean(all_rows * all_rows, axis=-1, keepdims=True) + NORM_EPS)
    h_one = (all_rows * inv_all * gain_one).astype(BF)
    rank_qkv = dot(h_one, qkv_down_sel).astype(BF)
    qkv, cols_all = project(
        seq_slots.astype(jnp.int32), h_one, rank_qkv, up_diag, cosine, sine, col_slots
    )
    heads_out, lse = attend(place, first, qkv, start_col)

    def to_tokens(by_slot):
        parts = by_slot.reshape(ctx_count, tokens, QG)
        got = [
            swap(parts[j * copies], "ctx", j * copies) if j else parts[0] for j in range(GROUPS)
        ]
        return jnp.concatenate(got, axis=1)

    def to_heads(by_group):
        got = []
        for m in range(ctx_count):
            piece = by_group[:, (m // copies) * QG : (m // copies + 1) * QG]
            got.append(swap(piece, "ctx", m) if m else piece)
        return jnp.concatenate(got, axis=0)

    attended = to_tokens(heads_out)
    rank_out = dot(attended, out_down_sel).astype(BF)
    y_one = features + dot(attended, out_all) + dot(rank_out, out_up_sel)
    inv_two = lax.rsqrt(jnp.mean(y_one * y_one, axis=-1, keepdims=True) + NORM_EPS)
    h_two = (y_one * inv_two * gain_two).astype(BF)

    h_slots = gather_seq(h_two)
    y_parts, d_parts = [], []
    for m in range(0, seq_count, 2):
        y_pair, d_pair = experts(
            slot_adapters[m : m + 2],
            E_DEV * seq_index,
            h_slots[m : m + 2],
            pack_slots[m : m + 2],
            w_gate_up,
            w_down,
            aux_w,
            gu_up,
            down_a_t,
            down_b,
        )
        y_parts += y_pair
        d_parts += d_pair
    d_sum = reduce_seq(d_parts)
    y_sum = reduce_seq(y_parts)
    layer_output = (y_one + y_sum[:tokens]).astype(BF)[None]

    grad_two = cotangent[0].astype(F32)
    logits = dot(h_two, router)
    picked = jnp.where(hot, logits, NEG)
    weights = jnp.exp(picked - jnp.max(picked, axis=-1, keepdims=True))
    gates = weights / jnp.sum(weights, axis=-1, keepdims=True)
    d_gates = d_sum[:, D + EXP_AT : D + EXP_AT + experts_all]
    d_logits = (gates * (d_gates - jnp.sum(gates * d_gates, axis=-1, keepdims=True))).astype(BF)
    d_rank_gu = d_sum[:, D : D + 2 * RANK].astype(BF)
    d_h_two = d_sum[:, :D] + dot(d_logits, router.T) + dot(d_rank_gu, gu_down_sel.T)
    d_y_one = grad_two + norm_backward(y_one, inv_two, gain_two, d_h_two)
    d_attn = d_y_one.astype(BF)
    d_rank_out = dot(d_attn, out_up_sel.T).astype(BF)
    d_attended = (dot(d_attn, out_all.T) + dot(d_rank_out, out_down_sel.T)).astype(BF)
    d_heads = to_heads(d_attended)

    grad_out_down = dot(d_rank_out.T, attended).reshape(RANK, GROUPS, QG)[:, group_slots]
    grad_out_down = grad_out_down.reshape(RANK, GROUPS, PAIRS, 2, HEAD_DIM)
    grad_out_down = jnp.transpose(grad_out_down, (0, 1, 3, 2, 4)).reshape(RANK, QW)
    early = jnp.concatenate(
        [
            y_sum[tokens:],
            grad_out_down,
            dot(rank_out.T, d_attn),
            dot(d_rank_gu.T, h_two),
        ],
        axis=0,
    ).astype(BF)
    early_rows = early.shape[0]
    early = early.reshape(ctx_count, early_rows // ctx_count, D)[ctx_slots]
    early = reduce_slots([early[m] for m in range(ctx_count)], "ctx", ctx_masks[::-1]).astype(BF)
    early = jnp.stack(gather_seq(early))
    early = jnp.stack(gather_slots(early, "ctx", ctx_masks))[ctx_slots]

    d_qkv = attend_back(place, first, qkv, start_col, heads_out, lse, d_heads, cosine, sine)
    d_rows = dot_nt(d_qkv, cols_all).astype(BF).reshape(ctx_count, tokens, D)
    live = [m for m in range(ctx_count) if m % copies == 0]
    d_rank_qkv = dot_nt(d_qkv, up_diag)
    for mask in [copies * m for m in doublings(GROUPS)]:
        low = d_rank_qkv.astype(BF)
        arrived = swap(low, "ctx", mask).reshape(ctx_count, tokens, 3 * RANK)
        arrived = arrived[jnp.arange(ctx_count) ^ mask].reshape(length, 3 * RANK)
        d_rank_qkv = low.astype(F32) + arrived.astype(F32)
    d_rank_qkv = d_rank_qkv.astype(BF)
    d_h_one = reduce_ctx(d_rows, copies) + dot_nt(d_rank_qkv[:tokens], qkv_down_sel)
    input_grad = (d_y_one + norm_backward(features, inv_one, gain_one, d_h_one))[None]

    slice_width = D // ctx_count
    h_slice = lax.dynamic_slice_in_dim(h_one, ctx_index * slice_width, slice_width, 1)
    down_grad = dot(d_rank_qkv.T, h_slice).reshape(3, RANK, slice_width)
    late = jnp.concatenate(
        [
            dot(rank_qkv[:, :RANK].T, d_qkv[:, :QG]),
            dot(rank_qkv[:, RANK : 2 * RANK].T, d_qkv[:, QG : QG + KG]),
            dot(rank_qkv[:, 2 * RANK :].T, d_qkv[:, QG + KG :]),
            down_grad[0],
            down_grad[1],
            down_grad[2],
        ],
        axis=1,
    ).astype(BF)
    late = jnp.stack(gather_seq(late))
    late = jnp.stack(gather_slots(late, "ctx", ctx_masks))[ctx_slots]

    source_hot = (slot_adapters[:, None] == jnp.arange(ADAPT)[None, :]).astype(BF)

    def by_adapter(values):
        return jnp.einsum("sa,csrd->acrd", source_hot, values, preferred_element_type=F32)

    early = by_adapter(early).reshape(ADAPT, early_rows, D)
    grad_gate = early[:, :RANK, :FF]
    grad_up = early[:, :RANK, FF : 2 * FF]
    grad_gu_up = jnp.stack([grad_gate, grad_up], axis=1)
    grad_down_a = jnp.swapaxes(early[:, :RANK, 2 * FF :], 1, 2)
    grad_down_b = early[:, RANK : 2 * RANK]
    grad_out_down = jnp.swapaxes(early[:, 2 * RANK : 3 * RANK], 1, 2)
    grad_out_up = early[:, 3 * RANK : 4 * RANK]
    grad_gu_down = jnp.swapaxes(early[:, 4 * RANK :], 1, 2)
    late = by_adapter(late)
    heads_late = late[:, ::copies]
    grad_q = heads_late[..., :QG].reshape(ADAPT, GROUPS, RANK, PAIRS, 2, HEAD_DIM)
    grad_q = jnp.transpose(grad_q, (0, 2, 1, 4, 3, 5)).reshape(ADAPT, RANK, QW)
    merge = lambda part: jnp.transpose(part, (0, 2, 1, 3)).reshape(ADAPT, RANK, -1)
    grad_qkv_up = jnp.concatenate(
        [grad_q, merge(heads_late[..., QG : QG + KG]), merge(heads_late[..., QG + KG : LOCAL])],
        axis=2,
    )
    down_part = late[..., LOCAL:].reshape(ADAPT, ctx_count, RANK, 3, slice_width)
    grad_qkv_down = jnp.transpose(down_part, (0, 1, 4, 3, 2)).reshape(ADAPT, D, 3 * RANK)
    return (
        layer_output,
        input_grad,
        grad_qkv_down,
        grad_qkv_up,
        grad_out_down,
        grad_out_up,
        grad_gu_down,
        grad_gu_up,
        grad_down_a,
        grad_down_b,
    )


def reduce_ctx(parts, copies):
    parts = dict(enumerate(parts))
    masks = doublings(len(parts))
    for mask in masks:
        for m in [m for m in parts if m & mask]:
            sent = parts.pop(m)
            if mask >= copies:
                parts[m ^ mask] = add_low(parts[m ^ mask], swap(sent, "ctx", mask))
    return parts[0].astype(F32)


def solution(mesh):
    over_seq = P("seq", None)
    placed = (
        P("seq", "ctx", None),
        P("seq", "ctx", None),
        over_seq,
        P("seq", "ctx", None),
        P(),
        P(),
        over_seq,
        over_seq,
        P(),
        P(),
        P("seq", None, None),
        P("seq", None, None),
    ) + (P(),) * 8
    return jax.shard_map(
        on_device,
        mesh=mesh,
        in_specs=placed,
        out_specs=(P("seq", "ctx", None), P("seq", "ctx", None)) + (P(),) * 8,
        check_vma=False,
    )
```

time: 1380 us -> 831 us (0.60)
  waiting for transfers between devices: 704 us -> 337 us
  matrix products: 195 us -> 39.3 us
  blocking collectives: 142 us -> 0 us
  Pallas kernels: 0 us -> 127 us
  starting transfers between devices: 24.1 us -> 111 us
  local copies, waits for them, and re-layouts: 190 us -> 147 us
  other arithmetic: 80.3 us -> 60.2 us
    all_to_all x5 -> x0, waiting for transfers between devices: 381 us -> none  [the longest x1 132 us: on_device(): lax.all_to_all(send_rows, 'seq', split_axis=0, concat_axis=0, tiled=True)]
    ppermute x0 -> x82, waiting for transfers between devices: none -> 337 us  [swap(): return lax.ppermute(block, axis, [(i, i ^ mask) for i in range(count)])]
    psum x1 -> x0, waiting for transfers between devices: 173 us -> none  [on_device(): lax.psum((term_qkv_down, term_qkv_up, term_out_down, term_out_up, term_gu...]
    dot_general x65 -> x23, matrix products: 195 us -> 39.3 us  [the longest x18 27.5 us: dot(): return jnp.dot(left_arr, right_arr, preferred_element_type=F32)]
    all_to_all x1 -> x0, blocking collectives: 142 us -> none  [on_device(): lax.all_to_all(send_grads, 'seq', split_axis=0, concat_axis=0, tiled=True)]
    pallas_call x0 -> x7, Pallas kernels: none -> 127 us  [the longest x4 70.7 us: experts(): pl.pallas_call(body, grid_spec=pltpu.PrefetchScalarGridSpec(num_scalar_pr...]
    all_gather x4 -> x0, waiting for transfers between devices: 114 us -> none  [the longest x1 114 us: on_device(): lax.all_gather(w_qkv, 'seq', axis=0, tiled=True)]
    ppermute x0 -> x82, starting transfers between devices: none -> 111 us  [swap(): return lax.ppermute(block, axis, [(i, i ^ mask) for i in range(count)])]
  transfers between devices with their start and end apart: 12 -> 82, of which waited for: 8 -> 30; matrix products, arithmetic and copies ran while one was open for 15% -> 26% of each run, Pallas kernels for 0% -> 15%
where the time goes in v1:
time: 831 us; the launch traced here: 825 us
  waiting for transfers between devices  337 us (41%)
  local copies, waits for them, and re-layouts  147 us (18%)
  Pallas kernels  127 us (15%)
  starting transfers between devices  111 us (13%)
  other arithmetic  60.2 us (7%)
  matrix products  39.3 us (5%)
    ppermute x82, waiting for transfers between devices, swap(): return lax.ppermute(block, axis, [(i, i ^ mask) for i in range(count)])  337 us
    ppermute x82, starting transfers between devices, swap(): return lax.ppermute(block, axis, [(i, i ^ mask) for i in range(count)])  111 us
    pallas_call x4, Pallas kernels, experts(): pl.pallas_call(body, grid_spec=pltpu.PrefetchScalarGridSpec(num_scalar_pr...  70.7 us
    unnamed x173, local copies, waits for them, and re-layouts  29.7 us
    pallas_call x1, Pallas kernels, attend(): pl.pallas_call(attend_kernel, in_specs=[SMEM_SPEC, SMEM_SPEC, VMEM_SPEC,...  28 us
    dot_general x18, matrix products, dot(): return jnp.dot(left_arr, right_arr, preferred_element_type=F32)  27.5 us
    pallas_call x1, Pallas kernels, attend_back(): pl.pallas_call(attend_back_kernel, in_specs=[SMEM_SPEC, SMEM_SPEC] + [VME...  19.6 us
    transpose x1, local copies, waits for them, and re-layouts, on_device(): jnp.transpose(out_all, (1, 0, 2)).reshape(GROUPS, 2, PAIRS, HEAD_DIM, D)  18.1 us
  transfers between devices with their start and end apart: 82, of which 30 were waited for; matrix products, arithmetic and copies ran while one was open for 26% of the time, Pallas kernels for 15%

profile of v1, /device:TPU:0, one launch (start us, length us, event | category | flops | bytes accessed | tf_op | source)
XLA Modules:
  0.0 825.0 jit_solution(9475859091869457169)
XLA Ops:
  79.0 19.8 %collective-permute-done.21 = bf16[1536,384]{1,0:T(8,128)(2,1)} collective-permute-done((bf16[1536,384]{1,0:T(8,128)(2,1)S(1)}, bf16[1536,384]{1,0:T(8,128)(2,1)}, u32[]{:S(2)}, u32[]{:S(2)}) %collective-permute-start.21) | collective-permute-done | bytes 1179680 | tf_op jit(solution)/shard_map/ppermute | solution.py:56
  98.9 8.3 %project.1 = (bf16[1024,640]{1,0:T(8,128)(2,1)}, bf16[1536,640]{1,0:T(8,128)(2,1)}) custom-call(s32[8]{0:T(128)} %iota_xor_fusion.1.order_ref, bf16[1024,1536]{1,0:T(8,128)(2,1)} %copy-done.6, bf16[1024,48]{1,0:T(8,128)(2,1)} %convolution_convert_fusion.3.t_ref, bf16[48,640]{1,0:T(8,128)(2,1)} %fusion.53.up_ref, f32[1024,128]{1,0:T(8,128)} %pad_maximum_fusion.7.cos_ref, ...), custom_call_target="tpu_custom_call" | custom-call | flops 2013265920 | bytes 4456448 | tf_op jit(solution)/shard_map/project/pallas_call | solution.py:149
  107.1 28.0 %attend.1 = (bf16[1024,384]{1,0:T(8,128)(2,1)}, f32[3072,128]{1,0:T(8,128)}) custom-call(s32[8]{0:T(128)} %fusion.73.place_ref, s32[4]{0:T(128)} %and_select_fusion.first_ref, bf16[1024,640]{1,0:T(8,128)(2,1)} %get-tuple-element.30.qkv_ref, s32[1024,1]{1,0:T(8,128)} %copy.155.start_ref), custom_call_target="tpu_custom_call" | custom-call | flops 1610612736 | bytes 3145728 | tf_op jit(solution)/shard_map/attend/pallas_call | solution.py:270
  156.4 5.9 gather_fusion.4
  162.3 18.1 %copy.156 = bf16[1536,4,384]{2,1,0:T(4,128)(2,1)} copy(bf16[1536,4,384]{2,0,1:T(8,128)(2,1)} %bitcast.242) | data formatting | bytes 9437184 | tf_op jit(solution)/shard_map/transpose | solution.py:633
  180.4 9.1 %reshape.402 = bf16[4,2,3,64,1536]{4,3,2,1,0:T(8,128)(2,1)} reshape(bf16[1536,4,384]{2,1,0:T(4,128)(2,1)} %copy.156) | data formatting | bytes 9437184 | tf_op jit(solution)/shard_map/reshape | solution.py:633
  194.4 5.5 gather_fusion.5
  210.8 39.4 %collective-permute-done.31.refs_2_ = bf16[256,1664]{1,0:T(8,128)(2,1)} collective-permute-done((bf16[256,1664]{1,0:T(8,128)(2,1)}, bf16[256,1664]{1,0:T(8,128)(2,1)}, u32[]{:S(2)}, u32[]{:S(2)}) %collective-permute-start.31) | collective-permute-done | bytes 852000 | tf_op jit(solution)/shard_map/ppermute | solution.py:56
  258.4 25.6 %collective-permute-done.29.refs_0_ = bf16[256,1536]{1,0:T(8,128)(2,1)} collective-permute-done((bf16[256,1536]{1,0:T(8,128)(2,1)}, bf16[256,1536]{1,0:T(8,128)(2,1)}, u32[]{:S(2)}, u32[]{:S(2)}) %collective-permute-start.29) | collective-permute-done | bytes 786464 | tf_op jit(solution)/shard_map/ppermute | solution.py:56
  286.0 17.6 %experts.7 = (bf16[288,1536]{1,0:T(8,128)(2,1)}, bf16[288,1536]{1,0:T(8,128)(2,1)}, bf16[256,1664]{1,0:T(8,128)(2,1)}, bf16[256,1664]{1,0:T(8,128)(2,1)}) custom-call(s32[3]{0:T(128)} %pad_add_fusion.4.ids_ref, bf16[256,1536]{1,0:T(8,128)(2,1)} %multiply_convert_fusion.refs_0_, bf16[256,1536]{1,0:T(8,128)(2,1)} %collective-permute-done.41.refs_1_, ...), custom_call_target="tpu_custom_call" | custom-call | flops 6442450944 | bytes 15728640 | tf_op jit(solution)/shard_map/experts/pallas_call | solution.py:516
  306.8 17.7 %experts.4 = (bf16[288,1536]{1,0:T(8,128)(2,1)}, bf16[288,1536]{1,0:T(8,128)(2,1)}, bf16[256,1664]{1,0:T(8,128)(2,1)}, bf16[256,1664]{1,0:T(8,128)(2,1)}) custom-call(s32[3]{0:T(128)} %pad_add_fusion.1.ids_ref, bf16[256,1536]{1,0:T(8,128)(2,1)} %collective-permute-done.23.refs_0_, bf16[256,1536]{1,0:T(8,128)(2,1)} %collective-permute-done.24.refs_1_, ...), custom_call_target="tpu_custom_call" | custom-call | flops 6442450944 | bytes 15728640 | tf_op jit(solution)/shard_map/experts/pallas_call | solution.py:516
  325.8 15.3 %collective-permute-done.30.refs_1_ = bf16[256,1536]{1,0:T(8,128)(2,1)} collective-permute-done((bf16[256,1536]{1,0:T(8,128)(2,1)}, bf16[256,1536]{1,0:T(8,128)(2,1)}, u32[]{:S(2)}, u32[]{:S(2)}) %collective-permute-start.30) | collective-permute-done | bytes 786464 | tf_op jit(solution)/shard_map/ppermute | solution.py:56
  341.9 17.5 %experts.5 = (bf16[288,1536]{1,0:T(8,128)(2,1)}, bf16[288,1536]{1,0:T(8,128)(2,1)}, bf16[256,1664]{1,0:T(8,128)(2,1)}, bf16[256,1664]{1,0:T(8,128)(2,1)}) custom-call(s32[3]{0:T(128)} %pad_add_fusion.2.ids_ref, bf16[256,1536]{1,0:T(8,128)(2,1)} %collective-permute-done.29.refs_0_, bf16[256,1536]{1,0:T(8,128)(2,1)} %collective-permute-done.30.refs_1_, ...), custom_call_target="tpu_custom_call" | custom-call | flops 6442450944 | bytes 15728640 | tf_op jit(solution)/shard_map/experts/pallas_call | solution.py:516
  360.7 33.7 %collective-permute-done.36.refs_1_ = bf16[256,1536]{1,0:T(8,128)(2,1)} collective-permute-done((bf16[256,1536]{1,0:T(8,128)(2,1)}, bf16[256,1536]{1,0:T(8,128)(2,1)}, u32[]{:S(2)}, u32[]{:S(2)}) %collective-permute-start.36) | collective-permute-done | bytes 786464 | tf_op jit(solution)/shard_map/ppermute | solution.py:56
  395.2 18.0 %experts.6 = (bf16[288,1536]{1,0:T(8,128)(2,1)}, bf16[288,1536]{1,0:T(8,128)(2,1)}, bf16[256,1664]{1,0:T(8,128)(2,1)}, bf16[256,1664]{1,0:T(8,128)(2,1)}) custom-call(s32[3]{0:T(128)} %pad_add_fusion.3.ids_ref, bf16[256,1536]{1,0:T(8,128)(2,1)} %collective-permute-done.35.refs_0_, bf16[256,1536]{1,0:T(8,128)(2,1)} %collective-permute-done.36.refs_1_, ...), custom_call_target="tpu_custom_call" | custom-call | flops 6442450944 | bytes 15728640 | tf_op jit(solution)/shard_map/experts/pallas_call | solution.py:516
  413.2 18.5 %collective-permute-done.44 = bf16[256,1664]{1,0:T(8,128)(2,1)} collective-permute-done((bf16[256,1664]{1,0:T(8,128)(2,1)}, bf16[256,1664]{1,0:T(8,128)(2,1)}, u32[]{:S(2)}, u32[]{:S(2)}) %collective-permute-start.44) | collective-permute-done | bytes 852000 | tf_op jit(solution)/shard_map/ppermute | solution.py:56
  434.1 34.8 %collective-permute-done.46 = bf16[256,1664]{1,0:T(8,128)(2,1)} collective-permute-done((bf16[256,1664]{1,0:T(8,128)(2,1)}, bf16[256,1664]{1,0:T(8,128)(2,1)}, u32[]{:S(2)}, u32[]{:S(2)}) %collective-permute-start.46) | collective-permute-done | bytes 852000 | tf_op jit(solution)/shard_map/ppermute | solution.py:56
  471.1 16.0 %collective-permute-done.48 = bf16[256,1664]{1,0:T(8,128)(2,1)S(1)} collective-permute-done((bf16[256,1664]{1,0:T(8,128)(2,1)}, bf16[256,1664]{1,0:T(8,128)(2,1)S(1)}, u32[]{:S(2)}, u32[]{:S(2)}) %collective-permute-start.48) | collective-permute-done | bytes 852000 | tf_op jit(solution)/shard_map/ppermute | solution.py:56
  494.6 10.6 %collective-permute-done.39 = bf16[288,1536]{1,0:T(8,128)(2,1)S(1)} collective-permute-done((bf16[288,1536]{1,0:T(8,128)(2,1)S(1)}, bf16[288,1536]{1,0:T(8,128)(2,1)S(1)}, u32[]{:S(2)}, u32[]{:S(2)}) %collective-permute-start.39) | collective-permute-done | bytes 884768 | tf_op jit(solution)/shard_map/ppermute | solution.py:56
  510.8 35.4 %collective-permute-start.34 = (bf16[288,1536]{1,0:T(8,128)(2,1)S(1)}, bf16[288,1536]{1,0:T(8,128)(2,1)S(1)}, u32[]{:S(2)}, u32[]{:S(2)}) collective-permute-start(bf16[288,1536]{1,0:T(8,128)(2,1)S(1)} %add_convert_fusion.1), channel_id=1, source_target_pairs={{0,16},{4,20},{8,24},{12,28},{16,0},{20,4},{24,8},{28,12},{1,17},{... | collective-permute-start | bytes 2654216 | tf_op jit(solution)/shard_map/ppermute | solution.py:56
  546.3 54.6 %collective-permute-done.47 = bf16[256,1664]{1,0:T(8,128)(2,1)S(1)} collective-permute-done((bf16[256,1664]{1,0:T(8,128)(2,1)S(1)}, bf16[256,1664]{1,0:T(8,128)(2,1)S(1)}, u32[]{:S(2)}, u32[]{:S(2)}) %collective-permute-start.47) | collective-permute-done | bytes 852000 | tf_op jit(solution)/shard_map/ppermute | solution.py:56
  607.2 29.1 %collective-permute-done.34 = bf16[288,1536]{1,0:T(8,128)(2,1)S(1)} collective-permute-done((bf16[288,1536]{1,0:T(8,128)(2,1)S(1)}, bf16[288,1536]{1,0:T(8,128)(2,1)S(1)}, u32[]{:S(2)}, u32[]{:S(2)}) %collective-permute-start.34) | collective-permute-done | bytes 884768 | tf_op jit(solution)/shard_map/ppermute | solution.py:56
  674.1 19.6 %attend_back.1 = bf16[1024,640]{1,0:T(8,128)(2,1)} custom-call(s32[8]{0:T(128)} %fusion.73.place_ref, s32[4]{0:T(128)} %and_select_fusion.first_ref, bf16[1024,640]{1,0:T(8,128)(2,1)} %get-tuple-element.30.qkv_ref, s32[1024,1]{1,0:T(8,128)} %copy.155.start_ref, bf16[1024,384]{1,0:T(8,128)(2,1)} %get-tuple-element.31.o_ref, ...), custom_call_target="tpu_custom_call" | custom-call | flops 4026531840 | bytes 6291456 | tf_op jit(solution)/shard_map/attend_back/pallas_call | solution.py:377
  750.5 6.8 collective-permute-done.67
  (483 shorter events, 316.0 us)
Async XLA Ops:
  79.0 71.0 %collective-permute-start.20 = (bf16[1536,384]{1,0:T(8,128)(2,1)S(1)}, bf16[1536,384]{1,0:T(8,128)(2,1)}, u32[]{:S(2)}, u32[]{:S(2)}) collective-permute-start(bf16[1536,384]{1,0:T(8,128)(2,1)S(1)} %bitcast.252), channel_id=1, source_target_pairs={{0,1},{1,0},{2,3},{3,2},{4,5},{5,4},{6,7},{7,6},{8,9},{9,8},{10,11... | collective-permute-start | bytes 3538952 | tf_op jit(solution)/shard_map/ppermute | solution.py:56
  98.8 53.5 %collective-permute-start.22 = (bf16[1536,384]{1,0:T(8,128)(2,1)}, bf16[1536,384]{1,0:T(8,128)(2,1)}, u32[]{:S(2)}, u32[]{:S(2)}) collective-permute-start(bf16[1536,384]{1,0:T(8,128)(2,1)} %collective-permute-done.21), channel_id=1, source_target_pairs={{0,1},{1,0},{2,3},{3,2},{4,5},{5,4},{6,7},{7,6},{8,9},{9,8},{10,11... | collective-permute-start | bytes 3538952 | tf_op jit(solution)/shard_map/ppermute | solution.py:56
  140.4 69.8 %collective-permute-start.25 = (bf16[256,1664]{1,0:T(8,128)(2,1)}, bf16[256,1664]{1,0:T(8,128)(2,1)}, u32[]{:S(2)}, u32[]{:S(2)}) collective-permute-start(bf16[256,1664]{1,0:T(8,128)(2,1)} %fusion.20.refs_2_), channel_id=1, source_target_pairs={{0,24},{4,28},{8,16},{12,20},{16,8},{20,12},{24,0},{28,4},{1,25},{... | collective-permute-start | bytes 2555912 | tf_op jit(solution)/shard_map/ppermute | solution.py:56
  144.8 105.3 %collective-permute-start.31 = (bf16[256,1664]{1,0:T(8,128)(2,1)}, bf16[256,1664]{1,0:T(8,128)(2,1)}, u32[]{:S(2)}, u32[]{:S(2)}) collective-permute-start(bf16[256,1664]{1,0:T(8,128)(2,1)} %fusion.20.refs_2_), channel_id=1, source_target_pairs={{0,16},{4,20},{8,24},{12,28},{16,0},{20,4},{24,8},{28,12},{1,17},{... | collective-permute-start | bytes 2555912 | tf_op jit(solution)/shard_map/ppermute | solution.py:56
  147.3 105.9 %collective-permute-start.37 = (bf16[256,1664]{1,0:T(8,128)(2,1)}, bf16[256,1664]{1,0:T(8,128)(2,1)}, u32[]{:S(2)}, u32[]{:S(2)}) collective-permute-start(bf16[256,1664]{1,0:T(8,128)(2,1)} %fusion.20.refs_2_), channel_id=1, source_target_pairs={{0,8},{4,12},{8,0},{12,4},{16,24},{20,28},{24,16},{28,20},{1,9},{5... | collective-permute-start | bytes 2555912 | tf_op jit(solution)/shard_map/ppermute | solution.py:56
  150.0 104.5 %collective-permute-start.42 = (bf16[256,1664]{1,0:T(8,128)(2,1)}, bf16[256,1664]{1,0:T(8,128)(2,1)}, u32[]{:S(2)}, u32[]{:S(2)}) collective-permute-start(bf16[256,1664]{1,0:T(8,128)(2,1)} %fusion.20.refs_2_), channel_id=1, source_target_pairs={{0,4},{4,0},{8,12},{12,8},{16,20},{20,16},{24,28},{28,24},{1,5},{5... | collective-permute-start | bytes 2555912 | tf_op jit(solution)/shard_map/ppermute | solution.py:56
  210.2 73.8 %collective-permute-start.29 = (bf16[256,1536]{1,0:T(8,128)(2,1)}, bf16[256,1536]{1,0:T(8,128)(2,1)}, u32[]{:S(2)}, u32[]{:S(2)}) collective-permute-start(bf16[256,1536]{1,0:T(8,128)(2,1)} %multiply_convert_fusion.refs_0_), channel_id=1, source_target_pairs={{0,16},{4,20},{8,24},{12,28},{16,0},{20,4},{24,8},{28,12},{1,17},{... | collective-permute-start | bytes 2359304 | tf_op jit(solution)/shard_map/ppermute | solution.py:56
  254.6 51.4 %collective-permute-start.24 = (bf16[256,1536]{1,0:T(8,128)(2,1)}, bf16[256,1536]{1,0:T(8,128)(2,1)}, u32[]{:S(2)}, u32[]{:S(2)}) collective-permute-start(bf16[256,1536]{1,0:T(8,128)(2,1)} %collective-permute-done.23.refs_0_), channel_id=1, source_target_pairs={{0,4},{4,0},{8,12},{12,8},{16,20},{20,16},{24,28},{28,24},{1,5},{5... | collective-permute-start | bytes 2359304 | tf_op jit(solution)/shard_map/ppermute | solution.py:56
  284.8 56.4 %collective-permute-start.30 = (bf16[256,1536]{1,0:T(8,128)(2,1)}, bf16[256,1536]{1,0:T(8,128)(2,1)}, u32[]{:S(2)}, u32[]{:S(2)}) collective-permute-start(bf16[256,1536]{1,0:T(8,128)(2,1)} %collective-permute-done.29.refs_0_), channel_id=1, source_target_pairs={{0,4},{4,0},{8,12},{12,8},{16,20},{20,16},{24,28},{28,24},{1,5},{5... | collective-permute-start | bytes 2359304 | tf_op jit(solution)/shard_map/ppermute | solution.py:56
  303.6 55.8 %collective-permute-start.38 = (bf16[256,1664]{1,0:T(8,128)(2,1)}, bf16[256,1664]{1,0:T(8,128)(2,1)}, u32[]{:S(2)}, u32[]{:S(2)}) collective-permute-start(bf16[256,1664]{1,0:T(8,128)(2,1)} %collective-permute-done.37.refs_2_), channel_id=1, source_target_pairs={{0,4},{4,0},{8,12},{12,8},{16,20},{20,16},{24,28},{28,24},{1,5},{5... | collective-permute-start | bytes 2555912 | tf_op jit(solution)/shard_map/ppermute | solution.py:56
  304.4 201.8 %collective-permute-start.50 = (bf16[256,1664]{1,0:T(8,128)(2,1)}, bf16[256,1664]{1,0:T(8,128)(2,1)}, u32[]{:S(2)}, u32[]{:S(2)}) collective-permute-start(bf16[256,1664]{1,0:T(8,128)(2,1)} %get-tuple-element.46), channel_id=1, source_target_pairs={{0,4},{4,0},{8,12},{12,8},{16,20},{20,16},{24,28},{28,24},{1,5},{5... | collective-permute-start | bytes 2555912 | tf_op jit(solution)/shard_map/ppermute | solution.py:56
  306.0 88.5 %collective-permute-start.36 = (bf16[256,1536]{1,0:T(8,128)(2,1)}, bf16[256,1536]{1,0:T(8,128)(2,1)}, u32[]{:S(2)}, u32[]{:S(2)}) collective-permute-start(bf16[256,1536]{1,0:T(8,128)(2,1)} %collective-permute-done.35.refs_0_), channel_id=1, source_target_pairs={{0,4},{4,0},{8,12},{12,8},{16,20},{20,16},{24,28},{28,24},{1,5},{5... | collective-permute-start | bytes 2359304 | tf_op jit(solution)/shard_map/ppermute | solution.py:56
  324.5 165.5 %collective-permute-start.27 = (bf16[288,1536]{1,0:T(8,128)(2,1)}, bf16[288,1536]{1,0:T(8,128)(2,1)}, u32[]{:S(2)}, u32[]{:S(2)}) collective-permute-start(bf16[288,1536]{1,0:T(8,128)(2,1)} %get-tuple-element.33), channel_id=1, source_target_pairs={{0,4},{4,0},{8,12},{12,8},{16,20},{20,16},{24,28},{28,24},{1,5},{5... | collective-permute-start | bytes 2654216 | tf_op jit(solution)/shard_map/ppermute | solution.py:56
  341.1 90.6 %collective-permute-start.44 = (bf16[256,1664]{1,0:T(8,128)(2,1)}, bf16[256,1664]{1,0:T(8,128)(2,1)}, u32[]{:S(2)}, u32[]{:S(2)}) collective-permute-start(bf16[256,1664]{1,0:T(8,128)(2,1)} %get-tuple-element.41), channel_id=1, source_target_pairs={{0,4},{4,0},{8,12},{12,8},{16,20},{20,16},{24,28},{28,24},{1,5},{5... | collective-permute-start | bytes 2555912 | tf_op jit(solution)/shard_map/ppermute | solution.py:56
  359.4 132.1 %collective-permute-start.33 = (bf16[288,1536]{1,0:T(8,128)(2,1)}, bf16[288,1536]{1,0:T(8,128)(2,1)}, u32[]{:S(2)}, u32[]{:S(2)}) collective-permute-start(bf16[288,1536]{1,0:T(8,128)(2,1)} %get-tuple-element.35), channel_id=1, source_target_pairs={{0,4},{4,0},{8,12},{12,8},{16,20},{20,16},{24,28},{28,24},{1,5},{5... | collective-permute-start | bytes 2654216 | tf_op jit(solution)/shard_map/ppermute | solution.py:56
  394.5 74.4 %collective-permute-start.46 = (bf16[256,1664]{1,0:T(8,128)(2,1)}, bf16[256,1664]{1,0:T(8,128)(2,1)}, u32[]{:S(2)}, u32[]{:S(2)}) collective-permute-start(bf16[256,1664]{1,0:T(8,128)(2,1)} %get-tuple-element.43), channel_id=1, source_target_pairs={{0,4},{4,0},{8,12},{12,8},{16,20},{20,16},{24,28},{28,24},{1,5},{5... | collective-permute-start | bytes 2555912 | tf_op jit(solution)/shard_map/ppermute | solution.py:56
  431.7 55.4 %collective-permute-start.48 = (bf16[256,1664]{1,0:T(8,128)(2,1)}, bf16[256,1664]{1,0:T(8,128)(2,1)S(1)}, u32[]{:S(2)}, u32[]{:S(2)}) collective-permute-start(bf16[256,1664]{1,0:T(8,128)(2,1)} %get-tuple-element.45), channel_id=1, source_target_pairs={{0,4},{4,0},{8,12},{12,8},{16,20},{20,16},{24,28},{28,24},{1,5},{5... | collective-permute-start | bytes 2555912 | tf_op jit(solution)/shard_map/ppermute | solution.py:56
  489.9 111.0 %collective-permute-start.47 = (bf16[256,1664]{1,0:T(8,128)(2,1)S(1)}, bf16[256,1664]{1,0:T(8,128)(2,1)S(1)}, u32[]{:S(2)}, u32[]{:S(2)}) collective-permute-start(bf16[256,1664]{1,0:T(8,128)(2,1)S(1)} %add_convert_fusion.4), channel_id=1, source_target_pairs={{0,16},{4,20},{8,24},{12,28},{16,0},{20,4},{24,8},{28,12},{1,17},{... | collective-permute-start | bytes 2555912 | tf_op jit(solution)/shard_map/ppermute | solution.py:56
  491.5 109.4 %collective-permute-start.49 = (bf16[256,1664]{1,0:T(8,128)(2,1)S(1)}, bf16[256,1664]{1,0:T(8,128)(2,1)S(1)}, u32[]{:S(2)}, u32[]{:S(2)}) collective-permute-start(bf16[256,1664]{1,0:T(8,128)(2,1)S(1)} %add_convert_fusion.3), channel_id=1, source_target_pairs={{0,8},{4,12},{8,0},{12,4},{16,24},{20,28},{24,16},{28,20},{1,9},{5... | collective-permute-start | bytes 2555912 | tf_op jit(solution)/shard_map/ppermute | solution.py:56
  505.2 102.0 %collective-permute-start.43 = (bf16[288,1536]{1,0:T(8,128)(2,1)S(1)}, bf16[288,1536]{1,0:T(8,128)(2,1)S(1)}, u32[]{:S(2)}, u32[]{:S(2)}) collective-permute-start(bf16[288,1536]{1,0:T(8,128)(2,1)S(1)} %copy-done.57), channel_id=1, source_target_pairs={{0,4},{4,0},{8,12},{12,8},{16,20},{20,16},{24,28},{28,24},{1,5},{5... | collective-permute-start | bytes 2654216 | tf_op jit(solution)/shard_map/ppermute | solution.py:56
  506.2 101.0 %collective-permute-start.28 = (bf16[288,1536]{1,0:T(8,128)(2,1)S(1)}, bf16[288,1536]{1,0:T(8,128)(2,1)S(1)}, u32[]{:S(2)}, u32[]{:S(2)}) collective-permute-start(bf16[288,1536]{1,0:T(8,128)(2,1)S(1)} %add_convert_fusion.2), channel_id=1, source_target_pairs={{0,24},{4,28},{8,16},{12,20},{16,8},{20,12},{24,0},{28,4},{1,25},{... | collective-permute-start | bytes 2654216 | tf_op jit(solution)/shard_map/ppermute | solution.py:56
  510.8 125.4 %collective-permute-start.34 = (bf16[288,1536]{1,0:T(8,128)(2,1)S(1)}, bf16[288,1536]{1,0:T(8,128)(2,1)S(1)}, u32[]{:S(2)}, u32[]{:S(2)}) collective-permute-start(bf16[288,1536]{1,0:T(8,128)(2,1)S(1)} %add_convert_fusion.1), channel_id=1, source_target_pairs={{0,16},{4,20},{8,24},{12,28},{16,0},{20,4},{24,8},{28,12},{1,17},{... | collective-permute-start | bytes 2654216 | tf_op jit(solution)/shard_map/ppermute | solution.py:56
  750.0 69.4 %collective-permute-start.54 = (bf16[256,1536]{1,0:T(8,128)(2,1)}, bf16[256,1536]{1,0:T(8,128)(2,1)}, u32[]{:S(2)}, u32[]{:S(2)}) collective-permute-start(bf16[256,1536]{1,0:T(8,128)(2,1)} %get-tuple-element.64), channel_id=1, source_target_pairs={{0,1},{1,0},{2,3},{3,2},{4,5},{5,4},{6,7},{7,6},{8,9},{9,8},{10,11... | collective-permute-start | bytes 2359304 | tf_op jit(solution)/shard_map/ppermute | solution.py:56
  760.3 59.1 %collective-permute-start.56 = (bf16[256,1536]{1,0:T(8,128)(2,1)}, bf16[256,1536]{1,0:T(8,128)(2,1)}, u32[]{:S(2)}, u32[]{:S(2)}) collective-permute-start(bf16[256,1536]{1,0:T(8,128)(2,1)} %add_convert_fusion.7), channel_id=1, source_target_pairs={{0,2},{1,3},{2,0},{3,1},{4,6},{5,7},{6,4},{7,5},{8,10},{9,11},{10,... | collective-permute-start | bytes 2359304 | tf_op jit(solution)/shard_map/ppermute | solution.py:56
  (127 other events, 2569.4 us)

commit v2 on v1

--- a/solution.py
+++ b/solution.py
@@ -61,24 +61,146 @@
     for mask in masks:
         for have in list(slots):
             slots[have ^ mask] = swap(slots[have], axis, mask)
-    return [slots[m] for m in range(len(slots))]
-
-
-def gather_seq(block):
+    return [slots[m] for m in sorted(slots)]
+
+
+def together(*arrays):
+    return lax.optimization_barrier(arrays)
+
+
+def line_swap(block, pairs):
+    return lax.ppermute(block, "seq", [(2 * i + j, 2 * k + j) for i, k in pairs for j in (0, 1)])
+
+
+def outward(block):
+    return line_swap(block, [(1, 0), (2, 3)])
+
+
+def inward(block):
+    return line_swap(block, [(0, 1), (3, 2)])
+
+
+def middle(block):
+    return line_swap(block, [(1, 2), (2, 1)])
+
+
+class Steps:
+    def __init__(self, work):
+        self.work = work
+        self.moving = self.result = None
+        self.resume(None)
+
+    def resume(self, arrived):
+        try:
+            self.moving = self.work.send(arrived)
+        except StopIteration as end:
+            self.moving, self.result = None, end.value
+
+    def beside(self, *others):
+        if self.moving is None:
+            return others
+        arrived, others = lax.optimization_barrier((tuple(self.moving), others))
+        self.resume(arrived)
+        return others
+
+    def finish(self):
+        while self.moving is not None:
+            self.beside()
+        return self.result
+
+
+def gather_line(block, slots):
     count = lax.axis_size("seq")
     if count != 8:
-        return gather_slots(block, "seq", doublings(count))
-    even = [block] + [swap(block, "seq", m) for m in (2, 4, 6)]
-    odd = [swap(item, "seq", 1) for item in even]
-    return [item for both in zip(even, odd) for item in both]
+        slots += gather_slots(block, "seq", doublings(count))
+        return slots
+    two, six, one = yield swap(block, "seq", 2), middle(block), swap(block, "seq", 1)
+    slots += [block, one]
+    four, far, three = yield middle(two), outward(six), swap(two, "seq", 1)
+    slots += [two, three]
+    four = four + far
+    far, five = yield outward(four), swap(four, "seq", 1)
+    slots += [four, five]
+    six = six + far
+    (seven,) = yield (swap(six, "seq", 1),)
+    slots += [six, seven]
+    return slots
+
+
+def gather_seq(block):
+    return Steps(gather_line(block, [])).finish()
+
+
+def reduce_line(parts, one=None):
+    count = lax.axis_size("seq")
+    if count != 8:
+        return [reduce_slots(parts, "seq", doublings(count))]
+    (seven,) = yield (swap(parts[7], "seq", 1),)
+    six = add_low(parts[6], seven)
+    near, five = yield inward(six), swap(parts[5], "seq", 1)
+    four = add_low(parts[4], five, near)
+    near, far, three = yield inward(four), middle(four), swap(parts[3], "seq", 1)
+    six = add_low(six, near)
+    two = add_low(parts[2], three, far)
+    last = [swap(two, "seq", 2), middle(six)]
+    if one is None:
+        last.append(swap(parts[1], "seq", 1))
+    last = yield last
+    return [parts[0], *last] + ([] if one is None else [one])
+
+
+def exchange_experts(block, packs, pack_slots, compute):
+    count = lax.axis_size("seq")
+    slots, y_parts, d_parts = [], [], []
+    rows = Steps(gather_line(block, slots))
+
+    def pair(m):
+        y_pair, d_pair = compute(m, slots[m : m + 2])
+        return [*y_pair, *d_pair]
+
+    def keep(done):
+        y_parts.extend(done[:2])
+        d_parts.extend(done[2:])
+
+    if count != 8:
+        packs.finish()
+        for m in range(0, count, 2):
+            keep(pair(m))
+        return y_parts, Steps(reduce_line(d_parts)).finish()
+    packs.beside(*rows.beside())
+    for m in (0, 2, 4):
+        done = pair(m)
+        keep(packs.beside(*rows.beside(*done)))
+    one = swap(d_parts[1], "seq", 1)
+    *done, one = lax.optimization_barrier((*pair(6), one))
+    keep(done)
+    return y_parts, Steps(reduce_line(d_parts, one)).finish()
 
 
 def doublings(count):
     return [1 << bit for bit in range(count.bit_length() - 1)]
 
 
-def add_low(left_arr, right_arr):
-    return (left_arr.astype(F32) + right_arr.astype(F32)).astype(BF)
+def add_low(*terms):
+    total = terms[0].astype(F32)
+    for term in terms[1:]:
+        total = total + term.astype(F32)
+    return lax.optimization_barrier(total.astype(BF))
+
+
+def gather_groups(block, copies):
+    return gather_slots(block, "ctx", [copies * m for m in doublings(GROUPS)[::-1]])
+
+
+def reduce_groups(parts, copies, whole):
+    parts = dict(enumerate(parts))
+    for mask in doublings(GROUPS):
+        for m in [m for m in parts if m & mask]:
+            parts[m ^ mask] = add_low(parts[m ^ mask], swap(parts.pop(m), "ctx", copies * mask))
+    total = parts[0]
+    for mask in doublings(copies) if whole else []:
+        total = add_low(total, swap(total, "ctx", mask))
+    return total
 
 
 def reduce_slots(parts, axis, masks):
@@ -94,22 +216,6 @@
     return parts[0]
 
 
-def reduce_seq(parts):
-    count = lax.axis_size("seq")
-    if count != 8:
-        return reduce_slots(parts, "seq", doublings(count))
-    total = None
-    for m in (6, 4, 2, 0):
-        arrived = swap(parts[m + 1], "seq", 1)
-        if m:
-            arrived = swap(add_low(parts[m], arrived), "seq", m)
-        else:
-            arrived = arrived.astype(F32) + parts[0].astype(F32)
-        arrived = arrived.astype(F32)
-        total = arrived if total is None else total + arrived
-    return total
-
-
 def rotate(values, cosine, sine, sign):
     lane = lax.broadcasted_iota(jnp.int32, values.shape, 1)
     ahead = pltpu.roll(values, LANES - HEAD_DIM // 2, 1)
@@ -127,7 +233,7 @@
     def _():
         for m, shard in enumerate(shards):
             start = pl.multiple_of(order_ref[m] * rows, rows)
-            w_ref[pl.ds(start, rows), :] = shard[...]
+            w_ref[pl.ds(start, rows), :] = shard[:, :LOCAL]
         full_ref[...] = w_ref[...]
 
     pre = dot(h_ref[...], w_ref[...]) + dot(t_ref[...], up_ref[...])
@@ -158,7 +264,7 @@
                 per_block(LANES),
                 per_block(LANES),
             ]
-            + [whole((rows, LOCAL))] * len(shards),
+            + [whole((rows, LOCAL + QG))] * len(shards),
             out_specs=[per_block(LOCAL), whole((D, LOCAL))],
             scratch_shapes=[pltpu.VMEM((D, LOCAL), BF)],
         ),
@@ -212,7 +318,8 @@
     return jnp.concatenate([bias] * PAIRS, axis=0)
 
 
-def attend_kernel(place_ref, first_ref, qkv_ref, start_ref, o_ref, lse_ref, q_s, k_s, v_s, m_s, acc_s):
+def attend_kernel(copies, place_ref, first_ref, qkv_ref, start_ref, o_ref, lse_ref, *refs):
+    piece_refs, (q_s, k_s, v_s, score_s, m_s, acc_s) = refs[:GROUPS], refs[GROUPS:]
     stack_rows(place_ref, qkv_ref, q_s, 0)
     split_keys(place_ref, qkv_ref, QG, k_s, False)
     split_keys(place_ref, qkv_ref, QG + KG, v_s, True)
@@ -223,32 +330,39 @@
         q_first = pl.multiple_of(qb * BLK, BLK)
         q_rows = pl.ds(pl.multiple_of(qb * tall, tall), tall)
         start_col = start_ref[pl.ds(q_first, BLK), :]
+        queries = q_s[q_rows, :]
         m_s[...] = jnp.full(m_s.shape, NEG, F32)
         acc_s[...] = jnp.zeros(acc_s.shape, F32)
 
-        def key_block(kb, unused):
+        def score_block(kb, unused):
             k_first = pl.multiple_of(kb * BLK, BLK)
             bias = tile_bias(start_col, q_first, k_first)
-            queries = q_s[q_rows, :]
             for side in range(2):
                 scores = dot_nt(queries, k_s[side, pl.ds(k_first, BLK), :]) + bias
-                old = m_s[side]
-                new = jnp.maximum(old, jnp.max(scores, axis=1, keepdims=True))
-                prob = jnp.exp(scores - new)
-                m_s[side] = new
-                acc_s[side] = acc_s[side] * jnp.exp(old - new) + dot(
-                    prob.astype(BF), v_s[side, pl.ds(k_first, BLK), :]
+                score_s[kb, side] = scores
+                m_s[side] = jnp.maximum(
+                    m_s[side], jnp.maximum(scores[:, :LANES], scores[:, LANES:])
                 )
             return unused
 
-        lax.fori_loop(first_ref[qb], qb + 1, key_block, 0)
+        lax.fori_loop(first_ref[qb], qb + 1, score_block, 0)
+        peaks = [jnp.max(m_s[side], axis=1, keepdims=True) for side in range(2)]
+
+        def value_block(kb, unused):
+            k_first = pl.multiple_of(kb * BLK, BLK)
+            for side in range(2):
+                prob = jnp.exp(score_s[kb, side] - peaks[side]).astype(BF)
+                acc_s[side] += dot(prob, v_s[side, pl.ds(k_first, BLK), :])
+            return unused
+
+        lax.fori_loop(first_ref[qb], qb + 1, value_block, 0)
         low, high = acc_s[0], acc_s[1]
         low_sum = low[:, HEAD_DIM : HEAD_DIM + 1]
         high_sum = high[:, 0:1]
         is_low = half_mask(low.shape, 0)
         out = jnp.where(is_low, low / low_sum, high / high_sum).astype(BF)
         lse_ref[q_rows, :] = jnp.where(
-            is_low, m_s[0] + jnp.log(low_sum), m_s[1] + jnp.log(high_sum)
+            is_low, peaks[0] + jnp.log(low_sum), peaks[1] + jnp.log(high_sum)
         )
         for i in range(2):
             rows = pl.ds(pl.multiple_of(place_ref[2 * qb + i] * half, half), half)
@@ -258,28 +372,33 @@
         return unused
 
     lax.fori_loop(0, qkv_ref.shape[0] // BLK, query_block, 0)
+    for j, piece in enumerate(piece_refs):
+        tokens = piece.shape[0]
+        piece[...] = o_ref[j * copies * tokens : (j * copies + 1) * tokens, :]
 
 
 SMEM_SPEC = pl.BlockSpec(memory_space=pltpu.SMEM)
 VMEM_SPEC = pl.BlockSpec(memory_space=pltpu.VMEM)
 
 
-def attend(place, first, qkv, start_col):
+def attend(place, first, qkv, start_col, copies):
     length = qkv.shape[0]
     tall = PAIRS * BLK
     return pl.pallas_call(
-        attend_kernel,
+        functools.partial(attend_kernel, copies),
         in_specs=[SMEM_SPEC, SMEM_SPEC, VMEM_SPEC, VMEM_SPEC],
-        out_specs=[VMEM_SPEC, VMEM_SPEC],
+        out_specs=[VMEM_SPEC] * (2 + GROUPS),
         out_shape=[
             jax.ShapeDtypeStruct((length, QG), BF),
             jax.ShapeDtypeStruct((PAIRS * length, LANES), F32),
-        ],
+        ]
+        + [jax.ShapeDtypeStruct((length // (GROUPS * copies), QG), BF)] * GROUPS,
         scratch_shapes=[
             pltpu.VMEM((PAIRS * length, LANES), BF),
             pltpu.VMEM((2, length, LANES), BF),
             pltpu.VMEM((2, length, LANES), BF),
-            pltpu.VMEM((2, tall, 1), F32),
+            pltpu.VMEM((length // BLK, 2, tall, BLK), F32),
+            pltpu.VMEM((2, tall, LANES), F32),
             pltpu.VMEM((2, tall, LANES), F32),
         ],
         cost_estimate=pl.CostEstimate(
@@ -296,22 +415,17 @@
     start_ref,
     o_ref,
     lse_ref,
-    do_ref,
     cos_ref,
     sin_ref,
-    dqkv_ref,
-    q_s,
-    o_s,
-    do_s,
-    k_s,
-    v_s,
-    dk_s,
-    dv_s,
-    dq_s,
+    *refs,
 ):
+    do_refs = refs[:-10]
+    dqkv_ref, join_s, q_s, o_s, do_s, k_s, v_s, dk_s, dv_s, dq_s = refs[-10:]
+    for m, piece in enumerate(do_refs):
+        join_s[m * piece.shape[0] : (m + 1) * piece.shape[0], :] = piece[...]
     stack_rows(place_ref, qkv_ref, q_s, 0)
     stack_rows(place_ref, o_ref, o_s, 0)
-    stack_rows(place_ref, do_ref, do_s, 0)
+    stack_rows(place_ref, join_s, do_s, 0)
     split_keys(place_ref, qkv_ref, QG, k_s, False)
     split_keys(place_ref, qkv_ref, QG + KG, v_s, False)
     dk_s[...] = jnp.zeros(dk_s.shape, F32)
@@ -370,16 +484,17 @@
         dqkv_ref[rows, QG + KG : LOCAL] = jnp.where(is_low, dv_s[0, at, :], dv_s[1, at, :]).astype(BF)
 
 
-def attend_back(place, first, qkv, start_col, out, lse, d_out, cosine, sine):
+def attend_back(place, first, qkv, start_col, out, lse, cosine, sine, d_out):
     length = qkv.shape[0]
     tall = PAIRS * BLK
     stacked = pltpu.VMEM((PAIRS * length, LANES), BF)
     return pl.pallas_call(
         attend_back_kernel,
-        in_specs=[SMEM_SPEC, SMEM_SPEC] + [VMEM_SPEC] * 7,
+        in_specs=[SMEM_SPEC, SMEM_SPEC] + [VMEM_SPEC] * (6 + len(d_out)),
         out_specs=VMEM_SPEC,
         out_shape=jax.ShapeDtypeStruct((length, LOCAL), BF),
         scratch_shapes=[
+            pltpu.VMEM((length, QG), BF),
             stacked,
             stacked,
             stacked,
@@ -393,7 +508,7 @@
             flops=10 * length * length * QG, bytes_accessed=16 * length * QG, transcendentals=0
         ),
         name="attend_back",
-    )(place, first, qkv, start_col, out, lse, d_out, cosine, sine)
+    )(place, first, qkv, start_col, out, lse, cosine, sine, *d_out)
 
 
 def expert_kernel(ids_ref, h_refs, p_refs, wgu_ref, wd_ref, tables, y_refs, d_refs, scratch):
@@ -489,9 +604,10 @@
         for j in range(count):
             tokens = h_refs[j].shape[0]
             put = jnp.concatenate([sel_s[j, e] for e in range(E_DEV)], axis=1)
-            y_refs[j][:tokens, :] = dot(put, yrow_s[j]).astype(BF)
-            y_refs[j][tokens:, :] = grad_s[j].astype(BF)
-            d_refs[j][...] = dot(put, drow_s[j]).astype(BF)
+            y_refs[j][...] = dot(put, yrow_s[j]).astype(BF)
+            d_refs[j][:tokens, :] = dot(put, drow_s[j]).astype(BF)
+            d_refs[j][tokens:, :D] = grad_s[j].astype(BF)
+            d_refs[j][tokens:, D:] = jnp.zeros((2 * RANK, LANES), BF)
 
 
 def experts(adapters, base, rows, packs, w_gate_up, w_down, aux_w, gu_up, down_a, down_b):
@@ -512,7 +628,7 @@
         expert_kernel(ids_ref, h_refs, p_refs, wgu_ref, wd_ref, tables, y_refs, d_refs, refs)
 
     picked = [(LANES, D), (2, RANK, FF), (RANK, FF), (RANK, D)]
-    shapes = [(tokens + 2 * RANK, D)] * count + [(tokens, EXT)] * count
+    shapes = [(tokens, D)] * count + [(tokens + 2 * RANK, EXT)] * count
     outs = pl.pallas_call(
         body,
         grid_spec=pltpu.PrefetchScalarGridSpec(
@@ -553,7 +669,279 @@
         *([down_a] * count),
         *([down_b] * count),
     )
-    return outs[:count], outs[count:]
+    return list(outs[:count]), list(outs[count:])
+
+
+def join_kernel(*refs):
+    parts, out_ref = refs[:-1], refs[-1]
+    for m, part in enumerate(parts):
+        out_ref[m] = part[...]
+
+
+def join(parts):
+    return pl.pallas_call(
+        join_kernel,
+        in_specs=[VMEM_SPEC] * len(parts),
+        out_specs=VMEM_SPEC,
+        out_shape=jax.ShapeDtypeStruct((len(parts),) + parts[0].shape, parts[0].dtype),
+        name="join",
+    )(*parts)
+
+
+def order_rows_kernel(order_ref, *refs):
+    parts, out_ref = refs[:-1], refs[-1]
+    rows = parts[0].shape[0]
+    step = HEAD_DIM // 2
+    for m, part in enumerate(parts):
+        for i in range(rows // step):
+            first = order_ref[m] * rows + i * step
+            head = first // HEAD_DIM
+            key, pair = head // PAIRS, head % PAIRS
+            at = (key // 2) * QG + pair * LANES + (key % 2) * HEAD_DIM + first % HEAD_DIM
+            at = pl.multiple_of(at, step)
+            out_ref[pl.ds(at, step), :] = part[i * step : (i + 1) * step, LOCAL:]
+
+
+def order_rows(order, parts):
+    return pl.pallas_call(
+        order_rows_kernel,
+        in_specs=[SMEM_SPEC] + [VMEM_SPEC] * len(parts),
+        out_specs=VMEM_SPEC,
+        out_shape=jax.ShapeDtypeStruct((QW, QG), BF),
+        name="order_rows",
+    )(order, *parts)
+
+
+def lanes_of(index):
+    return pl.ds(pl.multiple_of(index * QG, LANES), QG)
+
+
+def out_kernel(group_ref, x_ref, gain_ref, down_ref, up_ref, *refs):
+    o_refs, w_refs = refs[:GROUPS], refs[GROUPS : 2 * GROUPS]
+    att_ref, rank_ref, y_ref, h_ref = refs[2 * GROUPS :]
+    group = group_ref[0]
+    for j in range(GROUPS):
+        att_ref[:, lanes_of(group ^ j)] = o_refs[j][...]
+    attended = att_ref[...]
+    for j in range(GROUPS):
+        y_ref[:, lanes_of(group ^ j)] = dot(attended, w_refs[j][...])
+    rank_out = dot_nt(attended, down_ref[...]).astype(BF)
+    rank_ref[...] = rank_out
+    y_one = x_ref[...].astype(F32) + y_ref[...] + dot(rank_out, up_ref[...])
+    y_ref[...] = y_one
+    inverse = lax.rsqrt(jnp.mean(y_one * y_one, axis=1, keepdims=True) + NORM_EPS)
+    h_ref[...] = (y_one * inverse * gain_ref[...]).astype(BF)
+
+
+def project_out(group, rows, gain, down_t, up, outs, w_parts):
+    tokens = rows.shape[0]
+    return pl.pallas_call(
+        out_kernel,
+        in_specs=[SMEM_SPEC] + [VMEM_SPEC] * (4 + 2 * GROUPS),
+        out_specs=[VMEM_SPEC] * 4,
+        out_shape=[
+            jax.ShapeDtypeStruct((tokens, QW), BF),
+            jax.ShapeDtypeStruct((tokens, RANK), BF),
+            jax.ShapeDtypeStruct((tokens, D), F32),
+            jax.ShapeDtypeStruct((tokens, D), BF),
+        ],
+        cost_estimate=pl.CostEstimate(
+            flops=2 * tokens * QW * D, bytes_accessed=2 * QW * D + 12 * tokens * D, transcendentals=0
+        ),
+        name="project_out",
+    )(group, rows, gain, down_t, up, *outs, *w_parts)
+
+
+def natural_heads(tiles):
+    is_low = half_mask(tiles[0].shape, 0)
+    turn = lambda tile: pltpu.roll(tile, HEAD_DIM, 1)
+    return [
+        jnp.where(is_low, tiles[0], turn(tiles[1])),
+        jnp.where(is_low, tiles[2], tiles[0]),
+        jnp.where(is_low, turn(tiles[1]), tiles[2]),
+    ]
+
+
+def middle_kernel(count, terms, info_ref, *refs):
+    refs = list(refs)
+    take = lambda n: [refs.pop(0) for _ in range(n)]
+    d_refs = take(terms)
+    pack_ref, y_ref, h_ref, gain_ref, aux_ref, att_ref, rank_ref, down_ref, up_ref = take(9)
+    w_refs = take(GROUPS)
+    (dy_ref,) = take(1)
+    do_refs, early_refs = take(count), take(GROUPS)
+    do_s, early_s = refs
+    group, ctx_index, copies = info_ref[0], info_ref[1], count // GROUPS
+    tokens = y_ref.shape[0]
+    d_sum = d_refs[0][...].astype(F32)
+    for ref in d_refs[1:]:
+        d_sum = d_sum + ref[...].astype(F32)
+    early_s[0 : 2 * RANK, :] = d_sum[tokens:, :D]
+    d_ext = d_sum[:tokens, D:]
+    h_two = h_ref[...]
+    lane = lax.broadcasted_iota(jnp.int32, (tokens, LANES), 1)
+    chosen = pack_ref[:, D:EXT].astype(F32) > 0.0
+    picked = jnp.where(chosen, dot_nt(h_two, aux_ref[...]), NEG)
+    weights = jnp.exp(picked - jnp.max(picked, axis=1, keepdims=True))
+    gates = weights / jnp.sum(weights, axis=1, keepdims=True)
+    mixed = jnp.sum(jnp.where(chosen, gates * d_ext, 0.0), axis=1, keepdims=True)
+    d_logits = jnp.where(chosen, gates * (d_ext - mixed), 0.0)
+    d_ext = jnp.where(lane < EXP_AT, d_ext, d_logits).astype(BF)
+    d_h = d_sum[:tokens, :D] + dot(d_ext, aux_ref[...])
+    y_one = y_ref[...]
+    inverse = lax.rsqrt(jnp.mean(y_one * y_one, axis=1, keepdims=True) + NORM_EPS)
+    scaled = gain_ref[...] * d_h
+    d_y = pack_ref[:, :D].astype(F32) + inverse * scaled
+    d_y = d_y - y_one * inverse**3 * jnp.mean(y_one * scaled, axis=1, keepdims=True)
+    dy_ref[...] = d_y
+    d_attn = d_y.astype(BF)
+    d_rank = dot_nt(d_attn, up_ref[...]).astype(BF)
+    do_s[...] = dot(d_rank, down_ref[...])
+    for j in range(GROUPS):
+        at = lanes_of(group ^ j)
+        early_s[3 * RANK : 4 * RANK, at] = dot_tn(rank_ref[...], dy_ref[:, at].astype(BF))
+        do_s[...] += dot_nt(dy_ref[:, at].astype(BF), w_refs[j][...])
+    for m in range(count):
+        do_refs[m][...] = do_s[:, lanes_of((ctx_index ^ m) // copies)].astype(BF)
+    down_grad = dot_tn(d_rank, att_ref[...])
+    for g in range(GROUPS):
+        tiles = [down_grad[:, g * QG + i * LANES : g * QG + (i + 1) * LANES] for i in range(PAIRS)]
+        for i, tile in enumerate(natural_heads(tiles)):
+            early_s[2 * RANK : 3 * RANK, g * QG + i * LANES : g * QG + (i + 1) * LANES] = tile
+    early_s[4 * RANK :, :] = dot_tn(d_ext, h_two)[: 2 * RANK]
+    for j in range(GROUPS):
+        early_refs[j][...] = early_s[:, lanes_of(group ^ j)].astype(BF)
+
+
+def middle_back(info, count, terms, pack, y_one, h_two, gain, aux, attended, rank_out, down_t, up, w_parts):
+    tokens = y_one.shape[0]
+    outs = pl.pallas_call(
+        functools.partial(middle_kernel, count, len(terms)),
+        in_specs=[SMEM_SPEC] + [VMEM_SPEC] * (len(terms) + 9 + GROUPS),
+        out_specs=[VMEM_SPEC] * (1 + count + GROUPS),
+        out_shape=[jax.ShapeDtypeStruct((tokens, D), F32)]
+        + [jax.ShapeDtypeStruct((tokens, QG), BF)] * count
+        + [jax.ShapeDtypeStruct((6 * RANK, QG), BF)] * GROUPS,
+        scratch_shapes=[pltpu.VMEM((tokens, QW), F32), pltpu.VMEM((6 * RANK, D), F32)],
+        cost_estimate=pl.CostEstimate(
+            flops=2 * tokens * QW * D, bytes_accessed=2 * QW * D + 20 * tokens * D, transcendentals=0
+        ),
+        name="middle_back",
+    )(info, *terms, pack, y_one, h_two, gain, aux, attended, rank_out, down_t, up, *w_parts)
+    return outs[0], list(outs[1 : 1 + count]), list(outs[1 + count :])
+
+
+def inputs_kernel(group_ref, dqkv_ref, w_ref, up_ref, down_ref, t_ref, h_ref, *refs):
+    count = len(refs) - 3 - GROUPS
+    rows_refs, grad_ref, piece_refs = refs[:count], refs[count], refs[count + 1 : -2]
+    grad_s, down_s = refs[-2:]
+    step = pl.program_id(0)
+
+    @pl.when(step == 0)
+    def _():
+        grad_s[...] = jnp.zeros(grad_s.shape, F32)
+        down_s[...] = jnp.zeros(down_s.shape, F32)
+
+    d_qkv = dqkv_ref[...]
+    d_rank = dot_nt(d_qkv, up_ref[...]).astype(BF)
+    rows = (dot_nt(d_qkv, w_ref[...]) + dot_nt(d_rank, down_ref[...])).astype(BF)
+    for m in range(count):
+
+        @pl.when(step == m)
+        def _():
+            rows_refs[m][...] = rows
+
+    ranks = t_ref[...]
+    grad_s[...] += dot_tn(ranks, d_qkv)
+    down_s[...] += dot_tn(d_rank, h_ref[...])
+
+    @pl.when(step == count - 1)
+    def _():
+        tiles = [grad_s[:RANK, i * LANES : (i + 1) * LANES] for i in range(PAIRS)]
+        for i, tile in enumerate(natural_heads(tiles)):
+            grad_ref[:, i * LANES : (i + 1) * LANES] = tile.astype(BF)
+        keys = slice(QG, QG + KG)
+        grad_ref[:, keys] = grad_s[RANK : 2 * RANK, keys].astype(BF)
+        grad_ref[:, QG + KG :] = grad_s[2 * RANK :, QG + KG :].astype(BF)
+        for j in range(GROUPS):
+            piece = down_s[:, lanes_of(group_ref[0] ^ j)].astype(BF)
+            for i in range(3):
+                piece_refs[j][:, i * QG : (i + 1) * QG] = piece[i * RANK : (i + 1) * RANK]
+
+
+def inputs_back(group, count, d_qkv, cols_all, up_diag, down_sel, rank_qkv, h_one):
+    length = d_qkv.shape[0]
+    tokens = length // count
+    per_block = lambda width: pl.BlockSpec((tokens, width), lambda i: (i, 0))
+    whole = lambda shape: pl.BlockSpec(shape, lambda i: (0, 0))
+    shapes = [(tokens, D)] * count + [(RANK, LOCAL)] + [(RANK, 3 * QG)] * GROUPS
+    outs = pl.pallas_call(
+        inputs_kernel,
+        grid=(count,),
+        in_specs=[
+            SMEM_SPEC,
+            per_block(LOCAL),
+            whole((D, LOCAL)),
+            whole((3 * RANK, LOCAL)),
+            whole((D, 3 * RANK)),
+            per_block(3 * RANK),
+            per_block(D),
+        ],
+        out_specs=[whole(shape) for shape in shapes],
+        out_shape=[jax.ShapeDtypeStruct(shape, BF) for shape in shapes],
+        scratch_shapes=[pltpu.VMEM((3 * RANK, LOCAL), F32), pltpu.VMEM((3 * RANK, D), F32)],
+        cost_estimate=pl.CostEstimate(
+            flops=2 * length * D * LOCAL, bytes_accessed=4 * length * (D + LOCAL), transcendentals=0
+        ),
+        name="inputs_back",
+    )(group, d_qkv, cols_all, up_diag, down_sel, rank_qkv, h_one)
+    return list(outs[:count]), outs[count], list(outs[count + 1 :])
+
+
+def place_kernel(ids_ref, *refs):
+    parts = refs[:2]
+    up_ref, down_ref, gu_ref, da_ref, db_ref, od_ref, ou_ref, gd_ref, sum_s = refs[2:]
+    sources = parts[0].shape[0]
+    up_ref[...] = jnp.zeros(up_ref.shape, F32)
+    down_ref[...] = jnp.zeros(down_ref.shape, F32)
+    sum_s[...] = jnp.zeros(sum_s.shape, F32)
+    for j in range(GROUPS):
+        group = ids_ref[sources] ^ j
+        keys = lambda first: pl.ds(pl.multiple_of(first + group * KG, LANES), KG)
+        rows = slice((j // 2) * RANK, (j // 2 + 1) * RANK)
+        for m in range(sources):
+            a = ids_ref[m]
+            take = lambda first, width: parts[j % 2][m, rows, first : first + width].astype(F32)
+            up_ref[a, :, lanes_of(group)] += take(0, QG)
+            up_ref[a, :, keys(QW)] += take(QG, KG)
+            up_ref[a, :, keys(QW + KVW)] += take(QG + KG, KG)
+            for i in range(3):
+                at = slice(i * RANK, (i + 1) * RANK)
+                down_ref[a, at, lanes_of(group)] += take(LOCAL + i * QG, QG)
+            for i in range(6):
+                at = slice(i * RANK, (i + 1) * RANK)
+                sum_s[a, at, lanes_of(group)] += take(LOCAL + (3 + i) * QG, QG)
+    for a in range(ADAPT):
+        gu_ref[a, 0] = sum_s[a, :RANK, :FF]
+        gu_ref[a, 1] = sum_s[a, :RANK, FF : 2 * FF]
+        da_ref[a] = sum_s[a, :RANK, 2 * FF :]
+        db_ref[a] = sum_s[a, RANK : 2 * RANK]
+        od_ref[a] = sum_s[a, 2 * RANK : 3 * RANK]
+        ou_ref[a] = sum_s[a, 3 * RANK : 4 * RANK]
+        gd_ref[a] = sum_s[a, 4 * RANK :]
+
+
+def place_grads(ids, near, far):
+    shapes = [(RANK, QW + 2 * KVW), (3 * RANK, D), (2, RANK, FF), (RANK, FF), (RANK, D)]
+    shapes += [(RANK, QW), (RANK, D), (2 * RANK, D)]
+    return pl.pallas_call(
+        place_kernel,
+        in_specs=[SMEM_SPEC] + [VMEM_SPEC] * 2,
+        out_specs=[VMEM_SPEC] * len(shapes),
+        out_shape=[jax.ShapeDtypeStruct((ADAPT,) + shape, F32) for shape in shapes],
+        scratch_shapes=[pltpu.VMEM((ADAPT, 6 * RANK, D), F32)],
+        name="place_grads",
+    )(ids, near, far)
 
 
 def norm_backward(values, inverse, gain_vec, upstream):
@@ -610,29 +998,25 @@
     group = ctx_index // copies
     half = tokens // 2
     ctx_masks = doublings(ctx_count)[::-1]
-    seq_slots = seq_index ^ jnp.arange(seq_count)
+    seq_slots = (seq_index ^ jnp.arange(seq_count)).astype(jnp.int32)
     ctx_slots = ctx_index ^ jnp.arange(ctx_count)
-    group_slots = group ^ jnp.arange(GROUPS)
     own_rows = inputs[0]
 
     row_slots = gather_slots(own_rows, "ctx", ctx_masks)
     own_q, own_k, own_v = local_columns(w_qkv, group)
-    own_cols = jnp.concatenate([pair_columns(own_q), own_k, own_v], axis=1)
-    col_slots = gather_seq(own_cols)
+    own_out = lax.dynamic_slice_in_dim(w_out, group * QG, QG, 1)
+    col_slots = gather_seq(jnp.concatenate([pair_columns(own_q), own_k, own_v, own_out], axis=1))
     chosen = expert_ids[0]
     hot = jnp.any(chosen[:, :, None] == jnp.arange(experts_all)[None, None, :], axis=1)
     hot_low = hot.astype(BF)
     before = (jnp.arange(tokens)[:, None] >= jnp.arange(tokens)[None, :]).astype(BF)
     ranks = dot(before, hot_low).astype(BF) * hot_low
     ranks = jnp.pad(ranks, ((0, 0), (EXP_AT, LANES - EXP_AT - experts_all)))
-    pack_slots = gather_seq(jnp.concatenate([cotangent[0], ranks], axis=1))
-    out_part = D // ctx_count
-    own_out = lax.dynamic_slice_in_dim(w_out, ctx_index * out_part, out_part, 1)
-    out_slots = jnp.stack(gather_seq(own_out))[seq_slots].reshape(QW, out_part)
-    out_all = jnp.stack(gather_slots(out_slots, "ctx", ctx_masks))[ctx_slots]
-    out_all = jnp.transpose(out_all, (1, 0, 2)).reshape(GROUPS, 2, PAIRS, HEAD_DIM, D)
-    out_all = jnp.transpose(out_all, (0, 2, 1, 3, 4)).reshape(GROUPS, QG, D)[group_slots]
-    out_all = out_all.reshape(QW, D)
+    pack = jnp.concatenate([cotangent[0], ranks], axis=1)
+    pack, *col_slots = together(pack, *col_slots)
+    pack_slots = []
+    packs = Steps(gather_line(pack, pack_slots))
+    out_parts = gather_groups(order_rows(seq_slots, col_slots), copies)
 
     seg_row = segment_ids[0]
     position = jnp.arange(length)
@@ -643,9 +1027,7 @@
     place = (2 * (owner ^ ctx_index) + (block_of >= ctx_count)).astype(jnp.int32)
     first = (start[::BLK] // BLK).astype(jnp.int32)
     offset = (position - start).reshape(2 * ctx_count, half)[block_id].reshape(-1)
-    frequency = 10000.0 ** (
-        -2.0 * jnp.arange(HEAD_DIM // 2).astype(F32) / HEAD_DIM
-    )
+    frequency = 10000.0 ** (-2.0 * jnp.arange(HEAD_DIM // 2).astype(F32) / HEAD_DIM)
     angles = offset.astype(F32)[:, None] * frequency[None, :]
     cosine, sine = jnp.cos(angles), jnp.sin(angles)
     cosine = jnp.concatenate([cosine] * 4, axis=1)
@@ -653,26 +1035,25 @@
     start_col = start[:, None]
     adapter = adapter_ids[seq_index]
     slot_adapters = adapter_ids[seq_slots]
+    slots_and_group = jnp.concatenate([slot_adapters, group[None]]).astype(jnp.int32)
+    group_info = group[None].astype(jnp.int32)
 
     def pick(table):
         return lax.dynamic_index_in_dim(table, adapter, 0, keepdims=False)
 
     qkv_down_sel = pick(qkv_down)
     up_q, up_k, up_v = local_columns(pick(qkv_up), group)
-    up_q = pair_columns(up_q)
     up_diag = jnp.concatenate(
         [
-            jnp.pad(up_q, ((0, 0), (0, 2 * KG))),
+            jnp.pad(pair_columns(up_q), ((0, 0), (0, 2 * KG))),
             jnp.pad(up_k, ((0, 0), (QG, KG))),
             jnp.pad(up_v, ((0, 0), (QG + KG, 0))),
         ],
         axis=0,
     )
-    out_down_sel = pick(out_down).reshape(GROUPS, 2, PAIRS, HEAD_DIM, RANK)
-    out_down_sel = jnp.transpose(out_down_sel, (0, 2, 1, 3, 4)).reshape(GROUPS, QG, RANK)
-    out_down_sel = out_down_sel[group_slots].reshape(QW, RANK)
+    out_down_sel = pick(out_down).T.reshape(RANK, GROUPS, 2, PAIRS, HEAD_DIM)
+    out_down_sel = jnp.transpose(out_down_sel, (0, 1, 3, 2, 4)).reshape(RANK, QW)
     out_up_sel = pick(out_up)
-    gu_down_sel = pick(gu_down)
     aux_w = jnp.concatenate(
         [
             jnp.swapaxes(gu_down, 1, 2),
@@ -683,44 +1064,25 @@
     )
     down_a_t = jnp.swapaxes(down_a, 1, 2)
 
-    features = own_rows.astype(F32)
-    inv_one = lax.rsqrt(jnp.mean(features * features, axis=-1, keepdims=True) + NORM_EPS)
     all_rows = jnp.concatenate(row_slots, axis=0).astype(F32)
     inv_all = lax.rsqrt(jnp.mean(all_rows * all_rows, axis=-1, keepdims=True) + NORM_EPS)
     h_one = (all_rows * inv_all * gain_one).astype(BF)
     rank_qkv = dot(h_one, qkv_down_sel).astype(BF)
-    qkv, cols_all = project(
-        seq_slots.astype(jnp.int32), h_one, rank_qkv, up_diag, cosine, sine, col_slots
-    )
-    heads_out, lse = attend(place, first, qkv, start_col)
-
-    def to_tokens(by_slot):
-        parts = by_slot.reshape(ctx_count, tokens, QG)
-        got = [
-            swap(parts[j * copies], "ctx", j * copies) if j else parts[0] for j in range(GROUPS)
-        ]
-        return jnp.concatenate(got, axis=1)
-
-    def to_heads(by_group):
-        got = []
-        for m in range(ctx_count):
-            piece = by_group[:, (m // copies) * QG : (m // copies + 1) * QG]
-            got.append(swap(piece, "ctx", m) if m else piece)
-        return jnp.concatenate(got, axis=0)
-
-    attended = to_tokens(heads_out)
-    rank_out = dot(attended, out_down_sel).astype(BF)
-    y_one = features + dot(attended, out_all) + dot(rank_out, out_up_sel)
-    inv_two = lax.rsqrt(jnp.mean(y_one * y_one, axis=-1, keepdims=True) + NORM_EPS)
-    h_two = (y_one * inv_two * gain_two).astype(BF)
-
-    h_slots = gather_seq(h_two)
-    y_parts, d_parts = [], []
-    for m in range(0, seq_count, 2):
-        y_pair, d_pair = experts(
+    qkv, cols_all = project(seq_slots, h_one, rank_qkv, up_diag, cosine, sine, col_slots)
+    heads_out, lse, *pieces = packs.beside(*attend(place, first, qkv, start_col, copies))
+    heads_here = [
+        swap(piece, "ctx", j * copies) if j else piece for j, piece in enumerate(pieces)
+    ]
+    attended, rank_out, y_one, h_two = project_out(
+        group_info, own_rows, gain_two[None], out_down_sel, out_up_sel, heads_here, out_parts
+    )
+    attended, rank_out, y_one, h_two = packs.beside(attended, rank_out, y_one, h_two)
+
+    def compute(m, rows):
+        return experts(
             slot_adapters[m : m + 2],
             E_DEV * seq_index,
-            h_slots[m : m + 2],
+            rows,
             pack_slots[m : m + 2],
             w_gate_up,
             w_down,
@@ -729,110 +1091,73 @@
             down_a_t,
             down_b,
         )
-        y_parts += y_pair
-        d_parts += d_pair
-    d_sum = reduce_seq(d_parts)
-    y_sum = reduce_seq(y_parts)
-    layer_output = (y_one + y_sum[:tokens]).astype(BF)[None]
-
-    grad_two = cotangent[0].astype(F32)
-    logits = dot(h_two, router)
-    picked = jnp.where(hot, logits, NEG)
-    weights = jnp.exp(picked - jnp.max(picked, axis=-1, keepdims=True))
-    gates = weights / jnp.sum(weights, axis=-1, keepdims=True)
-    d_gates = d_sum[:, D + EXP_AT : D + EXP_AT + experts_all]
-    d_logits = (gates * (d_gates - jnp.sum(gates * d_gates, axis=-1, keepdims=True))).astype(BF)
-    d_rank_gu = d_sum[:, D : D + 2 * RANK].astype(BF)
-    d_h_two = d_sum[:, :D] + dot(d_logits, router.T) + dot(d_rank_gu, gu_down_sel.T)
-    d_y_one = grad_two + norm_backward(y_one, inv_two, gain_two, d_h_two)
-    d_attn = d_y_one.astype(BF)
-    d_rank_out = dot(d_attn, out_up_sel.T).astype(BF)
-    d_attended = (dot(d_attn, out_all.T) + dot(d_rank_out, out_down_sel.T)).astype(BF)
-    d_heads = to_heads(d_attended)
-
-    grad_out_down = dot(d_rank_out.T, attended).reshape(RANK, GROUPS, QG)[:, group_slots]
-    grad_out_down = grad_out_down.reshape(RANK, GROUPS, PAIRS, 2, HEAD_DIM)
-    grad_out_down = jnp.transpose(grad_out_down, (0, 1, 3, 2, 4)).reshape(RANK, QW)
-    early = jnp.concatenate(
-        [
-            y_sum[tokens:],
-            grad_out_down,
-            dot(rank_out.T, d_attn),
-            dot(d_rank_gu.T, h_two),
-        ],
-        axis=0,
-    ).astype(BF)
-    early_rows = early.shape[0]
-    early = early.reshape(ctx_count, early_rows // ctx_count, D)[ctx_slots]
-    early = reduce_slots([early[m] for m in range(ctx_count)], "ctx", ctx_masks[::-1]).astype(BF)
-    early = jnp.stack(gather_seq(early))
-    early = jnp.stack(gather_slots(early, "ctx", ctx_masks))[ctx_slots]
-
-    d_qkv = attend_back(place, first, qkv, start_col, heads_out, lse, d_heads, cosine, sine)
-    d_rows = dot_nt(d_qkv, cols_all).astype(BF).reshape(ctx_count, tokens, D)
-    live = [m for m in range(ctx_count) if m % copies == 0]
-    d_rank_qkv = dot_nt(d_qkv, up_diag)
-    for mask in [copies * m for m in doublings(GROUPS)]:
-        low = d_rank_qkv.astype(BF)
-        arrived = swap(low, "ctx", mask).reshape(ctx_count, tokens, 3 * RANK)
-        arrived = arrived[jnp.arange(ctx_count) ^ mask].reshape(length, 3 * RANK)
-        d_rank_qkv = low.astype(F32) + arrived.astype(F32)
-    d_rank_qkv = d_rank_qkv.astype(BF)
-    d_h_one = reduce_ctx(d_rows, copies) + dot_nt(d_rank_qkv[:tokens], qkv_down_sel)
-    input_grad = (d_y_one + norm_backward(features, inv_one, gain_one, d_h_one))[None]
-
-    slice_width = D // ctx_count
-    h_slice = lax.dynamic_slice_in_dim(h_one, ctx_index * slice_width, slice_width, 1)
-    down_grad = dot(d_rank_qkv.T, h_slice).reshape(3, RANK, slice_width)
-    late = jnp.concatenate(
-        [
-            dot(rank_qkv[:, :RANK].T, d_qkv[:, :QG]),
-            dot(rank_qkv[:, RANK : 2 * RANK].T, d_qkv[:, QG : QG + KG]),
-            dot(rank_qkv[:, 2 * RANK :].T, d_qkv[:, QG + KG :]),
-            down_grad[0],
-            down_grad[1],
-            down_grad[2],
-        ],
-        axis=1,
-    ).astype(BF)
-    late = jnp.stack(gather_seq(late))
-    late = jnp.stack(gather_slots(late, "ctx", ctx_masks))[ctx_slots]
-
-    source_hot = (slot_adapters[:, None] == jnp.arange(ADAPT)[None, :]).astype(BF)
-
-    def by_adapter(values):
-        return jnp.einsum("sa,csrd->acrd", source_hot, values, preferred_element_type=F32)
-
-    early = by_adapter(early).reshape(ADAPT, early_rows, D)
-    grad_gate = early[:, :RANK, :FF]
-    grad_up = early[:, :RANK, FF : 2 * FF]
-    grad_gu_up = jnp.stack([grad_gate, grad_up], axis=1)
-    grad_down_a = jnp.swapaxes(early[:, :RANK, 2 * FF :], 1, 2)
-    grad_down_b = early[:, RANK : 2 * RANK]
-    grad_out_down = jnp.swapaxes(early[:, 2 * RANK : 3 * RANK], 1, 2)
-    grad_out_up = early[:, 3 * RANK : 4 * RANK]
-    grad_gu_down = jnp.swapaxes(early[:, 4 * RANK :], 1, 2)
-    late = by_adapter(late)
-    heads_late = late[:, ::copies]
-    grad_q = heads_late[..., :QG].reshape(ADAPT, GROUPS, RANK, PAIRS, 2, HEAD_DIM)
-    grad_q = jnp.transpose(grad_q, (0, 2, 1, 4, 3, 5)).reshape(ADAPT, RANK, QW)
-    merge = lambda part: jnp.transpose(part, (0, 2, 1, 3)).reshape(ADAPT, RANK, -1)
-    grad_qkv_up = jnp.concatenate(
-        [grad_q, merge(heads_late[..., QG : QG + KG]), merge(heads_late[..., QG + KG : LOCAL])],
-        axis=2,
-    )
-    down_part = late[..., LOCAL:].reshape(ADAPT, ctx_count, RANK, 3, slice_width)
-    grad_qkv_down = jnp.transpose(down_part, (0, 1, 4, 3, 2)).reshape(ADAPT, D, 3 * RANK)
-    return (
-        layer_output,
-        input_grad,
+
+    y_parts, d_terms = exchange_experts(h_two, packs, pack_slots, compute)
+    d_terms, y_parts = lax.optimization_barrier((d_terms, y_parts))
+    y_sums = Steps(reduce_line(y_parts))
+
+    d_y_one, d_heads, early = middle_back(
+        jnp.stack([group, ctx_index]).astype(jnp.int32),
+        ctx_count,
+        d_terms,
+        pack,
+        y_one,
+        h_two,
+        gain_two[None],
+        pick(aux_w),
+        attended,
+        rank_out,
+        out_down_sel,
+        out_up_sel,
+        out_parts,
+    )
+    d_heads = [swap(piece, "ctx", m) if m else piece for m, piece in enumerate(d_heads)]
+    d_y_one, *d_heads = y_sums.beside(d_y_one, *d_heads)
+
+    (d_qkv,) = y_sums.beside(
+        attend_back(place, first, qkv, start_col, heads_out, lse, cosine, sine, d_heads)
+    )
+    d_rows, late, late_down = inputs_back(
+        group_info, ctx_count, d_qkv, cols_all, up_diag, qkv_down_sel, rank_qkv, h_one
+    )
+
+    early = reduce_groups(early, copies, True)
+    late_down = reduce_groups(late_down, copies, False)
+    early, late, late_down = y_sums.beside(early, late, late_down)
+    grads = jnp.concatenate(
+        [late, late_down] + [early[i * RANK : (i + 1) * RANK] for i in range(6)], axis=1
+    )
+    grads = jnp.concatenate([grads, swap(grads, "ctx", 2 * copies)], axis=0)
+    grads = join(gather_seq(grads))
+    (
+        grad_qkv_up,
         grad_qkv_down,
-        grad_qkv_up,
+        grad_gu_up,
+        grad_down_a,
+        grad_down_b,
         grad_out_down,
         grad_out_up,
         grad_gu_down,
+    ) = place_grads(slots_and_group, grads, swap(grads, "ctx", copies))
+
+    layer_output = y_one
+    for term in y_sums.finish():
+        layer_output = layer_output + term.astype(F32)
+
+    d_h_one = reduce_ctx(d_rows, copies)
+    features = own_rows.astype(F32)
+    inv_one = lax.rsqrt(jnp.mean(features * features, axis=-1, keepdims=True) + NORM_EPS)
+    input_grad = d_y_one + norm_backward(features, inv_one, gain_one, d_h_one)
+    return (
+        layer_output.astype(BF)[None],
+        input_grad[None],
+        jnp.swapaxes(grad_qkv_down, 1, 2),
+        grad_qkv_up,
+        jnp.swapaxes(grad_out_down, 1, 2),
+        grad_out_up,
+        jnp.swapaxes(grad_gu_down, 1, 2),
         grad_gu_up,
-        grad_down_a,
+        jnp.swapaxes(grad_down_a, 1, 2),
         grad_down_b,
     )
 

time: 831 us -> 546 us (0.66)
  local copies, waits for them, and re-layouts: 147 us -> 20.7 us
  waiting for transfers between devices: 337 us -> 213 us
  matrix products: 39.3 us -> 1.89 us
  Pallas kernels: 127 us -> 154 us
  other arithmetic: 60.2 us -> 46.5 us
  starting transfers between devices: 111 us -> 99.2 us
    ppermute x82 -> x53, waiting for transfers between devices: 337 us -> 149 us  [swap(): return lax.ppermute(block, axis, [(i, i ^ mask) for i in range(count)])]
    ppermute x0 -> x24, waiting for transfers between devices: none -> 63.2 us  [line_swap(): lax.ppermute(block, 'seq', [(2 * i + j, 2 * k + j) for i, k in pairs for...]
    ppermute x82 -> x53, starting transfers between devices: 111 us -> 57.4 us  [swap(): return lax.ppermute(block, axis, [(i, i ^ mask) for i in range(count)])]
    ppermute x0 -> x24, starting transfers between devices: none -> 41.8 us  [line_swap(): lax.ppermute(block, 'seq', [(2 * i + j, 2 * k + j) for i, k in pairs for...]
    transpose x8 -> x2, local copies, waits for them, and re-layouts: 33.7 us -> 0.89 us  [the longest x1 0.8 us: on_device(): out_down_sel = pick(out_down).T.reshape(RANK, GROUPS, 2, PAIRS, HEAD_DIM)]
    reshape x15 -> x2, local copies, waits for them, and re-layouts: 32.5 us -> 0.91 us  [the longest x1 0.75 us: on_device(): jnp.transpose(out_down_sel, (0, 1, 3, 2, 4)).reshape(RANK, QW)]
    gather x10 -> x0, local copies, waits for them, and re-layouts: 30.3 us -> none  [the longest x1 5.88 us: on_device(): out_all = jnp.stack(gather_slots(out_slots, 'ctx', ctx_masks))[ctx_slots]]
    pallas_call x1 -> x7, Pallas kernels: 28 us -> 56 us  [the longest x1 13 us: attend(): pl.pallas_call(functools.partial(attend_kernel, copies), in_specs=[SMEM_S...]
  transfers between devices with their start and end apart: 82 -> 77, of which waited for: 30 -> 31; matrix products, arithmetic and copies ran while one was open for 26% -> 11% of each run, Pallas kernels for 15% -> 27%
where the time goes in v2:
time: 546 us; the launch traced here: 539 us
  waiting for transfers between devices  213 us (39%)
  Pallas kernels  154 us (28%)
  starting transfers between devices  99.2 us (18%)
  other arithmetic  46.5 us (9%)
  local copies, waits for them, and re-layouts  20.7 us (4%)
    ppermute x53, waiting for transfers between devices, swap(): return lax.ppermute(block, axis, [(i, i ^ mask) for i in range(count)])  149 us
    pallas_call x4, Pallas kernels, experts(): pl.pallas_call(body, grid_spec=pltpu.PrefetchScalarGridSpec(num_scalar_pr...  70.3 us
    ppermute x24, waiting for transfers between devices, line_swap(): lax.ppermute(block, 'seq', [(2 * i + j, 2 * k + j) for i, k in pairs for...  63.2 us
    ppermute x53, starting transfers between devices, swap(): return lax.ppermute(block, axis, [(i, i ^ mask) for i in range(count)])  57.4 us
    ppermute x24, starting transfers between devices, line_swap(): lax.ppermute(block, 'seq', [(2 * i + j, 2 * k + j) for i, k in pairs for...  41.8 us
    pallas_call x1, Pallas kernels, attend_back(): pl.pallas_call(attend_back_kernel, in_specs=[SMEM_SPEC, SMEM_SPEC] + [VME...  19.7 us
    pallas_call x1, Pallas kernels, attend(): pl.pallas_call(functools.partial(attend_kernel, copies), in_specs=[SMEM_S...  13 us
    pallas_call x1, Pallas kernels, inputs_back(): pl.pallas_call(inputs_kernel, grid=(count,), in_specs=[SMEM_SPEC, per_blo...  11.6 us
  transfers between devices with their start and end apart: 77, of which 31 were waited for; matrix products, arithmetic and copies ran while one was open for 11% of the time, Pallas kernels for 27%

profile of v2, /device:TPU:0, one launch (start us, length us, event | category | flops | bytes accessed | tf_op | source)
XLA Modules:
  0.0 539.1 jit_solution(5698257327671030048)
XLA Ops:
  43.7 8.3 %collective-permute-done.6 = bf16[192,1024]{1,0:T(8,128)(2,1)S(1)} collective-permute-done((bf16[192,1024]{1,0:T(8,128)(2,1)S(1)}, bf16[192,1024]{1,0:T(8,128)(2,1)S(1)}, u32[]{:S(2)}, u32[]{:S(2)}) %collective-permute-start.6) | collective-permute-done | bytes 393248 | tf_op jit(solution)/shard_map/ppermute | solution.py:72
  80.5 13.4 %collective-permute-done.22.refs_6_.refs_15_ = bf16[1536,384]{1,0:T(8,128)(2,1)S(1)} collective-permute-done((bf16[1536,384]{1,0:T(8,128)(2,1)}, bf16[1536,384]{1,0:T(8,128)(2,1)S(1)}, u32[]{:S(2)}, u32[]{:S(2)}) %collective-permute-start.22) | collective-permute-done | bytes 1179680 | tf_op jit(solution)/shard_map/ppermute | solution.py:56
  93.9 8.1 %project.1 = (bf16[1024,640]{1,0:T(8,128)(2,1)}, bf16[1536,640]{1,0:T(8,128)(2,1)}) custom-call(s32[8]{0:T(128)} %iota_xor_fusion.1.order_ref, bf16[1024,1536]{1,0:T(8,128)(2,1)} %copy-done.5, bf16[1024,48]{1,0:T(8,128)(2,1)} %convolution_convert_fusion.t_ref, bf16[48,640]{1,0:T(8,128)(2,1)} %fusion.21.up_ref, f32[1024,128]{1,0:T(8,128)} %pad_maximum_fusion.1.cos_ref, ...), custom_call_target="tpu_custom_call" | custom-call | flops 2013265920 | bytes 4456448 | tf_op jit(solution)/shard_map/project/pallas_call | solution.py:255
  102.0 13.0 %attend.1 = (bf16[1024,384]{1,0:T(8,128)(2,1)}, f32[3072,128]{1,0:T(8,128)}, bf16[256,384]{1,0:T(8,128)(2,1)}, bf16[256,384]{1,0:T(8,128)(2,1)}, bf16[256,384]{1,0:T(8,128)(2,1)}, /*index=5*/bf16[256,384]{1,0:T(8,128)(2,1)}) custom-call(s32[8]{0:T(128)} %fusion.24.place_ref, s32[4]{0:T(128)} %and_select_fusion.first_ref, ...), custom_call_target="tpu_custom_call" | custom-call | flops 1610612736 | bytes 3145728 | tf_op jit(solution)/shard_map/attend/pallas_call | solution.py:387
  131.1 7.2 %project_out.1 = (bf16[256,1536]{1,0:T(8,128)(2,1)}, bf16[256,16]{1,0:T(8,128)(2,1)}, f32[256,1536]{1,0:T(8,128)}, bf16[256,1536]{1,0:T(8,128)(2,1)}) custom-call(s32[1]{0:T(128)} %bitcast.16.group_ref, bf16[256,1536]{1,0:T(8,128)(2,1)} %bitcast.54, f32[1,1536]{1,0:T(1,128)} %broadcast_in_dim.24.gain_ref.refs_7_, ...), custom_call_target="tpu_custom_call" | custom-call | flops 1207959552 | bytes 9437184 | tf_op jit(solution)/shard_map/project_out/pallas_call | solution.py:738
  138.2 6.8 %collective-permute-done.16 = bf16[256,1664]{1,0:T(8,128)(2,1)} collective-permute-done((bf16[256,1664]{1,0:T(8,128)(2,1)}, bf16[256,1664]{1,0:T(8,128)(2,1)}, u32[]{:S(2)}, u32[]{:S(2)}) %collective-permute-start.16) | collective-permute-done | bytes 852000 | tf_op jit(solution)/shard_map/ppermute | solution.py:72
  158.1 10.5 %collective-permute-done.27.refs_0_ = bf16[256,1536]{1,0:T(8,128)(2,1)} collective-permute-done((bf16[256,1536]{1,0:T(8,128)(2,1)}, bf16[256,1536]{1,0:T(8,128)(2,1)}, u32[]{:S(2)}, u32[]{:S(2)}) %collective-permute-start.27) | collective-permute-done | bytes 786464 | tf_op jit(solution)/shard_map/ppermute | solution.py:56
  174.7 17.5 %experts.4 = (bf16[256,1536]{1,0:T(8,128)(2,1)}, bf16[256,1536]{1,0:T(8,128)(2,1)}, bf16[288,1664]{1,0:T(8,128)(2,1)}, bf16[288,1664]{1,0:T(8,128)(2,1)}) custom-call(s32[3]{0:T(128)} %get-tuple-element.357.ids_ref, bf16[256,1536]{1,0:T(8,128)(2,1)} %get-tuple-element.213.refs_0_.refs_6_, bf16[256,1536]{1,0:T(8,128)(2,1)} %collective-permute-done.29.refs_1_, ...), custom_call_target="tpu_custom_call" | custom-call | flops 6442450944 | bytes 15728640 | tf_op jit(solution)/shard_map/experts/pallas_call | solution.py:632
  192.2 10.4 %collective-permute-done.31 = bf16[256,1536]{1,0:T(8,128)(2,1)} collective-permute-done((bf16[256,1536]{1,0:T(8,128)(2,1)S(1)}, bf16[256,1536]{1,0:T(8,128)(2,1)}, u32[]{:S(2)}, u32[]{:S(2)}) %collective-permute-start.31) | collective-permute-done | bytes 786464 | tf_op jit(solution)/shard_map/ppermute | solution.py:72
  210.9 17.5 %experts.5 = (bf16[256,1536]{1,0:T(8,128)(2,1)}, bf16[256,1536]{1,0:T(8,128)(2,1)}, bf16[288,1664]{1,0:T(8,128)(2,1)}, bf16[288,1664]{1,0:T(8,128)(2,1)}) custom-call(s32[3]{0:T(128)} %get-tuple-element.358.ids_ref, bf16[256,1536]{1,0:T(8,128)(2,1)} %collective-permute-done.27.refs_0_, bf16[256,1536]{1,0:T(8,128)(2,1)} %collective-permute-done.32.refs_1_, ...), custom_call_target="tpu_custom_call" | custom-call | flops 6442450944 | bytes 15728640 | tf_op jit(solution)/shard_map/experts/pallas_call | solution.py:632
  231.7 14.8 %collective-permute-done.26.refs_3_ = bf16[256,1664]{1,0:T(8,128)(2,1)} collective-permute-done((bf16[256,1664]{1,0:T(8,128)(2,1)S(1)}, bf16[256,1664]{1,0:T(8,128)(2,1)}, u32[]{:S(2)}, u32[]{:S(2)}) %collective-permute-start.26) | collective-permute-done | bytes 852000 | tf_op jit(solution)/shard_map/ppermute | solution.py:56
  246.9 17.5 %experts.6 = (bf16[256,1536]{1,0:T(8,128)(2,1)}, bf16[256,1536]{1,0:T(8,128)(2,1)}, bf16[288,1664]{1,0:T(8,128)(2,1)}, bf16[288,1664]{1,0:T(8,128)(2,1)}) custom-call(s32[3]{0:T(128)} %get-tuple-element.359.ids_ref, bf16[256,1536]{1,0:T(8,128)(2,1)} %add.237.refs_0_, bf16[256,1536]{1,0:T(8,128)(2,1)} %collective-permute-done.34.refs_1_, ...), custom_call_target="tpu_custom_call" | custom-call | flops 6442450944 | bytes 15728640 | tf_op jit(solution)/shard_map/experts/pallas_call | solution.py:632
  265.2 17.9 %experts.7 = (bf16[256,1536]{1,0:T(8,128)(2,1)}, bf16[256,1536]{1,0:T(8,128)(2,1)}, bf16[288,1664]{1,0:T(8,128)(2,1)}, bf16[288,1664]{1,0:T(8,128)(2,1)}) custom-call(s32[3]{0:T(128)} %get-tuple-element.360.ids_ref, bf16[256,1536]{1,0:T(8,128)(2,1)} %add.238.refs_0_, bf16[256,1536]{1,0:T(8,128)(2,1)} %copy-done.51, bf16[256,1664]{1,0:T(8,128)(2,1)} %copy-done.23, ...), custom_call_target="tpu_custom_call" | custom-call | flops 6442450944 | bytes 15728640 | tf_op jit(solution)/shard_map/experts/pallas_call | solution.py:632
  285.2 22.3 %collective-permute-done.37 = bf16[288,1664]{1,0:T(8,128)(2,1)S(1)} collective-permute-done((bf16[288,1664]{1,0:T(8,128)(2,1)}, bf16[288,1664]{1,0:T(8,128)(2,1)S(1)}, u32[]{:S(2)}, u32[]{:S(2)}) %collective-permute-start.37) | collective-permute-done | bytes 958496 | tf_op jit(solution)/shard_map/ppermute | solution.py:56
  317.0 11.1 %collective-permute-done.39 = bf16[288,1664]{1,0:T(8,128)(2,1)S(1)} collective-permute-done((bf16[288,1664]{1,0:T(8,128)(2,1)}, bf16[288,1664]{1,0:T(8,128)(2,1)S(1)}, u32[]{:S(2)}, u32[]{:S(2)}) %collective-permute-start.39) | collective-permute-done | bytes 958496 | tf_op jit(solution)/shard_map/ppermute | solution.py:56
  335.8 6.8 %collective-permute-done.42 = bf16[288,1664]{1,0:T(8,128)(2,1)S(1)} collective-permute-done((bf16[288,1664]{1,0:T(8,128)(2,1)S(1)}, bf16[288,1664]{1,0:T(8,128)(2,1)S(1)}, u32[]{:S(2)}, u32[]{:S(2)}) %collective-permute-start.42) | collective-permute-done | bytes 958496 | tf_op jit(solution)/shard_map/ppermute | solution.py:56
  350.6 6.9 %collective-permute-start.43 = (bf16[288,1664]{1,0:T(8,128)(2,1)S(1)}, bf16[288,1664]{1,0:T(8,128)(2,1)S(1)}, u32[]{:S(2)}, u32[]{:S(2)}) collective-permute-start(bf16[288,1664]{1,0:T(8,128)(2,1)S(1)} %add_convert_fusion.1), channel_id=1, source_target_pairs={{0,8},{4,12},{8,0},{12,4},{16,24},{20,28},{24,16},{28,20},{1,9},{5... | collective-permute-start | bytes 2875400 | tf_op jit(solution)/shard_map/ppermute | solution.py:56
  357.5 11.8 %collective-permute-done.43.refs_1_ = bf16[288,1664]{1,0:T(8,128)(2,1)S(1)} collective-permute-done((bf16[288,1664]{1,0:T(8,128)(2,1)S(1)}, bf16[288,1664]{1,0:T(8,128)(2,1)S(1)}, u32[]{:S(2)}, u32[]{:S(2)}) %collective-permute-start.43) | collective-permute-done | bytes 958496 | tf_op jit(solution)/shard_map/ppermute | solution.py:56
  377.4 11.2 %middle_back.1 = (f32[256,1536]{1,0:T(8,128)}, bf16[256,384]{1,0:T(8,128)(2,1)}, bf16[256,384]{1,0:T(8,128)(2,1)}, bf16[256,384]{1,0:T(8,128)(2,1)}, bf16[256,38...) custom-call(s32[2]{0:T(128)} %pad_add_fusion.5.info_ref, ...), custom_call_target="tpu_custom_call" | custom-call | flops 1207959552 | bytes 12582912 | tf_op jit(solution)/shard_map/middle_back/pallas_call | solution.py:818
  408.1 19.7 %attend_back.1.dqkv_ref = bf16[1024,640]{1,0:T(8,128)(2,1)} custom-call(s32[8]{0:T(128)} %fusion.24.place_ref, s32[4]{0:T(128)} %and_select_fusion.first_ref, bf16[1024,640]{1,0:T(8,128)(2,1)} %get-tuple-element.192.qkv_ref, s32[1024,1]{1,0:T(8,128)} %copy.67.start_ref, bf16[1024,384]{1,0:T(8,128)(2,1)} %get-tuple-element.289.o_ref, ...), custom_call_target="tpu_custom_call" | custom-call | flops 4026531840 | bytes 6291456 | tf_op jit(solution)/shard_map/attend_back/pallas_call | solution.py:491
  428.6 11.6 %inputs_back.1 = (bf16[256,1536]{1,0:T(8,128)(2,1)}, bf16[256,1536]{1,0:T(8,128)(2,1)}, bf16[256,1536]{1,0:T(8,128)(2,1)}, bf16[256,1536]{1,0:T(8,128)(2,1)}, bf...) custom-call(s32[1]{0:T(128)} %bitcast.16.group_ref, ...), custom_call_target="tpu_custom_call" | custom-call | flops 2013265920 | bytes 8912896 | tf_op jit(solution)/shard_map/inputs_back/pallas_call | solution.py:878
  448.9 12.3 %collective-permute-done.51 = bf16[256,1536]{1,0:T(8,128)(2,1)S(1)} collective-permute-done((bf16[256,1536]{1,0:T(8,128)(2,1)S(1)}, bf16[256,1536]{1,0:T(8,128)(2,1)S(1)}, u32[]{:S(2)}, u32[]{:S(2)}) %collective-permute-start.51) | collective-permute-done | bytes 786464 | tf_op jit(solution)/shard_map/ppermute | solution.py:72
  474.8 12.6 %collective-permute-done.69.refs_1_ = bf16[32,4096]{1,0:T(8,128)(2,1)S(1)} collective-permute-done((bf16[32,4096]{1,0:T(8,128)(2,1)S(1)}, bf16[32,4096]{1,0:T(8,128)(2,1)S(1)}, u32[]{:S(2)}, u32[]{:S(2)}) %collective-permute-start.69) | collective-permute-done | bytes 262176 | tf_op jit(solution)/shard_map/ppermute | solution.py:56
  491.2 8.8 %collective-permute-done.71 = bf16[32,4096]{1,0:T(8,128)(2,1)S(1)} collective-permute-done((bf16[32,4096]{1,0:T(8,128)(2,1)S(1)}, bf16[32,4096]{1,0:T(8,128)(2,1)S(1)}, u32[]{:S(2)}, u32[]{:S(2)}) %collective-permute-start.71) | collective-permute-done | bytes 262176 | tf_op jit(solution)/shard_map/ppermute | solution.py:72
  (358 shorter events, 237.4 us)
Async XLA Ops:
  11.1 32.0 %collective-permute-start.13 = (bf16[256,1536]{1,0:T(8,128)(2,1)S(1)}, bf16[256,1536]{1,0:T(8,128)(2,1)}, u32[]{:S(2)}, u32[]{:S(2)}) collective-permute-start(bf16[256,1536]{1,0:T(8,128)(2,1)S(1)} %bitcast.55), channel_id=1, source_target_pairs={{0,2},{1,3},{2,0},{3,1},{4,6},{5,7},{6,4},{7,5},{8,10},{9,11},{10,... | collective-permute-start | bytes 2359304 | tf_op jit(solution)/shard_map/ppermute | solution.py:56
  12.6 56.7 %collective-permute-start.12 = (bf16[256,1536]{1,0:T(8,128)(2,1)S(1)}, bf16[256,1536]{1,0:T(8,128)(2,1)}, u32[]{:S(2)}, u32[]{:S(2)}) collective-permute-start(bf16[256,1536]{1,0:T(8,128)(2,1)S(1)} %bitcast.56), channel_id=1, source_target_pairs={{0,1},{1,0},{2,3},{3,2},{4,5},{5,4},{6,7},{7,6},{8,9},{9,8},{10,11... | collective-permute-start | bytes 2359304 | tf_op jit(solution)/shard_map/ppermute | solution.py:56
  43.1 28.0 %collective-permute-start.14 = (bf16[256,1536]{1,0:T(8,128)(2,1)}, bf16[256,1536]{1,0:T(8,128)(2,1)}, u32[]{:S(2)}, u32[]{:S(2)}) collective-permute-start(bf16[256,1536]{1,0:T(8,128)(2,1)} %collective-permute-done.13), channel_id=1, source_target_pairs={{0,1},{1,0},{2,3},{3,2},{4,5},{5,4},{6,7},{7,6},{8,9},{9,8},{10,11... | collective-permute-start | bytes 2359304 | tf_op jit(solution)/shard_map/ppermute | solution.py:56
  67.7 26.2 %collective-permute-start.22 = (bf16[1536,384]{1,0:T(8,128)(2,1)}, bf16[1536,384]{1,0:T(8,128)(2,1)S(1)}, u32[]{:S(2)}, u32[]{:S(2)}) collective-permute-start(bf16[1536,384]{1,0:T(8,128)(2,1)} %order_rows.1.refs_4_.refs_13_), channel_id=1, source_target_pairs={{0,2},{1,3},{2,0},{3,1},{4,6},{5,7},{6,4},{7,5},{8,10},{9,11},{10,... | collective-permute-start | bytes 3538952 | tf_op jit(solution)/shard_map/ppermute | solution.py:56
  67.7 62.3 %collective-permute-start.21 = (bf16[1536,384]{1,0:T(8,128)(2,1)}, bf16[1536,384]{1,0:T(8,128)(2,1)S(1)}, u32[]{:S(2)}, u32[]{:S(2)}) collective-permute-start(bf16[1536,384]{1,0:T(8,128)(2,1)} %order_rows.1.refs_4_.refs_13_), channel_id=1, source_target_pairs={{0,1},{1,0},{2,3},{3,2},{4,5},{5,4},{6,7},{7,6},{8,9},{9,8},{10,11... | collective-permute-start | bytes 3538952 | tf_op jit(solution)/shard_map/ppermute | solution.py:56
  67.8 47.2 %collective-permute-start.10 = (bf16[256,1664]{1,0:T(8,128)(2,1)}, bf16[256,1664]{1,0:T(8,128)(2,1)}, u32[]{:S(2)}, u32[]{:S(2)}) collective-permute-start(bf16[256,1664]{1,0:T(8,128)(2,1)} %fusion.11.refs_2_.refs_4_), channel_id=1, source_target_pairs={{8,16},{12,20},{16,8},{20,12},{9,17},{13,21},{17,9},{21,13},{10,18... | collective-permute-start | bytes 2555912 | tf_op jit(solution)/shard_map/ppermute | solution.py:72
  69.4 45.6 %collective-permute-start.11 = (bf16[256,1664]{1,0:T(8,128)(2,1)}, bf16[256,1664]{1,0:T(8,128)(2,1)}, u32[]{:S(2)}, u32[]{:S(2)}) collective-permute-start(bf16[256,1664]{1,0:T(8,128)(2,1)} %fusion.11.refs_2_.refs_4_), channel_id=1, source_target_pairs={{0,4},{4,0},{8,12},{12,8},{16,20},{20,16},{24,28},{28,24},{1,5},{5... | collective-permute-start | bytes 2555912 | tf_op jit(solution)/shard_map/ppermute | solution.py:56
  71.1 43.9 %collective-permute-start.9 = (bf16[256,1664]{1,0:T(8,128)(2,1)}, bf16[256,1664]{1,0:T(8,128)(2,1)}, u32[]{:S(2)}, u32[]{:S(2)}) collective-permute-start(bf16[256,1664]{1,0:T(8,128)(2,1)} %fusion.11.refs_2_.refs_4_), channel_id=1, source_target_pairs={{0,8},{4,12},{8,0},{12,4},{16,24},{20,28},{24,16},{28,20},{1,9},{5... | collective-permute-start | bytes 2555912 | tf_op jit(solution)/shard_map/ppermute | solution.py:56
  93.9 36.2 %collective-permute-start.23 = (bf16[1536,384]{1,0:T(8,128)(2,1)S(1)}, bf16[1536,384]{1,0:T(8,128)(2,1)}, u32[]{:S(2)}, u32[]{:S(2)}) collective-permute-start(bf16[1536,384]{1,0:T(8,128)(2,1)S(1)} %collective-permute-done.22.refs_6_.refs_15_), channel_id=1, source_target_pairs={{0,1},{1,0},{2,3},{3,2},{4,5},{5,4},{6,7},{7,6},{8,9},{9,8},{10,11... | collective-permute-start | bytes 3538952 | tf_op jit(solution)/shard_map/ppermute | solution.py:56
  155.0 52.8 %collective-permute-start.24 = (bf16[256,1664]{1,0:T(8,128)(2,1)S(1)}, bf16[256,1664]{1,0:T(8,128)(2,1)S(1)}, u32[]{:S(2)}, u32[]{:S(2)}) collective-permute-start(bf16[256,1664]{1,0:T(8,128)(2,1)S(1)} %add.234.refs_2_), channel_id=1, source_target_pairs={{8,0},{12,4},{16,24},{20,28},{9,1},{13,5},{17,25},{21,29},{10,2},{... | collective-permute-start | bytes 2555912 | tf_op jit(solution)/shard_map/ppermute | solution.py:72
  156.3 51.5 %collective-permute-start.25 = (bf16[256,1664]{1,0:T(8,128)(2,1)S(1)}, bf16[256,1664]{1,0:T(8,128)(2,1)}, u32[]{:S(2)}, u32[]{:S(2)}) collective-permute-start(bf16[256,1664]{1,0:T(8,128)(2,1)S(1)} %add.234.refs_2_), channel_id=1, source_target_pairs={{0,4},{4,0},{8,12},{12,8},{16,20},{20,16},{24,28},{28,24},{1,5},{5... | collective-permute-start | bytes 2555912 | tf_op jit(solution)/shard_map/ppermute | solution.py:56
  172.4 31.0 %collective-permute-start.32 = (bf16[256,1536]{1,0:T(8,128)(2,1)}, bf16[256,1536]{1,0:T(8,128)(2,1)}, u32[]{:S(2)}, u32[]{:S(2)}) collective-permute-start(bf16[256,1536]{1,0:T(8,128)(2,1)} %collective-permute-done.27.refs_0_), channel_id=1, source_target_pairs={{0,4},{4,0},{8,12},{12,8},{16,20},{20,16},{24,28},{28,24},{1,5},{5... | collective-permute-start | bytes 2359304 | tf_op jit(solution)/shard_map/ppermute | solution.py:56
  172.7 29.9 %collective-permute-start.31 = (bf16[256,1536]{1,0:T(8,128)(2,1)S(1)}, bf16[256,1536]{1,0:T(8,128)(2,1)}, u32[]{:S(2)}, u32[]{:S(2)}) collective-permute-start(bf16[256,1536]{1,0:T(8,128)(2,1)S(1)} %collective-permute-done.28), channel_id=1, source_target_pairs={{8,0},{12,4},{16,24},{20,28},{9,1},{13,5},{17,25},{21,29},{10,2},{... | collective-permute-start | bytes 2359304 | tf_op jit(solution)/shard_map/ppermute | solution.py:72
  209.2 37.3 %collective-permute-start.26 = (bf16[256,1664]{1,0:T(8,128)(2,1)S(1)}, bf16[256,1664]{1,0:T(8,128)(2,1)}, u32[]{:S(2)}, u32[]{:S(2)}) collective-permute-start(bf16[256,1664]{1,0:T(8,128)(2,1)S(1)} %add.235.refs_2_), channel_id=1, source_target_pairs={{0,4},{4,0},{8,12},{12,8},{16,20},{20,16},{24,28},{28,24},{1,5},{5... | collective-permute-start | bytes 2555912 | tf_op jit(solution)/shard_map/ppermute | solution.py:56
  230.6 33.7 %collective-permute-start.35 = (bf16[256,1536]{1,0:T(8,128)(2,1)}, bf16[256,1536]{1,0:T(8,128)(2,1)S(1)}, u32[]{:S(2)}, u32[]{:S(2)}) collective-permute-start(bf16[256,1536]{1,0:T(8,128)(2,1)} %add.238.refs_0_), channel_id=1, source_target_pairs={{0,4},{4,0},{8,12},{12,8},{16,20},{20,16},{24,28},{28,24},{1,5},{5... | collective-permute-start | bytes 2359304 | tf_op jit(solution)/shard_map/ppermute | solution.py:56
  246.5 36.7 %collective-permute-start.36 = (bf16[288,1664]{1,0:T(8,128)(2,1)}, bf16[288,1664]{1,0:T(8,128)(2,1)S(1)}, u32[]{:S(2)}, u32[]{:S(2)}) collective-permute-start(bf16[288,1664]{1,0:T(8,128)(2,1)} %get-tuple-element.250), channel_id=1, source_target_pairs={{0,4},{4,0},{8,12},{12,8},{16,20},{20,16},{24,28},{28,24},{1,5},{5... | collective-permute-start | bytes 2875400 | tf_op jit(solution)/shard_map/ppermute | solution.py:56
  284.8 43.3 %collective-permute-start.39 = (bf16[288,1664]{1,0:T(8,128)(2,1)}, bf16[288,1664]{1,0:T(8,128)(2,1)S(1)}, u32[]{:S(2)}, u32[]{:S(2)}) collective-permute-start(bf16[288,1664]{1,0:T(8,128)(2,1)} %get-tuple-element.253), channel_id=1, source_target_pairs={{0,4},{4,0},{8,12},{12,8},{16,20},{20,16},{24,28},{28,24},{1,5},{5... | collective-permute-start | bytes 2875400 | tf_op jit(solution)/shard_map/ppermute | solution.py:56
  315.5 27.1 %collective-permute-start.42 = (bf16[288,1664]{1,0:T(8,128)(2,1)S(1)}, bf16[288,1664]{1,0:T(8,128)(2,1)S(1)}, u32[]{:S(2)}, u32[]{:S(2)}) collective-permute-start(bf16[288,1664]{1,0:T(8,128)(2,1)S(1)} %copy-done.48), channel_id=1, source_target_pairs={{0,4},{4,0},{8,12},{12,8},{16,20},{20,16},{24,28},{28,24},{1,5},{5... | collective-permute-start | bytes 2875400 | tf_op jit(solution)/shard_map/ppermute | solution.py:56
  369.3 32.3 %collective-permute-start.45 = (bf16[256,1536]{1,0:T(8,128)(2,1)}, bf16[256,1536]{1,0:T(8,128)(2,1)}, u32[]{:S(2)}, u32[]{:S(2)}) collective-permute-start(bf16[256,1536]{1,0:T(8,128)(2,1)} %get-tuple-element.275), channel_id=1, source_target_pairs={{0,4},{4,0},{8,12},{12,8},{16,20},{20,16},{24,28},{28,24},{1,5},{5... | collective-permute-start | bytes 2359304 | tf_op jit(solution)/shard_map/ppermute | solution.py:56
  391.5 36.3 %collective-permute-start.50 = (bf16[256,1536]{1,0:T(8,128)(2,1)}, bf16[256,1536]{1,0:T(8,128)(2,1)S(1)}, u32[]{:S(2)}, u32[]{:S(2)}) collective-permute-start(bf16[256,1536]{1,0:T(8,128)(2,1)} %get-tuple-element.288), channel_id=1, source_target_pairs={{0,4},{4,0},{8,12},{12,8},{16,20},{20,16},{24,28},{28,24},{1,5},{5... | collective-permute-start | bytes 2359304 | tf_op jit(solution)/shard_map/ppermute | solution.py:56
  398.1 50.8 %collective-permute-start.53 = (bf16[256,1536]{1,0:T(8,128)(2,1)}, bf16[256,1536]{1,0:T(8,128)(2,1)S(1)}, u32[]{:S(2)}, u32[]{:S(2)}) collective-permute-start(bf16[256,1536]{1,0:T(8,128)(2,1)} %get-tuple-element.297), channel_id=1, source_target_pairs={{0,4},{4,0},{8,12},{12,8},{16,20},{20,16},{24,28},{28,24},{1,5},{5... | collective-permute-start | bytes 2359304 | tf_op jit(solution)/shard_map/ppermute | solution.py:56
  462.9 59.9 %collective-permute-start.62 = (bf16[256,1536]{1,0:T(8,128)(2,1)}, bf16[256,1536]{1,0:T(8,128)(2,1)}, u32[]{:S(2)}, u32[]{:S(2)}) collective-permute-start(bf16[256,1536]{1,0:T(8,128)(2,1)} %get-tuple-element.312), channel_id=1, source_target_pairs={{0,4},{4,0},{8,12},{12,8},{16,20},{20,16},{24,28},{28,24},{1,5},{5... | collective-permute-start | bytes 2359304 | tf_op jit(solution)/shard_map/ppermute | solution.py:56
  474.7 36.4 %collective-permute-start.63 = (bf16[256,1536]{1,0:T(8,128)(2,1)S(1)}, bf16[256,1536]{1,0:T(8,128)(2,1)S(1)}, u32[]{:S(2)}, u32[]{:S(2)}) collective-permute-start(bf16[256,1536]{1,0:T(8,128)(2,1)S(1)} %copy-done.49), channel_id=1, source_target_pairs={{0,1},{1,0},{2,3},{3,2},{4,5},{5,4},{6,7},{7,6},{8,9},{9,8},{10,11... | collective-permute-start | bytes 2359304 | tf_op jit(solution)/shard_map/ppermute | solution.py:56
  489.9 31.4 %collective-permute-start.65 = (bf16[256,1536]{1,0:T(8,128)(2,1)S(1)}, bf16[256,1536]{1,0:T(8,128)(2,1)}, u32[]{:S(2)}, u32[]{:S(2)}) collective-permute-start(bf16[256,1536]{1,0:T(8,128)(2,1)S(1)} %add_convert_fusion.5), channel_id=1, source_target_pairs={{0,2},{1,3},{2,0},{3,1},{4,6},{5,7},{6,4},{7,5},{8,10},{9,11},{10,... | collective-permute-start | bytes 2359304 | tf_op jit(solution)/shard_map/ppermute | solution.py:56
  (109 other events, 1524.0 us)

commit v3 on v2

v3 whole, which is shorter than its diff:
```python
import functools

import jax
import jax.numpy as jnp
from jax import lax
from jax.experimental import pallas as pl
from jax.experimental.pallas import tpu as pltpu
from jax.sharding import PartitionSpec as P

D = 1536
HEADS = 24
KV_HEADS = 8
HEAD_DIM = 64
FF = 512
RANK = 16
ADAPT = 8
E_DEV = 2
CAP = 128
QW = 1536
KVW = 512
NORM_EPS = 1e-05

GROUPS = KV_HEADS // 2
PAIRS = HEADS // KV_HEADS
QG = QW // GROUPS
KG = KVW // GROUPS
LOCAL = QG + 2 * KG
BLK = 256
LANES = 128
EXP_AT = 2 * RANK
GATE_AT = 96
EXT = D + LANES
NEG = -1e30

BF = jnp.bfloat16
F32 = jnp.float32
NT = (((1,), (1,)), ((), ()))
TN = (((0,), (0,)), ((), ()))


def dot(left_arr, right_arr):
    return jnp.dot(left_arr, right_arr, preferred_element_type=F32)


def dot_nt(left_arr, right_arr):
    return lax.dot_general(left_arr, right_arr, NT, preferred_element_type=F32)


def dot_tn(left_arr, right_arr):
    return lax.dot_general(left_arr, right_arr, TN, preferred_element_type=F32)


def swap(block, axis, mask):
    count = lax.axis_size(axis)
    return lax.ppermute(block, axis, [(i, i ^ mask) for i in range(count)])


def gather_slots(block, axis, masks):
    slots = {0: block}
    for mask in masks:
        for have in list(slots):
            slots[have ^ mask] = swap(slots[have], axis, mask)
    return [slots[m] for m in sorted(slots)]


def together(*arrays):
    return lax.optimization_barrier(arrays)


def gather_rest(block, arrived, masks):
    slots = {0: block}
    for mask, first in zip(masks, arrived):
        for have in list(slots):
            slots[have ^ mask] = swap(slots[have], "ctx", mask) if have else first
    return [slots[m] for m in sorted(slots)]


def line_swap(block, pairs):
    return lax.ppermute(block, "seq", [(2 * i + j, 2 * k + j) for i, k in pairs for j in (0, 1)])


def outward(block):
    return line_swap(block, [(1, 0), (2, 3)])


def inward(block):
    return line_swap(block, [(0, 1), (3, 2)])


def middle(block):
    return line_swap(block, [(1, 2), (2, 1)])


class Steps:
    def __init__(self, work):
        self.work = work
        self.moving = self.result = None
        self.resume(None)

    def resume(self, arrived):
        try:
            self.moving = self.work.send(arrived)
        except StopIteration as end:
            self.moving, self.result = None, end.value

    def beside(self, *others):
        if self.moving is None:
            return others
        arrived, others = lax.optimization_barrier((tuple(self.moving), others))
        self.resume(arrived)
        return others

    def join(self, other, *others):
        if self.moving is None or other.moving is None:
            return self.beside(*other.beside(*others))
        mine, theirs, others = lax.optimization_barrier(
            (tuple(self.moving), tuple(other.moving), others)
        )
        self.resume(mine)
        other.resume(theirs)
        return others

    def finish(self):
        while self.moving is not None:
            self.beside()
        return self.result


def gather_line(block, slots):
    count = lax.axis_size("seq")
    if count != 8:
        slots += gather_slots(block, "seq", doublings(count))
        return slots
    slots.append(block)
    two, six, one = yield swap(block, "seq", 2), middle(block), swap(block, "seq", 1)
    slots += [one, two]
    four, far, three = yield middle(two), outward(six), swap(two, "seq", 1)
    four = four + far
    slots += [three, four]
    far, five = yield outward(four), swap(four, "seq", 1)
    six = six + far
    slots += [five, six]
    (seven,) = yield (swap(six, "seq", 1),)
    slots.append(seven)
    return slots


def gather_seq(block):
    return Steps(gather_line(block, [])).finish()


def reduce_line(parts, one=None):
    count = lax.axis_size("seq")
    if count != 8:
        return [reduce_slots(parts, "seq", doublings(count))]
    (seven,) = yield (swap(parts[7], "seq", 1),)
    six = add_low(parts[6], seven)
    near, five = yield inward(six), swap(parts[5], "seq", 1)
    four = add_low(parts[4], five, near)
    near, far, three = yield inward(four), middle(four), swap(parts[3], "seq", 1)
    six = add_low(six, near)
    two = add_low(parts[2], three, far)
    last = [swap(two, "seq", 2), middle(six)]
    if one is None:
        last.append(swap(parts[1], "seq", 1))
    last = yield last
    return [parts[0], *last] + ([] if one is None else [one])


def exchange_experts(block, packs, compute):
    count = lax.axis_size("seq")
    slots, y_parts, d_parts = [], [], []
    rows = Steps(gather_line(block, slots))

    def slots_of(m, some):
        some_y, some_d = compute(m, slots[m : m + some])
        return [*some_y, *some_d]

    def keep(done, some):
        y_parts.extend(done[:some])
        d_parts.extend(done[some:])

    if count != 8:
        packs.finish()
        for m in range(0, count, 2):
            keep(slots_of(m, 2), 2)
        return Steps(reduce_line(y_parts)), Steps(reduce_line(d_parts)).finish()
    keep(rows.join(packs, *slots_of(0, 1)), 1)
    for m in (1, 3, 5):
        keep(rows.beside(*slots_of(m, 2)), 2)
    one = swap(d_parts[1], "seq", 1)
    *done, one = lax.optimization_barrier((*slots_of(7, 1), one))
    keep(done, 1)
    terms = Steps(reduce_line(d_parts, one))
    terms.beside()
    terms.beside()
    y_sums = Steps(reduce_line(list(terms.beside(*y_parts))))
    return y_sums, terms.finish()


def doublings(count):
    return [1 << bit for bit in range(count.bit_length() - 1)]


def add_low(*terms):
    total = terms[0].astype(F32)
    for term in terms[1:]:
        total = total + term.astype(F32)
    return lax.optimization_barrier(total.astype(BF))


def gather_groups(block, copies):
    two, one = yield swap(block, "ctx", 2 * copies), swap(block, "ctx", copies)
    return [block, one, two, swap(two, "ctx", copies)]


def reduce_slots(parts, axis, masks):
    parts = dict(enumerate(parts))
    for step, mask in enumerate(masks):
        last = step == len(masks) - 1
        for m in [m for m in parts if m & mask]:
            arrived = swap(parts.pop(m), axis, mask)
            mine = parts[m ^ mask]
            parts[m ^ mask] = (
                mine.astype(F32) + arrived.astype(F32) if last else add_low(mine, arrived)
            )
    return parts[0]


def rotate(values, cosine, sine, sign):
    lane = lax.broadcasted_iota(jnp.int32, values.shape, 1)
    ahead = pltpu.roll(values, LANES - HEAD_DIM // 2, 1)
    behind = pltpu.roll(values, HEAD_DIM // 2, 1)
    other = jnp.where(lane % HEAD_DIM < HEAD_DIM // 2, ahead, behind)
    return values * cosine + (sign * other) * sine


def project_kernel(info_ref, h_ref, t_ref, table_ref, cos_ref, sin_ref, *rest):
    shards = rest[:-4]
    qkv_ref, full_ref, up_ref, w_ref = rest[-4:]
    rows = shards[0].shape[0]
    group = info_ref[len(shards) + 1]

    @pl.when(pl.program_id(0) == 0)
    def _():
        for m, shard in enumerate(shards):
            start = pl.multiple_of(info_ref[m] * rows, rows)
            w_ref[pl.ds(start, rows), :] = shard[:, :LOCAL]
        full_ref[...] = w_ref[...]
        up_ref[...] = jnp.zeros(up_ref.shape, BF)
        columns = lambda first, width: table_ref[
            0, :, pl.ds(pl.multiple_of(first + group * width, LANES), width)
        ]
        up_ref[:RANK, :QG] = columns(0, QG)
        up_ref[RANK : 2 * RANK, QG : QG + KG] = columns(QW, KG)
        up_ref[2 * RANK :, QG + KG :] = columns(QW + KVW, KG)

    pre = dot(h_ref[...], w_ref[...]) + dot(t_ref[...], up_ref[...])
    cosine, sine = cos_ref[...], sin_ref[...]
    tiles = [rotate(tile, cosine, sine, 1.0) * 0.125 for tile in lane_tiles(pre)]
    tiles = paired_heads(tiles)
    tiles.append(rotate(pre[:, QG : QG + KG], cosine, sine, 1.0))
    tiles.append(pre[:, QG + KG :])
    for j, tile in enumerate(tiles):
        qkv_ref[:, j * LANES : (j + 1) * LANES] = tile.astype(BF)


def project(order, adapter, group, h_one, rank_qkv, table, cosine, sine, shards):
    length = h_one.shape[0]
    rows = shards[0].shape[0]
    count = len(shards)
    per_block = lambda width: pl.BlockSpec((BLK, width), lambda i, info: (i, 0))
    whole = lambda shape: pl.BlockSpec(shape, lambda i, info: (0, 0))
    return pl.pallas_call(
        project_kernel,
        grid_spec=pltpu.PrefetchScalarGridSpec(
            num_scalar_prefetch=1,
            grid=(length // BLK,),
            in_specs=[
                per_block(D),
                per_block(3 * RANK),
                pl.BlockSpec((1,) + table.shape[1:], lambda i, info: (info[count], 0, 0)),
                per_block(LANES),
                per_block(LANES),
            ]
            + [whole((rows, LOCAL + QG))] * count,
            out_specs=[per_block(LOCAL), whole((D, LOCAL)), whole((3 * RANK, LOCAL))],
            scratch_shapes=[pltpu.VMEM((D, LOCAL), BF)],
        ),
        out_shape=[
            jax.ShapeDtypeStruct((length, LOCAL), BF),
            jax.ShapeDtypeStruct((D, LOCAL), BF),
            jax.ShapeDtypeStruct((3 * RANK, LOCAL), BF),
        ],
        cost_estimate=pl.CostEstimate(
            flops=2 * length * D * LOCAL, bytes_accessed=2 * length * (D + LOCAL), transcendentals=0
        ),
        name="project",
    )(
        jnp.concatenate([order, adapter[None], group[None]]).astype(jnp.int32),
        h_one,
        rank_qkv,
        table,
        cosine,
        sine,
        *shards,
    )


def half_mask(shape, half):
    lane = lax.broadcasted_iota(jnp.int32, shape, 1)
    return (lane < HEAD_DIM) if half == 0 else (lane >= HEAD_DIM)


def turned(tile):
    return pltpu.roll(tile.astype(F32), HEAD_DIM, 1).astype(tile.dtype)


def paired_heads(tiles):
    is_low = half_mask(tiles[0].shape, 0)
    return [
        jnp.where(is_low, tiles[0], tiles[1]),
        jnp.where(is_low, turned(tiles[0]), turned(tiles[2])),
        jnp.where(is_low, tiles[1], tiles[2]),
    ]


def natural_heads(tiles):
    is_low = half_mask(tiles[0].shape, 0)
    return [
        jnp.where(is_low, tiles[0], turned(tiles[1])),
        jnp.where(is_low, tiles[2], tiles[0]),
        jnp.where(is_low, turned(tiles[1]), tiles[2]),
    ]


def lane_tiles(block):
    return [block[:, i * LANES : (i + 1) * LANES] for i in range(PAIRS)]


def stack_rows(place_ref, source_ref, target_ref, paired):
    half = BLK // 2
    for b in range(source_ref.shape[0] // half):
        rows = pl.ds(pl.multiple_of(place_ref[b] * half, half), half)
        tiles = lane_tiles(source_ref[rows, :QG])
        for pair, tile in enumerate(tiles if paired else paired_heads(tiles)):
            at = (b // 2) * PAIRS * BLK + pair * BLK + (b % 2) * half
            target_ref[at : at + half, :] = tile


def split_keys(place_ref, qkv_ref, first_lane, target_ref, ones):
    half = BLK // 2
    for b in range(qkv_ref.shape[0] // half):
        rows = pl.ds(pl.multiple_of(place_ref[b] * half, half), half)
        both = qkv_ref[rows, first_lane : first_lane + LANES]
        for side in range(2):
            other = jnp.zeros_like(both)
            if ones:
                lane = lax.broadcasted_iota(jnp.int32, both.shape, 1)
                spare = HEAD_DIM if side == 0 else 0
                other = jnp.where(lane == spare, 1.0, 0.0).astype(BF)
            target_ref[side, b * half : (b + 1) * half, :] = jnp.where(
                half_mask(both.shape, side), both, other
            )


def tile_bias(start_col, q_first, k_first):
    shape = (BLK, BLK)
    key = k_first + lax.broadcasted_iota(jnp.int32, shape, 1)
    query = q_first + lax.broadcasted_iota(jnp.int32, shape, 0)
    bias = jnp.where((key >= start_col) & (key <= query), 0.0, NEG)
    return jnp.concatenate([bias] * PAIRS, axis=0)


def attend_kernel(copies, place_ref, first_ref, qkv_ref, start_ref, o_ref, lse_ref, *refs):
    piece_refs, (q_s, k_s, v_s, score_s, m_s, acc_s) = refs[:GROUPS], refs[GROUPS:]
    stack_rows(place_ref, qkv_ref, q_s, True)
    split_keys(place_ref, qkv_ref, QG, k_s, False)
    split_keys(place_ref, qkv_ref, QG + KG, v_s, True)
    half = BLK // 2
    tall = PAIRS * BLK

    def query_block(qb, unused):
        q_first = pl.multiple_of(qb * BLK, BLK)
        q_rows = pl.ds(pl.multiple_of(qb * tall, tall), tall)
        start_col = start_ref[pl.ds(q_first, BLK), :]
        queries = q_s[q_rows, :]
        m_s[...] = jnp.full(m_s.shape, NEG, F32)
        acc_s[...] = jnp.zeros(acc_s.shape, F32)

        def score_block(kb, unused):
            k_first = pl.multiple_of(kb * BLK, BLK)
            bias = tile_bias(start_col, q_first, k_first)
            for side in range(2):
                scores = dot_nt(queries, k_s[side, pl.ds(k_first, BLK), :]) + bias
                score_s[kb, side] = scores
                m_s[side] = jnp.maximum(
                    m_s[side], jnp.maximum(scores[:, :LANES], scores[:, LANES:])
                )
            return unused

        lax.fori_loop(first_ref[qb], qb + 1, score_block, 0)
        peaks = [jnp.max(m_s[side], axis=1, keepdims=True) for side in range(2)]

        def value_block(kb, unused):
            k_first = pl.multiple_of(kb * BLK, BLK)
            for side in range(2):
                prob = jnp.exp(score_s[kb, side] - peaks[side]).astype(BF)
                acc_s[side] += dot(prob, v_s[side, pl.ds(k_first, BLK), :])
            return unused

        lax.fori_loop(first_ref[qb], qb + 1, value_block, 0)
        low, high = acc_s[0], acc_s[1]
        low_sum = low[:, HEAD_DIM : HEAD_DIM + 1]
        high_sum = high[:, 0:1]
        is_low = half_mask(low.shape, 0)
        out = jnp.where(is_low, low / low_sum, high / high_sum).astype(BF)
        lse_ref[q_rows, :] = jnp.where(
            is_low, peaks[0] + jnp.log(low_sum), peaks[1] + jnp.log(high_sum)
        )
        for i in range(2):
            rows = pl.ds(pl.multiple_of(place_ref[2 * qb + i] * half, half), half)
            tiles = [out[pair * BLK + i * half :][:half] for pair in range(PAIRS)]
            for pair, tile in enumerate(natural_heads(tiles)):
                o_ref[rows, pair * LANES : (pair + 1) * LANES] = tile
        return unused

    lax.fori_loop(0, qkv_ref.shape[0] // BLK, query_block, 0)
    for j, piece in enumerate(piece_refs):
        tokens = piece.shape[0]
        piece[...] = o_ref[j * copies * tokens : (j * copies + 1) * tokens, :]


SMEM_SPEC = pl.BlockSpec(memory_space=pltpu.SMEM)
VMEM_SPEC = pl.BlockSpec(memory_space=pltpu.VMEM)


def attend(place, first, qkv, start_col, copies):
    length = qkv.shape[0]
    tall = PAIRS * BLK
    return pl.pallas_call(
        functools.partial(attend_kernel, copies),
        in_specs=[SMEM_SPEC, SMEM_SPEC, VMEM_SPEC, VMEM_SPEC],
        out_specs=[VMEM_SPEC] * (2 + GROUPS),
        out_shape=[
            jax.ShapeDtypeStruct((length, QG), BF),
            jax.ShapeDtypeStruct((PAIRS * length, LANES), F32),
        ]
        + [jax.ShapeDtypeStruct((length // (GROUPS * copies), QG), BF)] * GROUPS,
        scratch_shapes=[
            pltpu.VMEM((PAIRS * length, LANES), BF),
            pltpu.VMEM((2, length, LANES), BF),
            pltpu.VMEM((2, length, LANES), BF),
            pltpu.VMEM((length // BLK, 2, tall, BLK), F32),
            pltpu.VMEM((2, tall, LANES), F32),
            pltpu.VMEM((2, tall, LANES), F32),
        ],
        cost_estimate=pl.CostEstimate(
            flops=4 * length * length * QG, bytes_accessed=8 * length * QG, transcendentals=0
        ),
        name="attend",
    )(place, first, qkv, start_col)


def attend_back_kernel(
    place_ref,
    first_ref,
    qkv_ref,
    start_ref,
    o_ref,
    lse_ref,
    cos_ref,
    sin_ref,
    *refs,
):
    do_refs = refs[:-10]
    dqkv_ref, join_s, q_s, o_s, do_s, k_s, v_s, dk_s, dv_s, dq_s = refs[-10:]
    for m, piece in enumerate(do_refs):
        join_s[m * piece.shape[0] : (m + 1) * piece.shape[0], :] = piece[...]
    stack_rows(place_ref, qkv_ref, q_s, True)
    stack_rows(place_ref, o_ref, o_s, False)
    stack_rows(place_ref, join_s, do_s, False)
    split_keys(place_ref, qkv_ref, QG, k_s, False)
    split_keys(place_ref, qkv_ref, QG + KG, v_s, False)
    dk_s[...] = jnp.zeros(dk_s.shape, F32)
    dv_s[...] = jnp.zeros(dv_s.shape, F32)
    half = BLK // 2
    tall = PAIRS * BLK

    def query_block(qb, unused):
        q_first = pl.multiple_of(qb * BLK, BLK)
        q_rows = pl.ds(pl.multiple_of(qb * tall, tall), tall)
        start_col = start_ref[pl.ds(q_first, BLK), :]
        dq_s[...] = jnp.zeros(dq_s.shape, F32)
        product = do_s[q_rows, :].astype(F32) * o_s[q_rows, :].astype(F32)
        lse = lse_ref[q_rows, :]
        lse_of = (lse[:, 0:1], lse[:, HEAD_DIM : HEAD_DIM + 1])
        delta_of = [
            jnp.sum(jnp.where(half_mask(product.shape, side), product, 0.0), axis=1, keepdims=True)
            for side in range(2)
        ]

        def key_block(kb, unused):
            k_first = pl.multiple_of(kb * BLK, BLK)
            k_rows = pl.ds(k_first, BLK)
            bias = tile_bias(start_col, q_first, k_first)
            queries = q_s[q_rows, :]
            d_out = do_s[q_rows, :]
            for side in range(2):
                keys = k_s[side, k_rows, :]
                scores = dot_nt(queries, keys) + bias
                prob = jnp.exp(scores - lse_of[side])
                d_prob = dot_nt(d_out, v_s[side, k_rows, :])
                d_score = (prob * (d_prob - delta_of[side])).astype(BF)
                dv_s[side, k_rows, :] += dot_tn(prob.astype(BF), d_out)
                dk_s[side, k_rows, :] += dot_tn(d_score, queries)
                dq_s[...] += dot(d_score, keys)
            return unused

        lax.fori_loop(first_ref[qb], qb + 1, key_block, 0)
        for i in range(2):
            rows = pl.ds(pl.multiple_of(place_ref[2 * qb + i] * half, half), half)
            cosine, sine = cos_ref[rows, :], sin_ref[rows, :]
            tiles = []
            for pair in range(PAIRS):
                at = pair * BLK + i * half
                tiles.append(rotate(dq_s[at : at + half, :] * 0.125, cosine, sine, -1.0))
            for pair, tile in enumerate(natural_heads(tiles)):
                dqkv_ref[rows, pair * LANES : (pair + 1) * LANES] = tile.astype(BF)
        return unused

    lax.fori_loop(0, qkv_ref.shape[0] // BLK, query_block, 0)
    for b in range(qkv_ref.shape[0] // half):
        rows = pl.ds(pl.multiple_of(place_ref[b] * half, half), half)
        at = slice(b * half, (b + 1) * half)
        is_low = half_mask((half, LANES), 0)
        back = jnp.where(is_low, dk_s[0, at, :], dk_s[1, at, :])
        back = rotate(back, cos_ref[rows, :], sin_ref[rows, :], -1.0)
        dqkv_ref[rows, QG : QG + KG] = back.astype(BF)
        dqkv_ref[rows, QG + KG : LOCAL] = jnp.where(is_low, dv_s[0, at, :], dv_s[1, at, :]).astype(BF)


def attend_back(place, first, qkv, start_col, out, lse, cosine, sine, d_out):
    length = qkv.shape[0]
    tall = PAIRS * BLK
    stacked = pltpu.VMEM((PAIRS * length, LANES), BF)
    return pl.pallas_call(
        attend_back_kernel,
        in_specs=[SMEM_SPEC, SMEM_SPEC] + [VMEM_SPEC] * (6 + len(d_out)),
        out_specs=VMEM_SPEC,
        out_shape=jax.ShapeDtypeStruct((length, LOCAL), BF),
        scratch_shapes=[
            pltpu.VMEM((length, QG), BF),
            stacked,
            stacked,
            stacked,
            pltpu.VMEM((2, length, LANES), BF),
            pltpu.VMEM((2, length, LANES), BF),
            pltpu.VMEM((2, length, LANES), F32),
            pltpu.VMEM((2, length, LANES), F32),
            pltpu.VMEM((tall, LANES), F32),
        ],
        cost_estimate=pl.CostEstimate(
            flops=10 * length * length * QG, bytes_accessed=16 * length * QG, transcendentals=0
        ),
        name="attend_back",
    )(place, first, qkv, start_col, out, lse, cosine, sine, *d_out)


def expert_kernel(ids_ref, h_refs, p_refs, wgu_ref, wd_ref, tables, y_refs, d_refs, scratch):
    aux_w, gu_refs, da_refs, db_refs = tables
    wgu_s, wd_s, gu_s, put_s, x_s, g_s, extra_s, yrow_s, drow_s, grad_s, sems = scratch
    count = len(h_refs)
    tokens = h_refs[0].shape[0]

    def fetch(e):
        return [
            pltpu.make_async_copy(wgu_ref.at[e], wgu_s.at[e], sems.at[0, e]),
            pltpu.make_async_copy(wd_ref.at[e], wd_s.at[e], sems.at[1, e]),
        ]

    for e in range(E_DEV):
        for copy in fetch(e):
            copy.start()
    wide = lax.broadcasted_iota(jnp.int32, (tokens, LANES), 1)
    narrow = lax.broadcasted_iota(jnp.int32, (CAP, LANES), 1)
    base = EXP_AT + ids_ref[count]
    grad_s[...] = jnp.zeros(grad_s.shape, F32)
    gu_s[...] = jnp.zeros(gu_s.shape, BF)
    part = lambda arr, j: arr[j * CAP : (j + 1) * CAP]
    for j in range(count):
        gu_s[j, 0, 0:RANK, :] = gu_refs[j][0, 0]
        gu_s[j, 1, RANK : 2 * RANK, :] = gu_refs[j][0, 1]
        both = dot_nt(h_refs[j][...], aux_w[j][0])
        ranks = p_refs[j][:, D:EXT].astype(F32)
        chosen = ranks > 0.0
        picked = jnp.where(chosen, both, NEG)
        weights = jnp.exp(picked - jnp.max(picked, axis=1, keepdims=True))
        gates = weights / jnp.sum(weights, axis=1, keepdims=True)
        aux = jnp.where(wide < EXP_AT, both, 0.0)
        tall = ranks.T
        which = lax.broadcasted_iota(jnp.int32, tall.shape, 0)
        slot = lax.broadcasted_iota(jnp.int32, (CAP, tokens), 0).astype(F32) + 1.0
        takes = []
        for e in range(E_DEV):
            column = jnp.sum(jnp.where(wide == base + e, ranks, 0.0), axis=1, keepdims=True)
            row = jnp.sum(jnp.where(which == base + e, tall, 0.0), axis=0, keepdims=True)
            takes.append(jnp.where(slot == row, 1.0, 0.0).astype(BF))
            put_s[j, :, e * CAP : (e + 1) * CAP] = jnp.where(
                wide.astype(F32) + 1.0 == column, 1.0, 0.0
            ).astype(BF)
            gate = jnp.sum(jnp.where(wide == base + e, gates, 0.0), axis=1, keepdims=True)
            gate_one = gate.astype(BF).astype(F32)
            gate_two = (gate - gate_one).astype(BF).astype(F32)
            first = GATE_AT + 3 * e
            aux = jnp.where(wide == first, gate_one, aux)
            aux = jnp.where(wide == first + 1, gate_two, aux)
            aux = jnp.where(wide == first + 2, gate - gate_one - gate_two, aux)
        take = jnp.concatenate(takes, axis=0)
        at = slice(j * CAP, (j + 1) * CAP)
        rows = dot(take, h_refs[j][...]).astype(BF)
        upstream = dot(take, p_refs[j][:, :D]).astype(BF)
        extra = dot(take, aux.astype(BF))
        for e in range(E_DEV):
            x_s[e, at, :] = part(rows, e)
            g_s[e, at, :] = part(upstream, e)
            extra_s[e, at, :] = part(extra, e)

    def each(make):
        return jnp.concatenate([make(j) for j in range(count)], axis=0)

    def expert(e, unused):
        for copy in fetch(e):
            copy.wait()
        extra = extra_s[e]
        low_extra = extra.astype(BF)
        place = lax.broadcasted_iota(jnp.int32, extra.shape, 1) - (GATE_AT + 3 * e)
        gate = jnp.sum(jnp.where((place >= 0) & (place < 3), extra, 0.0), axis=1, keepdims=True)
        both = dot(x_s[e], wgu_s[e])
        gate_pre = both[:, :FF] + each(lambda j: dot(part(low_extra, j), gu_s[j, 0]))
        up_pre = both[:, FF:] + each(lambda j: dot(part(low_extra, j), gu_s[j, 1]))
        sigmoid = jax.nn.sigmoid(gate_pre)
        silu = gate_pre * sigmoid
        active = (silu * up_pre).astype(BF)
        down = [dot_nt(part(active, j), da_refs[j][0]).astype(BF) for j in range(count)]
        result = dot(active, wd_s[e]) + each(lambda j: dot(down[j], db_refs[j][0]))
        result = result.astype(BF).astype(F32)
        grad_in = g_s[e].astype(F32)
        d_gate_val = jnp.sum(grad_in * result, axis=1, keepdims=True)
        weighted = (gate * result).astype(BF)
        d_result = (gate * grad_in).astype(BF)
        d_down = [dot_nt(part(d_result, j), db_refs[j][0]).astype(BF) for j in range(count)]
        d_active = dot_nt(d_result, wd_s[e]) + each(lambda j: dot(d_down[j], da_refs[j][0]))
        d_gate = (d_active * up_pre * sigmoid * (1.0 + gate_pre * (1.0 - sigmoid))).astype(BF)
        d_up = (d_active * silu).astype(BF)
        d_rows = dot_nt(jnp.concatenate([d_gate, d_up], axis=1), wgu_s[e]).astype(BF)
        at = pl.ds(pl.multiple_of(e * CAP, CAP), CAP)
        for j in range(count):
            yrow_s[j, at, :] = part(weighted, j)
            drow_s[j, at, :D] = part(d_rows, j)
            d_extra = dot_nt(part(d_gate, j), gu_s[j, 0]) + dot_nt(part(d_up, j), gu_s[j, 1])
            d_extra = d_extra + jnp.where(narrow == base + e, part(d_gate_val, j), 0.0)
            drow_s[j, at, D:] = d_extra.astype(BF)
            ranks_in = part(low_extra, j)
            grad_s[j, 0:RANK, 0:FF] += dot_tn(ranks_in, part(d_gate, j))[0:RANK]
            grad_s[j, 0:RANK, FF : 2 * FF] += dot_tn(ranks_in, part(d_up, j))[RANK : 2 * RANK]
            grad_s[j, 0:RANK, 2 * FF :] += dot_tn(d_down[j], part(active, j))
            grad_s[j, RANK:, :] += dot_tn(down[j], part(d_result, j))
        return unused

    lax.fori_loop(0, E_DEV, expert, 0)
    for j in range(count):
        put = put_s[j]
        y_refs[j][...] = dot(put, yrow_s[j]).astype(BF)
        d_refs[j][:tokens, :] = dot(put, drow_s[j]).astype(BF)
        d_refs[j][tokens:, :D] = grad_s[j].astype(BF)
        d_refs[j][tokens:, D:] = jnp.zeros((2 * RANK, LANES), BF)


def experts(adapters, base, rows, packs, w_gate_up, w_down, aux_w, gu_up, down_a, down_b):
    count = len(rows)
    tokens = rows[0].shape[0]
    whole = lambda width: pl.BlockSpec((tokens, width), lambda e, ids: (0, 0))

    def table(shape, j):
        return pl.BlockSpec((1,) + shape, lambda e, ids: (ids[j],) + (0,) * len(shape))

    def body(ids_ref, *refs):
        refs = list(refs)
        take = lambda n: [refs.pop(0) for _ in range(n)]
        h_refs, p_refs = take(count), take(count)
        wgu_ref, wd_ref = take(2)
        tables = [take(count) for _ in range(4)]
        y_refs, d_refs = take(count), take(count)
        expert_kernel(ids_ref, h_refs, p_refs, wgu_ref, wd_ref, tables, y_refs, d_refs, refs)

    picked = [(LANES, D), (2, RANK, FF), (RANK, FF), (RANK, D)]
    shapes = [(tokens, D)] * count + [(tokens + 2 * RANK, EXT)] * count
    height = count * CAP
    outs = pl.pallas_call(
        body,
        grid_spec=pltpu.PrefetchScalarGridSpec(
            num_scalar_prefetch=1,
            grid=(1,),
            in_specs=[whole(D)] * count
            + [whole(EXT)] * count
            + [pl.BlockSpec(memory_space=pl.ANY)] * 2
            + [table(shape, j) for shape in picked for j in range(count)],
            out_specs=[pl.BlockSpec(shape, lambda e, ids: (0, 0)) for shape in shapes],
            scratch_shapes=[
                pltpu.VMEM((E_DEV, D, 2 * FF), BF),
                pltpu.VMEM((E_DEV, FF, D), BF),
                pltpu.VMEM((count, 2, LANES, FF), BF),
                pltpu.VMEM((count, tokens, E_DEV * CAP), BF),
                pltpu.VMEM((E_DEV, height, D), BF),
                pltpu.VMEM((E_DEV, height, D), BF),
                pltpu.VMEM((E_DEV, height, LANES), F32),
                pltpu.VMEM((count, E_DEV * CAP, D), BF),
                pltpu.VMEM((count, E_DEV * CAP, EXT), BF),
                pltpu.VMEM((count, 2 * RANK, D), F32),
                pltpu.SemaphoreType.DMA((2, E_DEV)),
            ],
        ),
        out_shape=[jax.ShapeDtypeStruct(shape, BF) for shape in shapes],
        cost_estimate=pl.CostEstimate(
            flops=16 * count * E_DEV * CAP * D * FF,
            bytes_accessed=2 * E_DEV * 3 * D * FF + 8 * count * tokens * D,
            transcendentals=0,
        ),
        name="experts",
    )(
        jnp.concatenate([adapters, base[None]]).astype(jnp.int32),
        *rows,
        *packs,
        w_gate_up,
        w_down,
        *([aux_w] * count),
        *([gu_up] * count),
        *([down_a] * count),
        *([down_b] * count),
    )
    return list(outs[:count]), list(outs[count:])


def join_kernel(*refs):
    parts, out_ref = refs[:-1], refs[-1]
    for m, part in enumerate(parts):
        out_ref[m] = part[...]


def join(parts):
    return pl.pallas_call(
        join_kernel,
        in_specs=[VMEM_SPEC] * len(parts),
        out_specs=VMEM_SPEC,
        out_shape=jax.ShapeDtypeStruct((len(parts),) + parts[0].shape, parts[0].dtype),
        name="join",
    )(*parts)


def order_rows_kernel(order_ref, *refs):
    parts, out_ref = refs[:-1], refs[-1]
    rows = parts[0].shape[0]
    for m, part in enumerate(parts):
        out_ref[pl.ds(pl.multiple_of(order_ref[m] * rows, rows), rows), :] = part[:, LOCAL:]


def order_rows(order, parts):
    return pl.pallas_call(
        order_rows_kernel,
        in_specs=[SMEM_SPEC] + [VMEM_SPEC] * len(parts),
        out_specs=VMEM_SPEC,
        out_shape=jax.ShapeDtypeStruct((QW, QG), BF),
        name="order_rows",
    )(order, *parts)


def lanes_of(index):
    return pl.ds(pl.multiple_of(index * QG, LANES), QG)


def by_adapter(table):
    return pl.BlockSpec((1,) + table.shape[1:], lambda i, info: (info[0], 0, 0))


def out_kernel(info_ref, x_ref, gain_ref, down_ref, up_ref, *refs):
    o_refs, w_refs = refs[:GROUPS], refs[GROUPS : 2 * GROUPS]
    att_ref, rank_ref, y_ref, h_ref = refs[2 * GROUPS :]
    group = info_ref[1]
    for j in range(GROUPS):
        att_ref[:, lanes_of(group ^ j)] = o_refs[j][...]
    attended = att_ref[...]
    for j in range(GROUPS):
        y_ref[:, lanes_of(group ^ j)] = dot(attended, w_refs[j][...])
    rank_out = dot_nt(attended, down_ref[0]).astype(BF)
    rank_ref[...] = rank_out
    y_one = x_ref[...].astype(F32) + y_ref[...] + dot(rank_out, up_ref[0])
    y_ref[...] = y_one
    inverse = lax.rsqrt(jnp.mean(y_one * y_one, axis=1, keepdims=True) + NORM_EPS)
    h_ref[...] = (y_one * inverse * gain_ref[...]).astype(BF)


def project_out(info, rows, gain, down_t, up, outs, w_parts):
    tokens = rows.shape[0]
    return pl.pallas_call(
        out_kernel,
        grid_spec=pltpu.PrefetchScalarGridSpec(
            num_scalar_prefetch=1,
            grid=(1,),
            in_specs=[VMEM_SPEC] * 2
            + [by_adapter(down_t), by_adapter(up)]
            + [VMEM_SPEC] * (2 * GROUPS),
            out_specs=[VMEM_SPEC] * 4,
        ),
        out_shape=[
            jax.ShapeDtypeStruct((tokens, QW), BF),
            jax.ShapeDtypeStruct((tokens, RANK), BF),
            jax.ShapeDtypeStruct((tokens, D), F32),
            jax.ShapeDtypeStruct((tokens, D), BF),
        ],
        cost_estimate=pl.CostEstimate(
            flops=2 * tokens * QW * D, bytes_accessed=2 * QW * D + 12 * tokens * D, transcendentals=0
        ),
        name="project_out",
    )(info, rows, gain, down_t, up, *outs, *w_parts)


def middle_kernel(count, terms, info_ref, *refs):
    refs = list(refs)
    take = lambda n: [refs.pop(0) for _ in range(n)]
    d_refs = take(terms)
    pack_ref, y_ref, h_ref, gain_ref, aux_ref, att_ref, rank_ref, down_ref, up_ref = take(9)
    w_refs = take(GROUPS)
    (dy_ref,) = take(1)
    do_refs, early_refs = take(count), take(GROUPS)
    do_s, early_s = refs
    group, ctx_index, copies = info_ref[1], info_ref[2], count // GROUPS
    tokens = y_ref.shape[0]
    d_sum = d_refs[0][...].astype(F32)
    for ref in d_refs[1:]:
        d_sum = d_sum + ref[...].astype(F32)
    early_s[0 : 2 * RANK, :] = d_sum[tokens:, :D]
    d_ext = d_sum[:tokens, D:]
    h_two = h_ref[...]
    lane = lax.broadcasted_iota(jnp.int32, (tokens, LANES), 1)
    chosen = pack_ref[:, D:EXT].astype(F32) > 0.0
    picked = jnp.where(chosen, dot_nt(h_two, aux_ref[0]), NEG)
    weights = jnp.exp(picked - jnp.max(picked, axis=1, keepdims=True))
    gates = weights / jnp.sum(weights, axis=1, keepdims=True)
    mixed = jnp.sum(jnp.where(chosen, gates * d_ext, 0.0), axis=1, keepdims=True)
    d_logits = jnp.where(chosen, gates * (d_ext - mixed), 0.0)
    d_ext = jnp.where(lane < EXP_AT, d_ext, d_logits).astype(BF)
    d_h = d_sum[:tokens, :D] + dot(d_ext, aux_ref[0])
    y_one = y_ref[...]
    inverse = lax.rsqrt(jnp.mean(y_one * y_one, axis=1, keepdims=True) + NORM_EPS)
    scaled = gain_ref[...] * d_h
    d_y = pack_ref[:, :D].astype(F32) + inverse * scaled
    d_y = d_y - y_one * inverse**3 * jnp.mean(y_one * scaled, axis=1, keepdims=True)
    dy_ref[...] = d_y
    d_attn = d_y.astype(BF)
    d_rank = dot_nt(d_attn, up_ref[0]).astype(BF)
    do_s[...] = dot(d_rank, down_ref[0])
    for j in range(GROUPS):
        at = lanes_of(group ^ j)
        early_s[3 * RANK : 4 * RANK, at] = dot_tn(rank_ref[...], dy_ref[:, at].astype(BF))
        do_s[...] += dot_nt(dy_ref[:, at].astype(BF), w_refs[j][...])
    for m in range(count):
        do_refs[m][...] = do_s[:, lanes_of((ctx_index ^ m) // copies)].astype(BF)
    early_s[2 * RANK : 3 * RANK, :] = dot_tn(d_rank, att_ref[...])
    early_s[4 * RANK :, :] = dot_tn(d_ext, h_two)[: 2 * RANK]
    for j in range(GROUPS):
        for i in range(6):
            block = early_s[i * RANK : (i + 1) * RANK, lanes_of(group ^ j)]
            early_refs[j][:, i * QG : (i + 1) * QG] = block.astype(BF)


def middle_back(info, count, terms, pack, y_one, h_two, gain, aux, attended, rank_out, down_t, up, w_parts):
    tokens = y_one.shape[0]
    outs = pl.pallas_call(
        functools.partial(middle_kernel, count, len(terms)),
        grid_spec=pltpu.PrefetchScalarGridSpec(
            num_scalar_prefetch=1,
            grid=(1,),
            in_specs=[VMEM_SPEC] * (len(terms) + 4)
            + [by_adapter(aux)]
            + [VMEM_SPEC] * 2
            + [by_adapter(down_t), by_adapter(up)]
            + [VMEM_SPEC] * GROUPS,
            out_specs=[VMEM_SPEC] * (1 + count + GROUPS),
            scratch_shapes=[pltpu.VMEM((tokens, QW), F32), pltpu.VMEM((6 * RANK, D), F32)],
        ),
        out_shape=[jax.ShapeDtypeStruct((tokens, D), F32)]
        + [jax.ShapeDtypeStruct((tokens, QG), BF)] * count
        + [jax.ShapeDtypeStruct((RANK, 6 * QG), BF)] * GROUPS,
        cost_estimate=pl.CostEstimate(
            flops=2 * tokens * QW * D, bytes_accessed=2 * QW * D + 20 * tokens * D, transcendentals=0
        ),
        name="middle_back",
    )(info, *terms, pack, y_one, h_two, gain, aux, attended, rank_out, down_t, up, *w_parts)
    return outs[0], list(outs[1 : 1 + count]), list(outs[1 + count :])


def ranks_kernel(group_ref, dqkv_ref, up_ref, t_ref, h_ref, *refs):
    early_refs, (rank_ref, keep_ref, send_ref) = refs[:GROUPS], refs[GROUPS:]
    d_qkv = dqkv_ref[...]
    d_rank = dot_nt(d_qkv, up_ref[...]).astype(BF)
    rank_ref[...] = d_rank
    grad = dot_tn(t_ref[...], d_qkv)
    keep_ref[:, :QG] = grad[:RANK, :QG].astype(BF)
    keep_ref[:, QG : QG + KG] = grad[RANK : 2 * RANK, QG : QG + KG].astype(BF)
    keep_ref[:, QG + KG : LOCAL] = grad[2 * RANK :, QG + KG :].astype(BF)
    send_ref[:, :LOCAL] = jnp.zeros((RANK, LOCAL), BF)
    for j in range(GROUPS):
        target = send_ref if j % 2 else keep_ref
        down = dot_tn(d_rank, h_ref[:, lanes_of(group_ref[0] ^ j)]).astype(BF)
        first = LOCAL + (j // 2) * 3 * QG
        for i in range(3):
            target[:, first + i * QG : first + (i + 1) * QG] = down[i * RANK : (i + 1) * RANK]
        first = LOCAL + 6 * QG + (j // 2) * 6 * QG
        target[:, first : first + 6 * QG] = early_refs[j][...]


HALF = LOCAL + 18 * QG
BOTH = HALF + LOCAL


def ranks_back(group, d_qkv, up_diag, rank_qkv, h_one, early):
    length = d_qkv.shape[0]
    return pl.pallas_call(
        ranks_kernel,
        in_specs=[SMEM_SPEC] + [VMEM_SPEC] * (4 + GROUPS),
        out_specs=[VMEM_SPEC] * 3,
        out_shape=[
            jax.ShapeDtypeStruct((length, 3 * RANK), BF),
            jax.ShapeDtypeStruct((RANK, HALF), BF),
            jax.ShapeDtypeStruct((RANK, HALF), BF),
        ],
        name="ranks_back",
    )(group, d_qkv, up_diag, rank_qkv, h_one, *early)


def mix_kernel(near_ref, far_ref, out_ref):
    out_ref[:, :LOCAL] = near_ref[:, :LOCAL]
    out_ref[:, LOCAL : 2 * LOCAL] = far_ref[:, :LOCAL]
    first = LOCAL
    for width in (3 * QG, 6 * QG):
        for mine, theirs in ((0, width), (width, 0)):
            total = near_ref[:, first + mine : first + mine + width].astype(F32)
            total = total + far_ref[:, first + theirs : first + theirs + width].astype(F32)
            at = LOCAL + first + mine
            out_ref[:, at : at + width] = total.astype(BF)
        first += 2 * width


def mix(near, far):
    return pl.pallas_call(
        mix_kernel,
        in_specs=[VMEM_SPEC] * 2,
        out_specs=VMEM_SPEC,
        out_shape=jax.ShapeDtypeStruct((RANK, BOTH), BF),
        name="mix",
    )(near, far)


def inputs_kernel(dqkv_ref, rank_ref, w_ref, down_ref, *rows_refs):
    rows = dot_nt(dqkv_ref[...], w_ref[...]) + dot_nt(rank_ref[...], down_ref[...])
    rows = rows.astype(BF)
    for m, ref in enumerate(rows_refs):

        @pl.when(pl.program_id(0) == m)
        def _():
            ref[...] = rows


def inputs_back(count, d_qkv, d_rank, cols_all, down_sel):
    length = d_qkv.shape[0]
    tokens = length // count
    per_block = lambda width: pl.BlockSpec((tokens, width), lambda i: (i, 0))
    whole = lambda shape: pl.BlockSpec(shape, lambda i: (0, 0))
    return pl.pallas_call(
        inputs_kernel,
        grid=(count,),
        in_specs=[
            per_block(LOCAL),
            per_block(3 * RANK),
            whole((D, LOCAL)),
            whole((D, 3 * RANK)),
        ],
        out_specs=[whole((tokens, D))] * count,
        out_shape=[jax.ShapeDtypeStruct((tokens, D), BF)] * count,
        cost_estimate=pl.CostEstimate(
            flops=2 * length * D * LOCAL, bytes_accessed=4 * length * (D + LOCAL), transcendentals=0
        ),
        name="inputs_back",
    )(d_qkv, d_rank, cols_all, down_sel)


def place_kernel(ids_ref, *refs):
    parts = refs[:2]
    up_ref, down_ref, gu_ref, da_ref, db_ref, od_ref, ou_ref, gd_ref, sum_s = refs[2:]
    sources = parts[0].shape[0]
    up_ref[...] = jnp.zeros(up_ref.shape, F32)
    down_ref[...] = jnp.zeros(down_ref.shape, F32)
    sum_s[...] = jnp.zeros(sum_s.shape, F32)
    for j in range(GROUPS):
        group = ids_ref[sources] ^ j
        keys = lambda first: pl.ds(pl.multiple_of(first + group * KG, LANES), KG)
        far = j // 2
        down_at = 2 * LOCAL + far * 3 * QG
        early_at = 2 * LOCAL + 6 * QG + far * 6 * QG
        for m in range(sources):
            a = ids_ref[m]
            take = lambda first, width: parts[j % 2][m, :, first : first + width].astype(F32)
            up_ref[a, :, lanes_of(group)] += take(far * LOCAL, QG)
            up_ref[a, :, keys(QW)] += take(far * LOCAL + QG, KG)
            up_ref[a, :, keys(QW + KVW)] += take(far * LOCAL + QG + KG, KG)
            for i in range(3):
                at = slice(i * RANK, (i + 1) * RANK)
                down_ref[a, at, lanes_of(group)] += take(down_at + i * QG, QG)
            for i in range(6):
                at = slice(i * RANK, (i + 1) * RANK)
                sum_s[a, at, lanes_of(group)] += take(early_at + i * QG, QG)
    for a in range(ADAPT):
        gu_ref[a, 0] = sum_s[a, :RANK, :FF]
        gu_ref[a, 1] = sum_s[a, :RANK, FF : 2 * FF]
        da_ref[a] = sum_s[a, :RANK, 2 * FF :]
        db_ref[a] = sum_s[a, RANK : 2 * RANK]
        od_ref[a] = sum_s[a, 2 * RANK : 3 * RANK]
        ou_ref[a] = sum_s[a, 3 * RANK : 4 * RANK]
        gd_ref[a] = sum_s[a, 4 * RANK :]


def place_grads(ids, near, far):
    shapes = [(RANK, QW + 2 * KVW), (3 * RANK, D), (2, RANK, FF), (RANK, FF), (RANK, D)]
    shapes += [(RANK, QW), (RANK, D), (2 * RANK, D)]
    return pl.pallas_call(
        place_kernel,
        in_specs=[SMEM_SPEC] + [VMEM_SPEC] * 2,
        out_specs=[VMEM_SPEC] * len(shapes),
        out_shape=[jax.ShapeDtypeStruct((ADAPT,) + shape, F32) for shape in shapes],
        scratch_shapes=[pltpu.VMEM((ADAPT, 6 * RANK, D), F32)],
        name="place_grads",
    )(ids, near, far)


def norm_backward(values, inverse, gain_vec, upstream):
    scaled = gain_vec * upstream
    return inverse * scaled - values * inverse**3 * jnp.mean(
        values * scaled, axis=-1, keepdims=True
    )


def local_columns(table, group):
    lead = table.shape[:-1]
    cut = lambda first, width: lax.dynamic_slice_in_dim(
        table, first + group * width, width, table.ndim - 1
    )
    return cut(0, QG), cut(QW, KG), cut(QW + KVW, KG)


def on_device(
    inputs,
    cotangent,
    segment_ids,
    expert_ids,
    adapter_ids,
    gain_one,
    w_qkv,
    w_out,
    gain_two,
    router,
    w_gate_up,
    w_down,
    qkv_down,
    qkv_up,
    out_down,
    out_up,
    gu_down,
    gu_up,
    down_a,
    down_b,
):
    ctx_count = lax.axis_size("ctx")
    seq_count = lax.axis_size("seq")
    ctx_index = lax.axis_index("ctx")
    seq_index = lax.axis_index("seq")
    tokens = inputs.shape[1]
    length = tokens * ctx_count
    experts_all = router.shape[1]
    copies = ctx_count // GROUPS
    group = ctx_index // copies
    half = tokens // 2
    ctx_masks = doublings(ctx_count)[::-1]
    seq_slots = (seq_index ^ jnp.arange(seq_count)).astype(jnp.int32)
    ctx_slots = ctx_index ^ jnp.arange(ctx_count)
    own_rows = inputs[0]

    moving_rows = [swap(own_rows, "ctx", mask) for mask in ctx_masks]
    own_q, own_k, own_v = local_columns(w_qkv, group)
    own_out = lax.dynamic_slice_in_dim(w_out, group * QG, QG, 1)
    col_slots = []
    cols = Steps(
        gather_line(
            jnp.concatenate([own_q, own_k, own_v, own_out], axis=1), col_slots
        )
    )
    chosen = expert_ids[0]
    hot = jnp.any(chosen[:, :, None] == jnp.arange(experts_all)[None, None, :], axis=1)
    hot_low = hot.astype(BF)
    before = (jnp.arange(tokens)[:, None] >= jnp.arange(tokens)[None, :]).astype(BF)
    ranks = dot(before, hot_low).astype(BF) * hot_low
    ranks = jnp.pad(ranks, ((0, 0), (EXP_AT, LANES - EXP_AT - experts_all)))
    pack = jnp.concatenate([cotangent[0], ranks], axis=1)
    cols.beside()
    seg_row = segment_ids[0]
    position = jnp.arange(length)
    start = jnp.sum((seg_row[None, :] < seg_row[:, None]).astype(jnp.int32), axis=1)
    block_id = jnp.stack([ctx_slots, 2 * ctx_count - 1 - ctx_slots], axis=1).reshape(-1)
    block_of = jnp.arange(2 * ctx_count)
    owner = jnp.minimum(block_of, 2 * ctx_count - 1 - block_of)
    place = (2 * (owner ^ ctx_index) + (block_of >= ctx_count)).astype(jnp.int32)
    first = (start[::BLK] // BLK).astype(jnp.int32)
    offset = (position - start).reshape(2 * ctx_count, half)[block_id].reshape(-1)
    lane = jnp.arange(LANES) % HEAD_DIM
    frequency = 10000.0 ** (-2.0 * (lane % (HEAD_DIM // 2)).astype(F32) / HEAD_DIM)
    angles = offset.astype(F32)[:, None] * frequency[None, :]
    cosine = jnp.cos(angles)
    sine = jnp.sin(angles) * jnp.where(lane < HEAD_DIM // 2, -1.0, 1.0)[None, :]
    start_col = start[:, None]
    adapter = adapter_ids[seq_index]
    slot_adapters = adapter_ids[seq_slots]
    slots_and_group = jnp.concatenate([slot_adapters, group[None]]).astype(jnp.int32)
    group_info = group[None].astype(jnp.int32)
    info = jnp.stack([adapter, group, ctx_index]).astype(jnp.int32)

    def pick(table):
        return lax.dynamic_index_in_dim(table, adapter, 0, keepdims=False)

    qkv_down_sel = pick(qkv_down)
    out_down_t = jnp.swapaxes(out_down, 1, 2)
    aux_w = jnp.concatenate(
        [
            jnp.swapaxes(gu_down, 1, 2),
            jnp.broadcast_to(router.T[None], (ADAPT, experts_all, D)),
            jnp.zeros((ADAPT, LANES - 2 * RANK - experts_all, D), BF),
        ],
        axis=1,
    )
    down_a_t = jnp.swapaxes(down_a, 1, 2)

    pack, start_col, cosine, sine, place, first, *moving_rows = cols.beside(
        pack, start_col, cosine, sine, place, first, *moving_rows
    )
    row_slots = gather_rest(own_rows, moving_rows, ctx_masks)
    all_rows = jnp.concatenate(row_slots, axis=0).astype(F32)
    inv_all = lax.rsqrt(jnp.mean(all_rows * all_rows, axis=-1, keepdims=True) + NORM_EPS)
    h_one = (all_rows * inv_all * gain_one).astype(BF)
    rank_qkv = dot(h_one, qkv_down_sel).astype(BF)
    h_one, rank_qkv, pack = cols.beside(h_one, rank_qkv, pack)
    pack_slots = []
    packs = Steps(gather_line(pack, pack_slots))
    cols.finish()
    outs = Steps(gather_groups(order_rows(seq_slots, col_slots), copies))
    qkv, cols_all, up_diag = packs.beside(
        *project(
            seq_slots, adapter, group, h_one, rank_qkv, qkv_up, cosine, sine, col_slots
        )
    )
    heads_out, lse, *pieces = packs.beside(
        *outs.beside(*attend(place, first, qkv, start_col, copies))
    )
    heads_here = packs.beside(
        *[swap(piece, "ctx", j * copies) if j else piece for j, piece in enumerate(pieces)]
    )
    out_parts = outs.finish()
    attended, rank_out, y_one, h_two = project_out(
        info, own_rows, gain_two[None], out_down_t, out_up, heads_here, out_parts
    )

    def compute(m, rows):
        return experts(
            slot_adapters[m : m + len(rows)],
            E_DEV * seq_index,
            rows,
            pack_slots[m : m + len(rows)],
            w_gate_up,
            w_down,
            aux_w,
            gu_up,
            down_a_t,
            down_b,
        )

    y_sums, d_terms = exchange_experts(h_two, packs, compute)

    d_y_one, d_heads, early = middle_back(
        info,
        ctx_count,
        d_terms,
        pack,
        y_one,
        h_two,
        gain_two[None],
        aux_w,
        attended,
        rank_out,
        out_down_t,
        out_up,
        out_parts,
    )
    (d_y_one,) = y_sums.beside(d_y_one)
    d_heads = [swap(piece, "ctx", m) if m else piece for m, piece in enumerate(d_heads)]
    d_heads = y_sums.beside(*d_heads)

    (d_qkv,) = y_sums.beside(
        attend_back(place, first, qkv, start_col, heads_out, lse, cosine, sine, d_heads)
    )
    d_rank_qkv, keep, sent = ranks_back(group_info, d_qkv, up_diag, rank_qkv, h_one, early)

    halves = add_low(keep, swap(sent, "ctx", copies))
    for mask in doublings(copies):
        shared = halves[:, HALF - 12 * QG :]
        shared = add_low(shared, swap(shared, "ctx", mask))
        halves = jnp.concatenate([halves[:, : HALF - 12 * QG], shared], axis=1)
    halves, d_rank_qkv = lax.optimization_barrier((halves, d_rank_qkv))
    arrived, *d_rows = together(
        swap(halves, "ctx", 2 * copies),
        *inputs_back(ctx_count, d_qkv, d_rank_qkv, cols_all, qkv_down_sel),
    )
    d_rows = d_rows[::copies]
    near = add_low(d_rows[0], swap(d_rows[1], "ctx", copies))
    far = add_low(d_rows[2], swap(d_rows[3], "ctx", copies))
    slots = []
    grads = Steps(gather_line(mix(halves, arrived), slots))
    near, far = grads.join(y_sums, near, far)
    d_h_one = near.astype(F32) + swap(far, "ctx", 2 * copies).astype(F32)
    features = own_rows.astype(F32)
    inv_one = lax.rsqrt(jnp.mean(features * features, axis=-1, keepdims=True) + NORM_EPS)
    input_grad = d_y_one + norm_backward(features, inv_one, gain_one, d_h_one)
    layer_output = y_one
    for term in y_sums.finish():
        layer_output = layer_output + term.astype(F32)
    layer_output = layer_output.astype(BF)
    grads.beside()
    grads.beside()
    input_grad, layer_output = grads.beside(input_grad, layer_output)
    grads.finish()
    grads = join(slots)
    (
        grad_qkv_up,
        grad_qkv_down,
        grad_gu_up,
        grad_down_a,
        grad_down_b,
        grad_out_down,
        grad_out_up,
        grad_gu_down,
    ) = place_grads(slots_and_group, grads, swap(grads, "ctx", copies))

    return (
        layer_output[None],
        input_grad[None],
        jnp.swapaxes(grad_qkv_down, 1, 2),
        grad_qkv_up,
        jnp.swapaxes(grad_out_down, 1, 2),
        grad_out_up,
        jnp.swapaxes(grad_gu_down, 1, 2),
        grad_gu_up,
        jnp.swapaxes(grad_down_a, 1, 2),
        grad_down_b,
    )


def solution(mesh):
    over_seq = P("seq", None)
    placed = (
        P("seq", "ctx", None),
        P("seq", "ctx", None),
        over_seq,
        P("seq", "ctx", None),
        P(),
        P(),
        over_seq,
        over_seq,
        P(),
        P(),
        P("seq", None, None),
        P("seq", None, None),
    ) + (P(),) * 8
    return jax.shard_map(
        on_device,
        mesh=mesh,
        in_specs=placed,
        out_specs=(P("seq", "ctx", None), P("seq", "ctx", None)) + (P(),) * 8,
        check_vma=False,
    )
```

time: 546 us -> 488 us (0.89)
  waiting for transfers between devices: 213 us -> 156 us
  Pallas kernels: 154 us -> 165 us
    ppermute x53 -> x48, waiting for transfers between devices: 149 us -> 114 us  [swap(): return lax.ppermute(block, axis, [(i, i ^ mask) for i in range(count)])]
    ppermute x24, waiting for transfers between devices: 63.2 us -> 42.2 us  [line_swap(): lax.ppermute(block, 'seq', [(2 * i + j, 2 * k + j) for i, k in pairs for...]
    pallas_call x4 -> x5, Pallas kernels: 70.3 us -> 76.2 us  [experts(): pl.pallas_call(body, grid_spec=pltpu.PrefetchScalarGridSpec(num_scalar_pr...]
    ppermute x53 -> x48, starting transfers between devices: 57.4 us -> 52.5 us  [swap(): return lax.ppermute(block, axis, [(i, i ^ mask) for i in range(count)])]
    pallas_call x3 -> x5, Pallas kernels: 29.9 us -> 33.8 us  [the longest x1 12 us: middle_back(): pl.pallas_call(functools.partial(middle_kernel, count, len(terms)), grid_...]
  transfers between devices with their start and end apart: 77 -> 72, of which waited for: 31 -> 30; matrix products, arithmetic and copies ran while one was open for 11% -> 10% of each run, Pallas kernels for 27% -> 31%
where the time goes in v3:
time: 488 us; the launch traced here: 479 us
  Pallas kernels  165 us (34%)
  waiting for transfers between devices  156 us (32%)
  starting transfers between devices  93.9 us (19%)
  other arithmetic  43 us (9%)
  local copies, waits for them, and re-layouts  15.3 us (3%)
    ppermute x48, waiting for transfers between devices, swap(): return lax.ppermute(block, axis, [(i, i ^ mask) for i in range(count)])  114 us
    pallas_call x5, Pallas kernels, experts(): pl.pallas_call(body, grid_spec=pltpu.PrefetchScalarGridSpec(num_scalar_pr...  76.2 us
    ppermute x48, starting transfers between devices, swap(): return lax.ppermute(block, axis, [(i, i ^ mask) for i in range(count)])  52.5 us
    ppermute x24, waiting for transfers between devices, line_swap(): lax.ppermute(block, 'seq', [(2 * i + j, 2 * k + j) for i, k in pairs for...  42.2 us
    ppermute x24, starting transfers between devices, line_swap(): lax.ppermute(block, 'seq', [(2 * i + j, 2 * k + j) for i, k in pairs for...  41.5 us
    pallas_call x1, Pallas kernels, attend_back(): pl.pallas_call(attend_back_kernel, in_specs=[SMEM_SPEC, SMEM_SPEC] + [VME...  20.3 us
    pallas_call x1, Pallas kernels, attend(): pl.pallas_call(functools.partial(attend_kernel, copies), in_specs=[SMEM_S...  13 us
    pallas_call x1, Pallas kernels, middle_back(): pl.pallas_call(functools.partial(middle_kernel, count, len(terms)), grid_...  12 us
  transfers between devices with their start and end apart: 72, of which 30 were waited for; matrix products, arithmetic and copies ran while one was open for 10% of the time, Pallas kernels for 31%

profile of v3, /device:TPU:0, one launch (start us, length us, event | category | flops | bytes accessed | tf_op | source)
XLA Modules:
  0.0 479.1 jit_solution(12602166396265030763)
XLA Ops:
  25.8 8.3 %collective-permute-done.4 = bf16[192,1024]{1,0:T(8,128)(2,1)} collective-permute-done((bf16[192,1024]{1,0:T(8,128)(2,1)}, bf16[192,1024]{1,0:T(8,128)(2,1)}, u32[]{:S(2)}, u32[]{:S(2)}) %collective-permute-start.4) | collective-permute-done | bytes 393248 | tf_op jit(solution)/shard_map/ppermute | solution.py:79
  59.2 6.1 %collective-permute-done.14.rest_7_.refs_7_ = bf16[192,1024]{1,0:T(8,128)(2,1)S(1)} collective-permute-done((bf16[192,1024]{1,0:T(8,128)(2,1)S(1)}, bf16[192,1024]{1,0:T(8,128)(2,1)S(1)}, u32[]{:S(2)}, u32[]{:S(2)}) %collective-permute-start.14) | collective-permute-done | bytes 393248 | tf_op jit(solution)/shard_map/ppermute | solution.py:55
  71.7 8.9 %project.1 = (bf16[1024,640]{1,0:T(8,128)(2,1)}, bf16[1536,640]{1,0:T(8,128)(2,1)}, bf16[48,640]{1,0:T(8,128)(2,1)}) custom-call(s32[10]{0:T(128)} %pad_add_fusion.2.info_ref, bf16[1024,1536]{1,0:T(8,128)(2,1)} %copy-done.3, bf16[1024,48]{1,0:T(8,128)(2,1)} %convolution_convert_fusion.t_ref, bf16[8,16,2560]{2,1,0:T(8,128)(2,1)} %table_ref.1, ...), custom_call_target="tpu_custom_call" | custom-call | flops 2013265920 | bytes 4456448 | tf_op jit(solution)/shard_map/project/pallas_call | solution.py:274
  85.9 13.0 %attend.1 = (bf16[1024,384]{1,0:T(8,128)(2,1)}, f32[3072,128]{1,0:T(8,128)}, bf16[256,384]{1,0:T(8,128)(2,1)}, bf16[256,384]{1,0:T(8,128)(2,1)}, bf16[256,384]{1,0:T(8,128)(2,1)}, /*index=5*/bf16[256,384]{1,0:T(8,128)(2,1)}) custom-call(s32[8]{0:T(128)} %fusion.16.place_ref, s32[4]{0:T(128)} %and_select_fusion.first_ref, ...), custom_call_target="tpu_custom_call" | custom-call | flops 1610612736 | bytes 3145728 | tf_op jit(solution)/shard_map/attend/pallas_call | solution.py:441
  99.0 7.8 %collective-permute-done.16 = bf16[256,1664]{1,0:T(8,128)(2,1)} collective-permute-done((bf16[256,1664]{1,0:T(8,128)(2,1)}, bf16[256,1664]{1,0:T(8,128)(2,1)}, u32[]{:S(2)}, u32[]{:S(2)}) %collective-permute-start.16) | collective-permute-done | bytes 852000 | tf_op jit(solution)/shard_map/ppermute | solution.py:79
  133.7 7.9 %project_out.1 = (bf16[256,1536]{1,0:T(8,128)(2,1)}, bf16[256,16]{1,0:T(8,128)(2,1)}, f32[256,1536]{1,0:T(8,128)}, bf16[256,1536]{1,0:T(8,128)(2,1)}) custom-call(s32[3]{0:T(128)} %pad_add_fusion.1.info_ref, bf16[256,1536]{1,0:T(8,128)(2,1)} %bitcast.37, f32[1,1536]{1,0:T(1,128)} %broadcast_in_dim.25.gain_ref.refs_7_, bf16[8,16,1536]{2,1,0:T(8,128)(2,1)} %bitcast.41, ...), custom_call_target="tpu_custom_call" | custom-call | flops 1207959552 | bytes 9437184 | tf_op jit(solution)/shard_map/project_out/pallas_call | solution.py:805
  149.0 13.7 %experts.5 = (bf16[256,1536]{1,0:T(8,128)(2,1)}, bf16[288,1664]{1,0:T(8,128)(2,1)}) custom-call(s32[2]{0:T(128)} %pad_add_fusion.3.ids_ref, bf16[256,1536]{1,0:T(8,128)(2,1)} %get-tuple-element.237.refs_0_.refs_6_, bf16[256,1664]{1,0:T(8,128)(2,1)} %copy-done.6, bf16[2,1536,1024]{2,1,0:T(8,128)(2,1)} %refs_2_.3, bf16[2,512,1536]{2,1,0:T(8,128)(2,1)} %refs_3_.3, ...), custom_call_target="tpu_custom_call" | custom-call | flops 3221225472 | bytes 12582912 | tf_op jit(solution)/shard_map/experts/pallas_call | solution.py:700
  171.2 16.3 %experts.6 = (bf16[256,1536]{1,0:T(8,128)(2,1)}, bf16[256,1536]{1,0:T(8,128)(2,1)}, bf16[288,1664]{1,0:T(8,128)(2,1)}, bf16[288,1664]{1,0:T(8,128)(2,1)}) custom-call(s32[3]{0:T(128)} %get-tuple-element.383.ids_ref, bf16[256,1536]{1,0:T(8,128)(2,1)} %copy-done.56, bf16[256,1536]{1,0:T(8,128)(2,1)} %collective-permute-done.26.refs_1_, ...), custom_call_target="tpu_custom_call" | custom-call | flops 6442450944 | bytes 15728640 | tf_op jit(solution)/shard_map/experts/pallas_call | solution.py:700
  191.8 16.1 %experts.7 = (bf16[256,1536]{1,0:T(8,128)(2,1)}, bf16[256,1536]{1,0:T(8,128)(2,1)}, bf16[288,1664]{1,0:T(8,128)(2,1)}, bf16[288,1664]{1,0:T(8,128)(2,1)}) custom-call(s32[3]{0:T(128)} %get-tuple-element.384.ids_ref, bf16[256,1536]{1,0:T(8,128)(2,1)} %copy-done.55, bf16[256,1536]{1,0:T(8,128)(2,1)} %copy-done.37, ...), custom_call_target="tpu_custom_call" | custom-call | flops 6442450944 | bytes 15728640 | tf_op jit(solution)/shard_map/experts/pallas_call | solution.py:700
  213.8 16.1 %experts.8 = (bf16[256,1536]{1,0:T(8,128)(2,1)}, bf16[256,1536]{1,0:T(8,128)(2,1)}, bf16[288,1664]{1,0:T(8,128)(2,1)}, bf16[288,1664]{1,0:T(8,128)(2,1)}) custom-call(s32[3]{0:T(128)} %pad_add_fusion.6.ids_ref, bf16[256,1536]{1,0:T(8,128)(2,1)} %copy-done.57, bf16[256,1536]{1,0:T(8,128)(2,1)} %add.208.refs_1_, ...), custom_call_target="tpu_custom_call" | custom-call | flops 6442450944 | bytes 15728640 | tf_op jit(solution)/shard_map/experts/pallas_call | solution.py:700
  231.5 13.9 %experts.9 = (bf16[256,1536]{1,0:T(8,128)(2,1)}, bf16[288,1664]{1,0:T(8,128)(2,1)}) custom-call(s32[2]{0:T(128)} %pad_add_fusion.7.ids_ref, bf16[256,1536]{1,0:T(8,128)(2,1)} %copy-done.29, bf16[256,1664]{1,0:T(8,128)(2,1)} %collective-permute-done.29.refs_1_, bf16[2,1536,1024]{2,1,0:T(8,128)(2,1)} %refs_2_.3, bf16[2,512,1536]{2,1,0:T(8,128)(2,1)} %refs_3_.3, ...), custom_call_target="tpu_custom_call" | custom-call | flops 3221225472 | bytes 12582912 | tf_op jit(solution)/shard_map/experts/pallas_call | solution.py:700
  250.2 22.4 %collective-permute-done.37 = bf16[288,1664]{1,0:T(8,128)(2,1)S(1)} collective-permute-done((bf16[288,1664]{1,0:T(8,128)(2,1)}, bf16[288,1664]{1,0:T(8,128)(2,1)S(1)}, u32[]{:S(2)}, u32[]{:S(2)}) %collective-permute-start.37) | collective-permute-done | bytes 958496 | tf_op jit(solution)/shard_map/ppermute | solution.py:55
  272.8 6.2 %collective-permute-start.38 = (bf16[288,1664]{1,0:T(8,128)(2,1)S(1)}, bf16[288,1664]{1,0:T(8,128)(2,1)S(1)}, u32[]{:S(2)}, u32[]{:S(2)}) collective-permute-start(bf16[288,1664]{1,0:T(8,128)(2,1)S(1)} %add_convert_fusion.3), channel_id=1, source_target_pairs={{0,8},{4,12},{24,16},{28,20},{1,9},{5,13},{25,17},{29,21},{2,10},{... | collective-permute-start | bytes 2875400 | tf_op jit(solution)/shard_map/ppermute | solution.py:79
  279.7 13.4 %collective-permute-done.39 = bf16[288,1664]{1,0:T(8,128)(2,1)S(1)} collective-permute-done((bf16[288,1664]{1,0:T(8,128)(2,1)}, bf16[288,1664]{1,0:T(8,128)(2,1)S(1)}, u32[]{:S(2)}, u32[]{:S(2)}) %collective-permute-start.39) | collective-permute-done | bytes 958496 | tf_op jit(solution)/shard_map/ppermute | solution.py:55
  294.1 5.8 %collective-permute-start.40 = (bf16[288,1664]{1,0:T(8,128)(2,1)S(1)}, bf16[288,1664]{1,0:T(8,128)(2,1)S(1)}, u32[]{:S(2)}, u32[]{:S(2)}) collective-permute-start(bf16[288,1664]{1,0:T(8,128)(2,1)S(1)} %add_convert_fusion.2), channel_id=1, source_target_pairs={{0,8},{4,12},{24,16},{28,20},{1,9},{5,13},{25,17},{29,21},{2,10},{... | collective-permute-start | bytes 2875400 | tf_op jit(solution)/shard_map/ppermute | solution.py:79
  300.6 6.8 %collective-permute-done.42 = bf16[288,1664]{1,0:T(8,128)(2,1)S(1)} collective-permute-done((bf16[288,1664]{1,0:T(8,128)(2,1)S(1)}, bf16[288,1664]{1,0:T(8,128)(2,1)S(1)}, u32[]{:S(2)}, u32[]{:S(2)}) %collective-permute-start.42) | collective-permute-done | bytes 958496 | tf_op jit(solution)/shard_map/ppermute | solution.py:55
  307.4 6.2 %collective-permute-done.40 = bf16[288,1664]{1,0:T(8,128)(2,1)S(1)} collective-permute-done((bf16[288,1664]{1,0:T(8,128)(2,1)S(1)}, bf16[288,1664]{1,0:T(8,128)(2,1)S(1)}, u32[]{:S(2)}, u32[]{:S(2)}) %collective-permute-start.40) | collective-permute-done | bytes 958496 | tf_op jit(solution)/shard_map/ppermute | solution.py:79
  314.9 9.2 %collective-permute-start.44 = (bf16[288,1664]{1,0:T(8,128)(2,1)S(1)}, bf16[288,1664]{1,0:T(8,128)(2,1)S(1)}, u32[]{:S(2)}, u32[]{:S(2)}) collective-permute-start(bf16[288,1664]{1,0:T(8,128)(2,1)S(1)} %add_convert_fusion.1), channel_id=1, source_target_pairs={{0,8},{4,12},{8,0},{12,4},{16,24},{20,28},{24,16},{28,20},{1,9},{5... | collective-permute-start | bytes 2875400 | tf_op jit(solution)/shard_map/ppermute | solution.py:55
  326.2 9.8 %collective-permute-done.44.refs_1_ = bf16[288,1664]{1,0:T(8,128)(2,1)S(1)} collective-permute-done((bf16[288,1664]{1,0:T(8,128)(2,1)S(1)}, bf16[288,1664]{1,0:T(8,128)(2,1)S(1)}, u32[]{:S(2)}, u32[]{:S(2)}) %collective-permute-start.44) | collective-permute-done | bytes 958496 | tf_op jit(solution)/shard_map/ppermute | solution.py:55
  336.9 12.0 %middle_back.1 = (f32[256,1536]{1,0:T(8,128)}, bf16[256,384]{1,0:T(8,128)(2,1)}, bf16[256,384]{1,0:T(8,128)(2,1)}, bf16[256,384]{1,0:T(8,128)(2,1)}, bf16[256,38...) custom-call(s32[3]{0:T(128)} %pad_add_fusion.1.info_ref, ...), custom_call_target="tpu_custom_call" | custom-call | flops 1207959552 | bytes 12582912 | tf_op jit(solution)/shard_map/middle_back/pallas_call | solution.py:879
  371.3 20.3 %attend_back.1.dqkv_ref = bf16[1024,640]{1,0:T(8,128)(2,1)} custom-call(s32[8]{0:T(128)} %fusion.16.place_ref, s32[4]{0:T(128)} %and_select_fusion.first_ref, bf16[1024,640]{1,0:T(8,128)(2,1)} %get-tuple-element.211.qkv_ref, s32[1024,1]{1,0:T(8,128)} %copy.44.start_ref, bf16[1024,384]{1,0:T(8,128)(2,1)} %get-tuple-element.308.o_ref, ...), custom_call_target="tpu_custom_call" | custom-call | flops 4026531840 | bytes 6291456 | tf_op jit(solution)/shard_map/attend_back/pallas_call | solution.py:547
  399.8 7.7 %inputs_back.1 = (bf16[256,1536]{1,0:T(8,128)(2,1)}, bf16[256,1536]{1,0:T(8,128)(2,1)}, bf16[256,1536]{1,0:T(8,128)(2,1)}, bf16[256,1536]{1,0:T(8,128)(2,1)}) custom-call(bf16[1024,640]{1,0:T(8,128)(2,1)} %attend_back.1.dqkv_ref, bf16[1024,48]{1,0:T(8,128)(2,1)} %get-tuple-element.324.rank_ref, bf16[1536,640]{1,0:T(8,128)(2,1)} %get-tuple-element.325.w_ref, ...), custom_call_target="tpu_custom_call" | custom-call | flops 2013265920 | bytes 8912896 | tf_op jit(solution)/shard_map/inputs_back/pallas_call | solution.py:980
  422.0 14.4 %collective-permute-done.56.refs_2_ = bf16[16,8192]{1,0:T(8,128)(2,1)S(1)} collective-permute-done((bf16[16,8192]{1,0:T(8,128)(2,1)}, bf16[16,8192]{1,0:T(8,128)(2,1)S(1)}, u32[]{:S(2)}, u32[]{:S(2)}) %collective-permute-start.56) | collective-permute-done | bytes 262176 | tf_op jit(solution)/shard_map/ppermute | solution.py:55
  472.2 6.4 %place_grads.1 = (f32[8,16,2560]{2,1,0:T(8,128)}, f32[8,48,1536]{2,1,0:T(8,128)}, f32[8,2,16,512]{3,2,1,0:T(8,128)}, f32[8,16,512]{2,1,0:T(8,128)}, f32[8,16,153...) custom-call(s32[9]{0:T(128)} %pad_add_fusion.8.ids_ref, ...), custom_call_target="tpu_custom_call" | custom-call | tf_op jit(solution)/shard_map/place_grads/pallas_call | solution.py:1036
  (335 shorter events, 206.2 us)
Async XLA Ops:
  8.8 25.3 %collective-permute-start.6 = (bf16[256,1536]{1,0:T(8,128)(2,1)}, bf16[256,1536]{1,0:T(8,128)(2,1)}, u32[]{:S(2)}, u32[]{:S(2)}) collective-permute-start(bf16[256,1536]{1,0:T(8,128)(2,1)} %bitcast.35), channel_id=1, source_target_pairs={{0,2},{1,3},{2,0},{3,1},{4,6},{5,7},{6,4},{7,5},{8,10},{9,11},{10,... | collective-permute-start | bytes 2359304 | tf_op jit(solution)/shard_map/ppermute | solution.py:55
  10.3 23.8 %collective-permute-start.7 = (bf16[256,1536]{1,0:T(8,128)(2,1)}, bf16[256,1536]{1,0:T(8,128)(2,1)}, u32[]{:S(2)}, u32[]{:S(2)}) collective-permute-start(bf16[256,1536]{1,0:T(8,128)(2,1)} %bitcast.36), channel_id=1, source_target_pairs={{0,1},{1,0},{2,3},{3,2},{4,5},{5,4},{6,7},{7,6},{8,9},{9,8},{10,11... | collective-permute-start | bytes 2359304 | tf_op jit(solution)/shard_map/ppermute | solution.py:55
  53.7 26.9 %collective-permute-start.11 = (bf16[256,1664]{1,0:T(8,128)(2,1)S(1)}, bf16[256,1664]{1,0:T(8,128)(2,1)}, u32[]{:S(2)}, u32[]{:S(2)}) collective-permute-start(bf16[256,1664]{1,0:T(8,128)(2,1)S(1)} %fusion.10.refs_1_.refs_4_), channel_id=1, source_target_pairs={{0,8},{4,12},{8,0},{12,4},{16,24},{20,28},{24,16},{28,20},{1,9},{5... | collective-permute-start | bytes 2555912 | tf_op jit(solution)/shard_map/ppermute | solution.py:55
  55.6 25.1 %collective-permute-start.12 = (bf16[256,1664]{1,0:T(8,128)(2,1)S(1)}, bf16[256,1664]{1,0:T(8,128)(2,1)}, u32[]{:S(2)}, u32[]{:S(2)}) collective-permute-start(bf16[256,1664]{1,0:T(8,128)(2,1)S(1)} %fusion.10.refs_1_.refs_4_), channel_id=1, source_target_pairs={{8,16},{12,20},{16,8},{20,12},{9,17},{13,21},{17,9},{21,13},{10,18... | collective-permute-start | bytes 2555912 | tf_op jit(solution)/shard_map/ppermute | solution.py:79
  57.1 25.1 %collective-permute-start.13 = (bf16[256,1664]{1,0:T(8,128)(2,1)S(1)}, bf16[256,1664]{1,0:T(8,128)(2,1)}, u32[]{:S(2)}, u32[]{:S(2)}) collective-permute-start(bf16[256,1664]{1,0:T(8,128)(2,1)S(1)} %fusion.10.refs_1_.refs_4_), channel_id=1, source_target_pairs={{0,4},{4,0},{8,12},{12,8},{16,20},{20,16},{24,28},{28,24},{1,5},{5... | collective-permute-start | bytes 2555912 | tf_op jit(solution)/shard_map/ppermute | solution.py:55
  68.9 30.0 %collective-permute-start.18 = (bf16[1536,384]{1,0:T(8,128)(2,1)}, bf16[1536,384]{1,0:T(8,128)(2,1)S(1)}, u32[]{:S(2)}, u32[]{:S(2)}) collective-permute-start(bf16[1536,384]{1,0:T(8,128)(2,1)} %order_rows.1.refs_4_.refs_13_), channel_id=1, source_target_pairs={{0,2},{1,3},{2,0},{3,1},{4,6},{5,7},{6,4},{7,5},{8,10},{9,11},{10,... | collective-permute-start | bytes 3538952 | tf_op jit(solution)/shard_map/ppermute | solution.py:55
  70.4 28.5 %collective-permute-start.19 = (bf16[1536,384]{1,0:T(8,128)(2,1)}, bf16[1536,384]{1,0:T(8,128)(2,1)}, u32[]{:S(2)}, u32[]{:S(2)}) collective-permute-start(bf16[1536,384]{1,0:T(8,128)(2,1)} %order_rows.1.refs_4_.refs_13_), channel_id=1, source_target_pairs={{0,1},{1,0},{2,3},{3,2},{4,5},{5,4},{6,7},{7,6},{8,9},{9,8},{10,11... | collective-permute-start | bytes 3538952 | tf_op jit(solution)/shard_map/ppermute | solution.py:55
  83.0 23.8 %collective-permute-start.16 = (bf16[256,1664]{1,0:T(8,128)(2,1)}, bf16[256,1664]{1,0:T(8,128)(2,1)}, u32[]{:S(2)}, u32[]{:S(2)}) collective-permute-start(bf16[256,1664]{1,0:T(8,128)(2,1)} %collective-permute-done.12), channel_id=1, source_target_pairs={{8,0},{12,4},{16,24},{20,28},{9,1},{13,5},{17,25},{21,29},{10,2},{... | collective-permute-start | bytes 2555912 | tf_op jit(solution)/shard_map/ppermute | solution.py:79
  84.3 22.5 %collective-permute-start.17 = (bf16[256,1664]{1,0:T(8,128)(2,1)}, bf16[256,1664]{1,0:T(8,128)(2,1)}, u32[]{:S(2)}, u32[]{:S(2)}) collective-permute-start(bf16[256,1664]{1,0:T(8,128)(2,1)} %collective-permute-done.11.refs_3_), channel_id=1, source_target_pairs={{0,4},{4,0},{8,12},{12,8},{16,20},{20,16},{24,28},{28,24},{1,5},{5... | collective-permute-start | bytes 2555912 | tf_op jit(solution)/shard_map/ppermute | solution.py:55
  98.9 33.8 %collective-permute-start.25 = (bf16[1536,384]{1,0:T(8,128)(2,1)S(1)}, bf16[1536,384]{1,0:T(8,128)(2,1)S(1)}, u32[]{:S(2)}, u32[]{:S(2)}) collective-permute-start(bf16[1536,384]{1,0:T(8,128)(2,1)S(1)} %collective-permute-done.18.refs_6_.refs_15_), channel_id=1, source_target_pairs={{0,1},{1,0},{2,3},{3,2},{4,5},{5,4},{6,7},{7,6},{8,9},{9,8},{10,11... | collective-permute-start | bytes 3538952 | tf_op jit(solution)/shard_map/ppermute | solution.py:55
  132.1 30.6 %collective-permute-start.29 = (bf16[256,1664]{1,0:T(8,128)(2,1)}, bf16[256,1664]{1,0:T(8,128)(2,1)}, u32[]{:S(2)}, u32[]{:S(2)}) collective-permute-start(bf16[256,1664]{1,0:T(8,128)(2,1)} %add.205.refs_3_), channel_id=1, source_target_pairs={{0,4},{4,0},{8,12},{12,8},{16,20},{20,16},{24,28},{28,24},{1,5},{5... | collective-permute-start | bytes 2555912 | tf_op jit(solution)/shard_map/ppermute | solution.py:55
  141.6 21.1 %collective-permute-start.26 = (bf16[256,1536]{1,0:T(8,128)(2,1)}, bf16[256,1536]{1,0:T(8,128)(2,1)}, u32[]{:S(2)}, u32[]{:S(2)}) collective-permute-start(bf16[256,1536]{1,0:T(8,128)(2,1)} %get-tuple-element.237.refs_0_.refs_6_), channel_id=1, source_target_pairs={{0,8},{4,12},{8,0},{12,4},{16,24},{20,28},{24,16},{28,20},{1,9},{5... | collective-permute-start | bytes 2359304 | tf_op jit(solution)/shard_map/ppermute | solution.py:55
  145.2 22.2 %collective-permute-start.28 = (bf16[256,1536]{1,0:T(8,128)(2,1)}, bf16[256,1536]{1,0:T(8,128)(2,1)S(1)}, u32[]{:S(2)}, u32[]{:S(2)}) collective-permute-start(bf16[256,1536]{1,0:T(8,128)(2,1)} %get-tuple-element.237.refs_0_.refs_6_), channel_id=1, source_target_pairs={{0,4},{4,0},{8,12},{12,8},{16,20},{20,16},{24,28},{28,24},{1,5},{5... | collective-permute-start | bytes 2359304 | tf_op jit(solution)/shard_map/ppermute | solution.py:55
  211.9 36.3 %collective-permute-start.36 = (bf16[288,1664]{1,0:T(8,128)(2,1)}, bf16[288,1664]{1,0:T(8,128)(2,1)S(1)}, u32[]{:S(2)}, u32[]{:S(2)}) collective-permute-start(bf16[288,1664]{1,0:T(8,128)(2,1)} %get-tuple-element.270), channel_id=1, source_target_pairs={{0,4},{4,0},{8,12},{12,8},{16,20},{20,16},{24,28},{28,24},{1,5},{5... | collective-permute-start | bytes 2875400 | tf_op jit(solution)/shard_map/ppermute | solution.py:55
  248.2 24.4 %collective-permute-start.37 = (bf16[288,1664]{1,0:T(8,128)(2,1)}, bf16[288,1664]{1,0:T(8,128)(2,1)S(1)}, u32[]{:S(2)}, u32[]{:S(2)}) collective-permute-start(bf16[288,1664]{1,0:T(8,128)(2,1)} %get-tuple-element.271), channel_id=1, source_target_pairs={{0,4},{4,0},{8,12},{12,8},{16,20},{20,16},{24,28},{28,24},{1,5},{5... | collective-permute-start | bytes 2875400 | tf_op jit(solution)/shard_map/ppermute | solution.py:55
  249.2 43.9 %collective-permute-start.39 = (bf16[288,1664]{1,0:T(8,128)(2,1)}, bf16[288,1664]{1,0:T(8,128)(2,1)S(1)}, u32[]{:S(2)}, u32[]{:S(2)}) collective-permute-start(bf16[288,1664]{1,0:T(8,128)(2,1)} %get-tuple-element.272), channel_id=1, source_target_pairs={{0,4},{4,0},{8,12},{12,8},{16,20},{20,16},{24,28},{28,24},{1,5},{5... | collective-permute-start | bytes 2875400 | tf_op jit(solution)/shard_map/ppermute | solution.py:55
  279.1 28.3 %collective-permute-start.42 = (bf16[288,1664]{1,0:T(8,128)(2,1)S(1)}, bf16[288,1664]{1,0:T(8,128)(2,1)S(1)}, u32[]{:S(2)}, u32[]{:S(2)}) collective-permute-start(bf16[288,1664]{1,0:T(8,128)(2,1)S(1)} %copy-done.54), channel_id=1, source_target_pairs={{0,4},{4,0},{8,12},{12,8},{16,20},{20,16},{24,28},{28,24},{1,5},{5... | collective-permute-start | bytes 2875400 | tf_op jit(solution)/shard_map/ppermute | solution.py:55
  324.1 24.8 %collective-permute-start.43 = (bf16[256,1536]{1,0:T(8,128)(2,1)}, bf16[256,1536]{1,0:T(8,128)(2,1)}, u32[]{:S(2)}, u32[]{:S(2)}) collective-permute-start(bf16[256,1536]{1,0:T(8,128)(2,1)} %get-tuple-element.286), channel_id=1, source_target_pairs={{0,4},{4,0},{8,12},{12,8},{16,20},{20,16},{24,28},{28,24},{1,5},{5... | collective-permute-start | bytes 2359304 | tf_op jit(solution)/shard_map/ppermute | solution.py:55
  324.6 31.7 %collective-permute-start.47 = (bf16[256,1536]{1,0:T(8,128)(2,1)}, bf16[256,1536]{1,0:T(8,128)(2,1)}, u32[]{:S(2)}, u32[]{:S(2)}) collective-permute-start(bf16[256,1536]{1,0:T(8,128)(2,1)} %get-tuple-element.300), channel_id=1, source_target_pairs={{0,4},{4,0},{8,12},{12,8},{16,20},{20,16},{24,28},{28,24},{1,5},{5... | collective-permute-start | bytes 2359304 | tf_op jit(solution)/shard_map/ppermute | solution.py:55
  356.3 35.2 %collective-permute-start.53 = (bf16[256,1536]{1,0:T(8,128)(2,1)}, bf16[256,1536]{1,0:T(8,128)(2,1)S(1)}, u32[]{:S(2)}, u32[]{:S(2)}) collective-permute-start(bf16[256,1536]{1,0:T(8,128)(2,1)} %get-tuple-element.307), channel_id=1, source_target_pairs={{0,4},{4,0},{8,12},{12,8},{16,20},{20,16},{24,28},{28,24},{1,5},{5... | collective-permute-start | bytes 2359304 | tf_op jit(solution)/shard_map/ppermute | solution.py:55
  367.9 23.6 %collective-permute-start.51 = (bf16[256,1536]{1,0:T(8,128)(2,1)}, bf16[256,1536]{1,0:T(8,128)(2,1)S(1)}, u32[]{:S(2)}, u32[]{:S(2)}) collective-permute-start(bf16[256,1536]{1,0:T(8,128)(2,1)} %add_convert_fusion.9), channel_id=1, source_target_pairs={{0,8},{4,12},{24,16},{28,20},{1,9},{5,13},{25,17},{29,21},{2,10},{... | collective-permute-start | bytes 2359304 | tf_op jit(solution)/shard_map/ppermute | solution.py:79
  408.8 27.7 %collective-permute-start.60 = (bf16[256,1536]{1,0:T(8,128)(2,1)}, bf16[256,1536]{1,0:T(8,128)(2,1)}, u32[]{:S(2)}, u32[]{:S(2)}) collective-permute-start(bf16[256,1536]{1,0:T(8,128)(2,1)} %add_convert_fusion.7), channel_id=1, source_target_pairs={{8,16},{12,20},{16,8},{20,12},{9,17},{13,21},{17,9},{21,13},{10,18... | collective-permute-start | bytes 2359304 | tf_op jit(solution)/shard_map/ppermute | solution.py:79
  411.1 25.3 %collective-permute-start.59 = (bf16[256,1536]{1,0:T(8,128)(2,1)S(1)}, bf16[256,1536]{1,0:T(8,128)(2,1)}, u32[]{:S(2)}, u32[]{:S(2)}) collective-permute-start(bf16[256,1536]{1,0:T(8,128)(2,1)S(1)} %add_convert_fusion.8), channel_id=1, source_target_pairs={{0,8},{4,12},{8,0},{12,4},{16,24},{20,28},{24,16},{28,20},{1,9},{5... | collective-permute-start | bytes 2359304 | tf_op jit(solution)/shard_map/ppermute | solution.py:55
  413.5 22.9 %collective-permute-start.56 = (bf16[16,8192]{1,0:T(8,128)(2,1)}, bf16[16,8192]{1,0:T(8,128)(2,1)S(1)}, u32[]{:S(2)}, u32[]{:S(2)}) collective-permute-start(bf16[16,8192]{1,0:T(8,128)(2,1)} %mix.1.refs_0_), channel_id=1, source_target_pairs={{0,8},{4,12},{8,0},{12,4},{16,24},{20,28},{24,16},{28,20},{1,9},{5... | collective-permute-start | bytes 786440 | tf_op jit(solution)/shard_map/ppermute | solution.py:55
  (112 other events, 1472.5 us)

commit v4 on v3

--- a/solution.py
+++ b/solution.py
@@ -29,13 +29,19 @@
 LANES = 128
 EXP_AT = 2 * RANK
 GATE_AT = 96
+SLOTS_AT = 4
 EXT = D + LANES
+TURN = 8
 NEG = -1e30
 
 BF = jnp.bfloat16
 F32 = jnp.float32
 NT = (((1,), (1,)), ((), ()))
 TN = (((0,), (0,)), ((), ()))
+
+
+def turned_rows(columns, tokens):
+    return TURN * -(-columns * tokens // (TURN * D))
 
 
 def dot(left_arr, right_arr):
@@ -235,16 +241,20 @@
     return values * cosine + (sign * other) * sine
 
 
+def by_adapter(table):
+    return pl.BlockSpec((1,) + table.shape[1:], lambda i, info: (info[0], 0, 0))
+
+
 def project_kernel(info_ref, h_ref, t_ref, table_ref, cos_ref, sin_ref, *rest):
     shards = rest[:-4]
     qkv_ref, full_ref, up_ref, w_ref = rest[-4:]
     rows = shards[0].shape[0]
-    group = info_ref[len(shards) + 1]
+    group = info_ref[1]
 
     @pl.when(pl.program_id(0) == 0)
     def _():
         for m, shard in enumerate(shards):
-            start = pl.multiple_of(info_ref[m] * rows, rows)
+            start = pl.multiple_of(info_ref[SLOTS_AT + m] * rows, rows)
             w_ref[pl.ds(start, rows), :] = shard[:, :LOCAL]
         full_ref[...] = w_ref[...]
         up_ref[...] = jnp.zeros(up_ref.shape, BF)
@@ -265,7 +275,7 @@
         qkv_ref[:, j * LANES : (j + 1) * LANES] = tile.astype(BF)
 
 
-def project(order, adapter, group, h_one, rank_qkv, table, cosine, sine, shards):
+def project(info, h_one, rank_qkv, table, cosine, sine, shards):
     length = h_one.shape[0]
     rows = shards[0].shape[0]
     count = len(shards)
@@ -279,7 +289,7 @@
             in_specs=[
                 per_block(D),
                 per_block(3 * RANK),
-                pl.BlockSpec((1,) + table.shape[1:], lambda i, info: (info[count], 0, 0)),
+                by_adapter(table),
                 per_block(LANES),
                 per_block(LANES),
             ]
@@ -296,15 +306,7 @@
             flops=2 * length * D * LOCAL, bytes_accessed=2 * length * (D + LOCAL), transcendentals=0
         ),
         name="project",
-    )(
-        jnp.concatenate([order, adapter[None], group[None]]).astype(jnp.int32),
-        h_one,
-        rank_qkv,
-        table,
-        cosine,
-        sine,
-        *shards,
-    )
+    )(info, h_one, rank_qkv, table, cosine, sine, *shards)
 
 
 def half_mask(shape, half):
@@ -346,6 +348,17 @@
         for pair, tile in enumerate(tiles if paired else paired_heads(tiles)):
             at = (b // 2) * PAIRS * BLK + pair * BLK + (b % 2) * half
             target_ref[at : at + half, :] = tile
+
+
+def read_turned(block, columns, tokens, first):
+    per = D // tokens
+    parts = []
+    for b in range(columns // TURN):
+        at = slice((b // per) * TURN, (b // per + 1) * TURN)
+        parts.append(block[at, (b % per) * tokens : (b % per + 1) * tokens])
+    before = [jnp.zeros((first, tokens), F32)] if first else []
+    after = [jnp.zeros((LANES - first - columns, tokens), F32)]
+    return jnp.concatenate(before + parts + after, axis=0)
 
 
 def split_keys(place_ref, qkv_ref, first_lane, target_ref, ones):
@@ -567,7 +580,7 @@
     )(place, first, qkv, start_col, out, lse, cosine, sine, *d_out)
 
 
-def expert_kernel(ids_ref, h_refs, p_refs, wgu_ref, wd_ref, tables, y_refs, d_refs, scratch):
+def expert_kernel(experts_all, ids_ref, h_refs, p_refs, wgu_ref, wd_ref, tables, y_refs, d_refs, scratch):
     aux_w, gu_refs, da_refs, db_refs = tables
     wgu_s, wd_s, gu_s, put_s, x_s, g_s, extra_s, yrow_s, drow_s, grad_s, sems = scratch
     count = len(h_refs)
@@ -584,7 +597,7 @@
             copy.start()
     wide = lax.broadcasted_iota(jnp.int32, (tokens, LANES), 1)
     narrow = lax.broadcasted_iota(jnp.int32, (CAP, LANES), 1)
-    base = EXP_AT + ids_ref[count]
+    base = EXP_AT + ids_ref[3]
     grad_s[...] = jnp.zeros(grad_s.shape, F32)
     gu_s[...] = jnp.zeros(gu_s.shape, BF)
     part = lambda arr, j: arr[j * CAP : (j + 1) * CAP]
@@ -592,13 +605,13 @@
         gu_s[j, 0, 0:RANK, :] = gu_refs[j][0, 0]
         gu_s[j, 1, RANK : 2 * RANK, :] = gu_refs[j][0, 1]
         both = dot_nt(h_refs[j][...], aux_w[j][0])
-        ranks = p_refs[j][:, D:EXT].astype(F32)
+        tall = read_turned(p_refs[j][tokens:, :].astype(F32), experts_all, tokens, EXP_AT)
+        ranks = tall.T
         chosen = ranks > 0.0
         picked = jnp.where(chosen, both, NEG)
         weights = jnp.exp(picked - jnp.max(picked, axis=1, keepdims=True))
         gates = weights / jnp.sum(weights, axis=1, keepdims=True)
         aux = jnp.where(wide < EXP_AT, both, 0.0)
-        tall = ranks.T
         which = lax.broadcasted_iota(jnp.int32, tall.shape, 0)
         slot = lax.broadcasted_iota(jnp.int32, (CAP, tokens), 0).astype(F32) + 1.0
         takes = []
@@ -619,7 +632,7 @@
         take = jnp.concatenate(takes, axis=0)
         at = slice(j * CAP, (j + 1) * CAP)
         rows = dot(take, h_refs[j][...]).astype(BF)
-        upstream = dot(take, p_refs[j][:, :D]).astype(BF)
+        upstream = dot(take, p_refs[j][:tokens, :]).astype(BF)
         extra = dot(take, aux.astype(BF))
         for e in range(E_DEV):
             x_s[e, at, :] = part(rows, e)
@@ -672,18 +685,25 @@
     for j in range(count):
         put = put_s[j]
         y_refs[j][...] = dot(put, yrow_s[j]).astype(BF)
-        d_refs[j][:tokens, :] = dot(put, drow_s[j]).astype(BF)
-        d_refs[j][tokens:, :D] = grad_s[j].astype(BF)
-        d_refs[j][tokens:, D:] = jnp.zeros((2 * RANK, LANES), BF)
-
-
-def experts(adapters, base, rows, packs, w_gate_up, w_down, aux_w, gu_up, down_a, down_b):
+        d_refs[j][:tokens, :] = dot(put, drow_s[j, :, :D]).astype(BF)
+        d_refs[j][tokens : tokens + 2 * RANK, :] = grad_s[j].astype(BF)
+        turned_ext = dot(put, drow_s[j, :, D:]).T.astype(BF)
+        per = D // tokens
+        for b in range(-(-(EXP_AT + experts_all) // TURN)):
+            at = tokens + 2 * RANK + (b // per) * TURN
+            lanes = slice((b % per) * tokens, (b % per + 1) * tokens)
+            d_refs[j][at : at + TURN, lanes] = turned_ext[b * TURN : (b + 1) * TURN]
+
+
+def experts(experts_all, info, first, rows, packs, w_gate_up, w_down, aux_w, gu_up, down_a, down_b):
     count = len(rows)
     tokens = rows[0].shape[0]
-    whole = lambda width: pl.BlockSpec((tokens, width), lambda e, ids: (0, 0))
+    whole = lambda arr: pl.BlockSpec(arr.shape, lambda e, ids: (0, 0))
+    d_rows = tokens + 2 * RANK + turned_rows(EXP_AT + experts_all, tokens)
 
     def table(shape, j):
-        return pl.BlockSpec((1,) + shape, lambda e, ids: (ids[j],) + (0,) * len(shape))
+        at = first + j
+        return pl.BlockSpec((1,) + shape, lambda e, ids: (ids[at],) + (0,) * len(shape))
 
     def body(ids_ref, *refs):
         refs = list(refs)
@@ -692,18 +712,17 @@
         wgu_ref, wd_ref = take(2)
         tables = [take(count) for _ in range(4)]
         y_refs, d_refs = take(count), take(count)
-        expert_kernel(ids_ref, h_refs, p_refs, wgu_ref, wd_ref, tables, y_refs, d_refs, refs)
+        expert_kernel(experts_all, ids_ref, h_refs, p_refs, wgu_ref, wd_ref, tables, y_refs, d_refs, refs)
 
     picked = [(LANES, D), (2, RANK, FF), (RANK, FF), (RANK, D)]
-    shapes = [(tokens, D)] * count + [(tokens + 2 * RANK, EXT)] * count
+    shapes = [(tokens, D)] * count + [(d_rows, D)] * count
     height = count * CAP
     outs = pl.pallas_call(
         body,
         grid_spec=pltpu.PrefetchScalarGridSpec(
             num_scalar_prefetch=1,
             grid=(1,),
-            in_specs=[whole(D)] * count
-            + [whole(EXT)] * count
+            in_specs=[whole(arr) for arr in [*rows, *packs]]
             + [pl.BlockSpec(memory_space=pl.ANY)] * 2
             + [table(shape, j) for shape in picked for j in range(count)],
             out_specs=[pl.BlockSpec(shape, lambda e, ids: (0, 0)) for shape in shapes],
@@ -729,7 +748,7 @@
         ),
         name="experts",
     )(
-        jnp.concatenate([adapters, base[None]]).astype(jnp.int32),
+        info,
         *rows,
         *packs,
         w_gate_up,
@@ -758,11 +777,12 @@
     )(*parts)
 
 
-def order_rows_kernel(order_ref, *refs):
+def order_rows_kernel(info_ref, *refs):
     parts, out_ref = refs[:-1], refs[-1]
     rows = parts[0].shape[0]
     for m, part in enumerate(parts):
-        out_ref[pl.ds(pl.multiple_of(order_ref[m] * rows, rows), rows), :] = part[:, LOCAL:]
+        start = pl.multiple_of(info_ref[SLOTS_AT + m] * rows, rows)
+        out_ref[pl.ds(start, rows), :] = part[:, LOCAL:]
 
 
 def order_rows(order, parts):
@@ -779,19 +799,26 @@
     return pl.ds(pl.multiple_of(index * QG, LANES), QG)
 
 
-def by_adapter(table):
-    return pl.BlockSpec((1,) + table.shape[1:], lambda i, info: (info[0], 0, 0))
+def start_copies(sources, target, sems):
+    copies = [
+        pltpu.make_async_copy(source, target.at[j], sems.at[j]) for j, source in enumerate(sources)
+    ]
+    for copy in copies:
+        copy.start()
+    return copies
 
 
 def out_kernel(info_ref, x_ref, gain_ref, down_ref, up_ref, *refs):
-    o_refs, w_refs = refs[:GROUPS], refs[GROUPS : 2 * GROUPS]
-    att_ref, rank_ref, y_ref, h_ref = refs[2 * GROUPS :]
+    o_refs, w_hbm = refs[:GROUPS], refs[GROUPS : 2 * GROUPS]
+    att_ref, rank_ref, y_ref, h_ref, w_s, sems = refs[2 * GROUPS :]
+    w_copies = start_copies(w_hbm, w_s, sems)
     group = info_ref[1]
     for j in range(GROUPS):
         att_ref[:, lanes_of(group ^ j)] = o_refs[j][...]
     attended = att_ref[...]
     for j in range(GROUPS):
-        y_ref[:, lanes_of(group ^ j)] = dot(attended, w_refs[j][...])
+        w_copies[j].wait()
+        y_ref[:, lanes_of(group ^ j)] = dot(attended, w_s[j])
     rank_out = dot_nt(attended, down_ref[0]).astype(BF)
     rank_ref[...] = rank_out
     y_one = x_ref[...].astype(F32) + y_ref[...] + dot(rank_out, up_ref[0])
@@ -809,8 +836,13 @@
             grid=(1,),
             in_specs=[VMEM_SPEC] * 2
             + [by_adapter(down_t), by_adapter(up)]
-            + [VMEM_SPEC] * (2 * GROUPS),
+            + [VMEM_SPEC] * GROUPS
+            + [pl.BlockSpec(memory_space=pl.ANY)] * GROUPS,
             out_specs=[VMEM_SPEC] * 4,
+            scratch_shapes=[
+                pltpu.VMEM((GROUPS, QW, QG), BF),
+                pltpu.SemaphoreType.DMA((GROUPS,)),
+            ],
         ),
         out_shape=[
             jax.ShapeDtypeStruct((tokens, QW), BF),
@@ -825,36 +857,37 @@
     )(info, rows, gain, down_t, up, *outs, *w_parts)
 
 
-def middle_kernel(count, terms, info_ref, *refs):
+def middle_kernel(count, terms, experts_all, info_ref, *refs):
     refs = list(refs)
     take = lambda n: [refs.pop(0) for _ in range(n)]
     d_refs = take(terms)
     pack_ref, y_ref, h_ref, gain_ref, aux_ref, att_ref, rank_ref, down_ref, up_ref = take(9)
-    w_refs = take(GROUPS)
+    w_hbm = take(GROUPS)
     (dy_ref,) = take(1)
     do_refs, early_refs = take(count), take(GROUPS)
-    do_s, early_s = refs
+    do_s, early_s, w_s, sems = refs
+    w_refs = start_copies(w_hbm, w_s, sems)
     group, ctx_index, copies = info_ref[1], info_ref[2], count // GROUPS
     tokens = y_ref.shape[0]
     d_sum = d_refs[0][...].astype(F32)
     for ref in d_refs[1:]:
         d_sum = d_sum + ref[...].astype(F32)
-    early_s[0 : 2 * RANK, :] = d_sum[tokens:, :D]
-    d_ext = d_sum[:tokens, D:]
+    early_s[0 : 2 * RANK, :] = d_sum[tokens : tokens + 2 * RANK]
+    d_ext = read_turned(d_sum[tokens + 2 * RANK :], EXP_AT + experts_all, tokens, 0).T
     h_two = h_ref[...]
     lane = lax.broadcasted_iota(jnp.int32, (tokens, LANES), 1)
-    chosen = pack_ref[:, D:EXT].astype(F32) > 0.0
+    chosen = read_turned(pack_ref[tokens:, :].astype(F32), experts_all, tokens, EXP_AT).T > 0.0
     picked = jnp.where(chosen, dot_nt(h_two, aux_ref[0]), NEG)
     weights = jnp.exp(picked - jnp.max(picked, axis=1, keepdims=True))
     gates = weights / jnp.sum(weights, axis=1, keepdims=True)
     mixed = jnp.sum(jnp.where(chosen, gates * d_ext, 0.0), axis=1, keepdims=True)
     d_logits = jnp.where(chosen, gates * (d_ext - mixed), 0.0)
     d_ext = jnp.where(lane < EXP_AT, d_ext, d_logits).astype(BF)
-    d_h = d_sum[:tokens, :D] + dot(d_ext, aux_ref[0])
+    d_h = d_sum[:tokens] + dot(d_ext, aux_ref[0])
     y_one = y_ref[...]
     inverse = lax.rsqrt(jnp.mean(y_one * y_one, axis=1, keepdims=True) + NORM_EPS)
     scaled = gain_ref[...] * d_h
-    d_y = pack_ref[:, :D].astype(F32) + inverse * scaled
+    d_y = pack_ref[:tokens, :].astype(F32) + inverse * scaled
     d_y = d_y - y_one * inverse**3 * jnp.mean(y_one * scaled, axis=1, keepdims=True)
     dy_ref[...] = d_y
     d_attn = d_y.astype(BF)
@@ -863,7 +896,8 @@
     for j in range(GROUPS):
         at = lanes_of(group ^ j)
         early_s[3 * RANK : 4 * RANK, at] = dot_tn(rank_ref[...], dy_ref[:, at].astype(BF))
-        do_s[...] += dot_nt(dy_ref[:, at].astype(BF), w_refs[j][...])
+        w_refs[j].wait()
+        do_s[...] += dot_nt(dy_ref[:, at].astype(BF), w_s[j])
     for m in range(count):
         do_refs[m][...] = do_s[:, lanes_of((ctx_index ^ m) // copies)].astype(BF)
     early_s[2 * RANK : 3 * RANK, :] = dot_tn(d_rank, att_ref[...])
@@ -874,10 +908,10 @@
             early_refs[j][:, i * QG : (i + 1) * QG] = block.astype(BF)
 
 
-def middle_back(info, count, terms, pack, y_one, h_two, gain, aux, attended, rank_out, down_t, up, w_parts):
+def middle_back(info, count, experts_all, terms, pack, y_one, h_two, gain, aux, attended, rank_out, down_t, up, w_parts):
     tokens = y_one.shape[0]
     outs = pl.pallas_call(
-        functools.partial(middle_kernel, count, len(terms)),
+        functools.partial(middle_kernel, count, len(terms), experts_all),
         grid_spec=pltpu.PrefetchScalarGridSpec(
             num_scalar_prefetch=1,
             grid=(1,),
@@ -885,9 +919,14 @@
             + [by_adapter(aux)]
             + [VMEM_SPEC] * 2
             + [by_adapter(down_t), by_adapter(up)]
-            + [VMEM_SPEC] * GROUPS,
+            + [pl.BlockSpec(memory_space=pl.ANY)] * GROUPS,
             out_specs=[VMEM_SPEC] * (1 + count + GROUPS),
-            scratch_shapes=[pltpu.VMEM((tokens, QW), F32), pltpu.VMEM((6 * RANK, D), F32)],
+            scratch_shapes=[
+                pltpu.VMEM((tokens, QW), F32),
+                pltpu.VMEM((6 * RANK, D), F32),
+                pltpu.VMEM((GROUPS, QW, QG), BF),
+                pltpu.SemaphoreType.DMA((GROUPS,)),
+            ],
         ),
         out_shape=[jax.ShapeDtypeStruct((tokens, D), F32)]
         + [jax.ShapeDtypeStruct((tokens, QG), BF)] * count
@@ -900,7 +939,7 @@
     return outs[0], list(outs[1 : 1 + count]), list(outs[1 + count :])
 
 
-def ranks_kernel(group_ref, dqkv_ref, up_ref, t_ref, h_ref, *refs):
+def ranks_kernel(info_ref, dqkv_ref, up_ref, t_ref, h_ref, *refs):
     early_refs, (rank_ref, keep_ref, send_ref) = refs[:GROUPS], refs[GROUPS:]
     d_qkv = dqkv_ref[...]
     d_rank = dot_nt(d_qkv, up_ref[...]).astype(BF)
@@ -912,7 +951,7 @@
     send_ref[:, :LOCAL] = jnp.zeros((RANK, LOCAL), BF)
     for j in range(GROUPS):
         target = send_ref if j % 2 else keep_ref
-        down = dot_tn(d_rank, h_ref[:, lanes_of(group_ref[0] ^ j)]).astype(BF)
+        down = dot_tn(d_rank, h_ref[:, lanes_of(info_ref[1] ^ j)]).astype(BF)
         first = LOCAL + (j // 2) * 3 * QG
         for i in range(3):
             target[:, first + i * QG : first + (i + 1) * QG] = down[i * RANK : (i + 1) * RANK]
@@ -924,7 +963,7 @@
 BOTH = HALF + LOCAL
 
 
-def ranks_back(group, d_qkv, up_diag, rank_qkv, h_one, early):
+def ranks_back(info, d_qkv, up_diag, rank_qkv, h_one, early):
     length = d_qkv.shape[0]
     return pl.pallas_call(
         ranks_kernel,
@@ -936,7 +975,7 @@
             jax.ShapeDtypeStruct((RANK, HALF), BF),
         ],
         name="ranks_back",
-    )(group, d_qkv, up_diag, rank_qkv, h_one, *early)
+    )(info, d_qkv, up_diag, rank_qkv, h_one, *early)
 
 
 def mix_kernel(near_ref, far_ref, out_ref):
@@ -995,7 +1034,7 @@
     )(d_qkv, d_rank, cols_all, down_sel)
 
 
-def place_kernel(ids_ref, *refs):
+def place_kernel(info_ref, *refs):
     parts = refs[:2]
     up_ref, down_ref, gu_ref, da_ref, db_ref, od_ref, ou_ref, gd_ref, sum_s = refs[2:]
     sources = parts[0].shape[0]
@@ -1003,13 +1042,13 @@
     down_ref[...] = jnp.zeros(down_ref.shape, F32)
     sum_s[...] = jnp.zeros(sum_s.shape, F32)
     for j in range(GROUPS):
-        group = ids_ref[sources] ^ j
+        group = info_ref[1] ^ j
         keys = lambda first: pl.ds(pl.multiple_of(first + group * KG, LANES), KG)
         far = j // 2
         down_at = 2 * LOCAL + far * 3 * QG
         early_at = 2 * LOCAL + 6 * QG + far * 6 * QG
         for m in range(sources):
-            a = ids_ref[m]
+            a = info_ref[SLOTS_AT + sources + m]
             take = lambda first, width: parts[j % 2][m, :, first : first + width].astype(F32)
             up_ref[a, :, lanes_of(group)] += take(far * LOCAL, QG)
             up_ref[a, :, keys(QW)] += take(far * LOCAL + QG, KG)
@@ -1030,7 +1069,7 @@
         gd_ref[a] = sum_s[a, 4 * RANK :]
 
 
-def place_grads(ids, near, far):
+def place_grads(info, near, far):
     shapes = [(RANK, QW + 2 * KVW), (3 * RANK, D), (2, RANK, FF), (RANK, FF), (RANK, D)]
     shapes += [(RANK, QW), (RANK, D), (2 * RANK, D)]
     return pl.pallas_call(
@@ -1040,7 +1079,7 @@
         out_shape=[jax.ShapeDtypeStruct((ADAPT,) + shape, F32) for shape in shapes],
         scratch_shapes=[pltpu.VMEM((ADAPT, 6 * RANK, D), F32)],
         name="place_grads",
-    )(ids, near, far)
+    )(info, near, far)
 
 
 def norm_backward(values, inverse, gain_vec, upstream):
@@ -1106,11 +1145,15 @@
     )
     chosen = expert_ids[0]
     hot = jnp.any(chosen[:, :, None] == jnp.arange(experts_all)[None, None, :], axis=1)
-    hot_low = hot.astype(BF)
-    before = (jnp.arange(tokens)[:, None] >= jnp.arange(tokens)[None, :]).astype(BF)
-    ranks = dot(before, hot_low).astype(BF) * hot_low
-    ranks = jnp.pad(ranks, ((0, 0), (EXP_AT, LANES - EXP_AT - experts_all)))
-    pack = jnp.concatenate([cotangent[0], ranks], axis=1)
+    hot_low = hot.astype(BF).T
+    before = (jnp.arange(tokens)[:, None] <= jnp.arange(tokens)[None, :]).astype(BF)
+    ranks = dot(hot_low, before).astype(BF) * hot_low
+    per = D // tokens
+    rank_rows = turned_rows(experts_all, tokens)
+    ranks = jnp.pad(ranks, ((0, rank_rows * per - experts_all), (0, 0)))
+    ranks = ranks.reshape(rank_rows // TURN, per, TURN, tokens)
+    ranks = jnp.transpose(ranks, (0, 2, 1, 3)).reshape(rank_rows, D)
+    pack = jnp.concatenate([cotangent[0], ranks], axis=0)
     cols.beside()
     seg_row = segment_ids[0]
     position = jnp.arange(length)
@@ -1129,9 +1172,9 @@
     start_col = start[:, None]
     adapter = adapter_ids[seq_index]
     slot_adapters = adapter_ids[seq_slots]
-    slots_and_group = jnp.concatenate([slot_adapters, group[None]]).astype(jnp.int32)
-    group_info = group[None].astype(jnp.int32)
-    info = jnp.stack([adapter, group, ctx_index]).astype(jnp.int32)
+    info = jnp.concatenate(
+        [jnp.stack([adapter, group, ctx_index, E_DEV * seq_index]), seq_slots, slot_adapters]
+    ).astype(jnp.int32)
 
     def pick(table):
         return lax.dynamic_index_in_dim(table, adapter, 0, keepdims=False)
@@ -1148,8 +1191,8 @@
     )
     down_a_t = jnp.swapaxes(down_a, 1, 2)
 
-    pack, start_col, cosine, sine, place, first, *moving_rows = cols.beside(
-        pack, start_col, cosine, sine, place, first, *moving_rows
+    pack, start_col, cosine, sine, place, first, info, *moving_rows = cols.beside(
+        pack, start_col, cosine, sine, place, first, info, *moving_rows
     )
     row_slots = gather_rest(own_rows, moving_rows, ctx_masks)
     all_rows = jnp.concatenate(row_slots, axis=0).astype(F32)
@@ -1160,11 +1203,9 @@
     pack_slots = []
     packs = Steps(gather_line(pack, pack_slots))
     cols.finish()
-    outs = Steps(gather_groups(order_rows(seq_slots, col_slots), copies))
+    outs = Steps(gather_groups(order_rows(info, col_slots), copies))
     qkv, cols_all, up_diag = packs.beside(
-        *project(
-            seq_slots, adapter, group, h_one, rank_qkv, qkv_up, cosine, sine, col_slots
-        )
+        *project(info, h_one, rank_qkv, qkv_up, cosine, sine, col_slots)
     )
     heads_out, lse, *pieces = packs.beside(
         *outs.beside(*attend(place, first, qkv, start_col, copies))
@@ -1179,8 +1220,9 @@
 
     def compute(m, rows):
         return experts(
-            slot_adapters[m : m + len(rows)],
-            E_DEV * seq_index,
+            experts_all,
+            info,
+            SLOTS_AT + seq_count + m,
             rows,
             pack_slots[m : m + len(rows)],
             w_gate_up,
@@ -1196,6 +1238,7 @@
     d_y_one, d_heads, early = middle_back(
         info,
         ctx_count,
+        experts_all,
         d_terms,
         pack,
         y_one,
@@ -1215,7 +1258,7 @@
     (d_qkv,) = y_sums.beside(
         attend_back(place, first, qkv, start_col, heads_out, lse, cosine, sine, d_heads)
     )
-    d_rank_qkv, keep, sent = ranks_back(group_info, d_qkv, up_diag, rank_qkv, h_one, early)
+    d_rank_qkv, keep, sent = ranks_back(info, d_qkv, up_diag, rank_qkv, h_one, early)
 
     halves = add_low(keep, swap(sent, "ctx", copies))
     for mask in doublings(copies):
@@ -1255,7 +1298,7 @@
         grad_out_down,
         grad_out_up,
         grad_gu_down,
-    ) = place_grads(slots_and_group, grads, swap(grads, "ctx", copies))
+    ) = place_grads(info, grads, swap(grads, "ctx", copies))
 
     return (
         layer_output[None],

time: 488 us -> 481 us (0.986)
  waiting for transfers between devices: 156 us -> 163 us
  other arithmetic: 43 us -> 37.4 us
  starting transfers between devices: 93.9 us -> 88.4 us
    ppermute x24, waiting for transfers between devices: 42.2 us -> 49.3 us  [line_swap(): lax.ppermute(block, 'seq', [(2 * i + j, 2 * k + j) for i, k in pairs for...]
  transfers between devices with their start and end apart: 72 -> 72, of which waited for: 30 -> 30; matrix products, arithmetic and copies ran while one was open for 10% -> 8% of each run, Pallas kernels for 31% -> 32%
where the time goes in v4:
time: 481 us; the launch traced here: 472 us
  Pallas kernels  164 us (34%)
  waiting for transfers between devices  163 us (34%)
  starting transfers between devices  88.4 us (18%)
  other arithmetic  37.4 us (8%)
  local copies, waits for them, and re-layouts  13.9 us (3%)
    ppermute x48, waiting for transfers between devices, swap(): return lax.ppermute(block, axis, [(i, i ^ mask) for i in range(count)])  113 us
    pallas_call x5, Pallas kernels, experts(): pl.pallas_call(body, grid_spec=pltpu.PrefetchScalarGridSpec(num_scalar_pr...  75.9 us
    ppermute x24, waiting for transfers between devices, line_swap(): lax.ppermute(block, 'seq', [(2 * i + j, 2 * k + j) for i, k in pairs for...  49.3 us
    ppermute x48, starting transfers between devices, swap(): return lax.ppermute(block, axis, [(i, i ^ mask) for i in range(count)])  48.4 us
    ppermute x24, starting transfers between devices, line_swap(): lax.ppermute(block, 'seq', [(2 * i + j, 2 * k + j) for i, k in pairs for...  40 us
    pallas_call x1, Pallas kernels, attend_back(): pl.pallas_call(attend_back_kernel, in_specs=[SMEM_SPEC, SMEM_SPEC] + [VME...  20.3 us
    pallas_call x1, Pallas kernels, attend(): pl.pallas_call(functools.partial(attend_kernel, copies), in_specs=[SMEM_S...  13 us
    pallas_call x1, Pallas kernels, middle_back(): pl.pallas_call(functools.partial(middle_kernel, count, len(terms), expert...  11.5 us
  transfers between devices with their start and end apart: 72, of which 30 were waited for; matrix products, arithmetic and copies ran while one was open for 8% of the time, Pallas kernels for 32%

profile of v4, /device:TPU:0, one launch (start us, length us, event | category | flops | bytes accessed | tf_op | source)
XLA Modules:
  0.0 472.3 jit_solution(6743826595420447984)
XLA Ops:
  26.4 7.6 %collective-permute-done.4 = bf16[192,1024]{1,0:T(8,128)(2,1)} collective-permute-done((bf16[192,1024]{1,0:T(8,128)(2,1)}, bf16[192,1024]{1,0:T(8,128)(2,1)}, u32[]{:S(2)}, u32[]{:S(2)}) %collective-permute-start.4) | collective-permute-done | bytes 393248 | tf_op jit(solution)/shard_map/ppermute | solution.py:85
  57.8 6.6 %collective-permute-done.14.rest_7_.refs_7_ = bf16[192,1024]{1,0:T(8,128)(2,1)S(1)} collective-permute-done((bf16[192,1024]{1,0:T(8,128)(2,1)S(1)}, bf16[192,1024]{1,0:T(8,128)(2,1)S(1)}, u32[]{:S(2)}, u32[]{:S(2)}) %collective-permute-start.14) | collective-permute-done | bytes 393248 | tf_op jit(solution)/shard_map/ppermute | solution.py:61
  69.6 8.9 %project.1 = (bf16[1024,640]{1,0:T(8,128)(2,1)}, bf16[1536,640]{1,0:T(8,128)(2,1)}, bf16[48,640]{1,0:T(8,128)(2,1)}) custom-call(s32[20]{0:T(128)} %concatenate.17.info_ref.ids_ref, bf16[1024,1536]{1,0:T(8,128)(2,1)} %copy-done.3, bf16[1024,48]{1,0:T(8,128)(2,1)} %convolution_convert_fusion.t_ref, bf16[8,16,2560]{2,1,0:T(8,128)(2,1)} %table_ref.1, ...), custom_call_target="tpu_custom_call" | custom-call | flops 2013265920 | bytes 4456448 | tf_op jit(solution)/shard_map/project/pallas_call | solution.py:284
  84.1 13.0 %attend.1 = (bf16[1024,384]{1,0:T(8,128)(2,1)}, f32[3072,128]{1,0:T(8,128)}, bf16[256,384]{1,0:T(8,128)(2,1)}, bf16[256,384]{1,0:T(8,128)(2,1)}, bf16[256,384]{1,0:T(8,128)(2,1)}, /*index=5*/bf16[256,384]{1,0:T(8,128)(2,1)}) custom-call(s32[8]{0:T(128)} %fusion.14.place_ref, s32[4]{0:T(128)} %and_select_fusion.first_ref, ...), custom_call_target="tpu_custom_call" | custom-call | flops 1610612736 | bytes 3145728 | tf_op jit(solution)/shard_map/attend/pallas_call | solution.py:454
  97.3 6.6 %collective-permute-done.16 = bf16[264,1536]{1,0:T(8,128)(2,1)} collective-permute-done((bf16[264,1536]{1,0:T(8,128)(2,1)}, bf16[264,1536]{1,0:T(8,128)(2,1)}, u32[]{:S(2)}, u32[]{:S(2)}) %collective-permute-start.16) | collective-permute-done | bytes 811040 | tf_op jit(solution)/shard_map/ppermute | solution.py:85
  118.3 6.7 %collective-permute-done.20 = bf16[264,1536]{1,0:T(8,128)(2,1)S(1)} collective-permute-done((bf16[264,1536]{1,0:T(8,128)(2,1)S(1)}, bf16[264,1536]{1,0:T(8,128)(2,1)S(1)}, u32[]{:S(2)}, u32[]{:S(2)}) %collective-permute-start.20) | collective-permute-done | bytes 811040 | tf_op jit(solution)/shard_map/ppermute | solution.py:85
  128.7 8.1 %project_out.1 = (bf16[256,1536]{1,0:T(8,128)(2,1)}, bf16[256,16]{1,0:T(8,128)(2,1)}, f32[256,1536]{1,0:T(8,128)}, bf16[256,1536]{1,0:T(8,128)(2,1)}) custom-call(s32[20]{0:T(128)} %concatenate.17.info_ref.ids_ref, bf16[256,1536]{1,0:T(8,128)(2,1)} %bitcast.44, f32[1,1536]{1,0:T(1,128)} %broadcast_in_dim.23.gain_ref.refs_7_, bf16[8,16,1536]{2,1,0:T(8,128)(2,1)} %bitcast.48, ...), custom_call_target="tpu_custom_call" | custom-call | flops 1207959552 | bytes 9437184 | tf_op jit(solution)/shard_map/project_out/pallas_call | solution.py:832
  143.8 13.7 %experts.5 = (bf16[256,1536]{1,0:T(8,128)(2,1)}, bf16[296,1536]{1,0:T(8,128)(2,1)}) custom-call(s32[20]{0:T(128)} %concatenate.17.info_ref.ids_ref, bf16[256,1536]{1,0:T(8,128)(2,1)} %get-tuple-element.239.refs_0_.refs_6_, bf16[264,1536]{1,0:T(8,128)(2,1)} %copy-done.7, bf16[2,1536,1024]{2,1,0:T(8,128)(2,1)} %refs_2_.3, bf16[2,512,1536]{2,1,0:T(8,128)(2,1)} %refs_3_.3, ...), custom_call_target="tpu_custom_call" | custom-call | flops 3221225472 | bytes 12582912 | tf_op jit(solution)/shard_map/experts/pallas_call | solution.py:720
  164.4 16.1 %experts.6 = (bf16[256,1536]{1,0:T(8,128)(2,1)}, bf16[256,1536]{1,0:T(8,128)(2,1)}, bf16[296,1536]{1,0:T(8,128)(2,1)}, bf16[296,1536]{1,0:T(8,128)(2,1)}) custom-call(s32[20]{0:T(128)} %concatenate.17.info_ref.ids_ref, bf16[256,1536]{1,0:T(8,128)(2,1)} %collective-permute-done.28.refs_0_, bf16[256,1536]{1,0:T(8,128)(2,1)} %collective-permute-done.26.refs_1_, ...), custom_call_target="tpu_custom_call" | custom-call | flops 6442450944 | bytes 15728640 | tf_op jit(solution)/shard_map/experts/pallas_call | solution.py:720
  185.9 16.1 %experts.7 = (bf16[256,1536]{1,0:T(8,128)(2,1)}, bf16[256,1536]{1,0:T(8,128)(2,1)}, bf16[296,1536]{1,0:T(8,128)(2,1)}, bf16[296,1536]{1,0:T(8,128)(2,1)}) custom-call(s32[20]{0:T(128)} %concatenate.17.info_ref.ids_ref, bf16[256,1536]{1,0:T(8,128)(2,1)} %collective-permute-done.32.refs_0_, bf16[256,1536]{1,0:T(8,128)(2,1)} %add.207.refs_1_, ...), custom_call_target="tpu_custom_call" | custom-call | flops 6442450944 | bytes 15728640 | tf_op jit(solution)/shard_map/experts/pallas_call | solution.py:720
  205.8 16.1 %experts.8 = (bf16[256,1536]{1,0:T(8,128)(2,1)}, bf16[256,1536]{1,0:T(8,128)(2,1)}, bf16[296,1536]{1,0:T(8,128)(2,1)}, bf16[296,1536]{1,0:T(8,128)(2,1)}) custom-call(s32[20]{0:T(128)} %concatenate.17.info_ref.ids_ref, bf16[256,1536]{1,0:T(8,128)(2,1)} %copy-done.56, bf16[256,1536]{1,0:T(8,128)(2,1)} %add.208.refs_1_, ...), custom_call_target="tpu_custom_call" | custom-call | flops 6442450944 | bytes 15728640 | tf_op jit(solution)/shard_map/experts/pallas_call | solution.py:720
  225.4 13.8 %experts.9 = (bf16[256,1536]{1,0:T(8,128)(2,1)}, bf16[296,1536]{1,0:T(8,128)(2,1)}) custom-call(s32[20]{0:T(128)} %concatenate.17.info_ref.ids_ref, bf16[256,1536]{1,0:T(8,128)(2,1)} %copy-done.31, bf16[264,1536]{1,0:T(8,128)(2,1)} %copy-done.29, bf16[2,1536,1024]{2,1,0:T(8,128)(2,1)} %refs_2_.3, bf16[2,512,1536]{2,1,0:T(8,128)(2,1)} %refs_3_.3, ...), custom_call_target="tpu_custom_call" | custom-call | flops 3221225472 | bytes 12582912 | tf_op jit(solution)/shard_map/experts/pallas_call | solution.py:720
  243.0 21.3 %collective-permute-done.37 = bf16[296,1536]{1,0:T(8,128)(2,1)S(1)} collective-permute-done((bf16[296,1536]{1,0:T(8,128)(2,1)}, bf16[296,1536]{1,0:T(8,128)(2,1)S(1)}, u32[]{:S(2)}, u32[]{:S(2)}) %collective-permute-start.37) | collective-permute-done | bytes 909344 | tf_op jit(solution)/shard_map/ppermute | solution.py:61
  264.5 5.9 %collective-permute-start.38 = (bf16[296,1536]{1,0:T(8,128)(2,1)S(1)}, bf16[296,1536]{1,0:T(8,128)(2,1)S(1)}, u32[]{:S(2)}, u32[]{:S(2)}) collective-permute-start(bf16[296,1536]{1,0:T(8,128)(2,1)S(1)} %add_convert_fusion.3), channel_id=1, source_target_pairs={{0,8},{4,12},{24,16},{28,20},{1,9},{5,13},{25,17},{29,21},{2,10},{... | collective-permute-start | bytes 2727944 | tf_op jit(solution)/shard_map/ppermute | solution.py:85
  271.0 12.8 %collective-permute-done.39 = bf16[296,1536]{1,0:T(8,128)(2,1)S(1)} collective-permute-done((bf16[296,1536]{1,0:T(8,128)(2,1)}, bf16[296,1536]{1,0:T(8,128)(2,1)S(1)}, u32[]{:S(2)}, u32[]{:S(2)}) %collective-permute-start.39) | collective-permute-done | bytes 909344 | tf_op jit(solution)/shard_map/ppermute | solution.py:61
  296.7 8.7 %collective-permute-done.40 = bf16[296,1536]{1,0:T(8,128)(2,1)S(1)} collective-permute-done((bf16[296,1536]{1,0:T(8,128)(2,1)S(1)}, bf16[296,1536]{1,0:T(8,128)(2,1)S(1)}, u32[]{:S(2)}, u32[]{:S(2)}) %collective-permute-start.40) | collective-permute-done | bytes 909344 | tf_op jit(solution)/shard_map/ppermute | solution.py:85
  306.6 9.4 %collective-permute-start.44 = (bf16[296,1536]{1,0:T(8,128)(2,1)S(1)}, bf16[296,1536]{1,0:T(8,128)(2,1)S(1)}, u32[]{:S(2)}, u32[]{:S(2)}) collective-permute-start(bf16[296,1536]{1,0:T(8,128)(2,1)S(1)} %add_convert_fusion.1), channel_id=1, source_target_pairs={{0,8},{4,12},{8,0},{12,4},{16,24},{20,28},{24,16},{28,20},{1,9},{5... | collective-permute-start | bytes 2727944 | tf_op jit(solution)/shard_map/ppermute | solution.py:61
  318.1 9.3 %collective-permute-done.44.refs_1_ = bf16[296,1536]{1,0:T(8,128)(2,1)S(1)} collective-permute-done((bf16[296,1536]{1,0:T(8,128)(2,1)S(1)}, bf16[296,1536]{1,0:T(8,128)(2,1)S(1)}, u32[]{:S(2)}, u32[]{:S(2)}) %collective-permute-start.44) | collective-permute-done | bytes 909344 | tf_op jit(solution)/shard_map/ppermute | solution.py:61
  328.3 11.5 %middle_back.1 = (f32[256,1536]{1,0:T(8,128)}, bf16[256,384]{1,0:T(8,128)(2,1)}, bf16[256,384]{1,0:T(8,128)(2,1)}, bf16[256,384]{1,0:T(8,128)(2,1)}, bf16[256,38...) custom-call(s32[20]{0:T(128)} %concatenate.17.info_ref.ids_ref, ...), custom_call_target="tpu_custom_call" | custom-call | flops 1207959552 | bytes 12582912 | tf_op jit(solution)/shard_map/middle_back/pallas_call | solution.py:913
  362.3 20.3 %attend_back.1.dqkv_ref = bf16[1024,640]{1,0:T(8,128)(2,1)} custom-call(s32[8]{0:T(128)} %fusion.14.place_ref, s32[4]{0:T(128)} %and_select_fusion.first_ref, bf16[1024,640]{1,0:T(8,128)(2,1)} %get-tuple-element.213.qkv_ref, s32[1024,1]{1,0:T(8,128)} %copy.40.start_ref, bf16[1024,384]{1,0:T(8,128)(2,1)} %get-tuple-element.310.o_ref, ...), custom_call_target="tpu_custom_call" | custom-call | flops 4026531840 | bytes 6291456 | tf_op jit(solution)/shard_map/attend_back/pallas_call | solution.py:560
  390.7 7.7 %inputs_back.1 = (bf16[256,1536]{1,0:T(8,128)(2,1)}, bf16[256,1536]{1,0:T(8,128)(2,1)}, bf16[256,1536]{1,0:T(8,128)(2,1)}, bf16[256,1536]{1,0:T(8,128)(2,1)}) custom-call(bf16[1024,640]{1,0:T(8,128)(2,1)} %attend_back.1.dqkv_ref, bf16[1024,48]{1,0:T(8,128)(2,1)} %get-tuple-element.326.rank_ref, bf16[1536,640]{1,0:T(8,128)(2,1)} %get-tuple-element.327.w_ref, ...), custom_call_target="tpu_custom_call" | custom-call | flops 2013265920 | bytes 8912896 | tf_op jit(solution)/shard_map/inputs_back/pallas_call | solution.py:1019
  413.0 14.9 %collective-permute-done.56.refs_2_ = bf16[16,8192]{1,0:T(8,128)(2,1)S(1)} collective-permute-done((bf16[16,8192]{1,0:T(8,128)(2,1)}, bf16[16,8192]{1,0:T(8,128)(2,1)S(1)}, u32[]{:S(2)}, u32[]{:S(2)}) %collective-permute-start.56) | collective-permute-done | bytes 262176 | tf_op jit(solution)/shard_map/ppermute | solution.py:61
  433.4 7.2 %collective-permute-done.65 = bf16[16,8192]{1,0:T(8,128)(2,1)S(1)} collective-permute-done((bf16[16,8192]{1,0:T(8,128)(2,1)S(1)}, bf16[16,8192]{1,0:T(8,128)(2,1)S(1)}, u32[]{:S(2)}, u32[]{:S(2)}) %collective-permute-start.65) | collective-permute-done | bytes 262176 | tf_op jit(solution)/shard_map/ppermute | solution.py:85
  465.5 6.4 %place_grads.1 = (f32[8,16,2560]{2,1,0:T(8,128)}, f32[8,48,1536]{2,1,0:T(8,128)}, f32[8,2,16,512]{3,2,1,0:T(8,128)}, f32[8,16,512]{2,1,0:T(8,128)}, f32[8,16,153...) custom-call(s32[20]{0:T(128)} %concatenate.17.info_ref.ids_ref, ...), custom_call_target="tpu_custom_call" | custom-call | tf_op jit(solution)/shard_map/place_grads/pallas_call | solution.py:1075
  (331 shorter events, 199.3 us)
Async XLA Ops:
  8.7 25.3 %collective-permute-start.6 = (bf16[256,1536]{1,0:T(8,128)(2,1)}, bf16[256,1536]{1,0:T(8,128)(2,1)}, u32[]{:S(2)}, u32[]{:S(2)}) collective-permute-start(bf16[256,1536]{1,0:T(8,128)(2,1)} %bitcast.42), channel_id=1, source_target_pairs={{0,2},{1,3},{2,0},{3,1},{4,6},{5,7},{6,4},{7,5},{8,10},{9,11},{10,... | collective-permute-start | bytes 2359304 | tf_op jit(solution)/shard_map/ppermute | solution.py:61
  10.2 23.8 %collective-permute-start.7 = (bf16[256,1536]{1,0:T(8,128)(2,1)}, bf16[256,1536]{1,0:T(8,128)(2,1)}, u32[]{:S(2)}, u32[]{:S(2)}) collective-permute-start(bf16[256,1536]{1,0:T(8,128)(2,1)} %bitcast.43), channel_id=1, source_target_pairs={{0,1},{1,0},{2,3},{3,2},{4,5},{5,4},{6,7},{7,6},{8,9},{9,8},{10,11... | collective-permute-start | bytes 2359304 | tf_op jit(solution)/shard_map/ppermute | solution.py:61
  52.9 25.6 %collective-permute-start.11 = (bf16[264,1536]{1,0:T(8,128)(2,1)S(1)}, bf16[264,1536]{1,0:T(8,128)(2,1)}, u32[]{:S(2)}, u32[]{:S(2)}) collective-permute-start(bf16[264,1536]{1,0:T(8,128)(2,1)S(1)} %pad_maximum_fusion.1.refs_1_.refs_4_), channel_id=1, source_target_pairs={{0,8},{4,12},{8,0},{12,4},{16,24},{20,28},{24,16},{28,20},{1,9},{5... | collective-permute-start | bytes 2433032 | tf_op jit(solution)/shard_map/ppermute | solution.py:61
  54.7 23.8 %collective-permute-start.12 = (bf16[264,1536]{1,0:T(8,128)(2,1)S(1)}, bf16[264,1536]{1,0:T(8,128)(2,1)}, u32[]{:S(2)}, u32[]{:S(2)}) collective-permute-start(bf16[264,1536]{1,0:T(8,128)(2,1)S(1)} %pad_maximum_fusion.1.refs_1_.refs_4_), channel_id=1, source_target_pairs={{8,16},{12,20},{16,8},{20,12},{9,17},{13,21},{17,9},{21,13},{10,18... | collective-permute-start | bytes 2433032 | tf_op jit(solution)/shard_map/ppermute | solution.py:85
  56.3 24.2 %collective-permute-start.13 = (bf16[264,1536]{1,0:T(8,128)(2,1)S(1)}, bf16[264,1536]{1,0:T(8,128)(2,1)S(1)}, u32[]{:S(2)}, u32[]{:S(2)}) collective-permute-start(bf16[264,1536]{1,0:T(8,128)(2,1)S(1)} %pad_maximum_fusion.1.refs_1_.refs_4_), channel_id=1, source_target_pairs={{0,4},{4,0},{8,12},{12,8},{16,20},{20,16},{24,28},{28,24},{1,5},{5... | collective-permute-start | bytes 2433032 | tf_op jit(solution)/shard_map/ppermute | solution.py:61
  68.1 29.1 %collective-permute-start.18 = (bf16[1536,384]{1,0:T(8,128)(2,1)}, bf16[1536,384]{1,0:T(8,128)(2,1)S(1)}, u32[]{:S(2)}, u32[]{:S(2)}) collective-permute-start(bf16[1536,384]{1,0:T(8,128)(2,1)} %order_rows.1.refs_4_.refs_13_), channel_id=1, source_target_pairs={{0,2},{1,3},{2,0},{3,1},{4,6},{5,7},{6,4},{7,5},{8,10},{9,11},{10,... | collective-permute-start | bytes 3538952 | tf_op jit(solution)/shard_map/ppermute | solution.py:61
  69.6 27.6 %collective-permute-start.19 = (bf16[1536,384]{1,0:T(8,128)(2,1)}, bf16[1536,384]{1,0:T(8,128)(2,1)}, u32[]{:S(2)}, u32[]{:S(2)}) collective-permute-start(bf16[1536,384]{1,0:T(8,128)(2,1)} %order_rows.1.refs_4_.refs_13_), channel_id=1, source_target_pairs={{0,1},{1,0},{2,3},{3,2},{4,5},{5,4},{6,7},{7,6},{8,9},{9,8},{10,11... | collective-permute-start | bytes 3538952 | tf_op jit(solution)/shard_map/ppermute | solution.py:61
  81.2 22.6 %collective-permute-start.16 = (bf16[264,1536]{1,0:T(8,128)(2,1)}, bf16[264,1536]{1,0:T(8,128)(2,1)}, u32[]{:S(2)}, u32[]{:S(2)}) collective-permute-start(bf16[264,1536]{1,0:T(8,128)(2,1)} %collective-permute-done.12), channel_id=1, source_target_pairs={{8,0},{12,4},{16,24},{20,28},{9,1},{13,5},{17,25},{21,29},{10,2},{... | collective-permute-start | bytes 2433032 | tf_op jit(solution)/shard_map/ppermute | solution.py:85
  82.5 21.3 %collective-permute-start.17 = (bf16[264,1536]{1,0:T(8,128)(2,1)}, bf16[264,1536]{1,0:T(8,128)(2,1)}, u32[]{:S(2)}, u32[]{:S(2)}) collective-permute-start(bf16[264,1536]{1,0:T(8,128)(2,1)} %collective-permute-done.11.refs_3_), channel_id=1, source_target_pairs={{0,4},{4,0},{8,12},{12,8},{16,20},{20,16},{24,28},{28,24},{1,5},{5... | collective-permute-start | bytes 2433032 | tf_op jit(solution)/shard_map/ppermute | solution.py:61
  97.2 30.5 %collective-permute-start.25 = (bf16[1536,384]{1,0:T(8,128)(2,1)S(1)}, bf16[1536,384]{1,0:T(8,128)(2,1)S(1)}, u32[]{:S(2)}, u32[]{:S(2)}) collective-permute-start(bf16[1536,384]{1,0:T(8,128)(2,1)S(1)} %collective-permute-done.18.refs_6_.refs_15_), channel_id=1, source_target_pairs={{0,1},{1,0},{2,3},{3,2},{4,5},{5,4},{6,7},{7,6},{8,9},{9,8},{10,11... | collective-permute-start | bytes 3538952 | tf_op jit(solution)/shard_map/ppermute | solution.py:61
  127.3 30.2 %collective-permute-start.29 = (bf16[264,1536]{1,0:T(8,128)(2,1)}, bf16[264,1536]{1,0:T(8,128)(2,1)S(1)}, u32[]{:S(2)}, u32[]{:S(2)}) collective-permute-start(bf16[264,1536]{1,0:T(8,128)(2,1)} %add.206.refs_3_), channel_id=1, source_target_pairs={{0,4},{4,0},{8,12},{12,8},{16,20},{20,16},{24,28},{28,24},{1,5},{5... | collective-permute-start | bytes 2433032 | tf_op jit(solution)/shard_map/ppermute | solution.py:61
  139.8 21.8 %collective-permute-start.28 = (bf16[256,1536]{1,0:T(8,128)(2,1)}, bf16[256,1536]{1,0:T(8,128)(2,1)}, u32[]{:S(2)}, u32[]{:S(2)}) collective-permute-start(bf16[256,1536]{1,0:T(8,128)(2,1)} %get-tuple-element.239.refs_0_.refs_6_), channel_id=1, source_target_pairs={{0,4},{4,0},{8,12},{12,8},{16,20},{20,16},{24,28},{28,24},{1,5},{5... | collective-permute-start | bytes 2359304 | tf_op jit(solution)/shard_map/ppermute | solution.py:61
  204.8 36.2 %collective-permute-start.36 = (bf16[296,1536]{1,0:T(8,128)(2,1)}, bf16[296,1536]{1,0:T(8,128)(2,1)S(1)}, u32[]{:S(2)}, u32[]{:S(2)}) collective-permute-start(bf16[296,1536]{1,0:T(8,128)(2,1)} %get-tuple-element.272), channel_id=1, source_target_pairs={{0,4},{4,0},{8,12},{12,8},{16,20},{20,16},{24,28},{28,24},{1,5},{5... | collective-permute-start | bytes 2727944 | tf_op jit(solution)/shard_map/ppermute | solution.py:61
  241.0 23.3 %collective-permute-start.37 = (bf16[296,1536]{1,0:T(8,128)(2,1)}, bf16[296,1536]{1,0:T(8,128)(2,1)S(1)}, u32[]{:S(2)}, u32[]{:S(2)}) collective-permute-start(bf16[296,1536]{1,0:T(8,128)(2,1)} %get-tuple-element.273), channel_id=1, source_target_pairs={{0,4},{4,0},{8,12},{12,8},{16,20},{20,16},{24,28},{28,24},{1,5},{5... | collective-permute-start | bytes 2727944 | tf_op jit(solution)/shard_map/ppermute | solution.py:61
  241.4 42.4 %collective-permute-start.39 = (bf16[296,1536]{1,0:T(8,128)(2,1)}, bf16[296,1536]{1,0:T(8,128)(2,1)S(1)}, u32[]{:S(2)}, u32[]{:S(2)}) collective-permute-start(bf16[296,1536]{1,0:T(8,128)(2,1)} %get-tuple-element.274), channel_id=1, source_target_pairs={{0,4},{4,0},{8,12},{12,8},{16,20},{20,16},{24,28},{28,24},{1,5},{5... | collective-permute-start | bytes 2727944 | tf_op jit(solution)/shard_map/ppermute | solution.py:61
  264.5 21.2 %collective-permute-start.38 = (bf16[296,1536]{1,0:T(8,128)(2,1)S(1)}, bf16[296,1536]{1,0:T(8,128)(2,1)S(1)}, u32[]{:S(2)}, u32[]{:S(2)}) collective-permute-start(bf16[296,1536]{1,0:T(8,128)(2,1)S(1)} %add_convert_fusion.3), channel_id=1, source_target_pairs={{0,8},{4,12},{24,16},{28,20},{1,9},{5,13},{25,17},{29,21},{2,10},{... | collective-permute-start | bytes 2727944 | tf_op jit(solution)/shard_map/ppermute | solution.py:85
  270.5 26.2 %collective-permute-start.42 = (bf16[296,1536]{1,0:T(8,128)(2,1)S(1)}, bf16[296,1536]{1,0:T(8,128)(2,1)S(1)}, u32[]{:S(2)}, u32[]{:S(2)}) collective-permute-start(bf16[296,1536]{1,0:T(8,128)(2,1)S(1)} %copy-done.54), channel_id=1, source_target_pairs={{0,4},{4,0},{8,12},{12,8},{16,20},{20,16},{24,28},{28,24},{1,5},{5... | collective-permute-start | bytes 2727944 | tf_op jit(solution)/shard_map/ppermute | solution.py:61
  316.1 23.8 %collective-permute-start.43 = (bf16[256,1536]{1,0:T(8,128)(2,1)}, bf16[256,1536]{1,0:T(8,128)(2,1)}, u32[]{:S(2)}, u32[]{:S(2)}) collective-permute-start(bf16[256,1536]{1,0:T(8,128)(2,1)} %get-tuple-element.288), channel_id=1, source_target_pairs={{0,4},{4,0},{8,12},{12,8},{16,20},{20,16},{24,28},{28,24},{1,5},{5... | collective-permute-start | bytes 2359304 | tf_op jit(solution)/shard_map/ppermute | solution.py:61
  316.1 31.2 %collective-permute-start.47 = (bf16[256,1536]{1,0:T(8,128)(2,1)}, bf16[256,1536]{1,0:T(8,128)(2,1)}, u32[]{:S(2)}, u32[]{:S(2)}) collective-permute-start(bf16[256,1536]{1,0:T(8,128)(2,1)} %get-tuple-element.302), channel_id=1, source_target_pairs={{0,4},{4,0},{8,12},{12,8},{16,20},{20,16},{24,28},{28,24},{1,5},{5... | collective-permute-start | bytes 2359304 | tf_op jit(solution)/shard_map/ppermute | solution.py:61
  347.3 35.2 %collective-permute-start.53 = (bf16[256,1536]{1,0:T(8,128)(2,1)}, bf16[256,1536]{1,0:T(8,128)(2,1)S(1)}, u32[]{:S(2)}, u32[]{:S(2)}) collective-permute-start(bf16[256,1536]{1,0:T(8,128)(2,1)} %get-tuple-element.309), channel_id=1, source_target_pairs={{0,4},{4,0},{8,12},{12,8},{16,20},{20,16},{24,28},{28,24},{1,5},{5... | collective-permute-start | bytes 2359304 | tf_op jit(solution)/shard_map/ppermute | solution.py:61
  358.9 23.6 %collective-permute-start.51 = (bf16[256,1536]{1,0:T(8,128)(2,1)}, bf16[256,1536]{1,0:T(8,128)(2,1)S(1)}, u32[]{:S(2)}, u32[]{:S(2)}) collective-permute-start(bf16[256,1536]{1,0:T(8,128)(2,1)} %add_convert_fusion.9), channel_id=1, source_target_pairs={{0,8},{4,12},{24,16},{28,20},{1,9},{5,13},{25,17},{29,21},{2,10},{... | collective-permute-start | bytes 2359304 | tf_op jit(solution)/shard_map/ppermute | solution.py:85
  399.7 28.2 %collective-permute-start.60 = (bf16[256,1536]{1,0:T(8,128)(2,1)}, bf16[256,1536]{1,0:T(8,128)(2,1)}, u32[]{:S(2)}, u32[]{:S(2)}) collective-permute-start(bf16[256,1536]{1,0:T(8,128)(2,1)} %add_convert_fusion.7), channel_id=1, source_target_pairs={{8,16},{12,20},{16,8},{20,12},{9,17},{13,21},{17,9},{21,13},{10,18... | collective-permute-start | bytes 2359304 | tf_op jit(solution)/shard_map/ppermute | solution.py:85
  402.1 25.8 %collective-permute-start.59 = (bf16[256,1536]{1,0:T(8,128)(2,1)S(1)}, bf16[256,1536]{1,0:T(8,128)(2,1)}, u32[]{:S(2)}, u32[]{:S(2)}) collective-permute-start(bf16[256,1536]{1,0:T(8,128)(2,1)S(1)} %add_convert_fusion.8), channel_id=1, source_target_pairs={{0,8},{4,12},{8,0},{12,4},{16,24},{20,28},{24,16},{28,20},{1,9},{5... | collective-permute-start | bytes 2359304 | tf_op jit(solution)/shard_map/ppermute | solution.py:61
  406.4 21.5 %collective-permute-start.56 = (bf16[16,8192]{1,0:T(8,128)(2,1)}, bf16[16,8192]{1,0:T(8,128)(2,1)S(1)}, u32[]{:S(2)}, u32[]{:S(2)}) collective-permute-start(bf16[16,8192]{1,0:T(8,128)(2,1)} %mix.1.refs_0_), channel_id=1, source_target_pairs={{0,8},{4,12},{8,0},{12,4},{16,24},{20,28},{24,16},{28,20},{1,9},{5... | collective-permute-start | bytes 786440 | tf_op jit(solution)/shard_map/ppermute | solution.py:61
  (114 other events, 1454.4 us)

commit v5 on v4

--- a/solution.py
+++ b/solution.py
@@ -246,8 +246,8 @@
 
 
 def project_kernel(info_ref, h_ref, t_ref, table_ref, cos_ref, sin_ref, *rest):
-    shards = rest[:-4]
-    qkv_ref, full_ref, up_ref, w_ref = rest[-4:]
+    shards = rest[:-3]
+    qkv_ref, w_ref, up_ref = rest[-3:]
     rows = shards[0].shape[0]
     group = info_ref[1]
 
@@ -256,7 +256,6 @@
         for m, shard in enumerate(shards):
             start = pl.multiple_of(info_ref[SLOTS_AT + m] * rows, rows)
             w_ref[pl.ds(start, rows), :] = shard[:, :LOCAL]
-        full_ref[...] = w_ref[...]
         up_ref[...] = jnp.zeros(up_ref.shape, BF)
         columns = lambda first, width: table_ref[
             0, :, pl.ds(pl.multiple_of(first + group * width, LANES), width)
@@ -295,7 +294,6 @@
             ]
             + [whole((rows, LOCAL + QG))] * count,
             out_specs=[per_block(LOCAL), whole((D, LOCAL)), whole((3 * RANK, LOCAL))],
-            scratch_shapes=[pltpu.VMEM((D, LOCAL), BF)],
         ),
         out_shape=[
             jax.ShapeDtypeStruct((length, LOCAL), BF),
@@ -377,6 +375,10 @@
             )
 
 
+def as_column(row):
+    return jnp.broadcast_to(row.astype(F32), (TURN, row.shape[1])).T[:, :1].astype(jnp.int32)
+
+
 def tile_bias(start_col, q_first, k_first):
     shape = (BLK, BLK)
     key = k_first + lax.broadcasted_iota(jnp.int32, shape, 1)
@@ -396,7 +398,7 @@
     def query_block(qb, unused):
         q_first = pl.multiple_of(qb * BLK, BLK)
         q_rows = pl.ds(pl.multiple_of(qb * tall, tall), tall)
-        start_col = start_ref[pl.ds(q_first, BLK), :]
+        start_col = as_column(start_ref[:, pl.ds(q_first, BLK)])
         queries = q_s[q_rows, :]
         m_s[...] = jnp.full(m_s.shape, NEG, F32)
         acc_s[...] = jnp.zeros(acc_s.shape, F32)
@@ -448,7 +450,7 @@
 VMEM_SPEC = pl.BlockSpec(memory_space=pltpu.VMEM)
 
 
-def attend(place, first, qkv, start_col, copies):
+def attend(place, first, qkv, start_row, copies):
     length = qkv.shape[0]
     tall = PAIRS * BLK
     return pl.pallas_call(
@@ -472,7 +474,7 @@
             flops=4 * length * length * QG, bytes_accessed=8 * length * QG, transcendentals=0
         ),
         name="attend",
-    )(place, first, qkv, start_col)
+    )(place, first, qkv, start_row)
 
 
 def attend_back_kernel(
@@ -503,7 +505,7 @@
     def query_block(qb, unused):
         q_first = pl.multiple_of(qb * BLK, BLK)
         q_rows = pl.ds(pl.multiple_of(qb * tall, tall), tall)
-        start_col = start_ref[pl.ds(q_first, BLK), :]
+        start_col = as_column(start_ref[:, pl.ds(q_first, BLK)])
         dq_s[...] = jnp.zeros(dq_s.shape, F32)
         product = do_s[q_rows, :].astype(F32) * o_s[q_rows, :].astype(F32)
         lse = lse_ref[q_rows, :]
@@ -553,7 +555,7 @@
         dqkv_ref[rows, QG + KG : LOCAL] = jnp.where(is_low, dv_s[0, at, :], dv_s[1, at, :]).astype(BF)
 
 
-def attend_back(place, first, qkv, start_col, out, lse, cosine, sine, d_out):
+def attend_back(place, first, qkv, start_row, out, lse, cosine, sine, d_out):
     length = qkv.shape[0]
     tall = PAIRS * BLK
     stacked = pltpu.VMEM((PAIRS * length, LANES), BF)
@@ -577,7 +579,7 @@
             flops=10 * length * length * QG, bytes_accessed=16 * length * QG, transcendentals=0
         ),
         name="attend_back",
-    )(place, first, qkv, start_col, out, lse, cosine, sine, *d_out)
+    )(place, first, qkv, start_row, out, lse, cosine, sine, *d_out)
 
 
 def expert_kernel(experts_all, ids_ref, h_refs, p_refs, wgu_ref, wd_ref, tables, y_refs, d_refs, scratch):
@@ -1035,12 +1037,14 @@
 
 
 def place_kernel(info_ref, *refs):
-    parts = refs[:2]
-    up_ref, down_ref, gu_ref, da_ref, db_ref, od_ref, ou_ref, gd_ref, sum_s = refs[2:]
-    sources = parts[0].shape[0]
+    up_ref, down_ref, gu_ref, da_ref, db_ref, od_ref, ou_ref, gd_ref, sum_s, parts, sems = refs[2:]
+    sources = parts.shape[1]
+    copies = start_copies(refs[:2], parts, sems)
     up_ref[...] = jnp.zeros(up_ref.shape, F32)
     down_ref[...] = jnp.zeros(down_ref.shape, F32)
     sum_s[...] = jnp.zeros(sum_s.shape, F32)
+    for copy in copies:
+        copy.wait()
     for j in range(GROUPS):
         group = info_ref[1] ^ j
         keys = lambda first: pl.ds(pl.multiple_of(first + group * KG, LANES), KG)
@@ -1049,7 +1053,7 @@
         early_at = 2 * LOCAL + 6 * QG + far * 6 * QG
         for m in range(sources):
             a = info_ref[SLOTS_AT + sources + m]
-            take = lambda first, width: parts[j % 2][m, :, first : first + width].astype(F32)
+            take = lambda first, width: parts[j % 2, m, :, first : first + width].astype(F32)
             up_ref[a, :, lanes_of(group)] += take(far * LOCAL, QG)
             up_ref[a, :, keys(QW)] += take(far * LOCAL + QG, KG)
             up_ref[a, :, keys(QW + KVW)] += take(far * LOCAL + QG + KG, KG)
@@ -1074,10 +1078,14 @@
     shapes += [(RANK, QW), (RANK, D), (2 * RANK, D)]
     return pl.pallas_call(
         place_kernel,
-        in_specs=[SMEM_SPEC] + [VMEM_SPEC] * 2,
+        in_specs=[SMEM_SPEC] + [pl.BlockSpec(memory_space=pl.ANY)] * 2,
         out_specs=[VMEM_SPEC] * len(shapes),
         out_shape=[jax.ShapeDtypeStruct((ADAPT,) + shape, F32) for shape in shapes],
-        scratch_shapes=[pltpu.VMEM((ADAPT, 6 * RANK, D), F32)],
+        scratch_shapes=[
+            pltpu.VMEM((ADAPT, 6 * RANK, D), F32),
+            pltpu.VMEM((2,) + near.shape, BF),
+            pltpu.SemaphoreType.DMA((2,)),
+        ],
         name="place_grads",
     )(info, near, far)
 
@@ -1169,7 +1177,7 @@
     angles = offset.astype(F32)[:, None] * frequency[None, :]
     cosine = jnp.cos(angles)
     sine = jnp.sin(angles) * jnp.where(lane < HEAD_DIM // 2, -1.0, 1.0)[None, :]
-    start_col = start[:, None]
+    start_row = start[None, :]
     adapter = adapter_ids[seq_index]
     slot_adapters = adapter_ids[seq_slots]
     info = jnp.concatenate(
@@ -1191,8 +1199,8 @@
     )
     down_a_t = jnp.swapaxes(down_a, 1, 2)
 
-    pack, start_col, cosine, sine, place, first, info, *moving_rows = cols.beside(
-        pack, start_col, cosine, sine, place, first, info, *moving_rows
+    pack, start_row, cosine, sine, place, first, info, *moving_rows = cols.beside(
+        pack, start_row, cosine, sine, place, first, info, *moving_rows
     )
     row_slots = gather_rest(own_rows, moving_rows, ctx_masks)
     all_rows = jnp.concatenate(row_slots, axis=0).astype(F32)
@@ -1208,7 +1216,7 @@
         *project(info, h_one, rank_qkv, qkv_up, cosine, sine, col_slots)
     )
     heads_out, lse, *pieces = packs.beside(
-        *outs.beside(*attend(place, first, qkv, start_col, copies))
+        *outs.beside(*attend(place, first, qkv, start_row, copies))
     )
     heads_here = packs.beside(
         *[swap(piece, "ctx", j * copies) if j else piece for j, piece in enumerate(pieces)]
@@ -1256,7 +1264,7 @@
     d_heads = y_sums.beside(*d_heads)
 
     (d_qkv,) = y_sums.beside(
-        attend_back(place, first, qkv, start_col, heads_out, lse, cosine, sine, d_heads)
+        attend_back(place, first, qkv, start_row, heads_out, lse, cosine, sine, d_heads)
     )
     d_rank_qkv, keep, sent = ranks_back(info, d_qkv, up_diag, rank_qkv, h_one, early)
 
@@ -1266,7 +1274,7 @@
         shared = add_low(shared, swap(shared, "ctx", mask))
         halves = jnp.concatenate([halves[:, : HALF - 12 * QG], shared], axis=1)
     halves, d_rank_qkv = lax.optimization_barrier((halves, d_rank_qkv))
-    arrived, *d_rows = together(
+    arrived, *d_rows = y_sums.beside(
         swap(halves, "ctx", 2 * copies),
         *inputs_back(ctx_count, d_qkv, d_rank_qkv, cols_all, qkv_down_sel),
     )
@@ -1275,7 +1283,7 @@
     far = add_low(d_rows[2], swap(d_rows[3], "ctx", copies))
     slots = []
     grads = Steps(gather_line(mix(halves, arrived), slots))
-    near, far = grads.join(y_sums, near, far)
+    near, far = grads.beside(near, far)
     d_h_one = near.astype(F32) + swap(far, "ctx", 2 * copies).astype(F32)
     features = own_rows.astype(F32)
     inv_one = lax.rsqrt(jnp.mean(features * features, axis=-1, keepdims=True) + NORM_EPS)

time: 481 us -> 473 us (0.983)
  starting transfers between devices: 88.4 us -> 96 us
  waiting for transfers between devices: 163 us -> 157 us
  other arithmetic: 37.4 us -> 32 us
  Pallas kernels: 164 us -> 159 us
    ppermute x48, waiting for transfers between devices: 113 us -> 104 us  [swap(): return lax.ppermute(block, axis, [(i, i ^ mask) for i in range(count)])]
    ppermute x48, starting transfers between devices: 48.4 us -> 56.5 us  [swap(): return lax.ppermute(block, axis, [(i, i ^ mask) for i in range(count)])]
where the time goes in v5:
time: 473 us; the launch traced here: 466 us
  Pallas kernels  159 us (34%)
  waiting for transfers between devices  157 us (33%)
  starting transfers between devices  96 us (20%)
  other arithmetic  32 us (7%)
  local copies, waits for them, and re-layouts  15.2 us (3%)
    ppermute x48, waiting for transfers between devices, swap(): return lax.ppermute(block, axis, [(i, i ^ mask) for i in range(count)])  104 us
    pallas_call x5, Pallas kernels, experts(): pl.pallas_call(body, grid_spec=pltpu.PrefetchScalarGridSpec(num_scalar_pr...  75.9 us
    ppermute x48, starting transfers between devices, swap(): return lax.ppermute(block, axis, [(i, i ^ mask) for i in range(count)])  56.5 us
    ppermute x24, waiting for transfers between devices, line_swap(): lax.ppermute(block, 'seq', [(2 * i + j, 2 * k + j) for i, k in pairs for...  53.3 us
    ppermute x24, starting transfers between devices, line_swap(): lax.ppermute(block, 'seq', [(2 * i + j, 2 * k + j) for i, k in pairs for...  39.6 us
    pallas_call x1, Pallas kernels, attend_back(): pl.pallas_call(attend_back_kernel, in_specs=[SMEM_SPEC, SMEM_SPEC] + [VME...  16.9 us
    pallas_call x1, Pallas kernels, attend(): pl.pallas_call(functools.partial(attend_kernel, copies), in_specs=[SMEM_S...  11.6 us
    pallas_call x1, Pallas kernels, middle_back(): pl.pallas_call(functools.partial(middle_kernel, count, len(terms), expert...  11.5 us
  transfers between devices with their start and end apart: 72, of which 30 were waited for; matrix products, arithmetic and copies ran while one was open for 8% of the time, Pallas kernels for 32%

profile of v5, /device:TPU:0, one launch (start us, length us, event | category | flops | bytes accessed | tf_op | source)
XLA Modules:
  0.0 465.6 jit_solution(4339654151192812399)
XLA Ops:
  26.4 7.6 %collective-permute-done.4 = bf16[192,1024]{1,0:T(8,128)(2,1)} collective-permute-done((bf16[192,1024]{1,0:T(8,128)(2,1)}, bf16[192,1024]{1,0:T(8,128)(2,1)}, u32[]{:S(2)}, u32[]{:S(2)}) %collective-permute-start.4) | collective-permute-done | bytes 393248 | tf_op jit(solution)/shard_map/ppermute | solution.py:85
  57.0 7.4 %collective-permute-done.14.rest_7_.refs_7_ = bf16[192,1024]{1,0:T(8,128)(2,1)S(1)} collective-permute-done((bf16[192,1024]{1,0:T(8,128)(2,1)S(1)}, bf16[192,1024]{1,0:T(8,128)(2,1)S(1)}, u32[]{:S(2)}, u32[]{:S(2)}) %collective-permute-start.14) | collective-permute-done | bytes 393248 | tf_op jit(solution)/shard_map/ppermute | solution.py:61
  69.6 8.8 %project.1 = (bf16[1024,640]{1,0:T(8,128)(2,1)}, bf16[1536,640]{1,0:T(8,128)(2,1)}, bf16[48,640]{1,0:T(8,128)(2,1)}) custom-call(s32[20]{0:T(128)} %concatenate.17.info_ref.ids_ref, bf16[1024,1536]{1,0:T(8,128)(2,1)} %copy-done.3, bf16[1024,48]{1,0:T(8,128)(2,1)} %convolution_convert_fusion.t_ref, bf16[8,16,2560]{2,1,0:T(8,128)(2,1)} %table_ref.1, ...), custom_call_target="tpu_custom_call" | custom-call | flops 2013265920 | bytes 4456448 | tf_op jit(solution)/shard_map/project/pallas_call | solution.py:283
  84.0 11.6 %attend.1 = (bf16[1024,384]{1,0:T(8,128)(2,1)}, f32[3072,128]{1,0:T(8,128)}, bf16[256,384]{1,0:T(8,128)(2,1)}, bf16[256,384]{1,0:T(8,128)(2,1)}, bf16[256,384]{1,0:T(8,128)(2,1)}, /*index=5*/bf16[256,384]{1,0:T(8,128)(2,1)}) custom-call(s32[8]{0:T(128)} %fusion.14.place_ref, s32[4]{0:T(128)} %and_select_fusion.first_ref, ...), custom_call_target="tpu_custom_call" | custom-call | flops 1610612736 | bytes 3145728 | tf_op jit(solution)/shard_map/attend/pallas_call | solution.py:456
  95.7 7.7 %collective-permute-done.16 = bf16[264,1536]{1,0:T(8,128)(2,1)} collective-permute-done((bf16[264,1536]{1,0:T(8,128)(2,1)S(1)}, bf16[264,1536]{1,0:T(8,128)(2,1)}, u32[]{:S(2)}, u32[]{:S(2)}) %collective-permute-start.16) | collective-permute-done | bytes 811040 | tf_op jit(solution)/shard_map/ppermute | solution.py:85
  118.2 6.7 %collective-permute-done.20 = bf16[264,1536]{1,0:T(8,128)(2,1)S(1)} collective-permute-done((bf16[264,1536]{1,0:T(8,128)(2,1)S(1)}, bf16[264,1536]{1,0:T(8,128)(2,1)S(1)}, u32[]{:S(2)}, u32[]{:S(2)}) %collective-permute-start.20) | collective-permute-done | bytes 811040 | tf_op jit(solution)/shard_map/ppermute | solution.py:85
  127.4 8.1 %project_out.1 = (bf16[256,1536]{1,0:T(8,128)(2,1)}, bf16[256,16]{1,0:T(8,128)(2,1)}, f32[256,1536]{1,0:T(8,128)}, bf16[256,1536]{1,0:T(8,128)(2,1)}) custom-call(s32[20]{0:T(128)} %concatenate.17.info_ref.ids_ref, bf16[256,1536]{1,0:T(8,128)(2,1)} %bitcast.44, f32[1,1536]{1,0:T(1,128)} %broadcast_in_dim.23.gain_ref.refs_7_, bf16[8,16,1536]{2,1,0:T(8,128)(2,1)} %bitcast.48, ...), custom_call_target="tpu_custom_call" | custom-call | flops 1207959552 | bytes 9437184 | tf_op jit(solution)/shard_map/project_out/pallas_call | solution.py:834
  142.5 13.8 %experts.5 = (bf16[256,1536]{1,0:T(8,128)(2,1)}, bf16[296,1536]{1,0:T(8,128)(2,1)}) custom-call(s32[20]{0:T(128)} %concatenate.17.info_ref.ids_ref, bf16[256,1536]{1,0:T(8,128)(2,1)} %get-tuple-element.239.refs_0_.refs_6_, bf16[264,1536]{1,0:T(8,128)(2,1)} %copy-done.7, bf16[2,1536,1024]{2,1,0:T(8,128)(2,1)} %refs_2_.3, bf16[2,512,1536]{2,1,0:T(8,128)(2,1)} %refs_3_.3, ...), custom_call_target="tpu_custom_call" | custom-call | flops 3221225472 | bytes 12582912 | tf_op jit(solution)/shard_map/experts/pallas_call | solution.py:722
  162.8 16.2 %experts.6 = (bf16[256,1536]{1,0:T(8,128)(2,1)}, bf16[256,1536]{1,0:T(8,128)(2,1)}, bf16[296,1536]{1,0:T(8,128)(2,1)}, bf16[296,1536]{1,0:T(8,128)(2,1)}) custom-call(s32[20]{0:T(128)} %concatenate.17.info_ref.ids_ref, bf16[256,1536]{1,0:T(8,128)(2,1)} %collective-permute-done.28.refs_0_, bf16[256,1536]{1,0:T(8,128)(2,1)} %collective-permute-done.26.refs_1_, ...), custom_call_target="tpu_custom_call" | custom-call | flops 6442450944 | bytes 15728640 | tf_op jit(solution)/shard_map/experts/pallas_call | solution.py:722
  183.5 16.1 %experts.7 = (bf16[256,1536]{1,0:T(8,128)(2,1)}, bf16[256,1536]{1,0:T(8,128)(2,1)}, bf16[296,1536]{1,0:T(8,128)(2,1)}, bf16[296,1536]{1,0:T(8,128)(2,1)}) custom-call(s32[20]{0:T(128)} %concatenate.17.info_ref.ids_ref, bf16[256,1536]{1,0:T(8,128)(2,1)} %collective-permute-done.32.refs_0_, bf16[256,1536]{1,0:T(8,128)(2,1)} %copy-done.36, ...), custom_call_target="tpu_custom_call" | custom-call | flops 6442450944 | bytes 15728640 | tf_op jit(solution)/shard_map/experts/pallas_call | solution.py:722
  203.3 16.0 %experts.8 = (bf16[256,1536]{1,0:T(8,128)(2,1)}, bf16[256,1536]{1,0:T(8,128)(2,1)}, bf16[296,1536]{1,0:T(8,128)(2,1)}, bf16[296,1536]{1,0:T(8,128)(2,1)}) custom-call(s32[20]{0:T(128)} %concatenate.17.info_ref.ids_ref, bf16[256,1536]{1,0:T(8,128)(2,1)} %copy-done.59, bf16[256,1536]{1,0:T(8,128)(2,1)} %copy-done.37, ...), custom_call_target="tpu_custom_call" | custom-call | flops 6442450944 | bytes 15728640 | tf_op jit(solution)/shard_map/experts/pallas_call | solution.py:722
  222.7 13.8 %experts.9 = (bf16[256,1536]{1,0:T(8,128)(2,1)}, bf16[296,1536]{1,0:T(8,128)(2,1)}) custom-call(s32[20]{0:T(128)} %concatenate.17.info_ref.ids_ref, bf16[256,1536]{1,0:T(8,128)(2,1)} %copy-done.30, bf16[264,1536]{1,0:T(8,128)(2,1)} %copy-done.28, bf16[2,1536,1024]{2,1,0:T(8,128)(2,1)} %refs_2_.3, bf16[2,512,1536]{2,1,0:T(8,128)(2,1)} %refs_3_.3, ...), custom_call_target="tpu_custom_call" | custom-call | flops 3221225472 | bytes 12582912 | tf_op jit(solution)/shard_map/experts/pallas_call | solution.py:722
  240.3 21.3 %collective-permute-done.37 = bf16[296,1536]{1,0:T(8,128)(2,1)S(1)} collective-permute-done((bf16[296,1536]{1,0:T(8,128)(2,1)}, bf16[296,1536]{1,0:T(8,128)(2,1)S(1)}, u32[]{:S(2)}, u32[]{:S(2)}) %collective-permute-start.37) | collective-permute-done | bytes 909344 | tf_op jit(solution)/shard_map/ppermute | solution.py:61
  261.9 6.7 %collective-permute-start.38 = (bf16[296,1536]{1,0:T(8,128)(2,1)S(1)}, bf16[296,1536]{1,0:T(8,128)(2,1)S(1)}, u32[]{:S(2)}, u32[]{:S(2)}) collective-permute-start(bf16[296,1536]{1,0:T(8,128)(2,1)S(1)} %add_convert_fusion.3), channel_id=1, source_target_pairs={{0,8},{4,12},{24,16},{28,20},{1,9},{5,13},{25,17},{29,21},{2,10},{... | collective-permute-start | bytes 2727944 | tf_op jit(solution)/shard_map/ppermute | solution.py:85
  269.3 11.9 %collective-permute-done.39 = bf16[296,1536]{1,0:T(8,128)(2,1)S(1)} collective-permute-done((bf16[296,1536]{1,0:T(8,128)(2,1)}, bf16[296,1536]{1,0:T(8,128)(2,1)S(1)}, u32[]{:S(2)}, u32[]{:S(2)}) %collective-permute-start.39) | collective-permute-done | bytes 909344 | tf_op jit(solution)/shard_map/ppermute | solution.py:61
  293.5 11.3 %collective-permute-done.40 = bf16[296,1536]{1,0:T(8,128)(2,1)S(1)} collective-permute-done((bf16[296,1536]{1,0:T(8,128)(2,1)S(1)}, bf16[296,1536]{1,0:T(8,128)(2,1)S(1)}, u32[]{:S(2)}, u32[]{:S(2)}) %collective-permute-start.40) | collective-permute-done | bytes 909344 | tf_op jit(solution)/shard_map/ppermute | solution.py:85
  306.2 6.9 %collective-permute-start.44 = (bf16[296,1536]{1,0:T(8,128)(2,1)S(1)}, bf16[296,1536]{1,0:T(8,128)(2,1)S(1)}, u32[]{:S(2)}, u32[]{:S(2)}) collective-permute-start(bf16[296,1536]{1,0:T(8,128)(2,1)S(1)} %add_convert_fusion.1), channel_id=1, source_target_pairs={{0,8},{4,12},{8,0},{12,4},{16,24},{20,28},{24,16},{28,20},{1,9},{5... | collective-permute-start | bytes 2727944 | tf_op jit(solution)/shard_map/ppermute | solution.py:61
  315.1 9.3 %collective-permute-done.44.refs_1_ = bf16[296,1536]{1,0:T(8,128)(2,1)S(1)} collective-permute-done((bf16[296,1536]{1,0:T(8,128)(2,1)S(1)}, bf16[296,1536]{1,0:T(8,128)(2,1)S(1)}, u32[]{:S(2)}, u32[]{:S(2)}) %collective-permute-start.44) | collective-permute-done | bytes 909344 | tf_op jit(solution)/shard_map/ppermute | solution.py:61
  325.3 11.5 %middle_back.1 = (f32[256,1536]{1,0:T(8,128)}, bf16[256,384]{1,0:T(8,128)(2,1)}, bf16[256,384]{1,0:T(8,128)(2,1)}, bf16[256,384]{1,0:T(8,128)(2,1)}, bf16[256,38...) custom-call(s32[20]{0:T(128)} %concatenate.17.info_ref.ids_ref, ...), custom_call_target="tpu_custom_call" | custom-call | flops 1207959552 | bytes 12582912 | tf_op jit(solution)/shard_map/middle_back/pallas_call | solution.py:915
  360.2 16.9 %attend_back.1.dqkv_ref = bf16[1024,640]{1,0:T(8,128)(2,1)} custom-call(s32[8]{0:T(128)} %fusion.14.place_ref, s32[4]{0:T(128)} %and_select_fusion.first_ref, bf16[1024,640]{1,0:T(8,128)(2,1)} %get-tuple-element.213.qkv_ref, s32[1,1024]{1,0:T(1,128)} %bitcast.65, bf16[1024,384]{1,0:T(8,128)(2,1)} %get-tuple-element.310.o_ref, ...), custom_call_target="tpu_custom_call" | custom-call | flops 4026531840 | bytes 6291456 | tf_op jit(solution)/shard_map/attend_back/pallas_call | solution.py:562
  383.7 6.9 %collective-permute-start.55 = (bf16[256,1536]{1,0:T(8,128)(2,1)S(1)}, bf16[256,1536]{1,0:T(8,128)(2,1)S(1)}, u32[]{:S(2)}, u32[]{:S(2)}) collective-permute-start(bf16[256,1536]{1,0:T(8,128)(2,1)S(1)} %add_convert_fusion.8), channel_id=1, source_target_pairs={{0,8},{4,12},{8,0},{12,4},{16,24},{20,28},{24,16},{28,20},{1,9},{5... | collective-permute-start | bytes 2359304 | tf_op jit(solution)/shard_map/ppermute | solution.py:61
  392.9 7.7 %inputs_back.1 = (bf16[256,1536]{1,0:T(8,128)(2,1)}, bf16[256,1536]{1,0:T(8,128)(2,1)}, bf16[256,1536]{1,0:T(8,128)(2,1)}, bf16[256,1536]{1,0:T(8,128)(2,1)}) custom-call(bf16[1024,640]{1,0:T(8,128)(2,1)} %attend_back.1.dqkv_ref, bf16[1024,48]{1,0:T(8,128)(2,1)} %get-tuple-element.331.rank_ref, bf16[1536,640]{1,0:T(8,128)(2,1)} %get-tuple-element.332.w_ref, ...), custom_call_target="tpu_custom_call" | custom-call | flops 2013265920 | bytes 8912896 | tf_op jit(solution)/shard_map/inputs_back/pallas_call | solution.py:1021
  400.7 8.2 %collective-permute-done.55 = bf16[256,1536]{1,0:T(8,128)(2,1)S(1)} collective-permute-done((bf16[256,1536]{1,0:T(8,128)(2,1)S(1)}, bf16[256,1536]{1,0:T(8,128)(2,1)S(1)}, u32[]{:S(2)}, u32[]{:S(2)}) %collective-permute-start.55) | collective-permute-done | bytes 786464 | tf_op jit(solution)/shard_map/ppermute | solution.py:61
  427.3 6.7 %collective-permute-done.65 = bf16[16,8192]{1,0:T(8,128)(2,1)S(1)} collective-permute-done((bf16[16,8192]{1,0:T(8,128)(2,1)S(1)}, bf16[16,8192]{1,0:T(8,128)(2,1)S(1)}, u32[]{:S(2)}, u32[]{:S(2)}) %collective-permute-start.65) | collective-permute-done | bytes 262176 | tf_op jit(solution)/shard_map/ppermute | solution.py:85
  (336 shorter events, 202.3 us)
Async XLA Ops:
  8.7 25.3 %collective-permute-start.6 = (bf16[256,1536]{1,0:T(8,128)(2,1)}, bf16[256,1536]{1,0:T(8,128)(2,1)}, u32[]{:S(2)}, u32[]{:S(2)}) collective-permute-start(bf16[256,1536]{1,0:T(8,128)(2,1)} %bitcast.42), channel_id=1, source_target_pairs={{0,2},{1,3},{2,0},{3,1},{4,6},{5,7},{6,4},{7,5},{8,10},{9,11},{10,... | collective-permute-start | bytes 2359304 | tf_op jit(solution)/shard_map/ppermute | solution.py:61
  10.2 23.8 %collective-permute-start.7 = (bf16[256,1536]{1,0:T(8,128)(2,1)}, bf16[256,1536]{1,0:T(8,128)(2,1)}, u32[]{:S(2)}, u32[]{:S(2)}) collective-permute-start(bf16[256,1536]{1,0:T(8,128)(2,1)} %bitcast.43), channel_id=1, source_target_pairs={{0,1},{1,0},{2,3},{3,2},{4,5},{5,4},{6,7},{7,6},{8,9},{9,8},{10,11... | collective-permute-start | bytes 2359304 | tf_op jit(solution)/shard_map/ppermute | solution.py:61
  52.9 25.5 %collective-permute-start.11 = (bf16[264,1536]{1,0:T(8,128)(2,1)S(1)}, bf16[264,1536]{1,0:T(8,128)(2,1)}, u32[]{:S(2)}, u32[]{:S(2)}) collective-permute-start(bf16[264,1536]{1,0:T(8,128)(2,1)S(1)} %pad_maximum_fusion.1.refs_1_.refs_4_), channel_id=1, source_target_pairs={{0,8},{4,12},{8,0},{12,4},{16,24},{20,28},{24,16},{28,20},{1,9},{5... | collective-permute-start | bytes 2433032 | tf_op jit(solution)/shard_map/ppermute | solution.py:61
  54.7 23.6 %collective-permute-start.12 = (bf16[264,1536]{1,0:T(8,128)(2,1)S(1)}, bf16[264,1536]{1,0:T(8,128)(2,1)S(1)}, u32[]{:S(2)}, u32[]{:S(2)}) collective-permute-start(bf16[264,1536]{1,0:T(8,128)(2,1)S(1)} %pad_maximum_fusion.1.refs_1_.refs_4_), channel_id=1, source_target_pairs={{8,16},{12,20},{16,8},{20,12},{9,17},{13,21},{17,9},{21,13},{10,18... | collective-permute-start | bytes 2433032 | tf_op jit(solution)/shard_map/ppermute | solution.py:85
  55.4 25.1 %collective-permute-start.13 = (bf16[264,1536]{1,0:T(8,128)(2,1)S(1)}, bf16[264,1536]{1,0:T(8,128)(2,1)}, u32[]{:S(2)}, u32[]{:S(2)}) collective-permute-start(bf16[264,1536]{1,0:T(8,128)(2,1)S(1)} %pad_maximum_fusion.1.refs_1_.refs_4_), channel_id=1, source_target_pairs={{0,4},{4,0},{8,12},{12,8},{16,20},{20,16},{24,28},{28,24},{1,5},{5... | collective-permute-start | bytes 2433032 | tf_op jit(solution)/shard_map/ppermute | solution.py:61
  68.1 27.5 %collective-permute-start.18 = (bf16[1536,384]{1,0:T(8,128)(2,1)}, bf16[1536,384]{1,0:T(8,128)(2,1)S(1)}, u32[]{:S(2)}, u32[]{:S(2)}) collective-permute-start(bf16[1536,384]{1,0:T(8,128)(2,1)} %order_rows.1.refs_4_.refs_13_), channel_id=1, source_target_pairs={{0,2},{1,3},{2,0},{3,1},{4,6},{5,7},{6,4},{7,5},{8,10},{9,11},{10,... | collective-permute-start | bytes 3538952 | tf_op jit(solution)/shard_map/ppermute | solution.py:61
  69.6 26.1 %collective-permute-start.19 = (bf16[1536,384]{1,0:T(8,128)(2,1)}, bf16[1536,384]{1,0:T(8,128)(2,1)}, u32[]{:S(2)}, u32[]{:S(2)}) collective-permute-start(bf16[1536,384]{1,0:T(8,128)(2,1)} %order_rows.1.refs_4_.refs_13_), channel_id=1, source_target_pairs={{0,1},{1,0},{2,3},{3,2},{4,5},{5,4},{6,7},{7,6},{8,9},{9,8},{10,11... | collective-permute-start | bytes 3538952 | tf_op jit(solution)/shard_map/ppermute | solution.py:61
  82.2 21.3 %collective-permute-start.16 = (bf16[264,1536]{1,0:T(8,128)(2,1)S(1)}, bf16[264,1536]{1,0:T(8,128)(2,1)}, u32[]{:S(2)}, u32[]{:S(2)}) collective-permute-start(bf16[264,1536]{1,0:T(8,128)(2,1)S(1)} %collective-permute-done.12), channel_id=1, source_target_pairs={{8,0},{12,4},{16,24},{20,28},{9,1},{13,5},{17,25},{21,29},{10,2},{... | collective-permute-start | bytes 2433032 | tf_op jit(solution)/shard_map/ppermute | solution.py:85
  95.6 30.8 %collective-permute-start.25 = (bf16[1536,384]{1,0:T(8,128)(2,1)S(1)}, bf16[1536,384]{1,0:T(8,128)(2,1)S(1)}, u32[]{:S(2)}, u32[]{:S(2)}) collective-permute-start(bf16[1536,384]{1,0:T(8,128)(2,1)S(1)} %collective-permute-done.18.refs_6_.refs_15_), channel_id=1, source_target_pairs={{0,1},{1,0},{2,3},{3,2},{4,5},{5,4},{6,7},{7,6},{8,9},{9,8},{10,11... | collective-permute-start | bytes 3538952 | tf_op jit(solution)/shard_map/ppermute | solution.py:61
  126.0 30.2 %collective-permute-start.29 = (bf16[264,1536]{1,0:T(8,128)(2,1)}, bf16[264,1536]{1,0:T(8,128)(2,1)S(1)}, u32[]{:S(2)}, u32[]{:S(2)}) collective-permute-start(bf16[264,1536]{1,0:T(8,128)(2,1)} %add.206.refs_3_), channel_id=1, source_target_pairs={{0,4},{4,0},{8,12},{12,8},{16,20},{20,16},{24,28},{28,24},{1,5},{5... | collective-permute-start | bytes 2433032 | tf_op jit(solution)/shard_map/ppermute | solution.py:61
  135.6 20.7 %collective-permute-start.26 = (bf16[256,1536]{1,0:T(8,128)(2,1)}, bf16[256,1536]{1,0:T(8,128)(2,1)}, u32[]{:S(2)}, u32[]{:S(2)}) collective-permute-start(bf16[256,1536]{1,0:T(8,128)(2,1)} %get-tuple-element.239.refs_0_.refs_6_), channel_id=1, source_target_pairs={{0,8},{4,12},{8,0},{12,4},{16,24},{20,28},{24,16},{28,20},{1,9},{5... | collective-permute-start | bytes 2359304 | tf_op jit(solution)/shard_map/ppermute | solution.py:61
  138.5 21.5 %collective-permute-start.28 = (bf16[256,1536]{1,0:T(8,128)(2,1)}, bf16[256,1536]{1,0:T(8,128)(2,1)}, u32[]{:S(2)}, u32[]{:S(2)}) collective-permute-start(bf16[256,1536]{1,0:T(8,128)(2,1)} %get-tuple-element.239.refs_0_.refs_6_), channel_id=1, source_target_pairs={{0,4},{4,0},{8,12},{12,8},{16,20},{20,16},{24,28},{28,24},{1,5},{5... | collective-permute-start | bytes 2359304 | tf_op jit(solution)/shard_map/ppermute | solution.py:61
  201.2 20.5 %collective-permute-start.35 = (bf16[256,1536]{1,0:T(8,128)(2,1)S(1)}, bf16[256,1536]{1,0:T(8,128)(2,1)S(1)}, u32[]{:S(2)}, u32[]{:S(2)}) collective-permute-start(bf16[256,1536]{1,0:T(8,128)(2,1)S(1)} %add.208.refs_1_), channel_id=1, source_target_pairs={{0,4},{4,0},{8,12},{12,8},{16,20},{20,16},{24,28},{28,24},{1,5},{5... | collective-permute-start | bytes 2359304 | tf_op jit(solution)/shard_map/ppermute | solution.py:61
  202.7 35.5 %collective-permute-start.36 = (bf16[296,1536]{1,0:T(8,128)(2,1)}, bf16[296,1536]{1,0:T(8,128)(2,1)S(1)}, u32[]{:S(2)}, u32[]{:S(2)}) collective-permute-start(bf16[296,1536]{1,0:T(8,128)(2,1)} %get-tuple-element.272), channel_id=1, source_target_pairs={{0,4},{4,0},{8,12},{12,8},{16,20},{20,16},{24,28},{28,24},{1,5},{5... | collective-permute-start | bytes 2727944 | tf_op jit(solution)/shard_map/ppermute | solution.py:61
  238.3 23.3 %collective-permute-start.37 = (bf16[296,1536]{1,0:T(8,128)(2,1)}, bf16[296,1536]{1,0:T(8,128)(2,1)S(1)}, u32[]{:S(2)}, u32[]{:S(2)}) collective-permute-start(bf16[296,1536]{1,0:T(8,128)(2,1)} %get-tuple-element.273), channel_id=1, source_target_pairs={{0,4},{4,0},{8,12},{12,8},{16,20},{20,16},{24,28},{28,24},{1,5},{5... | collective-permute-start | bytes 2727944 | tf_op jit(solution)/shard_map/ppermute | solution.py:61
  239.7 41.4 %collective-permute-start.39 = (bf16[296,1536]{1,0:T(8,128)(2,1)}, bf16[296,1536]{1,0:T(8,128)(2,1)S(1)}, u32[]{:S(2)}, u32[]{:S(2)}) collective-permute-start(bf16[296,1536]{1,0:T(8,128)(2,1)} %get-tuple-element.274), channel_id=1, source_target_pairs={{0,4},{4,0},{8,12},{12,8},{16,20},{20,16},{24,28},{28,24},{1,5},{5... | collective-permute-start | bytes 2727944 | tf_op jit(solution)/shard_map/ppermute | solution.py:61
  261.9 22.2 %collective-permute-start.38 = (bf16[296,1536]{1,0:T(8,128)(2,1)S(1)}, bf16[296,1536]{1,0:T(8,128)(2,1)S(1)}, u32[]{:S(2)}, u32[]{:S(2)}) collective-permute-start(bf16[296,1536]{1,0:T(8,128)(2,1)S(1)} %add_convert_fusion.3), channel_id=1, source_target_pairs={{0,8},{4,12},{24,16},{28,20},{1,9},{5,13},{25,17},{29,21},{2,10},{... | collective-permute-start | bytes 2727944 | tf_op jit(solution)/shard_map/ppermute | solution.py:85
  268.6 24.9 %collective-permute-start.42 = (bf16[296,1536]{1,0:T(8,128)(2,1)S(1)}, bf16[296,1536]{1,0:T(8,128)(2,1)S(1)}, u32[]{:S(2)}, u32[]{:S(2)}) collective-permute-start(bf16[296,1536]{1,0:T(8,128)(2,1)S(1)} %copy-done.58), channel_id=1, source_target_pairs={{0,4},{4,0},{8,12},{12,8},{16,20},{20,16},{24,28},{28,24},{1,5},{5... | collective-permute-start | bytes 2727944 | tf_op jit(solution)/shard_map/ppermute | solution.py:61
  313.1 23.8 %collective-permute-start.43 = (bf16[256,1536]{1,0:T(8,128)(2,1)}, bf16[256,1536]{1,0:T(8,128)(2,1)}, u32[]{:S(2)}, u32[]{:S(2)}) collective-permute-start(bf16[256,1536]{1,0:T(8,128)(2,1)} %get-tuple-element.288), channel_id=1, source_target_pairs={{0,4},{4,0},{8,12},{12,8},{16,20},{20,16},{24,28},{28,24},{1,5},{5... | collective-permute-start | bytes 2359304 | tf_op jit(solution)/shard_map/ppermute | solution.py:61
  313.7 30.6 %collective-permute-start.47 = (bf16[256,1536]{1,0:T(8,128)(2,1)}, bf16[256,1536]{1,0:T(8,128)(2,1)}, u32[]{:S(2)}, u32[]{:S(2)}) collective-permute-start(bf16[256,1536]{1,0:T(8,128)(2,1)} %get-tuple-element.302), channel_id=1, source_target_pairs={{0,4},{4,0},{8,12},{12,8},{16,20},{20,16},{24,28},{28,24},{1,5},{5... | collective-permute-start | bytes 2359304 | tf_op jit(solution)/shard_map/ppermute | solution.py:61
  344.3 32.8 %collective-permute-start.53 = (bf16[256,1536]{1,0:T(8,128)(2,1)}, bf16[256,1536]{1,0:T(8,128)(2,1)S(1)}, u32[]{:S(2)}, u32[]{:S(2)}) collective-permute-start(bf16[256,1536]{1,0:T(8,128)(2,1)} %get-tuple-element.309), channel_id=1, source_target_pairs={{0,4},{4,0},{8,12},{12,8},{16,20},{20,16},{24,28},{28,24},{1,5},{5... | collective-permute-start | bytes 2359304 | tf_op jit(solution)/shard_map/ppermute | solution.py:61
  356.5 20.6 %collective-permute-start.51 = (bf16[256,1536]{1,0:T(8,128)(2,1)}, bf16[256,1536]{1,0:T(8,128)(2,1)S(1)}, u32[]{:S(2)}, u32[]{:S(2)}) collective-permute-start(bf16[256,1536]{1,0:T(8,128)(2,1)} %add_convert_fusion.9), channel_id=1, source_target_pairs={{0,8},{4,12},{24,16},{28,20},{1,9},{5,13},{25,17},{29,21},{2,10},{... | collective-permute-start | bytes 2359304 | tf_op jit(solution)/shard_map/ppermute | solution.py:85
  359.5 41.1 %collective-permute-start.57 = (bf16[256,1536]{1,0:T(8,128)(2,1)}, bf16[256,1536]{1,0:T(8,128)(2,1)}, u32[]{:S(2)}, u32[]{:S(2)}) collective-permute-start(bf16[256,1536]{1,0:T(8,128)(2,1)} %get-tuple-element.330), channel_id=1, source_target_pairs={{0,4},{4,0},{8,12},{12,8},{16,20},{20,16},{24,28},{28,24},{1,5},{5... | collective-permute-start | bytes 2359304 | tf_op jit(solution)/shard_map/ppermute | solution.py:61
  383.7 25.1 %collective-permute-start.55 = (bf16[256,1536]{1,0:T(8,128)(2,1)S(1)}, bf16[256,1536]{1,0:T(8,128)(2,1)S(1)}, u32[]{:S(2)}, u32[]{:S(2)}) collective-permute-start(bf16[256,1536]{1,0:T(8,128)(2,1)S(1)} %add_convert_fusion.8), channel_id=1, source_target_pairs={{0,8},{4,12},{8,0},{12,4},{16,24},{20,28},{24,16},{28,20},{1,9},{5... | collective-permute-start | bytes 2359304 | tf_op jit(solution)/shard_map/ppermute | solution.py:61
  (117 other events, 1429.5 us)

commit v6 on v5

--- a/solution.py
+++ b/solution.py
@@ -764,17 +764,18 @@
 
 
 def join_kernel(*refs):
-    parts, out_ref = refs[:-1], refs[-1]
-    for m, part in enumerate(parts):
-        out_ref[m] = part[...]
+    parts, (out_ref, sems) = refs[:-2], refs[-2:]
+    for copy in start_copies(parts, out_ref, sems):
+        copy.wait()
 
 
 def join(parts):
     return pl.pallas_call(
         join_kernel,
-        in_specs=[VMEM_SPEC] * len(parts),
+        in_specs=[pl.BlockSpec(memory_space=pl.ANY)] * len(parts),
         out_specs=VMEM_SPEC,
         out_shape=jax.ShapeDtypeStruct((len(parts),) + parts[0].shape, parts[0].dtype),
+        scratch_shapes=[pltpu.SemaphoreType.DMA((len(parts),))],
         name="join",
     )(*parts)
 
@@ -942,7 +943,8 @@
 
 
 def ranks_kernel(info_ref, dqkv_ref, up_ref, t_ref, h_ref, *refs):
-    early_refs, (rank_ref, keep_ref, send_ref) = refs[:GROUPS], refs[GROUPS:]
+    early_refs, (rank_ref, keep_ref, send_ref, h_s, sems) = refs[:GROUPS], refs[GROUPS:]
+    (rows,) = start_copies([h_ref], h_s, sems)
     d_qkv = dqkv_ref[...]
     d_rank = dot_nt(d_qkv, up_ref[...]).astype(BF)
     rank_ref[...] = d_rank
@@ -951,9 +953,10 @@
     keep_ref[:, QG : QG + KG] = grad[RANK : 2 * RANK, QG : QG + KG].astype(BF)
     keep_ref[:, QG + KG : LOCAL] = grad[2 * RANK :, QG + KG :].astype(BF)
     send_ref[:, :LOCAL] = jnp.zeros((RANK, LOCAL), BF)
+    rows.wait()
     for j in range(GROUPS):
         target = send_ref if j % 2 else keep_ref
-        down = dot_tn(d_rank, h_ref[:, lanes_of(info_ref[1] ^ j)]).astype(BF)
+        down = dot_tn(d_rank, h_s[0, :, lanes_of(info_ref[1] ^ j)]).astype(BF)
         first = LOCAL + (j // 2) * 3 * QG
         for i in range(3):
             target[:, first + i * QG : first + (i + 1) * QG] = down[i * RANK : (i + 1) * RANK]
@@ -969,8 +972,12 @@
     length = d_qkv.shape[0]
     return pl.pallas_call(
         ranks_kernel,
-        in_specs=[SMEM_SPEC] + [VMEM_SPEC] * (4 + GROUPS),
+        in_specs=[SMEM_SPEC]
+        + [VMEM_SPEC] * 3
+        + [pl.BlockSpec(memory_space=pl.ANY)]
+        + [VMEM_SPEC] * GROUPS,
         out_specs=[VMEM_SPEC] * 3,
+        scratch_shapes=[pltpu.VMEM((1,) + h_one.shape, BF), pltpu.SemaphoreType.DMA((1,))],
         out_shape=[
             jax.ShapeDtypeStruct((length, 3 * RANK), BF),
             jax.ShapeDtypeStruct((RANK, HALF), BF),
@@ -1003,8 +1010,8 @@
     )(near, far)
 
 
-def inputs_kernel(dqkv_ref, rank_ref, w_ref, down_ref, *rows_refs):
-    rows = dot_nt(dqkv_ref[...], w_ref[...]) + dot_nt(rank_ref[...], down_ref[...])
+def inputs_kernel(info_ref, dqkv_ref, rank_ref, w_ref, down_ref, *rows_refs):
+    rows = dot_nt(dqkv_ref[...], w_ref[...]) + dot(rank_ref[...], down_ref[0])
     rows = rows.astype(BF)
     for m, ref in enumerate(rows_refs):
 
@@ -1013,36 +1020,38 @@
             ref[...] = rows
 
 
-def inputs_back(count, d_qkv, d_rank, cols_all, down_sel):
+def inputs_back(info, count, d_qkv, d_rank, cols_all, down_t):
     length = d_qkv.shape[0]
     tokens = length // count
-    per_block = lambda width: pl.BlockSpec((tokens, width), lambda i: (i, 0))
-    whole = lambda shape: pl.BlockSpec(shape, lambda i: (0, 0))
+    per_block = lambda width: pl.BlockSpec((tokens, width), lambda i, info: (i, 0))
+    whole = lambda shape: pl.BlockSpec(shape, lambda i, info: (0, 0))
     return pl.pallas_call(
         inputs_kernel,
-        grid=(count,),
-        in_specs=[
-            per_block(LOCAL),
-            per_block(3 * RANK),
-            whole((D, LOCAL)),
-            whole((D, 3 * RANK)),
-        ],
-        out_specs=[whole((tokens, D))] * count,
+        grid_spec=pltpu.PrefetchScalarGridSpec(
+            num_scalar_prefetch=1,
+            grid=(count,),
+            in_specs=[
+                per_block(LOCAL),
+                per_block(3 * RANK),
+                whole((D, LOCAL)),
+                by_adapter(down_t),
+            ],
+            out_specs=[whole((tokens, D))] * count,
+        ),
         out_shape=[jax.ShapeDtypeStruct((tokens, D), BF)] * count,
         cost_estimate=pl.CostEstimate(
             flops=2 * length * D * LOCAL, bytes_accessed=4 * length * (D + LOCAL), transcendentals=0
         ),
         name="inputs_back",
-    )(d_qkv, d_rank, cols_all, down_sel)
+    )(info, d_qkv, d_rank, cols_all, down_t)
 
 
 def place_kernel(info_ref, *refs):
     up_ref, down_ref, gu_ref, da_ref, db_ref, od_ref, ou_ref, gd_ref, sum_s, parts, sems = refs[2:]
     sources = parts.shape[1]
     copies = start_copies(refs[:2], parts, sems)
-    up_ref[...] = jnp.zeros(up_ref.shape, F32)
-    down_ref[...] = jnp.zeros(down_ref.shape, F32)
-    sum_s[...] = jnp.zeros(sum_s.shape, F32)
+    for ref in (up_ref, down_ref, db_ref, od_ref, ou_ref, gd_ref, sum_s):
+        ref[...] = jnp.zeros(ref.shape, F32)
     for copy in copies:
         copy.wait()
     for j in range(GROUPS):
@@ -1060,17 +1069,13 @@
             for i in range(3):
                 at = slice(i * RANK, (i + 1) * RANK)
                 down_ref[a, at, lanes_of(group)] += take(down_at + i * QG, QG)
-            for i in range(6):
-                at = slice(i * RANK, (i + 1) * RANK)
-                sum_s[a, at, lanes_of(group)] += take(early_at + i * QG, QG)
+            for i, ref in enumerate((sum_s, db_ref, od_ref, ou_ref, gd_ref, gd_ref)):
+                at = slice(RANK, 2 * RANK) if i == 5 else slice(0, RANK)
+                ref[a, at, lanes_of(group)] += take(early_at + i * QG, QG)
     for a in range(ADAPT):
-        gu_ref[a, 0] = sum_s[a, :RANK, :FF]
-        gu_ref[a, 1] = sum_s[a, :RANK, FF : 2 * FF]
-        da_ref[a] = sum_s[a, :RANK, 2 * FF :]
-        db_ref[a] = sum_s[a, RANK : 2 * RANK]
-        od_ref[a] = sum_s[a, 2 * RANK : 3 * RANK]
-        ou_ref[a] = sum_s[a, 3 * RANK : 4 * RANK]
-        gd_ref[a] = sum_s[a, 4 * RANK :]
+        gu_ref[a, 0] = sum_s[a, :, :FF]
+        gu_ref[a, 1] = sum_s[a, :, FF : 2 * FF]
+        da_ref[a] = sum_s[a, :, 2 * FF :]
 
 
 def place_grads(info, near, far):
@@ -1082,7 +1087,7 @@
         out_specs=[VMEM_SPEC] * len(shapes),
         out_shape=[jax.ShapeDtypeStruct((ADAPT,) + shape, F32) for shape in shapes],
         scratch_shapes=[
-            pltpu.VMEM((ADAPT, 6 * RANK, D), F32),
+            pltpu.VMEM((ADAPT, RANK, D), F32),
             pltpu.VMEM((2,) + near.shape, BF),
             pltpu.SemaphoreType.DMA((2,)),
         ],
@@ -1276,7 +1281,7 @@
     halves, d_rank_qkv = lax.optimization_barrier((halves, d_rank_qkv))
     arrived, *d_rows = y_sums.beside(
         swap(halves, "ctx", 2 * copies),
-        *inputs_back(ctx_count, d_qkv, d_rank_qkv, cols_all, qkv_down_sel),
+        *inputs_back(info, ctx_count, d_qkv, d_rank_qkv, cols_all, jnp.swapaxes(qkv_down, 1, 2)),
     )
     d_rows = d_rows[::copies]
     near = add_low(d_rows[0], swap(d_rows[1], "ctx", copies))

time: 473 us -> 471 us (level)
  transfers between devices with their start and end apart: 72 -> 72, of which waited for: 30 -> 30; matrix products, arithmetic and copies ran while one was open for 8% -> 7% of each run, Pallas kernels for 32% -> 33%
where the time goes in v6:
time: 471 us; the launch traced here: 461 us
  Pallas kernels  160 us (34%)
  waiting for transfers between devices  156 us (33%)
  starting transfers between devices  93.6 us (20%)
  other arithmetic  29.6 us (6%)
  local copies, waits for them, and re-layouts  15 us (3%)
    ppermute x48, waiting for transfers between devices, swap(): return lax.ppermute(block, axis, [(i, i ^ mask) for i in range(count)])  106 us
    pallas_call x5, Pallas kernels, experts(): pl.pallas_call(body, grid_spec=pltpu.PrefetchScalarGridSpec(num_scalar_pr...  76 us
    ppermute x48, starting transfers between devices, swap(): return lax.ppermute(block, axis, [(i, i ^ mask) for i in range(count)])  53.5 us
    ppermute x24, waiting for transfers between devices, line_swap(): lax.ppermute(block, 'seq', [(2 * i + j, 2 * k + j) for i, k in pairs for...  50.3 us
    ppermute x24, starting transfers between devices, line_swap(): lax.ppermute(block, 'seq', [(2 * i + j, 2 * k + j) for i, k in pairs for...  40 us
    pallas_call x1, Pallas kernels, attend_back(): pl.pallas_call(attend_back_kernel, in_specs=[SMEM_SPEC, SMEM_SPEC] + [VME...  16.9 us
    pallas_call x1, Pallas kernels, attend(): pl.pallas_call(functools.partial(attend_kernel, copies), in_specs=[SMEM_S...  11.6 us
    pallas_call x1, Pallas kernels, middle_back(): pl.pallas_call(functools.partial(middle_kernel, count, len(terms), expert...  11.5 us
  transfers between devices with their start and end apart: 72, of which 30 were waited for; matrix products, arithmetic and copies ran while one was open for 7% of the time, Pallas kernels for 33%

profile of v6, /device:TPU:0, one launch (start us, length us, event | category | flops | bytes accessed | tf_op | source)
XLA Modules:
  0.0 461.5 jit_solution(5682942787210732437)
XLA Ops:
  26.2 7.7 %collective-permute-done.4 = bf16[192,1024]{1,0:T(8,128)(2,1)} collective-permute-done((bf16[192,1024]{1,0:T(8,128)(2,1)}, bf16[192,1024]{1,0:T(8,128)(2,1)}, u32[]{:S(2)}, u32[]{:S(2)}) %collective-permute-start.4) | collective-permute-done | bytes 393248 | tf_op jit(solution)/shard_map/ppermute | solution.py:85
  56.8 7.4 %collective-permute-done.14.rest_7_.refs_7_ = bf16[192,1024]{1,0:T(8,128)(2,1)S(1)} collective-permute-done((bf16[192,1024]{1,0:T(8,128)(2,1)S(1)}, bf16[192,1024]{1,0:T(8,128)(2,1)S(1)}, u32[]{:S(2)}, u32[]{:S(2)}) %collective-permute-start.14) | collective-permute-done | bytes 393248 | tf_op jit(solution)/shard_map/ppermute | solution.py:61
  69.4 8.8 %project.1 = (bf16[1024,640]{1,0:T(8,128)(2,1)}, bf16[1536,640]{1,0:T(8,128)(2,1)}, bf16[48,640]{1,0:T(8,128)(2,1)}) custom-call(s32[20]{0:T(128)} %concatenate.17.info_ref.ids_ref, bf16[1024,1536]{1,0:T(8,128)(2,1)} %copy-done.1, bf16[1024,48]{1,0:T(8,128)(2,1)} %convolution_convert_fusion.t_ref, bf16[8,16,2560]{2,1,0:T(8,128)(2,1)} %table_ref.1, ...), custom_call_target="tpu_custom_call" | custom-call | flops 2013265920 | bytes 4456448 | tf_op jit(solution)/shard_map/project/pallas_call | solution.py:283
  83.8 11.6 %attend.1 = (bf16[1024,384]{1,0:T(8,128)(2,1)}, f32[3072,128]{1,0:T(8,128)}, bf16[256,384]{1,0:T(8,128)(2,1)}, bf16[256,384]{1,0:T(8,128)(2,1)}, bf16[256,384]{1,0:T(8,128)(2,1)}, /*index=5*/bf16[256,384]{1,0:T(8,128)(2,1)}) custom-call(s32[8]{0:T(128)} %fusion.16.place_ref, s32[4]{0:T(128)} %and_select_fusion.first_ref, ...), custom_call_target="tpu_custom_call" | custom-call | flops 1610612736 | bytes 3145728 | tf_op jit(solution)/shard_map/attend/pallas_call | solution.py:456
  95.5 7.7 %collective-permute-done.16 = bf16[264,1536]{1,0:T(8,128)(2,1)} collective-permute-done((bf16[264,1536]{1,0:T(8,128)(2,1)S(1)}, bf16[264,1536]{1,0:T(8,128)(2,1)}, u32[]{:S(2)}, u32[]{:S(2)}) %collective-permute-start.16) | collective-permute-done | bytes 811040 | tf_op jit(solution)/shard_map/ppermute | solution.py:85
  118.0 6.7 %collective-permute-done.20 = bf16[264,1536]{1,0:T(8,128)(2,1)S(1)} collective-permute-done((bf16[264,1536]{1,0:T(8,128)(2,1)S(1)}, bf16[264,1536]{1,0:T(8,128)(2,1)S(1)}, u32[]{:S(2)}, u32[]{:S(2)}) %collective-permute-start.20) | collective-permute-done | bytes 811040 | tf_op jit(solution)/shard_map/ppermute | solution.py:85
  127.4 8.1 %project_out.1 = (bf16[256,1536]{1,0:T(8,128)(2,1)}, bf16[256,16]{1,0:T(8,128)(2,1)}, f32[256,1536]{1,0:T(8,128)}, bf16[256,1536]{1,0:T(8,128)(2,1)}) custom-call(s32[20]{0:T(128)} %concatenate.17.info_ref.ids_ref, bf16[256,1536]{1,0:T(8,128)(2,1)} %bitcast.44, f32[1,1536]{1,0:T(1,128)} %broadcast_in_dim.23.gain_ref.refs_7_, bf16[8,16,1536]{2,1,0:T(8,128)(2,1)} %bitcast.48, ...), custom_call_target="tpu_custom_call" | custom-call | flops 1207959552 | bytes 9437184 | tf_op jit(solution)/shard_map/project_out/pallas_call | solution.py:835
  142.4 13.7 %experts.5 = (bf16[256,1536]{1,0:T(8,128)(2,1)}, bf16[296,1536]{1,0:T(8,128)(2,1)}) custom-call(s32[20]{0:T(128)} %concatenate.17.info_ref.ids_ref, bf16[256,1536]{1,0:T(8,128)(2,1)} %get-tuple-element.239.refs_0_.refs_6_, bf16[264,1536]{1,0:T(8,128)(2,1)} %copy-done.5, bf16[2,1536,1024]{2,1,0:T(8,128)(2,1)} %refs_2_.3, bf16[2,512,1536]{2,1,0:T(8,128)(2,1)} %refs_3_.3, ...), custom_call_target="tpu_custom_call" | custom-call | flops 3221225472 | bytes 12582912 | tf_op jit(solution)/shard_map/experts/pallas_call | solution.py:722
  163.6 16.3 %experts.6 = (bf16[256,1536]{1,0:T(8,128)(2,1)}, bf16[256,1536]{1,0:T(8,128)(2,1)}, bf16[296,1536]{1,0:T(8,128)(2,1)}, bf16[296,1536]{1,0:T(8,128)(2,1)}) custom-call(s32[20]{0:T(128)} %concatenate.17.info_ref.ids_ref, bf16[256,1536]{1,0:T(8,128)(2,1)} %copy-done.57, bf16[256,1536]{1,0:T(8,128)(2,1)} %collective-permute-done.26.refs_1_, ...), custom_call_target="tpu_custom_call" | custom-call | flops 6442450944 | bytes 15728640 | tf_op jit(solution)/shard_map/experts/pallas_call | solution.py:722
  183.2 16.1 %experts.7 = (bf16[256,1536]{1,0:T(8,128)(2,1)}, bf16[256,1536]{1,0:T(8,128)(2,1)}, bf16[296,1536]{1,0:T(8,128)(2,1)}, bf16[296,1536]{1,0:T(8,128)(2,1)}) custom-call(s32[20]{0:T(128)} %concatenate.17.info_ref.ids_ref, bf16[256,1536]{1,0:T(8,128)(2,1)} %collective-permute-done.32.refs_0_, bf16[256,1536]{1,0:T(8,128)(2,1)} %copy-done.35, ...), custom_call_target="tpu_custom_call" | custom-call | flops 6442450944 | bytes 15728640 | tf_op jit(solution)/shard_map/experts/pallas_call | solution.py:722
  202.5 16.1 %experts.8 = (bf16[256,1536]{1,0:T(8,128)(2,1)}, bf16[256,1536]{1,0:T(8,128)(2,1)}, bf16[296,1536]{1,0:T(8,128)(2,1)}, bf16[296,1536]{1,0:T(8,128)(2,1)}) custom-call(s32[20]{0:T(128)} %concatenate.17.info_ref.ids_ref, bf16[256,1536]{1,0:T(8,128)(2,1)} %copy-done.58, bf16[256,1536]{1,0:T(8,128)(2,1)} %copy-done.36, ...), custom_call_target="tpu_custom_call" | custom-call | flops 6442450944 | bytes 15728640 | tf_op jit(solution)/shard_map/experts/pallas_call | solution.py:722
  221.8 13.8 %experts.9 = (bf16[256,1536]{1,0:T(8,128)(2,1)}, bf16[296,1536]{1,0:T(8,128)(2,1)}) custom-call(s32[20]{0:T(128)} %concatenate.17.info_ref.ids_ref, bf16[256,1536]{1,0:T(8,128)(2,1)} %copy-done.29, bf16[264,1536]{1,0:T(8,128)(2,1)} %copy-done.27, bf16[2,1536,1024]{2,1,0:T(8,128)(2,1)} %refs_2_.3, bf16[2,512,1536]{2,1,0:T(8,128)(2,1)} %refs_3_.3, ...), custom_call_target="tpu_custom_call" | custom-call | flops 3221225472 | bytes 12582912 | tf_op jit(solution)/shard_map/experts/pallas_call | solution.py:722
  239.5 21.3 %collective-permute-done.37 = bf16[296,1536]{1,0:T(8,128)(2,1)S(1)} collective-permute-done((bf16[296,1536]{1,0:T(8,128)(2,1)}, bf16[296,1536]{1,0:T(8,128)(2,1)S(1)}, u32[]{:S(2)}, u32[]{:S(2)}) %collective-permute-start.37) | collective-permute-done | bytes 909344 | tf_op jit(solution)/shard_map/ppermute | solution.py:61
  261.0 6.3 %collective-permute-start.38 = (bf16[296,1536]{1,0:T(8,128)(2,1)S(1)}, bf16[296,1536]{1,0:T(8,128)(2,1)S(1)}, u32[]{:S(2)}, u32[]{:S(2)}) collective-permute-start(bf16[296,1536]{1,0:T(8,128)(2,1)S(1)} %add_convert_fusion.3), channel_id=1, source_target_pairs={{0,8},{4,12},{24,16},{28,20},{1,9},{5,13},{25,17},{29,21},{2,10},{... | collective-permute-start | bytes 2727944 | tf_op jit(solution)/shard_map/ppermute | solution.py:85
  268.0 12.3 %collective-permute-done.39 = bf16[296,1536]{1,0:T(8,128)(2,1)S(1)} collective-permute-done((bf16[296,1536]{1,0:T(8,128)(2,1)}, bf16[296,1536]{1,0:T(8,128)(2,1)S(1)}, u32[]{:S(2)}, u32[]{:S(2)}) %collective-permute-start.39) | collective-permute-done | bytes 909344 | tf_op jit(solution)/shard_map/ppermute | solution.py:61
  293.3 10.0 %collective-permute-done.40 = bf16[296,1536]{1,0:T(8,128)(2,1)S(1)} collective-permute-done((bf16[296,1536]{1,0:T(8,128)(2,1)S(1)}, bf16[296,1536]{1,0:T(8,128)(2,1)S(1)}, u32[]{:S(2)}, u32[]{:S(2)}) %collective-permute-start.40) | collective-permute-done | bytes 909344 | tf_op jit(solution)/shard_map/ppermute | solution.py:85
  304.7 8.3 %collective-permute-start.44 = (bf16[296,1536]{1,0:T(8,128)(2,1)S(1)}, bf16[296,1536]{1,0:T(8,128)(2,1)S(1)}, u32[]{:S(2)}, u32[]{:S(2)}) collective-permute-start(bf16[296,1536]{1,0:T(8,128)(2,1)S(1)} %add_convert_fusion.1), channel_id=1, source_target_pairs={{0,8},{4,12},{8,0},{12,4},{16,24},{20,28},{24,16},{28,20},{1,9},{5... | collective-permute-start | bytes 2727944 | tf_op jit(solution)/shard_map/ppermute | solution.py:61
  315.0 9.3 %collective-permute-done.44.refs_1_ = bf16[296,1536]{1,0:T(8,128)(2,1)S(1)} collective-permute-done((bf16[296,1536]{1,0:T(8,128)(2,1)S(1)}, bf16[296,1536]{1,0:T(8,128)(2,1)S(1)}, u32[]{:S(2)}, u32[]{:S(2)}) %collective-permute-start.44) | collective-permute-done | bytes 909344 | tf_op jit(solution)/shard_map/ppermute | solution.py:61
  325.1 11.5 %middle_back.1 = (f32[256,1536]{1,0:T(8,128)}, bf16[256,384]{1,0:T(8,128)(2,1)}, bf16[256,384]{1,0:T(8,128)(2,1)}, bf16[256,384]{1,0:T(8,128)(2,1)}, bf16[256,38...) custom-call(s32[20]{0:T(128)} %concatenate.17.info_ref.ids_ref, ...), custom_call_target="tpu_custom_call" | custom-call | flops 1207959552 | bytes 12582912 | tf_op jit(solution)/shard_map/middle_back/pallas_call | solution.py:916
  358.2 16.9 %attend_back.1.dqkv_ref = bf16[1024,640]{1,0:T(8,128)(2,1)} custom-call(s32[8]{0:T(128)} %fusion.16.place_ref, s32[4]{0:T(128)} %and_select_fusion.first_ref, bf16[1024,640]{1,0:T(8,128)(2,1)} %get-tuple-element.213.qkv_ref, s32[1,1024]{1,0:T(1,128)} %bitcast.64, bf16[1024,384]{1,0:T(8,128)(2,1)} %get-tuple-element.310.o_ref, ...), custom_call_target="tpu_custom_call" | custom-call | flops 4026531840 | bytes 6291456 | tf_op jit(solution)/shard_map/attend_back/pallas_call | solution.py:562
  388.8 8.3 %inputs_back.1 = (bf16[256,1536]{1,0:T(8,128)(2,1)}, bf16[256,1536]{1,0:T(8,128)(2,1)}, bf16[256,1536]{1,0:T(8,128)(2,1)}, bf16[256,1536]{1,0:T(8,128)(2,1)}) custom-call(s32[20]{0:T(128)} %concatenate.17.info_ref.ids_ref, bf16[1024,640]{1,0:T(8,128)(2,1)} %attend_back.1.dqkv_ref, bf16[1024,48]{1,0:T(8,128)(2,1)} %get-tuple-element.331.rank_ref, ...), custom_call_target="tpu_custom_call" | custom-call | flops 2013265920 | bytes 8912896 | tf_op jit(solution)/shard_map/inputs_back/pallas_call | solution.py:1028
  397.1 8.0 %collective-permute-done.55 = bf16[256,1536]{1,0:T(8,128)(2,1)S(1)} collective-permute-done((bf16[256,1536]{1,0:T(8,128)(2,1)S(1)}, bf16[256,1536]{1,0:T(8,128)(2,1)S(1)}, u32[]{:S(2)}, u32[]{:S(2)}) %collective-permute-start.55) | collective-permute-done | bytes 786464 | tf_op jit(solution)/shard_map/ppermute | solution.py:61
  422.8 7.3 %collective-permute-done.65 = bf16[16,8192]{1,0:T(8,128)(2,1)S(1)} collective-permute-done((bf16[16,8192]{1,0:T(8,128)(2,1)S(1)}, bf16[16,8192]{1,0:T(8,128)(2,1)S(1)}, u32[]{:S(2)}, u32[]{:S(2)}) %collective-permute-start.65) | collective-permute-done | bytes 262176 | tf_op jit(solution)/shard_map/ppermute | solution.py:85
  454.5 6.5 %place_grads.1 = (f32[8,16,2560]{2,1,0:T(8,128)}, f32[8,48,1536]{2,1,0:T(8,128)}, f32[8,2,16,512]{3,2,1,0:T(8,128)}, f32[8,16,512]{2,1,0:T(8,128)}, f32[8,16,153...) custom-call(s32[20]{0:T(128)} %concatenate.17.info_ref.ids_ref, ...), custom_call_target="tpu_custom_call" | custom-call | tf_op jit(solution)/shard_map/place_grads/pallas_call | solution.py:1084
  (332 shorter events, 197.3 us)
Async XLA Ops:
  8.6 25.3 %collective-permute-start.6 = (bf16[256,1536]{1,0:T(8,128)(2,1)}, bf16[256,1536]{1,0:T(8,128)(2,1)S(1)}, u32[]{:S(2)}, u32[]{:S(2)}) collective-permute-start(bf16[256,1536]{1,0:T(8,128)(2,1)} %bitcast.42), channel_id=1, source_target_pairs={{0,2},{1,3},{2,0},{3,1},{4,6},{5,7},{6,4},{7,5},{8,10},{9,11},{10,... | collective-permute-start | bytes 2359304 | tf_op jit(solution)/shard_map/ppermute | solution.py:61
  10.1 23.8 %collective-permute-start.7 = (bf16[256,1536]{1,0:T(8,128)(2,1)}, bf16[256,1536]{1,0:T(8,128)(2,1)}, u32[]{:S(2)}, u32[]{:S(2)}) collective-permute-start(bf16[256,1536]{1,0:T(8,128)(2,1)} %bitcast.43), channel_id=1, source_target_pairs={{0,1},{1,0},{2,3},{3,2},{4,5},{5,4},{6,7},{7,6},{8,9},{9,8},{10,11... | collective-permute-start | bytes 2359304 | tf_op jit(solution)/shard_map/ppermute | solution.py:61
  52.7 25.5 %collective-permute-start.11 = (bf16[264,1536]{1,0:T(8,128)(2,1)S(1)}, bf16[264,1536]{1,0:T(8,128)(2,1)}, u32[]{:S(2)}, u32[]{:S(2)}) collective-permute-start(bf16[264,1536]{1,0:T(8,128)(2,1)S(1)} %pad_maximum_fusion.1.refs_1_.refs_4_), channel_id=1, source_target_pairs={{0,8},{4,12},{8,0},{12,4},{16,24},{20,28},{24,16},{28,20},{1,9},{5... | collective-permute-start | bytes 2433032 | tf_op jit(solution)/shard_map/ppermute | solution.py:61
  54.5 23.6 %collective-permute-start.12 = (bf16[264,1536]{1,0:T(8,128)(2,1)S(1)}, bf16[264,1536]{1,0:T(8,128)(2,1)S(1)}, u32[]{:S(2)}, u32[]{:S(2)}) collective-permute-start(bf16[264,1536]{1,0:T(8,128)(2,1)S(1)} %pad_maximum_fusion.1.refs_1_.refs_4_), channel_id=1, source_target_pairs={{8,16},{12,20},{16,8},{20,12},{9,17},{13,21},{17,9},{21,13},{10,18... | collective-permute-start | bytes 2433032 | tf_op jit(solution)/shard_map/ppermute | solution.py:85
  55.3 25.1 %collective-permute-start.13 = (bf16[264,1536]{1,0:T(8,128)(2,1)S(1)}, bf16[264,1536]{1,0:T(8,128)(2,1)}, u32[]{:S(2)}, u32[]{:S(2)}) collective-permute-start(bf16[264,1536]{1,0:T(8,128)(2,1)S(1)} %pad_maximum_fusion.1.refs_1_.refs_4_), channel_id=1, source_target_pairs={{0,4},{4,0},{8,12},{12,8},{16,20},{20,16},{24,28},{28,24},{1,5},{5... | collective-permute-start | bytes 2433032 | tf_op jit(solution)/shard_map/ppermute | solution.py:61
  67.9 27.5 %collective-permute-start.18 = (bf16[1536,384]{1,0:T(8,128)(2,1)}, bf16[1536,384]{1,0:T(8,128)(2,1)S(1)}, u32[]{:S(2)}, u32[]{:S(2)}) collective-permute-start(bf16[1536,384]{1,0:T(8,128)(2,1)} %order_rows.1.refs_4_.refs_13_), channel_id=1, source_target_pairs={{0,2},{1,3},{2,0},{3,1},{4,6},{5,7},{6,4},{7,5},{8,10},{9,11},{10,... | collective-permute-start | bytes 3538952 | tf_op jit(solution)/shard_map/ppermute | solution.py:61
  69.4 26.0 %collective-permute-start.19 = (bf16[1536,384]{1,0:T(8,128)(2,1)}, bf16[1536,384]{1,0:T(8,128)(2,1)}, u32[]{:S(2)}, u32[]{:S(2)}) collective-permute-start(bf16[1536,384]{1,0:T(8,128)(2,1)} %order_rows.1.refs_4_.refs_13_), channel_id=1, source_target_pairs={{0,1},{1,0},{2,3},{3,2},{4,5},{5,4},{6,7},{7,6},{8,9},{9,8},{10,11... | collective-permute-start | bytes 3538952 | tf_op jit(solution)/shard_map/ppermute | solution.py:61
  82.0 21.3 %collective-permute-start.16 = (bf16[264,1536]{1,0:T(8,128)(2,1)S(1)}, bf16[264,1536]{1,0:T(8,128)(2,1)}, u32[]{:S(2)}, u32[]{:S(2)}) collective-permute-start(bf16[264,1536]{1,0:T(8,128)(2,1)S(1)} %collective-permute-done.12), channel_id=1, source_target_pairs={{8,0},{12,4},{16,24},{20,28},{9,1},{13,5},{17,25},{21,29},{10,2},{... | collective-permute-start | bytes 2433032 | tf_op jit(solution)/shard_map/ppermute | solution.py:85
  95.5 30.9 %collective-permute-start.25 = (bf16[1536,384]{1,0:T(8,128)(2,1)S(1)}, bf16[1536,384]{1,0:T(8,128)(2,1)S(1)}, u32[]{:S(2)}, u32[]{:S(2)}) collective-permute-start(bf16[1536,384]{1,0:T(8,128)(2,1)S(1)} %collective-permute-done.18.refs_6_.refs_15_), channel_id=1, source_target_pairs={{0,1},{1,0},{2,3},{3,2},{4,5},{5,4},{6,7},{7,6},{8,9},{9,8},{10,11... | collective-permute-start | bytes 3538952 | tf_op jit(solution)/shard_map/ppermute | solution.py:61
  125.9 30.2 %collective-permute-start.29 = (bf16[264,1536]{1,0:T(8,128)(2,1)}, bf16[264,1536]{1,0:T(8,128)(2,1)S(1)}, u32[]{:S(2)}, u32[]{:S(2)}) collective-permute-start(bf16[264,1536]{1,0:T(8,128)(2,1)} %add.206.refs_3_), channel_id=1, source_target_pairs={{0,4},{4,0},{8,12},{12,8},{16,20},{20,16},{24,28},{28,24},{1,5},{5... | collective-permute-start | bytes 2433032 | tf_op jit(solution)/shard_map/ppermute | solution.py:61
  135.5 20.6 %collective-permute-start.26 = (bf16[256,1536]{1,0:T(8,128)(2,1)}, bf16[256,1536]{1,0:T(8,128)(2,1)}, u32[]{:S(2)}, u32[]{:S(2)}) collective-permute-start(bf16[256,1536]{1,0:T(8,128)(2,1)} %get-tuple-element.239.refs_0_.refs_6_), channel_id=1, source_target_pairs={{0,8},{4,12},{8,0},{12,4},{16,24},{20,28},{24,16},{28,20},{1,9},{5... | collective-permute-start | bytes 2359304 | tf_op jit(solution)/shard_map/ppermute | solution.py:61
  138.5 21.4 %collective-permute-start.28 = (bf16[256,1536]{1,0:T(8,128)(2,1)}, bf16[256,1536]{1,0:T(8,128)(2,1)S(1)}, u32[]{:S(2)}, u32[]{:S(2)}) collective-permute-start(bf16[256,1536]{1,0:T(8,128)(2,1)} %get-tuple-element.239.refs_0_.refs_6_), channel_id=1, source_target_pairs={{0,4},{4,0},{8,12},{12,8},{16,20},{20,16},{24,28},{28,24},{1,5},{5... | collective-permute-start | bytes 2359304 | tf_op jit(solution)/shard_map/ppermute | solution.py:61
  200.4 20.5 %collective-permute-start.35 = (bf16[256,1536]{1,0:T(8,128)(2,1)S(1)}, bf16[256,1536]{1,0:T(8,128)(2,1)S(1)}, u32[]{:S(2)}, u32[]{:S(2)}) collective-permute-start(bf16[256,1536]{1,0:T(8,128)(2,1)S(1)} %add.208.refs_1_), channel_id=1, source_target_pairs={{0,4},{4,0},{8,12},{12,8},{16,20},{20,16},{24,28},{28,24},{1,5},{5... | collective-permute-start | bytes 2359304 | tf_op jit(solution)/shard_map/ppermute | solution.py:61
  201.5 36.0 %collective-permute-start.36 = (bf16[296,1536]{1,0:T(8,128)(2,1)}, bf16[296,1536]{1,0:T(8,128)(2,1)S(1)}, u32[]{:S(2)}, u32[]{:S(2)}) collective-permute-start(bf16[296,1536]{1,0:T(8,128)(2,1)} %get-tuple-element.272), channel_id=1, source_target_pairs={{0,4},{4,0},{8,12},{12,8},{16,20},{20,16},{24,28},{28,24},{1,5},{5... | collective-permute-start | bytes 2727944 | tf_op jit(solution)/shard_map/ppermute | solution.py:61
  237.5 23.3 %collective-permute-start.37 = (bf16[296,1536]{1,0:T(8,128)(2,1)}, bf16[296,1536]{1,0:T(8,128)(2,1)S(1)}, u32[]{:S(2)}, u32[]{:S(2)}) collective-permute-start(bf16[296,1536]{1,0:T(8,128)(2,1)} %get-tuple-element.273), channel_id=1, source_target_pairs={{0,4},{4,0},{8,12},{12,8},{16,20},{20,16},{24,28},{28,24},{1,5},{5... | collective-permute-start | bytes 2727944 | tf_op jit(solution)/shard_map/ppermute | solution.py:61
  237.8 42.4 %collective-permute-start.39 = (bf16[296,1536]{1,0:T(8,128)(2,1)}, bf16[296,1536]{1,0:T(8,128)(2,1)S(1)}, u32[]{:S(2)}, u32[]{:S(2)}) collective-permute-start(bf16[296,1536]{1,0:T(8,128)(2,1)} %get-tuple-element.274), channel_id=1, source_target_pairs={{0,4},{4,0},{8,12},{12,8},{16,20},{20,16},{24,28},{28,24},{1,5},{5... | collective-permute-start | bytes 2727944 | tf_op jit(solution)/shard_map/ppermute | solution.py:61
  261.0 21.8 %collective-permute-start.38 = (bf16[296,1536]{1,0:T(8,128)(2,1)S(1)}, bf16[296,1536]{1,0:T(8,128)(2,1)S(1)}, u32[]{:S(2)}, u32[]{:S(2)}) collective-permute-start(bf16[296,1536]{1,0:T(8,128)(2,1)S(1)} %add_convert_fusion.3), channel_id=1, source_target_pairs={{0,8},{4,12},{24,16},{28,20},{1,9},{5,13},{25,17},{29,21},{2,10},{... | collective-permute-start | bytes 2727944 | tf_op jit(solution)/shard_map/ppermute | solution.py:85
  267.3 26.0 %collective-permute-start.42 = (bf16[296,1536]{1,0:T(8,128)(2,1)S(1)}, bf16[296,1536]{1,0:T(8,128)(2,1)S(1)}, u32[]{:S(2)}, u32[]{:S(2)}) collective-permute-start(bf16[296,1536]{1,0:T(8,128)(2,1)S(1)} %copy-done.56), channel_id=1, source_target_pairs={{0,4},{4,0},{8,12},{12,8},{16,20},{20,16},{24,28},{28,24},{1,5},{5... | collective-permute-start | bytes 2727944 | tf_op jit(solution)/shard_map/ppermute | solution.py:61
  283.1 20.2 %collective-permute-start.40 = (bf16[296,1536]{1,0:T(8,128)(2,1)S(1)}, bf16[296,1536]{1,0:T(8,128)(2,1)S(1)}, u32[]{:S(2)}, u32[]{:S(2)}) collective-permute-start(bf16[296,1536]{1,0:T(8,128)(2,1)S(1)} %add_convert_fusion.2), channel_id=1, source_target_pairs={{0,8},{4,12},{24,16},{28,20},{1,9},{5,13},{25,17},{29,21},{2,10},{... | collective-permute-start | bytes 2727944 | tf_op jit(solution)/shard_map/ppermute | solution.py:85
  312.9 23.8 %collective-permute-start.43 = (bf16[256,1536]{1,0:T(8,128)(2,1)}, bf16[256,1536]{1,0:T(8,128)(2,1)}, u32[]{:S(2)}, u32[]{:S(2)}) collective-permute-start(bf16[256,1536]{1,0:T(8,128)(2,1)} %get-tuple-element.288), channel_id=1, source_target_pairs={{0,4},{4,0},{8,12},{12,8},{16,20},{20,16},{24,28},{28,24},{1,5},{5... | collective-permute-start | bytes 2359304 | tf_op jit(solution)/shard_map/ppermute | solution.py:61
  312.9 31.2 %collective-permute-start.47 = (bf16[256,1536]{1,0:T(8,128)(2,1)}, bf16[256,1536]{1,0:T(8,128)(2,1)S(1)}, u32[]{:S(2)}, u32[]{:S(2)}) collective-permute-start(bf16[256,1536]{1,0:T(8,128)(2,1)} %get-tuple-element.302), channel_id=1, source_target_pairs={{0,4},{4,0},{8,12},{12,8},{16,20},{20,16},{24,28},{28,24},{1,5},{5... | collective-permute-start | bytes 2359304 | tf_op jit(solution)/shard_map/ppermute | solution.py:61
  344.1 31.1 %collective-permute-start.53 = (bf16[256,1536]{1,0:T(8,128)(2,1)}, bf16[256,1536]{1,0:T(8,128)(2,1)S(1)}, u32[]{:S(2)}, u32[]{:S(2)}) collective-permute-start(bf16[256,1536]{1,0:T(8,128)(2,1)} %get-tuple-element.309), channel_id=1, source_target_pairs={{0,4},{4,0},{8,12},{12,8},{16,20},{20,16},{24,28},{28,24},{1,5},{5... | collective-permute-start | bytes 2359304 | tf_op jit(solution)/shard_map/ppermute | solution.py:61
  358.1 38.9 %collective-permute-start.57 = (bf16[256,1536]{1,0:T(8,128)(2,1)}, bf16[256,1536]{1,0:T(8,128)(2,1)}, u32[]{:S(2)}, u32[]{:S(2)}) collective-permute-start(bf16[256,1536]{1,0:T(8,128)(2,1)} %get-tuple-element.330), channel_id=1, source_target_pairs={{0,4},{4,0},{8,12},{12,8},{16,20},{20,16},{24,28},{28,24},{1,5},{5... | collective-permute-start | bytes 2359304 | tf_op jit(solution)/shard_map/ppermute | solution.py:61
  383.1 22.0 %collective-permute-start.55 = (bf16[256,1536]{1,0:T(8,128)(2,1)S(1)}, bf16[256,1536]{1,0:T(8,128)(2,1)S(1)}, u32[]{:S(2)}, u32[]{:S(2)}) collective-permute-start(bf16[256,1536]{1,0:T(8,128)(2,1)S(1)} %add_convert_fusion.8), channel_id=1, source_target_pairs={{0,8},{4,12},{8,0},{12,4},{16,24},{20,28},{24,16},{28,20},{1,9},{5... | collective-permute-start | bytes 2359304 | tf_op jit(solution)/shard_map/ppermute | solution.py:61
  (116 other events, 1390.4 us)
